TPU v7x, 512 devices: a whole 4x4x16 slice. The times are simulated.
512 devices in a mesh: slab: 128 (over y, z, core), sub: 4 (over x).
Axes of the slice: x: 4, y: 4, z: 16, core: 2. Of those that a mesh axis runs over, the one named last changes fastest.
Arguments:
- right_side: float32 [4, 524288], P(None, ('slab', 'sub')), may hold values from -6 to 6
- warm_start: float32 [4, 524288], P(None, ('slab', 'sub')), may hold values from -6 to 6
- fine_blocks: float32 [8192, 3, 4096], P(('slab', 'sub')), may hold values from -0.6 to 1.25, as said below
- fine_columns: int32 [8192, 3], P(('slab', 'sub')), may hold values from 0 to 8191, as said below
- fine_prolong: float32 [8192, 2, 4096], P(('slab', 'sub')), may hold values from -0.1875 to 0.1875
- owner_rows: int32 [8192, 2], P(('slab', 'sub')), may hold values from 0 to 1023, as said below
- send_slots: int32 [8192, 2], P(('slab', 'sub')), may hold values from 0 to 1, as said below
- receive_rows: int32 [128, 4, 128, 2], P('slab', 'sub'), may hold values from -1 to 7, as said below
- middle_blocks: float32 [1024, 3, 4096], P('slab'), may hold values from -0.6 to 1.25, as said below
- middle_columns: int32 [1024, 3], P('slab'), may hold values from 0 to 1023, as said below
- middle_prolong: float32 [1024, 4096], P('slab'), may hold values from -0.375 to 0.375
- coarse_blocks: float32 [256, 3, 4096], P('slab'), may hold values from -0.6 to 1.25, as said below
- coarse_columns: int32 [256, 3], P('slab'), may hold values from 0 to 255, as said below
Outputs:
- solution: float32 [4, 524288], P(None, ('slab', 'sub'))
- residual: float32 [4, 524288], P(None, ('slab', 'sub'))
Inputs may be any that keep to these rules, and one draw needn't show every extreme that they name: `fine_columns`: column 0 of each row is the row itself; every other column lies within 8 rows of it, inside the level. `middle_columns`: column 0 of each row is the row itself; every other column lies within 2 rows of it, inside the level. `coarse_columns`: column 0 of each row is the row itself; every other column lies within 1 row of it, inside the level. The owner of a block is owner_rows // 8; receive_rows[o, u, s, c] equals owner_rows % 8 of the block of device s * 4 + u that sits in slot c for owner o. `send_slots`: the blocks of one device occupy distinct pairs (owner, slot); one owner gets all 2 slots from every device. `receive_rows`: -1 marks a slot that no block of that device fills. `fine_blocks`: the diagonal entries of slot 0's block lie in 0.8 to 1.25. `middle_blocks`: the diagonal entries of slot 0's block lie in 0.8 to 1.25. `coarse_blocks`: the diagonal entries of slot 0's block lie in 0.8 to 1.25.
All inputs are finite; a program needn't handle non-finite values.
Results may differ from a plain program's by a relative error of at most 0.0003.
Values sent between devices are 32-bit elements; how exact they have to be, the bound alone decides.
No kernel may reach another device: no remote copies, remote signals or barrier semaphores. Data moves between devices by JAX's collectives and lax.ppermute only.
A program may use at most 64 MiB of HBM per device.

v0:
```python
import jax
import jax.numpy as jnp
from jax import lax
from jax.sharding import PartitionSpec as P

BS = 64
R1 = 8
H0 = 8
H1 = 2
H2 = 1
NRHS = 4
DEG0 = 3
DEG1 = 3
DEG2 = 4


LOWER_EDGE = 0.3
UPPER_EDGE = 2.2


def extended(block, sides, width):
    for axis, dim in sides:
        count = lax.axis_size(axis)
        forward = [(i, i + 1) for i in range(count - 1)]
        backward = [(target, source) for source, target in forward]
        low = lax.ppermute(
            lax.slice_in_dim(block, block.shape[dim] - width, None, axis=dim), axis, forward
        )
        high = lax.ppermute(lax.slice_in_dim(block, 0, width, axis=dim), axis, backward)
        block = jnp.concatenate([low, block, high], axis=dim)
    return block


def swapped(shard, axis, apart):
    return lax.ppermute(shard, axis, [(i, i ^ 1 << apart) for i in range(lax.axis_size(axis))])


def chebyshev(operate, inverse, solution, residual, degree, need_residual):
    center = 0.5 * (UPPER_EDGE + LOWER_EDGE)
    half_width = 0.5 * (UPPER_EDGE - LOWER_EDGE)
    scaled = center / half_width
    factor = 1.0 / scaled
    direction = inverse * residual / center
    for iteration in range(degree):
        solution = solution + direction
        if iteration < degree - 1 or need_residual:
            residual = residual - operate(direction)
        if iteration < degree - 1:
            factor_next = 1.0 / (2.0 * scaled - factor)
            direction = factor_next * factor * direction + 2.0 * factor_next / half_width * (
                inverse * residual
            )
            factor = factor_next
    return (solution, residual)


def block_matrices(blocks):
    return blocks.reshape(blocks.shape[0], blocks.shape[1], BS, BS)


def local_apply(matrices, columns, values, first_row, rim_rows, extend):
    rhs_count, row_count, block_size = values.shape
    widened = extend(values.reshape(rhs_count, row_count * block_size), rim_rows)
    widened = widened.reshape(rhs_count, row_count + 2 * rim_rows, block_size)
    local_columns = columns - first_row + rim_rows
    picked = widened[:, local_columns]
    return jnp.einsum("ikab,rikb->ria", matrices, picked, precision=lax.Precision.HIGHEST)


def fine_extend(flat, rim_rows):
    return extended(flat, ((("slab", "sub"), 1),), rim_rows * BS)


def coarse_extend(flat, rim_rows):
    return extended(flat, (("slab", 1),), rim_rows * BS)


def to_rows(values):
    return values.transpose(1, 0, 2).reshape(values.shape[1], values.shape[0] * values.shape[2])


def body(
    right_side,
    warm_start,
    fine_blocks,
    fine_columns,
    fine_prolong,
    owner_rows,
    send_slots,
    receive_rows,
    middle_blocks,
    middle_columns,
    middle_prolong,
    coarse_blocks,
    coarse_columns,
):
    fine_count = fine_columns.shape[0]
    middle_count = middle_columns.shape[0]
    coarse_count = coarse_columns.shape[0]
    ratio_rows = middle_count // coarse_count
    slab_count = lax.axis_size("slab")
    capacity = receive_rows.shape[3]
    slot_total = slab_count * capacity
    line_width = NRHS * BS
    fine_mats = block_matrices(fine_blocks)
    middle_mats_all = block_matrices(middle_blocks)
    coarse_mats = block_matrices(coarse_blocks)
    fine_first = lax.axis_index(("slab", "sub")) * fine_count
    middle_first = lax.axis_index("slab") * middle_count
    coarse_first = lax.axis_index("slab") * coarse_count

    def fine_apply(values):
        return local_apply(fine_mats, fine_columns, values, fine_first, H0, fine_extend)

    def middle_apply(values):
        return local_apply(middle_mats_all, middle_columns, values, middle_first, H1, coarse_extend)

    def coarse_apply(values):
        return local_apply(coarse_mats, coarse_columns, values, coarse_first, H2, coarse_extend)

    fine_inverse = 1.0 / jnp.diagonal(fine_mats[:, 0], axis1=1, axis2=2)
    middle_inverse = 1.0 / jnp.diagonal(middle_mats_all[:, 0], axis1=1, axis2=2)
    coarse_inverse = 1.0 / jnp.diagonal(coarse_mats[:, 0], axis1=1, axis2=2)
    target = right_side.reshape(NRHS, fine_count, BS)
    solution = warm_start.reshape(NRHS, fine_count, BS)
    residual = target - fine_apply(solution)
    solution, residual = chebyshev(fine_apply, fine_inverse, solution, residual, DEG0, True)
    prolong = fine_prolong.reshape(fine_count, 2, BS, BS)
    pieces = jnp.einsum("ieab,ria->ierb", prolong, residual, precision=lax.Precision.HIGHEST)
    pieces = pieces.reshape(2 * fine_count, line_width)
    position = (owner_rows // R1 * capacity + send_slots).reshape(2 * fine_count)
    send_table = (position[None, :] == jnp.arange(slot_total, dtype=jnp.int32)[:, None]).astype(
        jnp.float32
    )
    outgoing = jnp.dot(
        send_table, pieces, precision=lax.Precision.HIGHEST, preferred_element_type=jnp.float32
    )
    incoming = lax.all_to_all(
        outgoing.reshape(slab_count, capacity, line_width),
        "slab",
        split_axis=0,
        concat_axis=0,
        tiled=True,
    )
    rows_here = receive_rows.reshape(slot_total)
    receive_table = (
        rows_here[None, :] == jnp.arange(middle_count, dtype=jnp.int32)[:, None]
    ).astype(jnp.float32)
    partial_value = jnp.dot(
        receive_table,
        incoming.reshape(slot_total, line_width),
        precision=lax.Precision.HIGHEST,
        preferred_element_type=jnp.float32,
    )
    for bit_number in range(lax.axis_size("sub").bit_length() - 1):
        partial_value = partial_value + swapped(partial_value, "sub", bit_number)
    middle_rhs = partial_value.reshape(middle_count, NRHS, BS).transpose(1, 0, 2)
    middle_zero = jnp.zeros_like(middle_rhs)
    middle_solution, middle_residual = chebyshev(
        middle_apply, middle_inverse, middle_zero, middle_rhs, DEG1, True
    )
    middle_mats = middle_prolong.reshape(middle_count, BS, BS)
    lifted = jnp.einsum(
        "iab,ria->rib", middle_mats, middle_residual, precision=lax.Precision.HIGHEST
    )
    coarse_rhs = lifted.reshape(NRHS, coarse_count, ratio_rows, BS).sum(axis=2)
    coarse_zero = jnp.zeros_like(coarse_rhs)
    coarse_solution, unused = chebyshev(
        coarse_apply, coarse_inverse, coarse_zero, coarse_rhs, DEG2, False
    )
    spread = jnp.repeat(coarse_solution, ratio_rows, axis=1)
    middle_solution = middle_solution + jnp.einsum(
        "iab,rib->ria", middle_mats, spread, precision=lax.Precision.HIGHEST
    )
    middle_residual = middle_rhs - middle_apply(middle_solution)
    middle_solution, unused = chebyshev(
        middle_apply, middle_inverse, middle_solution, middle_residual, DEG1, False
    )
    rows_form = to_rows(middle_solution)
    back_out = jnp.dot(
        receive_table.T,
        rows_form,
        precision=lax.Precision.HIGHEST,
        preferred_element_type=jnp.float32,
    )
    back_in = lax.all_to_all(
        back_out.reshape(slab_count, capacity, line_width),
        "slab",
        split_axis=0,
        concat_axis=0,
        tiled=True,
    )
    per_piece = jnp.dot(
        send_table.T,
        back_in.reshape(slot_total, line_width),
        precision=lax.Precision.HIGHEST,
        preferred_element_type=jnp.float32,
    )
    per_piece = per_piece.reshape(fine_count, 2, NRHS, BS)
    solution = solution + jnp.einsum(
        "ieab,ierb->ria", prolong, per_piece, precision=lax.Precision.HIGHEST
    )
    residual = target - fine_apply(solution)
    solution, residual = chebyshev(fine_apply, fine_inverse, solution, residual, DEG0, True)
    return (solution.reshape(NRHS, fine_count * BS), residual.reshape(NRHS, fine_count * BS))


def solution(mesh):
    in_specs = (
        P(None, ("slab", "sub")),
        P(None, ("slab", "sub")),
        P(("slab", "sub"), None, None),
        P(("slab", "sub"), None),
        P(("slab", "sub"), None, None),
        P(("slab", "sub"), None),
        P(("slab", "sub"), None),
        P("slab", "sub", None, None),
        P("slab", None, None),
        P("slab", None),
        P("slab", None),
        P("slab", None, None),
        P("slab", None),
    )
    out_specs = (P(None, ("slab", "sub")), P(None, ("slab", "sub")))
    return jax.shard_map(body, mesh=mesh, in_specs=in_specs, out_specs=out_specs, check_vma=False)
```

profile of v0, /device:TPU:8, one launch (start us, length us, event | category | flops | bytes accessed | tf_op | source)
XLA Modules:
  0.0 366.1 jit_solution(17731082500813350064)
XLA Ops:
  1.3 12.9 %collective-permute-start.1 = (f32[4,512]{1,0:T(4,128)S(1)}, f32[4,512]{1,0:T(4,128)S(1)}, u32[]{:S(2)}, u32[]{:S(2)}) collective-permute-start(f32[4,512]{1,0:T(4,128)S(1)} %get-tuple-element.22), channel_id=1, source_target_pairs={{1,0},{2,1},{3,2},{4,3},{5,4},{6,5},{7,6},{8,7},{9,8},{10,9},{11,1... | collective-permute-start | bytes 24584 | tf_op jit(solution)/shard_map/ppermute | solution.py:29
  16.2 4.8 %copy.238 = f32[16,3,4096]{0,2,1:T(8,128)} copy(f32[16,3,4096]{2,0,1:T(8,128)} %param.15) | data formatting | bytes 1572864 | tf_op args[2]
  24.0 4.7 %copy.242 = f32[16,3,64,64]{3,2,1,0:T(8,128)S(1)} copy(f32[16,3,64,64]{0,3,2,1:T(8,128)} %bitcast.298) | data formatting | bytes 1572864 | tf_op jit(solution)/shard_map/reshape | solution.py:58
  31.6 7.9 %collective-permute-start.3 = (f32[4,512]{1,0:T(4,128)S(1)}, f32[4,512]{1,0:T(4,128)S(1)}, u32[]{:S(2)}, u32[]{:S(2)}) collective-permute-start(f32[4,512]{1,0:T(4,128)S(1)} %get-tuple-element.20), channel_id=1, source_target_pairs={{1,0},{2,1},{3,2},{4,3},{5,4},{6,5},{7,6},{8,7},{9,8},{10,9},{11,1... | collective-permute-start | bytes 24584 | tf_op jit(solution)/shard_map/ppermute | solution.py:29
  41.4 7.2 %collective-permute-done.2 = f32[4,512]{1,0:T(4,128)S(1)} collective-permute-done((f32[4,512]{1,0:T(4,128)S(1)}, f32[4,512]{1,0:T(4,128)S(1)}, u32[]{:S(2)}, u32[]{:S(2)}) %collective-permute-start.2) | collective-permute-done | bytes 8224 | tf_op jit(solution)/shard_map/ppermute | solution.py:26
  53.4 3.9 %collective-permute-start.4 = (f32[4,512]{1,0:T(4,128)S(1)}, f32[4,512]{1,0:T(4,128)S(1)}, u32[]{:S(2)}, u32[]{:S(2)}) collective-permute-start(f32[4,512]{1,0:T(4,128)S(1)} %get-tuple-element.17), channel_id=1, source_target_pairs={{0,1},{1,2},{2,3},{3,4},{4,5},{5,6},{6,7},{7,8},{8,9},{9,10},{10,1... | collective-permute-start | bytes 24584 | tf_op jit(solution)/shard_map/ppermute | solution.py:26
  57.4 5.2 %collective-permute-done.4 = f32[4,512]{1,0:T(4,128)S(1)} collective-permute-done((f32[4,512]{1,0:T(4,128)S(1)}, f32[4,512]{1,0:T(4,128)S(1)}, u32[]{:S(2)}, u32[]{:S(2)}) %collective-permute-start.4) | collective-permute-done | bytes 8224 | tf_op jit(solution)/shard_map/ppermute | solution.py:26
  67.3 3.9 %collective-permute-start.6 = (f32[4,512]{1,0:T(4,128)S(1)}, f32[4,512]{1,0:T(4,128)S(1)}, u32[]{:S(2)}, u32[]{:S(2)}) collective-permute-start(f32[4,512]{1,0:T(4,128)S(1)} %get-tuple-element.15), channel_id=1, source_target_pairs={{0,1},{1,2},{2,3},{3,4},{4,5},{5,6},{6,7},{7,8},{8,9},{9,10},{10,1... | collective-permute-start | bytes 24584 | tf_op jit(solution)/shard_map/ppermute | solution.py:26
  72.0 4.4 %collective-permute-done.6 = f32[4,512]{1,0:T(4,128)S(1)} collective-permute-done((f32[4,512]{1,0:T(4,128)S(1)}, f32[4,512]{1,0:T(4,128)S(1)}, u32[]{:S(2)}, u32[]{:S(2)}) %collective-permute-start.6) | collective-permute-done | bytes 8224 | tf_op jit(solution)/shard_map/ppermute | solution.py:26
  81.1 6.7 %all-to-all-start = ((f32[128,2,256]{2,1,0:T(2,128)}), f32[128,2,256]{2,1,0:T(2,128)S(1)}, u32[]{:S(2)}, u32[]{:S(2)}) async-start(f32[128,2,256]{2,1,0:T(2,128)} %copy.258), calls=%async_computation | async-start | bytes 524288 | tf_op jit(solution)/shard_map/all_to_all | solution.py:138
  88.1 4.1 %copy.250 = f32[8,3,4096]{0,2,1:T(8,128)} copy(f32[8,3,4096]{2,0,1:T(8,128)S(1)} %copy-done.1) | data formatting | bytes 786432 | tf_op args[8]
  96.9 4.0 %copy.266 = f32[2,3,4096]{0,2,1:T(8,128)} copy(f32[2,3,4096]{2,0,1:T(2,128)S(1)} %copy-done.13) | data formatting | bytes 196608 | tf_op args[11]
  104.0 6.3 %all-to-all-done = f32[128,2,256]{2,1,0:T(2,128)S(1)} async-done(((f32[128,2,256]{2,1,0:T(2,128)}), f32[128,2,256]{2,1,0:T(2,128)S(1)}, u32[]{:S(2)}, u32[]{:S(2)}) %all-to-all-start) | async-done | bytes 262176 | tf_op jit(solution)/shard_map/all_to_all | solution.py:138
  118.5 4.9 %collective-permute-done.9 = f32[8,256]{1,0:T(8,128)S(1)} collective-permute-done((f32[8,256]{1,0:T(8,128)S(1)}, f32[8,256]{1,0:T(8,128)S(1)}, u32[]{:S(2)}, u32[]{:S(2)}) %collective-permute-start.9) | collective-permute-done | bytes 8224 | tf_op jit(solution)/shard_map/ppermute | solution.py:35
  127.9 4.4 %copy.262 = f32[8,3,64,64]{3,2,1,0:T(8,128)S(1)} copy(f32[8,3,64,64]{0,3,2,1:T(8,128)} %bitcast.296) | data formatting | bytes 786432 | tf_op jit(solution)/shard_map/reshape | solution.py:58
  139.6 5.3 %collective-permute-start.13 = (f32[4,128]{1,0:T(4,128)S(1)}, f32[4,128]{1,0:T(4,128)S(1)}, u32[]{:S(2)}, u32[]{:S(2)}) collective-permute-start(f32[4,128]{1,0:T(4,128)S(1)} %get-tuple-element.32), channel_id=1, source_target_pairs={{4,0},{8,4},{12,8},{16,12},{20,16},{24,20},{28,24},{32,28},{36,32}... | collective-permute-start | bytes 6152 | tf_op jit(solution)/shard_map/ppermute | solution.py:29
  177.7 5.4 %collective-permute-start.17 = (f32[4,64]{1,0:T(4,128)}, f32[4,64]{1,0:T(4,128)S(1)}, u32[]{:S(2)}, u32[]{:S(2)}) collective-permute-start(f32[4,64]{1,0:T(4,128)} %get-tuple-element.40), channel_id=1, source_target_pairs={{4,0},{8,4},{12,8},{16,12},{20,16},{24,20},{28,24},{32,28},{36,32}... | collective-permute-start | bytes 3080 | tf_op jit(solution)/shard_map/ppermute | solution.py:29
  186.2 5.2 %copy.274 = f32[2,3,64,64]{3,2,1,0:T(8,128)} copy(f32[2,3,64,64]{0,3,2,1:T(8,128)} %bitcast.294) | data formatting | bytes 196608 | tf_op jit(solution)/shard_map/reshape | solution.py:58
  198.7 5.7 %collective-permute-start.19 = (f32[4,64]{1,0:T(4,128)S(1)}, f32[4,64]{1,0:T(4,128)S(1)}, u32[]{:S(2)}, u32[]{:S(2)}) collective-permute-start(f32[4,64]{1,0:T(4,128)S(1)} %get-tuple-element.38), channel_id=1, source_target_pairs={{4,0},{8,4},{12,8},{16,12},{20,16},{24,20},{28,24},{32,28},{36,32}... | collective-permute-start | bytes 3080 | tf_op jit(solution)/shard_map/ppermute | solution.py:29
  206.4 5.1 %collective-permute-done.18 = f32[4,64]{1,0:T(4,128)S(1)} collective-permute-done((f32[4,64]{1,0:T(4,128)S(1)}, f32[4,64]{1,0:T(4,128)S(1)}, u32[]{:S(2)}, u32[]{:S(2)}) %collective-permute-start.18) | collective-permute-done | bytes 1056 | tf_op jit(solution)/shard_map/ppermute | solution.py:26
  221.8 4.6 %collective-permute-done.20 = f32[4,64]{1,0:T(4,128)S(1)} collective-permute-done((f32[4,64]{1,0:T(4,128)S(1)}, f32[4,64]{1,0:T(4,128)S(1)}, u32[]{:S(2)}, u32[]{:S(2)}) %collective-permute-start.20) | collective-permute-done | bytes 1056 | tf_op jit(solution)/shard_map/ppermute | solution.py:26
  236.9 4.6 %collective-permute-done.22 = f32[4,128]{1,0:T(4,128)S(1)} collective-permute-done((f32[4,128]{1,0:T(4,128)S(1)}, f32[4,128]{1,0:T(4,128)S(1)}, u32[]{:S(2)}, u32[]{:S(2)}) %collective-permute-start.22) | collective-permute-done | bytes 2080 | tf_op jit(solution)/shard_map/ppermute | solution.py:26
  250.4 4.6 %collective-permute-done.24 = f32[4,128]{1,0:T(4,128)S(1)} collective-permute-done((f32[4,128]{1,0:T(4,128)S(1)}, f32[4,128]{1,0:T(4,128)S(1)}, u32[]{:S(2)}, u32[]{:S(2)}) %collective-permute-start.24) | collective-permute-done | bytes 2080 | tf_op jit(solution)/shard_map/ppermute | solution.py:26
  265.2 4.6 %collective-permute-done.26 = f32[4,128]{1,0:T(4,128)S(1)} collective-permute-done((f32[4,128]{1,0:T(4,128)S(1)}, f32[4,128]{1,0:T(4,128)S(1)}, u32[]{:S(2)}, u32[]{:S(2)}) %collective-permute-start.26) | collective-permute-done | bytes 2080 | tf_op jit(solution)/shard_map/ppermute | solution.py:26
  278.9 6.9 %all-to-all-start.1 = ((f32[128,2,256]{2,1,0:T(2,128)}), f32[128,2,256]{2,1,0:T(2,128)S(1)}, u32[]{:S(2)}, u32[]{:S(2)}) async-start(f32[128,2,256]{2,1,0:T(2,128)} %copy.290), calls=%async_computation.1 | async-start | bytes 524288 | tf_op jit(solution)/shard_map/all_to_all | solution.py:186
  285.8 22.7 %all-to-all-done.1 = f32[128,2,256]{2,1,0:T(2,128)S(1)} async-done(((f32[128,2,256]{2,1,0:T(2,128)}), f32[128,2,256]{2,1,0:T(2,128)S(1)}, u32[]{:S(2)}, u32[]{:S(2)}) %all-to-all-start.1) | async-done | bytes 262176 | tf_op jit(solution)/shard_map/all_to_all | solution.py:186
  312.1 3.9 %collective-permute-start.28 = (f32[4,512]{1,0:T(4,128)S(1)}, f32[4,512]{1,0:T(4,128)S(1)}, u32[]{:S(2)}, u32[]{:S(2)}) collective-permute-start(f32[4,512]{1,0:T(4,128)S(1)} %get-tuple-element.13), channel_id=1, source_target_pairs={{0,1},{1,2},{2,3},{3,4},{4,5},{5,6},{6,7},{7,8},{8,9},{9,10},{10,1... | collective-permute-start | bytes 24584 | tf_op jit(solution)/shard_map/ppermute | solution.py:26
  316.1 5.2 %collective-permute-done.28 = f32[4,512]{1,0:T(4,128)S(1)} collective-permute-done((f32[4,512]{1,0:T(4,128)S(1)}, f32[4,512]{1,0:T(4,128)S(1)}, u32[]{:S(2)}, u32[]{:S(2)}) %collective-permute-start.28) | collective-permute-done | bytes 8224 | tf_op jit(solution)/shard_map/ppermute | solution.py:26
  329.9 5.2 %collective-permute-done.30 = f32[4,512]{1,0:T(4,128)S(1)} collective-permute-done((f32[4,512]{1,0:T(4,128)S(1)}, f32[4,512]{1,0:T(4,128)S(1)}, u32[]{:S(2)}, u32[]{:S(2)}) %collective-permute-start.30) | collective-permute-done | bytes 8224 | tf_op jit(solution)/shard_map/ppermute | solution.py:26
  339.8 3.9 %collective-permute-start.32 = (f32[4,512]{1,0:T(4,128)S(1)}, f32[4,512]{1,0:T(4,128)S(1)}, u32[]{:S(2)}, u32[]{:S(2)}) collective-permute-start(f32[4,512]{1,0:T(4,128)S(1)} %get-tuple-element.9), channel_id=1, source_target_pairs={{0,1},{1,2},{2,3},{3,4},{4,5},{5,6},{6,7},{7,8},{8,9},{9,10},{10,1... | collective-permute-start | bytes 24584 | tf_op jit(solution)/shard_map/ppermute | solution.py:26
  343.7 5.2 %collective-permute-done.32 = f32[4,512]{1,0:T(4,128)S(1)} collective-permute-done((f32[4,512]{1,0:T(4,128)S(1)}, f32[4,512]{1,0:T(4,128)S(1)}, u32[]{:S(2)}, u32[]{:S(2)}) %collective-permute-start.32) | collective-permute-done | bytes 8224 | tf_op jit(solution)/shard_map/ppermute | solution.py:26
  358.2 4.6 %collective-permute-done.34 = f32[4,512]{1,0:T(4,128)S(1)} collective-permute-done((f32[4,512]{1,0:T(4,128)S(1)}, f32[4,512]{1,0:T(4,128)S(1)}, u32[]{:S(2)}, u32[]{:S(2)}) %collective-permute-start.34) | collective-permute-done | bytes 8224 | tf_op jit(solution)/shard_map/ppermute | solution.py:26
  (297 shorter events, 176.3 us)
Async XLA Ops:
  1.3 27.5 %collective-permute-start.1 = (f32[4,512]{1,0:T(4,128)S(1)}, f32[4,512]{1,0:T(4,128)S(1)}, u32[]{:S(2)}, u32[]{:S(2)}) collective-permute-start(f32[4,512]{1,0:T(4,128)S(1)} %get-tuple-element.22), channel_id=1, source_target_pairs={{1,0},{2,1},{3,2},{4,3},{5,4},{6,5},{7,6},{8,7},{9,8},{10,9},{11,1... | collective-permute-start | bytes 24584 | tf_op jit(solution)/shard_map/ppermute | solution.py:29
  14.3 14.6 %collective-permute-start = (f32[4,512]{1,0:T(4,128)S(1)}, f32[4,512]{1,0:T(4,128)S(1)}, u32[]{:S(2)}, u32[]{:S(2)}) collective-permute-start(f32[4,512]{1,0:T(4,128)S(1)} %get-tuple-element.21), channel_id=1, source_target_pairs={{0,1},{1,2},{2,3},{3,4},{4,5},{5,6},{6,7},{7,8},{8,9},{9,10},{10,1... | collective-permute-start | bytes 24584 | tf_op jit(solution)/shard_map/ppermute | solution.py:26
  31.6 9.8 %collective-permute-start.3 = (f32[4,512]{1,0:T(4,128)S(1)}, f32[4,512]{1,0:T(4,128)S(1)}, u32[]{:S(2)}, u32[]{:S(2)}) collective-permute-start(f32[4,512]{1,0:T(4,128)S(1)} %get-tuple-element.20), channel_id=1, source_target_pairs={{1,0},{2,1},{3,2},{4,3},{5,4},{6,5},{7,6},{8,7},{9,8},{10,9},{11,1... | collective-permute-start | bytes 24584 | tf_op jit(solution)/shard_map/ppermute | solution.py:29
  39.5 9.2 %collective-permute-start.2 = (f32[4,512]{1,0:T(4,128)S(1)}, f32[4,512]{1,0:T(4,128)S(1)}, u32[]{:S(2)}, u32[]{:S(2)}) collective-permute-start(f32[4,512]{1,0:T(4,128)S(1)} %get-tuple-element.19), channel_id=1, source_target_pairs={{0,1},{1,2},{2,3},{3,4},{4,5},{5,6},{6,7},{7,8},{8,9},{9,10},{10,1... | collective-permute-start | bytes 24584 | tf_op jit(solution)/shard_map/ppermute | solution.py:26
  51.4 6.0 %collective-permute-start.5 = (f32[4,512]{1,0:T(4,128)S(1)}, f32[4,512]{1,0:T(4,128)S(1)}, u32[]{:S(2)}, u32[]{:S(2)}) collective-permute-start(f32[4,512]{1,0:T(4,128)S(1)} %get-tuple-element.18), channel_id=1, source_target_pairs={{1,0},{2,1},{3,2},{4,3},{5,4},{6,5},{7,6},{8,7},{9,8},{10,9},{11,1... | collective-permute-start | bytes 24584 | tf_op jit(solution)/shard_map/ppermute | solution.py:29
  53.4 9.2 %collective-permute-start.4 = (f32[4,512]{1,0:T(4,128)S(1)}, f32[4,512]{1,0:T(4,128)S(1)}, u32[]{:S(2)}, u32[]{:S(2)}) collective-permute-start(f32[4,512]{1,0:T(4,128)S(1)} %get-tuple-element.17), channel_id=1, source_target_pairs={{0,1},{1,2},{2,3},{3,4},{4,5},{5,6},{6,7},{7,8},{8,9},{9,10},{10,1... | collective-permute-start | bytes 24584 | tf_op jit(solution)/shard_map/ppermute | solution.py:26
  65.3 6.7 %collective-permute-start.7 = (f32[4,512]{1,0:T(4,128)S(1)}, f32[4,512]{1,0:T(4,128)S(1)}, u32[]{:S(2)}, u32[]{:S(2)}) collective-permute-start(f32[4,512]{1,0:T(4,128)S(1)} %get-tuple-element.16), channel_id=1, source_target_pairs={{1,0},{2,1},{3,2},{4,3},{5,4},{6,5},{7,6},{8,7},{9,8},{10,9},{11,1... | collective-permute-start | bytes 24584 | tf_op jit(solution)/shard_map/ppermute | solution.py:29
  67.3 9.2 %collective-permute-start.6 = (f32[4,512]{1,0:T(4,128)S(1)}, f32[4,512]{1,0:T(4,128)S(1)}, u32[]{:S(2)}, u32[]{:S(2)}) collective-permute-start(f32[4,512]{1,0:T(4,128)S(1)} %get-tuple-element.15), channel_id=1, source_target_pairs={{0,1},{1,2},{2,3},{3,4},{4,5},{5,6},{6,7},{7,8},{8,9},{9,10},{10,1... | collective-permute-start | bytes 24584 | tf_op jit(solution)/shard_map/ppermute | solution.py:26
  81.1 29.3 %all-to-all-start = ((f32[128,2,256]{2,1,0:T(2,128)}), f32[128,2,256]{2,1,0:T(2,128)S(1)}, u32[]{:S(2)}, u32[]{:S(2)}) async-start(f32[128,2,256]{2,1,0:T(2,128)} %copy.258), calls=%async_computation | async-start | bytes 524288 | tf_op jit(solution)/shard_map/all_to_all | solution.py:138
  116.3 7.0 %collective-permute-start.9 = (f32[8,256]{1,0:T(8,128)S(1)}, f32[8,256]{1,0:T(8,128)S(1)}, u32[]{:S(2)}, u32[]{:S(2)}) collective-permute-start(f32[8,256]{1,0:T(8,128)S(1)} %add.201), channel_id=1, source_target_pairs={{0,2},{1,3},{2,0},{3,1},{4,6},{5,7},{6,4},{7,5},{8,10},{9,11},{10,... | collective-permute-start | bytes 24584 | tf_op jit(solution)/shard_map/ppermute | solution.py:35
  123.5 10.9 %collective-permute-start.11 = (f32[4,128]{1,0:T(4,128)S(1)}, f32[4,128]{1,0:T(4,128)S(1)}, u32[]{:S(2)}, u32[]{:S(2)}) collective-permute-start(f32[4,128]{1,0:T(4,128)S(1)} %get-tuple-element.34), channel_id=1, source_target_pairs={{4,0},{8,4},{12,8},{16,12},{20,16},{24,20},{28,24},{32,28},{36,32}... | collective-permute-start | bytes 6152 | tf_op jit(solution)/shard_map/ppermute | solution.py:29
  125.4 9.0 %collective-permute-start.10 = (f32[4,128]{1,0:T(4,128)S(1)}, f32[4,128]{1,0:T(4,128)S(1)}, u32[]{:S(2)}, u32[]{:S(2)}) collective-permute-start(f32[4,128]{1,0:T(4,128)S(1)} %get-tuple-element.33), channel_id=1, source_target_pairs={{0,4},{4,8},{8,12},{12,16},{16,20},{20,24},{24,28},{28,32},{32,36}... | collective-permute-start | bytes 6152 | tf_op jit(solution)/shard_map/ppermute | solution.py:26
  139.6 8.6 %collective-permute-start.13 = (f32[4,128]{1,0:T(4,128)S(1)}, f32[4,128]{1,0:T(4,128)S(1)}, u32[]{:S(2)}, u32[]{:S(2)}) collective-permute-start(f32[4,128]{1,0:T(4,128)S(1)} %get-tuple-element.32), channel_id=1, source_target_pairs={{4,0},{8,4},{12,8},{16,12},{20,16},{24,20},{28,24},{32,28},{36,32}... | collective-permute-start | bytes 6152 | tf_op jit(solution)/shard_map/ppermute | solution.py:29
  144.8 7.0 %collective-permute-start.12 = (f32[4,128]{1,0:T(4,128)S(1)}, f32[4,128]{1,0:T(4,128)S(1)}, u32[]{:S(2)}, u32[]{:S(2)}) collective-permute-start(f32[4,128]{1,0:T(4,128)S(1)} %get-tuple-element.31), channel_id=1, source_target_pairs={{0,4},{4,8},{8,12},{12,16},{16,20},{20,24},{24,28},{28,32},{32,36}... | collective-permute-start | bytes 6152 | tf_op jit(solution)/shard_map/ppermute | solution.py:26
  158.8 9.9 %collective-permute-start.15 = (f32[4,128]{1,0:T(4,128)}, f32[4,128]{1,0:T(4,128)}, u32[]{:S(2)}, u32[]{:S(2)}) collective-permute-start(f32[4,128]{1,0:T(4,128)} %get-tuple-element.30), channel_id=1, source_target_pairs={{4,0},{8,4},{12,8},{16,12},{20,16},{24,20},{28,24},{32,28},{36,32}... | collective-permute-start | bytes 6152 | tf_op jit(solution)/shard_map/ppermute | solution.py:29
  160.9 7.8 %collective-permute-start.14 = (f32[4,128]{1,0:T(4,128)}, f32[4,128]{1,0:T(4,128)}, u32[]{:S(2)}, u32[]{:S(2)}) collective-permute-start(f32[4,128]{1,0:T(4,128)} %get-tuple-element.29), channel_id=1, source_target_pairs={{0,4},{4,8},{8,12},{12,16},{16,20},{20,24},{24,28},{28,32},{32,36}... | collective-permute-start | bytes 6152 | tf_op jit(solution)/shard_map/ppermute | solution.py:26
  177.7 13.7 %collective-permute-start.17 = (f32[4,64]{1,0:T(4,128)}, f32[4,64]{1,0:T(4,128)S(1)}, u32[]{:S(2)}, u32[]{:S(2)}) collective-permute-start(f32[4,64]{1,0:T(4,128)} %get-tuple-element.40), channel_id=1, source_target_pairs={{4,0},{8,4},{12,8},{16,12},{20,16},{24,20},{28,24},{32,28},{36,32}... | collective-permute-start | bytes 3080 | tf_op jit(solution)/shard_map/ppermute | solution.py:29
  183.1 8.9 %collective-permute-start.16 = (f32[4,64]{1,0:T(4,128)}, f32[4,64]{1,0:T(4,128)}, u32[]{:S(2)}, u32[]{:S(2)}) collective-permute-start(f32[4,64]{1,0:T(4,128)} %get-tuple-element.39), channel_id=1, source_target_pairs={{0,4},{4,8},{8,12},{12,16},{16,20},{20,24},{24,28},{28,32},{32,36}... | collective-permute-start | bytes 3080 | tf_op jit(solution)/shard_map/ppermute | solution.py:26
  198.7 7.7 %collective-permute-start.19 = (f32[4,64]{1,0:T(4,128)S(1)}, f32[4,64]{1,0:T(4,128)S(1)}, u32[]{:S(2)}, u32[]{:S(2)}) collective-permute-start(f32[4,64]{1,0:T(4,128)S(1)} %get-tuple-element.38), channel_id=1, source_target_pairs={{4,0},{8,4},{12,8},{16,12},{20,16},{24,20},{28,24},{32,28},{36,32}... | collective-permute-start | bytes 3080 | tf_op jit(solution)/shard_map/ppermute | solution.py:29
  204.5 7.0 %collective-permute-start.18 = (f32[4,64]{1,0:T(4,128)S(1)}, f32[4,64]{1,0:T(4,128)S(1)}, u32[]{:S(2)}, u32[]{:S(2)}) collective-permute-start(f32[4,64]{1,0:T(4,128)S(1)} %get-tuple-element.37), channel_id=1, source_target_pairs={{0,4},{4,8},{8,12},{12,16},{16,20},{20,24},{24,28},{28,32},{32,36}... | collective-permute-start | bytes 3080 | tf_op jit(solution)/shard_map/ppermute | solution.py:26
  219.4 7.0 %collective-permute-start.20 = (f32[4,64]{1,0:T(4,128)S(1)}, f32[4,64]{1,0:T(4,128)S(1)}, u32[]{:S(2)}, u32[]{:S(2)}) collective-permute-start(f32[4,64]{1,0:T(4,128)S(1)} %get-tuple-element.35), channel_id=1, source_target_pairs={{0,4},{4,8},{8,12},{12,16},{16,20},{20,24},{24,28},{28,32},{32,36}... | collective-permute-start | bytes 3080 | tf_op jit(solution)/shard_map/ppermute | solution.py:26
  234.5 7.0 %collective-permute-start.22 = (f32[4,128]{1,0:T(4,128)S(1)}, f32[4,128]{1,0:T(4,128)S(1)}, u32[]{:S(2)}, u32[]{:S(2)}) collective-permute-start(f32[4,128]{1,0:T(4,128)S(1)} %get-tuple-element.27), channel_id=1, source_target_pairs={{0,4},{4,8},{8,12},{12,16},{16,20},{20,24},{24,28},{28,32},{32,36}... | collective-permute-start | bytes 6152 | tf_op jit(solution)/shard_map/ppermute | solution.py:26
  248.0 7.0 %collective-permute-start.24 = (f32[4,128]{1,0:T(4,128)S(1)}, f32[4,128]{1,0:T(4,128)S(1)}, u32[]{:S(2)}, u32[]{:S(2)}) collective-permute-start(f32[4,128]{1,0:T(4,128)S(1)} %get-tuple-element.25), channel_id=1, source_target_pairs={{0,4},{4,8},{8,12},{12,16},{16,20},{20,24},{24,28},{28,32},{32,36}... | collective-permute-start | bytes 6152 | tf_op jit(solution)/shard_map/ppermute | solution.py:26
  262.8 7.0 %collective-permute-start.26 = (f32[4,128]{1,0:T(4,128)S(1)}, f32[4,128]{1,0:T(4,128)S(1)}, u32[]{:S(2)}, u32[]{:S(2)}) collective-permute-start(f32[4,128]{1,0:T(4,128)S(1)} %get-tuple-element.23), channel_id=1, source_target_pairs={{0,4},{4,8},{8,12},{12,16},{16,20},{20,24},{24,28},{28,32},{32,36}... | collective-permute-start | bytes 6152 | tf_op jit(solution)/shard_map/ppermute | solution.py:26
  278.9 29.6 %all-to-all-start.1 = ((f32[128,2,256]{2,1,0:T(2,128)}), f32[128,2,256]{2,1,0:T(2,128)S(1)}, u32[]{:S(2)}, u32[]{:S(2)}) async-start(f32[128,2,256]{2,1,0:T(2,128)} %copy.290), calls=%async_computation.1 | async-start | bytes 524288 | tf_op jit(solution)/shard_map/all_to_all | solution.py:186
  310.2 5.9 %collective-permute-start.29 = (f32[4,512]{1,0:T(4,128)S(1)}, f32[4,512]{1,0:T(4,128)S(1)}, u32[]{:S(2)}, u32[]{:S(2)}) collective-permute-start(f32[4,512]{1,0:T(4,128)S(1)} %get-tuple-element.14), channel_id=1, source_target_pairs={{1,0},{2,1},{3,2},{4,3},{5,4},{6,5},{7,6},{8,7},{9,8},{10,9},{11,1... | collective-permute-start | bytes 24584 | tf_op jit(solution)/shard_map/ppermute | solution.py:29
  312.1 9.2 %collective-permute-start.28 = (f32[4,512]{1,0:T(4,128)S(1)}, f32[4,512]{1,0:T(4,128)S(1)}, u32[]{:S(2)}, u32[]{:S(2)}) collective-permute-start(f32[4,512]{1,0:T(4,128)S(1)} %get-tuple-element.13), channel_id=1, source_target_pairs={{0,1},{1,2},{2,3},{3,4},{4,5},{5,6},{6,7},{7,8},{8,9},{9,10},{10,1... | collective-permute-start | bytes 24584 | tf_op jit(solution)/shard_map/ppermute | solution.py:26
  324.0 5.9 %collective-permute-start.31 = (f32[4,512]{1,0:T(4,128)S(1)}, f32[4,512]{1,0:T(4,128)S(1)}, u32[]{:S(2)}, u32[]{:S(2)}) collective-permute-start(f32[4,512]{1,0:T(4,128)S(1)} %get-tuple-element.12), channel_id=1, source_target_pairs={{1,0},{2,1},{3,2},{4,3},{5,4},{6,5},{7,6},{8,7},{9,8},{10,9},{11,1... | collective-permute-start | bytes 24584 | tf_op jit(solution)/shard_map/ppermute | solution.py:29
  326.0 9.2 %collective-permute-start.30 = (f32[4,512]{1,0:T(4,128)S(1)}, f32[4,512]{1,0:T(4,128)S(1)}, u32[]{:S(2)}, u32[]{:S(2)}) collective-permute-start(f32[4,512]{1,0:T(4,128)S(1)} %get-tuple-element.11), channel_id=1, source_target_pairs={{0,1},{1,2},{2,3},{3,4},{4,5},{5,6},{6,7},{7,8},{8,9},{9,10},{10,1... | collective-permute-start | bytes 24584 | tf_op jit(solution)/shard_map/ppermute | solution.py:26
  339.8 9.2 %collective-permute-start.32 = (f32[4,512]{1,0:T(4,128)S(1)}, f32[4,512]{1,0:T(4,128)S(1)}, u32[]{:S(2)}, u32[]{:S(2)}) collective-permute-start(f32[4,512]{1,0:T(4,128)S(1)} %get-tuple-element.9), channel_id=1, source_target_pairs={{0,1},{1,2},{2,3},{3,4},{4,5},{5,6},{6,7},{7,8},{8,9},{9,10},{10,1... | collective-permute-start | bytes 24584 | tf_op jit(solution)/shard_map/ppermute | solution.py:26
  351.7 6.5 %collective-permute-start.35 = (f32[4,512]{1,0:T(4,128)S(1)}, f32[4,512]{1,0:T(4,128)S(1)}, u32[]{:S(2)}, u32[]{:S(2)}) collective-permute-start(f32[4,512]{1,0:T(4,128)S(1)} %get-tuple-element.8), channel_id=1, source_target_pairs={{1,0},{2,1},{3,2},{4,3},{5,4},{6,5},{7,6},{8,7},{9,8},{10,9},{11,1... | collective-permute-start | bytes 24584 | tf_op jit(solution)/shard_map/ppermute | solution.py:29
  353.6 9.2 %collective-permute-start.34 = (f32[4,512]{1,0:T(4,128)S(1)}, f32[4,512]{1,0:T(4,128)S(1)}, u32[]{:S(2)}, u32[]{:S(2)}) collective-permute-start(f32[4,512]{1,0:T(4,128)S(1)} %get-tuple-element.7), channel_id=1, source_target_pairs={{0,1},{1,2},{2,3},{3,4},{4,5},{5,6},{6,7},{7,8},{8,9},{9,10},{10,1... | collective-permute-start | bytes 24584 | tf_op jit(solution)/shard_map/ppermute | solution.py:26
  (31 other events, 422.2 us)
where the time goes:
time: 369 us; the launch traced here: 366 us
  starting transfers between devices  125 us (34%)
  waiting for transfers between devices  102 us (28%)
  local copies, waits for them, and re-layouts  91.5 us (25%)
  matrix products  37.8 us (10%)
  other arithmetic  8.17 us (2%)
    ppermute x17, waiting for transfers between devices, extended(): lax.ppermute(lax.slice_in_dim(block, block.shape[dim] - width, None, axis...  64.3 us
    ppermute x17, starting transfers between devices, extended(): lax.ppermute(lax.slice_in_dim(block, 0, width, axis=dim), axis, backward)  60.3 us
    ppermute x17, starting transfers between devices, extended(): lax.ppermute(lax.slice_in_dim(block, block.shape[dim] - width, None, axis...  47.5 us
    dot_general x17, matrix products, local_apply(): jnp.einsum('ikab,rikb->ria', matrices, picked, precision=lax.Precision.HI...  30.9 us
    all_to_all x1, waiting for transfers between devices, body(): lax.all_to_all(back_out.reshape(slab_count, capacity, line_width), 'slab'...  22.7 us
    gather x17, local copies, waits for them, and re-layouts, local_apply(): picked = widened[:, local_columns]  16.1 us
    reshape x34, local copies, waits for them, and re-layouts, local_apply(): widened = widened.reshape(rhs_count, row_count + 2 * rim_rows, block_size)  16.1 us
    unnamed x54, local copies, waits for them, and re-layouts  14.3 us
  transfers between devices with their start and end apart: 38, of which 17 were waited for; matrix products, arithmetic and copies ran while one was open for 14% of the time, Pallas kernels for 0%

commit v1 on v0

v1 whole, which is shorter than its diff:
```python
import jax
import jax.numpy as jnp
import numpy as np
from jax import lax
from jax.experimental import pallas as pl
from jax.experimental.pallas import tpu as pltpu
from jax.sharding import PartitionSpec as P

F32 = jnp.float32
BF16 = jnp.bfloat16
I32 = jnp.int32
BS = 64
NRHS = 4
R0 = 16
R1 = 8
R2 = 2
XN = 4
YN = 4
TN_ = 32

CENTER = 0.5 * (2.2 + 0.3)
HALF = 0.5 * (2.2 - 0.3)
SCALED = CENTER / HALF
FACTORS = [1.0 / SCALED]
for _ in range(3):
    FACTORS.append(1.0 / (2.0 * SCALED - FACTORS[-1]))
KEEP = [FACTORS[t + 1] * FACTORS[t] for t in range(3)]
GAIN = [2.0 * FACTORS[t + 1] / HALF for t in range(3)]

NN = ((1,), (0,))
NT = ((1,), (1,))
TN = ((0,), (0,))

FINE_ORDER = [(i % 2) * 8 + i // 2 for i in range(R0)]
RIM_ORDER = FINE_ORDER[8:] + FINE_ORDER[:8]
PLAIN_ORDER = list(range(16))


def kern(body, outs, args, smem=()):
    count = len(args)

    def kernel(*refs):
        ins = [r if i in smem else r[...] for i, r in enumerate(refs[:count])]
        for ref, value in zip(refs[count:], body(*ins)):
            ref[...] = value

    specs = [
        pl.BlockSpec(memory_space=pltpu.SMEM if i in smem else pltpu.VMEM) for i in range(count)
    ]
    return pl.pallas_call(
        kernel,
        in_specs=specs,
        out_specs=[pl.BlockSpec(memory_space=pltpu.VMEM) for _ in outs],
        out_shape=[jax.ShapeDtypeStruct(s, d) for s, d in outs],
        compiler_params=pltpu.CompilerParams(vmem_limit_bytes=48 << 20),
        name=body.__name__,
    )(*args)


def mm(a, b, dims):
    return lax.dot_general(a, b, (dims, ((), ())), preferred_element_type=F32)


def iota(shape, dim):
    return lax.broadcasted_iota(I32, shape, dim)


def split(v):
    hi = v.astype(BF16)
    return hi, (v - hi.astype(F32)).astype(BF16)


def stacked(v):
    hi, lo = split(v)
    return jnp.concatenate([hi, lo], axis=0)


def one_hot(size, idx):
    return (iota((size, idx.shape[1]), 0) == idx).astype(F32).astype(BF16)


def lanes_in(x):
    lane = iota(x.shape, 1)
    place = lane & 63
    return jnp.take_along_axis(x, (lane & 64) + 2 * (place & 31) + (place >> 5), axis=1)


def lanes_out(x):
    lane = iota(x.shape, 1)
    b = lane & 63
    return jnp.take_along_axis(x, (lane & 64) + (b & 1) * 32 + (b >> 1), axis=1)


def tiles(raw):
    return lanes_in(raw.reshape(raw.shape[0] * 32, 128))


def double(g):
    return jnp.concatenate([g, g], axis=1)


def spread(hi, lo):
    low = iota(hi.shape, 1) < 64
    zero = jnp.zeros_like(hi)
    top = jnp.concatenate([jnp.where(low, hi, zero), jnp.where(low, lo, zero)], axis=1)
    bottom = jnp.concatenate([jnp.where(low, zero, hi), jnp.where(low, zero, lo)], axis=1)
    return jnp.concatenate([top, bottom], axis=0).astype(BF16)


def gathered(x, table):
    g = mm(x, table, NN)
    return spread(g[:64], g[64:])


def pick(t, order):
    lane = iota((32, 128), 1)
    place = (lane & 63) >> 2
    y = jnp.zeros((32, 128), F32)
    for i in range(16):
        y = y + jnp.where(place == order[i], t[i * 32 : i * 32 + 32], 0.0)
    return jnp.concatenate([y[:, :64], y[:, 64:]], axis=0)


def forward(his, los, rights, order):
    hi = jnp.concatenate(his, axis=1) if len(his) > 1 else his[0]
    lo = jnp.concatenate(los, axis=1) if len(los) > 1 else los[0]
    right = jnp.concatenate(rights, axis=0) if len(rights) > 1 else rights[0]
    a = mm(hi, right, NN)
    return pick(a[:, :128] + a[:, 128:] + mm(lo, right[:, :128], NN), order)


def diagonal(m, order):
    sub = iota(m.shape, 0) & 31
    lane = iota(m.shape, 1)
    kept = jnp.where((lane == sub) | (lane == sub + 96), m, 0.0)
    ones = ((iota((128, 128), 0) >> 6) == (iota((128, 128), 1) >> 6)).astype(F32).astype(BF16)
    hi, lo = split(kept)
    return pick(mm(hi, ones, NN) + mm(lo, ones, NN), order)


def columns_of(rows):
    z = lanes_in(jnp.concatenate([rows[:, m * 128 : m * 128 + 128] for m in range(8)], axis=0))
    t = z.T
    return jnp.concatenate([t[:64], t[64:]], axis=1)


def rows_of(v):
    t = lanes_out(jnp.concatenate([v[:, :32], v[:, 32:]], axis=0).T)
    return jnp.concatenate([t[m * 4 : m * 4 + 4] for m in range(8)], axis=1)


def rim(left, right):
    lane = iota(left.shape, 1)
    return jnp.where((((lane & 63) >> 2) & 7) < 4, right, left)


def fine_tables(device, own, left, right):
    wide, near = [], []
    for k in range(3):
        g = own[k : k + 1]
        r = rim(left[k : k + 1], right[k : k + 1])
        base = (device - 1) * 64
        wide.append([one_hot(192, g - base), one_hot(192, r - base)])
        near.append(one_hot(128, (g & 63) + jnp.where((g >> 6) == device, 0, 64)))
    return wide, near


def fine_both(hi, lo, x, wide):
    return jnp.concatenate(
        [
            forward(
                [hi[c, k] for k in range(3)],
                [lo[c, k] for k in range(3)],
                [gathered(x, wide[k][c]) for k in range(3)],
                (FINE_ORDER, RIM_ORDER)[c],
            )
            for c in range(2)
        ],
        axis=1,
    )


def fine_own(hi, lo, x, near):
    return forward(
        [hi[0, k] for k in range(3)],
        [lo[0, k] for k in range(3)],
        [gathered(x, near[k]) for k in range(3)],
        FINE_ORDER,
    )


def first_passes(device, x, sides, rhs, hi, lo, inverse, idx):
    wide, near = fine_tables(device, *idx)
    window = stacked(jnp.concatenate([sides[0], x, sides[1]], axis=1))
    r = rhs - fine_both(hi, lo, window, wide)
    d = inverse * r / CENTER
    r1 = r[:, :64] - fine_own(hi, lo, stacked(d), near)
    d1 = d[:, :64]
    d2 = KEEP[0] * d1 + GAIN[0] * (inverse[:, :64] * r1)
    return x + d1, jnp.concatenate([d2, r1], axis=1)


def last_passes(device, x, own, left, right, hi, lo, inverse, idx):
    wide, near = fine_tables(device, *idx)
    window = stacked(jnp.concatenate([left[:, :64], own[:, :64], right[:, :64]], axis=1))
    rims = rim(jnp.concatenate([left[:, 64:]] * 2, axis=1), jnp.concatenate([right[:, 64:]] * 2, axis=1))
    rim_d = rim(double(left[:, :64]), double(right[:, :64]))
    r = jnp.concatenate([own[:, 64:], rims[:, :64]], axis=1) - fine_both(hi, lo, window, wide)
    d_old = jnp.concatenate([own[:, :64], rim_d[:, :64]], axis=1)
    d = KEEP[1] * d_old + GAIN[1] * (inverse * r)
    residual = r[:, :64] - fine_own(hi, lo, stacked(d), near)
    return x + own[:, :64] + d[:, :64], residual


def indices(payload):
    return payload[8:11, :128].astype(I32)


def fine_start(device, own, left, right, own_blocks, left_blocks, right_blocks):
    parts = []
    for k in range(3):
        parts.append(tiles(own_blocks[k]))
    for k in range(3):
        parts.append(jnp.concatenate([tiles(left_blocks[k]), tiles(right_blocks[k])], axis=0))
    entries = jnp.concatenate([diagonal(parts[0], FINE_ORDER), diagonal(parts[3], RIM_ORDER)], axis=1)
    inverse = jnp.where(entries == 0.0, 0.0, 1.0 / entries)
    pairs = [split(p) for p in parts]
    hi = jnp.stack([p[0] for p in pairs]).reshape(2, 3, 512, 128)
    lo = jnp.stack([p[1] for p in pairs]).reshape(2, 3, 512, 128)
    x = [columns_of(p[:4]) for p in (left, own, right)]
    b = [columns_of(p[4:8]) for p in (left, own, right)]
    rhs = jnp.concatenate([b[1], rim(b[0], b[2])], axis=1)
    idx = [indices(p) for p in (own, left, right)]
    x1, send = first_passes(device[0, 0], x[1], (x[0], x[2]), rhs, hi, lo, inverse, idx)
    return hi, lo, inverse, rhs, x1, send, jnp.stack(idx)


def restrict(dest, residual, p_hi, p_lo):
    both = jnp.concatenate([residual[:32], residual[32:]], axis=1)
    place = (iota((32, 128), 1) & 63) >> 2
    hi, lo = split(both)
    hi, lo = hi.astype(F32), lo.astype(F32)
    r_hi = jnp.concatenate([jnp.where(place == FINE_ORDER[i], hi, 0.0) for i in range(16)], axis=0).astype(BF16)
    r_lo = jnp.concatenate([jnp.where(place == FINE_ORDER[i], lo, 0.0) for i in range(16)], axis=0).astype(BF16)
    pieces = []
    for e in range(2):
        u = mm(p_hi[e], r_hi, TN) + mm(p_hi[e], r_lo, TN) + mm(p_lo[e], r_hi, TN)
        pieces.append(u[:64, :64] + u[64:, 64:])
    x = stacked(jnp.concatenate(pieces, axis=1))
    out = []
    for q in range(XN * YN):
        table = (iota((256, 128), 0) + q * 256 == dest).astype(F32).astype(BF16)
        g = mm(x, table, NT)
        out.append(g[:64] + g[64:])
    return jnp.stack(out)


def fine_down(device, x, own, left, right, hi, lo, inverse, idx, dest, p_hi, p_lo):
    solution, residual = last_passes(
        device[0, 0], x, own, left, right, hi, lo, inverse, [idx[i] for i in range(3)]
    )
    return solution, restrict(dest, residual, p_hi, p_lo)


def fine_middle(device, x, left, right, rhs, hi, lo, inverse, idx):
    sides = (left[:, :64], right[:, :64])
    x1, send = first_passes(
        device[0, 0], x[:, :64], sides, rhs, hi, lo, inverse, [idx[i] for i in range(3)]
    )
    return x1, send


def fine_end(device, x, own, left, right, hi, lo, inverse, idx):
    solution, residual = last_passes(
        device[0, 0], x, own, left, right, hi, lo, inverse, [idx[i] for i in range(3)]
    )
    return rows_of(solution), rows_of(residual)


def prolong_parts(blocks):
    parts = [split(tiles(blocks[:, e, :])) for e in range(2)]
    return jnp.stack([p[0] for p in parts]), jnp.stack([p[1] for p in parts])


def sum_rows(parts):
    total = jnp.sum(parts, axis=0)
    return (jnp.stack([total[2 * t : 2 * t + 2] for t in range(TN_)]),)


def sum_all(parts):
    return (jnp.broadcast_to(jnp.sum(parts, axis=0)[None], parts.shape),)


def windows(parts, idx):
    x = stacked(jnp.concatenate([parts[t] for t in range(TN_)], axis=0))
    out = []
    for q in range(XN * YN):
        half = idx[:, (q // 2) * 128 : (q // 2) * 128 + 128]
        if q % 2 == 0:
            g = mm(x, one_hot(256, half), NN)
            g = g[:64] + g[64:]
        v = g[:, (q % 2) * 64 : (q % 2) * 64 + 64]
        out.append(jnp.concatenate([v[:32], v[32:]], axis=1))
    return (jnp.stack(out),)


A1_ROWS = 3 * R1 * 32
P1_ROWS = R1 * 32
A2_ROWS = 3 * R2 * 32
D1_AT = A1_ROWS + P1_ROWS + A2_ROWS
D2_AT = D1_AT + 64
IX_AT = D2_AT + 64
PACK_ROWS = IX_AT + 8


def level_pack(blocks, prolong, coarse, idx):
    a1 = [tiles(blocks[k]) for k in range(3)]
    a2 = [lanes_in(coarse[k].reshape(R2 * 32, 128)) for k in range(3)]
    pad = jnp.zeros((256, 128), F32)
    d1 = 1.0 / diagonal_plain(jnp.concatenate([a1[0], pad], axis=0))[:, :32]
    pad = jnp.zeros((448, 128), F32)
    d2 = 1.0 / diagonal_plain(jnp.concatenate([a2[0], pad], axis=0))[:, :8]
    return (
        jnp.concatenate(
            a1
            + [tiles(prolong)]
            + a2
            + [jnp.concatenate([d1] * 4, axis=1), jnp.concatenate([d2] * 16, axis=1), idx],
            axis=0,
        ),
    )


def diagonal_plain(m):
    return diagonal(m, PLAIN_ORDER)


def middle(place, parts, m3, m2, m1, p0, p1, p2, p3, far_low, far_high, unpack):
    slab = place[0, 0]
    sub = place[0, 1]
    packs = [m3, m2, m1, p0, p1, p2, p3]
    lane128 = iota((1, 128), 1)
    pieces = []
    for x in range(XN):
        w = parts[x]
        for y in range(1, YN):
            w = w + parts[y * XN + x]
        pieces.append(jnp.concatenate([w[:, :64], w[:, 64:]], axis=0))
    g = mm(stacked(jnp.concatenate(pieces, axis=1)), one_hot(256, unpack), NN)
    rhs = g[:64] + g[64:]
    quarter = iota((64, 128), 1) >> 5
    tiled = [far_low] + [p[D1_AT : D1_AT + 64] for p in packs] + [far_high]
    d1 = []
    for q in range(3):
        v = jnp.zeros((64, 128), F32)
        for m in range(4):
            if q * 4 + m < 9:
                v = jnp.where(quarter == m, tiled[q * 4 + m], v)
        d1.append(v)
    d1 = jnp.concatenate(d1, axis=1)
    eighth = (iota((64, 128), 1) >> 3) & 7
    d2 = jnp.zeros((64, 128), F32)
    for m in range(7):
        d2 = jnp.where(eighth == m + 1, packs[m][D2_AT : D2_AT + 64], d2)
    d2 = d2[:, :64]
    halves = [split(p[: D1_AT]) for p in packs]

    def rows(part, m, start, count):
        return halves[max(m, 0)][part][start : start + count]

    def pair(part, c, start, count):
        return jnp.concatenate(
            [rows(part, 2 * c - 1, start, count), rows(part, 2 * c, start, count)], axis=0
        )

    a_hi = [[pair(0, c, k * 256, 256) for k in range(3)] for c in range(4)]
    a_lo = [[pair(1, c, k * 256, 256) for k in range(3)] for c in range(4)]
    ix = [p[IX_AT : IX_AT + 8].astype(I32) for p in packs]
    base = (slab - 4) * R1 * NRHS
    starts = [0, 0, 0, 128]
    tables = []
    for c in range(4):
        line = []
        for k in range(3):
            even = ix[2 * c - 1][k : k + 1] - base if c > 0 else jnp.full((1, 128), -1, I32)
            odd = ix[2 * c][k : k + 1] - base
            at = jnp.where(((lane128 >> 5) & 1) == 0, even, odd)
            line.append(one_hot(256, at - starts[c]))
        tables.append(line)

    def apply1(v, chunks):
        x = stacked(v)
        return [
            forward(
                a_hi[c], a_lo[c], [gathered(x[:, starts[c] : starts[c] + 256], t) for t in tables[c]], PLAIN_ORDER
            )
            for c in chunks
        ]

    tail = jnp.zeros((64, 128), F32)
    inv = d1[:, :256]
    d = d1 * rhs / CENTER
    y = d[:, :256]
    r = rhs[:, :256] - jnp.concatenate(apply1(d, range(4)), axis=1)
    for t in range(2):
        step = KEEP[t] * d[:, :256] + GAIN[t] * (inv * r)
        d = jnp.concatenate([step, tail], axis=1)
        y = y + step
        r = r - jnp.concatenate(apply1(d, range(4)), axis=1)
    x = stacked(r)
    low = iota((32, 128), 1) < 64
    q_lane = (iota((32, 128), 1) & 63) >> 2
    first = (lane128 & 63) >> 2
    r_hi, r_lo = [], []
    for kk in range(4):
        g = mm(x, one_hot(256, first * 16 + kk * 4 + (lane128 & 3)), NN)
        r_hi.append(jnp.where(low, g[:32], g[32:64]))
        r_lo.append(jnp.where(low, g[64:96], g[96:128]))
    u = jnp.zeros((128, 128), F32)
    for m in range(7):
        keep = [q_lane == 2 * (m + 1) + j // 4 for j in range(R1)]
        b_hi = jnp.concatenate([jnp.where(keep[j], r_hi[j % 4], 0.0) for j in range(R1)], axis=0).astype(BF16)
        b_lo = jnp.concatenate([jnp.where(keep[j], r_lo[j % 4], 0.0) for j in range(R1)], axis=0).astype(BF16)
        p_hi, p_lo = rows(0, m, A1_ROWS, P1_ROWS), rows(1, m, A1_ROWS, P1_ROWS)
        u = u + mm(p_hi, b_hi, TN) + mm(p_hi, b_lo, TN) + mm(p_lo, b_hi, TN)
    r = u[:64, :64] + u[64:, 64:]
    c_hi, c_lo, c_tables = [], [], []
    c_base = (slab - 4) * R2 * NRHS
    group = (lane128 >> 3) & 7
    for k in range(3):
        start = A1_ROWS + P1_ROWS + k * 64
        c_hi.append(jnp.concatenate([rows(0, m - 1, start, 64) for m in range(8)], axis=0))
        c_lo.append(jnp.concatenate([rows(1, m - 1, start, 64) for m in range(8)], axis=0))
        at = jnp.full((1, 128), -1, I32)
        for m in range(7):
            at = jnp.where(group == m + 1, ix[m][3 + k : 4 + k] - c_base, at)
        c_tables.append(one_hot(64, at))
    d = d2 * r / CENTER
    z = d
    for t in range(3):
        s = stacked(d)
        r = r - forward(c_hi, c_lo, [gathered(s, c_tables[k]) for k in range(3)], PLAIN_ORDER)
        d = KEEP[t] * d + GAIN[t] * (d2 * r)
        z = z + d
    s = stacked(z)
    new = []
    for c in (1, 2):
        at = ((16 * c + ((lane128 & 63) >> 2)) >> 2) * 4 + (lane128 & 3)
        lift = forward(
            [pair(0, c, A1_ROWS, P1_ROWS)], [pair(1, c, A1_ROWS, P1_ROWS)], [gathered(s, one_hot(64, at))], PLAIN_ORDER
        )
        new.append(y[:, c * 64 : c * 64 + 64] + lift)
    y = jnp.concatenate([y[:, :64], new[0], new[1], y[:, 192:256], tail], axis=1)
    side = jnp.zeros((64, 64), F32)

    def at_centre(v):
        return jnp.concatenate([side, v, side, tail], axis=1)

    inv = inv[:, 64:192]
    r = rhs[:, 64:192] - jnp.concatenate(apply1(y, (1, 2)), axis=1)
    d = inv * r / CENTER
    y = y[:, 64:192] + d
    r = r - jnp.concatenate(apply1(at_centre(d), (1, 2)), axis=1)
    d = KEEP[0] * d + GAIN[0] * (inv * r)
    y = y + d
    r = r[:, 64:] - apply1(at_centre(d), (2,))[0]
    own = y[:, 64:] + KEEP[1] * d[:, 64:] + GAIN[1] * (inv[:, 64:] * r)
    pick_rows = (iota((8, 64), 1) == iota((8, 64), 0) + sub * 8).astype(F32).astype(BF16)
    hi, lo = split(own)
    o = mm(pick_rows, hi, NT) + mm(pick_rows, lo, NT)
    o = jnp.concatenate([o[:4], o[4:]], axis=1)
    return (jnp.broadcast_to(o[None], (TN_, 4, 128)),)


def fine_up(rows_ref, odd_ref, all_ref, x_ref, hi_ref, lo_ref, out_ref, line):
    for p in range(32):
        v = all_ref[rows_ref[p]]
        line[p * 4 : p * 4 + 4, :] = jnp.where(odd_ref[p] == 1, pltpu.roll(v, 64, 1), v)
    w = line[:, :64].T
    hi, lo = split(w)
    hi, lo = hi.astype(F32), lo.astype(F32)
    rights = [
        spread(double(hi[:, e * 64 : e * 64 + 64]), double(lo[:, e * 64 : e * 64 + 64])) for e in range(2)
    ]
    x = x_ref[...] + forward([hi_ref[0], hi_ref[1]], [lo_ref[0], lo_ref[1]], rights, FINE_ORDER)
    out_ref[...] = double(x)


def fine_up_call(rows, odd, gathered_rows, x, hi, lo):
    smem, vmem = pl.BlockSpec(memory_space=pltpu.SMEM), pl.BlockSpec(memory_space=pltpu.VMEM)
    return pl.pallas_call(
        fine_up,
        in_specs=[smem, smem, vmem, vmem, vmem, vmem],
        out_specs=vmem,
        out_shape=jax.ShapeDtypeStruct((64, 128), F32),
        scratch_shapes=[pltpu.VMEM((128, 128), F32)],
        compiler_params=pltpu.CompilerParams(vmem_limit_bytes=48 << 20),
        name="fine_up",
    )(rows, odd, gathered_rows, x, hi, lo)


XY = [[(y * TN_ + t) * XN + x for y in range(YN) for x in range(XN)] for t in range(TN_)]
ZC = [[y * TN_ + t for t in range(TN_)] for y in range(YN)]


def across(value):
    return lax.all_to_all(value, ("slab", "sub"), 0, 0, tiled=True, axis_index_groups=XY)


def along(value):
    return lax.all_to_all(value, "slab", 0, 0, tiled=True, axis_index_groups=ZC)


def shifted(value, axis, by):
    n = lax.axis_size(axis)
    return lax.ppermute(value, axis, [(i, i + by) for i in range(n) if 0 <= i + by < n])


def unpack_table():
    idx = np.full((1, 384), -1, np.int32)
    for rel in range(-4, 5):
        for row in range(R1):
            x, pair_row = row // 2, row % 2
            m = rel + 4 - (1 if x == 0 else 0)
            if 0 <= m < 8:
                for r in range(NRHS):
                    idx[0, (rel + 4) * 32 + row * 4 + r] = x * 64 + m * 8 + pair_row * 4 + r
    return idx


def lane_index(columns, times):
    t = columns.T
    v = (t[:, :, None] * NRHS + jnp.arange(NRHS, dtype=I32)).reshape(3, -1)
    return jnp.concatenate([v] * times, axis=1).astype(F32)


def places(values):
    return values.reshape(8, 2, -1).transpose(2, 1, 0).reshape(values.shape[1], 16)


def body(
    right_side,
    warm_start,
    fine_blocks,
    fine_columns,
    fine_prolong,
    owner_rows,
    send_slots,
    receive_rows,
    middle_blocks,
    middle_columns,
    middle_prolong,
    coarse_blocks,
    coarse_columns,
):
    both = ("slab", "sub")
    slab = lax.axis_index("slab").astype(I32)
    sub = lax.axis_index("sub").astype(I32)
    device = (slab * XN + sub).reshape(1, 1)
    place = jnp.stack([slab, sub]).reshape(1, 2)
    rhs4 = jnp.arange(NRHS, dtype=I32)

    g = places(fine_columns)
    g = (g // 16) * 64 + ((g % 2) * 8 + (g % 16) // 2) * 4
    g = (g[:, :, None] + rhs4).reshape(3, 64)
    g = jnp.concatenate([g, g], axis=1).astype(F32)
    own = jnp.concatenate([warm_start, right_side, jnp.pad(g, ((0, 5), (0, 896)))], axis=0)
    left, right = shifted(own, both, 1), shifted(own, both, -1)
    blocks = fine_blocks.transpose(1, 0, 2)
    left_blocks = shifted(blocks[:, 8:], both, 1)
    right_blocks = shifted(blocks[:, :8], both, -1)

    ix = jnp.concatenate([lane_index(middle_columns, 4), lane_index(coarse_columns, 16)], axis=0)
    (pack,) = kern(
        level_pack,
        [((PACK_ROWS, 128), F32)],
        [middle_blocks.transpose(1, 0, 2), middle_prolong, coarse_blocks.transpose(1, 0, 2), jnp.pad(ix, ((0, 2), (0, 0)))],
    )
    near = [shifted(pack, "slab", by) for by in (3, 2, 1)] + [pack] + [shifted(pack, "slab", -by) for by in (1, 2, 3)]
    inverse1 = pack[D1_AT : D1_AT + 64]
    far = [shifted(inverse1, "slab", 4), shifted(inverse1, "slab", -4)]
    p_hi, p_lo = kern(prolong_parts, [((2, 512, 128), BF16)] * 2, [fine_prolong])

    sends = ((64, 128), F32)
    hi, lo, inverse, rhs, x1, send, idx = kern(
        fine_start,
        [((2, 3, 512, 128), BF16)] * 2 + [sends, sends, ((64, 64), F32), sends, ((3, 3, 128), I32)],
        [device, own, left, right, blocks, left_blocks, right_blocks],
        smem=(0,),
    )
    o = places(owner_rows)
    dest = ((o // 256) * XN + (o % 8) // 2) * 256 + ((o // 8) % TN_) * 8 + (o % 2) * 4
    dest = (dest[:, :, None] + rhs4).reshape(1, 128)
    x3, dense = kern(
        fine_down,
        [((64, 64), F32), ((16, 64, 256), F32)],
        [device, x1, send, shifted(send, both, 1), shifted(send, both, -1), hi, lo, inverse, idx, dest, p_hi, p_lo],
        smem=(0,),
    )

    (part,) = kern(sum_rows, [((TN_, 2, 256), F32)], [across(dense)])
    (part,) = kern(sum_all, [((TN_, 2, 256), F32)], [along(part)])
    q = jnp.arange(XN * YN * 64, dtype=I32)
    rel = (q % 64) // 8 - 4 + (sub == 0).astype(I32)
    wanted = (q // 256) * TN_ + slab % TN_ + rel
    wanted = jnp.where(wanted // TN_ == slab // TN_, (wanted % TN_) * 8 + q % 8, -1)
    wanted = jnp.where((rel >= -4) & (wanted >= 0), wanted, -1)
    (part,) = kern(windows, [((16, 32, 128), F32)], [along(part), wanted.reshape(1, 1024)])
    part = across(part)

    (share,) = kern(
        middle,
        [((TN_, 4, 128), F32)],
        [place, part] + near + far + [jnp.asarray(unpack_table())],
        smem=(0,),
    )
    line = along(share)
    every = across(jnp.broadcast_to(line[None], (XN * YN, TN_, 4, 128)))
    at = ((o // 256) * XN + (o % 8) // 2) * TN_ + (o // 8) % TN_
    x = fine_up_call(
        at.reshape(32), (o % 2).reshape(32), every.reshape(XN * YN * TN_, 4, 128), x3, p_hi, p_lo
    )

    x1, send = kern(
        fine_middle,
        [((64, 64), F32), sends],
        [device, x, shifted(x, both, 1), shifted(x, both, -1), rhs, hi, lo, inverse, idx],
        smem=(0,),
    )
    return tuple(
        kern(
            fine_end,
            [((NRHS, 1024), F32)] * 2,
            [device, x1, send, shifted(send, both, 1), shifted(send, both, -1), hi, lo, inverse, idx],
            smem=(0,),
        )
    )


def solution(mesh):
    in_specs = (
        P(None, ("slab", "sub")),
        P(None, ("slab", "sub")),
        P(("slab", "sub"), None, None),
        P(("slab", "sub"), None),
        P(("slab", "sub"), None, None),
        P(("slab", "sub"), None),
        P(("slab", "sub"), None),
        P("slab", "sub", None, None),
        P("slab", None, None),
        P("slab", None),
        P("slab", None),
        P("slab", None, None),
        P("slab", None),
    )
    out_specs = (P(None, ("slab", "sub")), P(None, ("slab", "sub")))
    return jax.shard_map(body, mesh=mesh, in_specs=in_specs, out_specs=out_specs, check_vma=False)
```

time: 369 us -> 257 us (0.70)
  the two profiles are of different devices: /device:TPU:8 before, /device:TPU:16 now
where the time goes in v1:
time: 257 us; the launch traced here: 256 us
  starting transfers between devices  119 us (46%)
  waiting for transfers between devices  71.8 us (28%)
  Pallas kernels  30.2 us (12%)
  blocking collectives  21.1 us (8%)
  local copies, waits for them, and re-layouts  11.9 us (5%)
    ppermute x18, starting transfers between devices, shifted(): lax.ppermute(value, axis, [(i, i + by) for i in range(n) if 0 <= i + by <...  80.3 us
    all_to_all x2, waiting for transfers between devices, along(): return lax.all_to_all(value, 'slab', 0, 0, tiled=True, axis_index_groups=ZC)  36.3 us
    pallas_call x10, Pallas kernels, kern(): pl.pallas_call(kernel, in_specs=specs, out_specs=[pl.BlockSpec(memory_spa...  29 us
    all_to_all x3, waiting for transfers between devices, across(): lax.all_to_all(value, ('slab', 'sub'), 0, 0, tiled=True, axis_index_group...  28.6 us
    all_to_all x2, starting transfers between devices, along(): return lax.all_to_all(value, 'slab', 0, 0, tiled=True, axis_index_groups=ZC)  21.1 us
    all_to_all x1, blocking collectives, along(): return lax.all_to_all(value, 'slab', 0, 0, tiled=True, axis_index_groups=ZC)  21.1 us
    all_to_all x3, starting transfers between devices, across(): lax.all_to_all(value, ('slab', 'sub'), 0, 0, tiled=True, axis_index_group...  17.4 us
    ppermute x18, waiting for transfers between devices, shifted(): lax.ppermute(value, axis, [(i, i + by) for i in range(n) if 0 <= i + by <...  6.86 us
  transfers between devices with their start and end apart: 23, of which 9 were waited for; matrix products, arithmetic and copies ran while one was open for 2% of the time, Pallas kernels for 1%

profile of v1, /device:TPU:16, one launch (start us, length us, event | category | flops | bytes accessed | tf_op | source)
XLA Modules:
  0.0 256.0 jit_solution(469762766315404716)
XLA Ops:
  2.5 3.4 %collective-permute-start = (f32[16,1024]{1,0:T(8,128)S(1)}, f32[16,1024]{1,0:T(8,128)S(1)}, u32[]{:S(2)}, u32[]{:S(2)}) collective-permute-start(f32[16,1024]{1,0:T(8,128)S(1)} %select_maximum_fusion.refs_1_), channel_id=1, source_target_pairs={{0,1},{1,2},{2,3},{3,4},{4,5},{5,6},{6,7},{7,8},{8,9},{9,10},{10,1... | collective-permute-start | bytes 196616 | tf_op jit(solution)/shard_map/ppermute | solution.py:516
  5.9 11.4 %collective-permute-start.1 = (f32[16,1024]{1,0:T(8,128)S(1)}, f32[16,1024]{1,0:T(8,128)S(1)}, u32[]{:S(2)}, u32[]{:S(2)}) collective-permute-start(f32[16,1024]{1,0:T(8,128)S(1)} %select_maximum_fusion.refs_1_), channel_id=1, source_target_pairs={{1,0},{2,1},{3,2},{4,3},{5,4},{6,5},{7,6},{8,7},{9,8},{10,9},{11,1... | collective-permute-start | bytes 196616 | tf_op jit(solution)/shard_map/ppermute | solution.py:516
  18.6 1.9 collective-permute-start.2
  20.6 7.9 %collective-permute-start.3 = (f32[3,8,4096]{2,1,0:T(8,128)S(1)}, f32[3,8,4096]{2,1,0:T(8,128)S(1)}, u32[]{:S(2)}, u32[]{:S(2)}) collective-permute-start(f32[3,8,4096]{2,1,0:T(8,128)S(1)} %get-tuple-element.28), channel_id=1, source_target_pairs={{1,0},{2,1},{3,2},{4,3},{5,4},{6,5},{7,6},{8,7},{9,8},{10,9},{11,1... | collective-permute-start | bytes 1179656 | tf_op jit(solution)/shard_map/ppermute | solution.py:516
  35.5 3.0 %fine_start.1 = (bf16[2,3,512,128]{3,2,1,0:T(8,128)(2,1)S(1)}, bf16[2,3,512,128]{3,2,1,0:T(8,128)(2,1)S(1)}, f32[64,128]{1,0:T(8,128)S(1)}, f32[64,128]{1,0:T(8,...) custom-call(s32[1,1]{1,0:T(1,128)} %bitcast.refs_0_, ...), custom_call_target="tpu_custom_call" | custom-call | tf_op jit(solution)/shard_map/fine_start/pallas_call | solution.py:50
  39.1 1.9 collective-permute-start.4
  41.0 8.0 %collective-permute-start.5 = (f32[64,128]{1,0:T(8,128)}, f32[64,128]{1,0:T(8,128)S(1)}, u32[]{:S(2)}, u32[]{:S(2)}) collective-permute-start(f32[64,128]{1,0:T(8,128)} %get-tuple-element.16.refs_2_), channel_id=1, source_target_pairs={{1,0},{2,1},{3,2},{4,3},{5,4},{6,5},{7,6},{8,7},{9,8},{10,9},{11,1... | collective-permute-start | bytes 98312 | tf_op jit(solution)/shard_map/ppermute | solution.py:516
  50.9 3.6 %fine_down.1 = (f32[64,64]{1,0:T(8,128)S(1)}, f32[16,64,256]{2,1,0:T(8,128)S(1)}) custom-call(s32[1,1]{1,0:T(1,128)} %bitcast.refs_0_, f32[64,64]{1,0:T(8,128)S(1)} %get-tuple-element.15.refs_1_, f32[64,128]{1,0:T(8,128)} %get-tuple-element.16.refs_2_, f32[64,128]{1,0:T(8,128)S(1)} %collective-permute-done.4.refs_3_, ...), custom_call_target="tpu_custom_call" | custom-call | tf_op jit(solution)/shard_map/fine_down/pallas_call | solution.py:50
  55.5 5.1 %all-to-all-start = ((f32[16,64,256]{2,1,0:T(8,128)}), f32[16,64,256]{2,1,0:T(8,128)S(1)}, u32[]{:S(2)}, u32[]{:S(2)}) async-start(f32[16,64,256]{2,1,0:T(8,128)} %copy-done.1), calls=%async_computation | async-start | bytes 2097152 | tf_op jit(solution)/shard_map/all_to_all | solution.py:507
  63.2 1.9 collective-permute-start.6
  65.1 8.0 %all-to-all-done.refs_0_ = f32[16,64,256]{2,1,0:T(8,128)S(1)} async-done(((f32[16,64,256]{2,1,0:T(8,128)}), f32[16,64,256]{2,1,0:T(8,128)S(1)}, u32[]{:S(2)}, u32[]{:S(2)}) %all-to-all-start) | async-done | bytes 1048608 | tf_op jit(solution)/shard_map/all_to_all | solution.py:507
  73.8 10.4 %all-to-all-start.1 = ((f32[32,2,256]{2,1,0:T(2,128)}), f32[32,2,256]{2,1,0:T(2,128)S(1)}, u32[]{:S(2)}, u32[]{:S(2)}) async-start(f32[32,2,256]{2,1,0:T(2,128)} %sum_rows.1), calls=%async_computation.1 | async-start | bytes 131072 | tf_op jit(solution)/shard_map/all_to_all | solution.py:511
  84.3 4.6 %collective-permute-start.12 = (f32[64,128]{1,0:T(8,128)S(1)}, f32[64,128]{1,0:T(8,128)S(1)}, u32[]{:S(2)}, u32[]{:S(2)}) collective-permute-start(f32[64,128]{1,0:T(8,128)S(1)} %slice.14), channel_id=1, source_target_pairs={{0,16},{4,20},{8,24},{12,28},{16,32},{20,36},{24,40},{28,44},{32,4... | collective-permute-start | bytes 98312 | tf_op jit(solution)/shard_map/ppermute | solution.py:516
  88.9 4.3 %collective-permute-start.13 = (f32[64,128]{1,0:T(8,128)S(1)}, f32[64,128]{1,0:T(8,128)S(1)}, u32[]{:S(2)}, u32[]{:S(2)}) collective-permute-start(f32[64,128]{1,0:T(8,128)S(1)} %slice.14), channel_id=1, source_target_pairs={{16,0},{20,4},{24,8},{28,12},{32,16},{36,20},{40,24},{44,28},{48,3... | collective-permute-start | bytes 98312 | tf_op jit(solution)/shard_map/ppermute | solution.py:516
  93.1 3.7 %collective-permute-start.7 = (f32[1352,128]{1,0:T(8,128)S(1)}, f32[1352,128]{1,0:T(8,128)S(1)}, u32[]{:S(2)}, u32[]{:S(2)}) collective-permute-start(f32[1352,128]{1,0:T(8,128)S(1)} %level_pack.1.refs_5_), channel_id=1, source_target_pairs={{0,8},{4,12},{8,16},{12,20},{16,24},{20,28},{24,32},{28,36},{32,40... | collective-permute-start | bytes 2076680 | tf_op jit(solution)/shard_map/ppermute | solution.py:516
  96.8 1.9 collective-permute-start.8
  98.8 5.8 %collective-permute-start.9 = (f32[1352,128]{1,0:T(8,128)S(1)}, f32[1352,128]{1,0:T(8,128)}, u32[]{:S(2)}, u32[]{:S(2)}) collective-permute-start(f32[1352,128]{1,0:T(8,128)S(1)} %level_pack.1.refs_5_), channel_id=1, source_target_pairs={{4,0},{8,4},{12,8},{16,12},{20,16},{24,20},{28,24},{32,28},{36,32}... | collective-permute-start | bytes 2076680 | tf_op jit(solution)/shard_map/ppermute | solution.py:516
  104.5 2.1 collective-permute-start.10
  106.7 1.9 collective-permute-start.11
  109.3 10.7 %all-to-all-start.2 = ((f32[32,2,256]{2,1,0:T(2,128)}), f32[32,2,256]{2,1,0:T(2,128)S(1)}, u32[]{:S(2)}, u32[]{:S(2)}) async-start(f32[32,2,256]{2,1,0:T(2,128)} %sum_all.1), calls=%async_computation.2 | async-start | bytes 131072 | tf_op jit(solution)/shard_map/all_to_all | solution.py:511
  120.1 36.3 %all-to-all-done.2.refs_0_ = f32[32,2,256]{2,1,0:T(2,128)S(1)} async-done(((f32[32,2,256]{2,1,0:T(2,128)}), f32[32,2,256]{2,1,0:T(2,128)S(1)}, u32[]{:S(2)}, u32[]{:S(2)}) %all-to-all-start.2) | async-done | bytes 65568 | tf_op jit(solution)/shard_map/all_to_all | solution.py:511
  157.5 6.0 %all-to-all-start.3 = ((f32[16,32,128]{2,1,0:T(8,128)}), f32[16,32,128]{2,1,0:T(8,128)S(1)}, u32[]{:S(2)}, u32[]{:S(2)}) async-start(f32[16,32,128]{2,1,0:T(8,128)} %windows.1), calls=%async_computation.3 | async-start | bytes 524288 | tf_op jit(solution)/shard_map/all_to_all | solution.py:507
  163.6 6.6 %all-to-all-done.3.refs_1_ = f32[16,32,128]{2,1,0:T(8,128)S(1)} async-done(((f32[16,32,128]{2,1,0:T(8,128)}), f32[16,32,128]{2,1,0:T(8,128)S(1)}, u32[]{:S(2)}, u32[]{:S(2)}) %all-to-all-start.3) | async-done | bytes 262176 | tf_op jit(solution)/shard_map/all_to_all | solution.py:507
  170.2 14.6 %middle.1 = f32[32,4,128]{2,1,0:T(4,128)S(1)} custom-call(s32[1,2]{1,0:T(1,128)S(1)} %add_bitcast_fusion.refs_0_, f32[16,32,128]{2,1,0:T(8,128)S(1)} %all-to-all-done.3.refs_1_, f32[1352,128]{1,0:T(8,128)} %collective-permute-done.6.refs_2_, f32[1352,128]{1,0:T(8,128)S(1)} %collective-permute-done.7.refs_3_, f32[1352,128]{1,0:T(8,128)} %collective-permute-done.8.refs_4_, ...), custom_call_target="tpu_custom_call" | custom-call | tf_op jit(solution)/shard_map/middle/pallas_call | solution.py:50
  184.8 21.1 %all_to_all.30 = f32[32,4,128]{2,1,0:T(4,128)S(1)} all-to-all(f32[32,4,128]{2,1,0:T(4,128)S(1)} %middle.1), channel_id=1, replica_groups={{0,4,8,12,16,20,24,28,32,36,40,44,48,52,56,60,64,68,72,76,80,84,88,92,9..., dimensions={0} | all-to-all | bytes 131072 | tf_op jit(solution)/shard_map/all_to_all | solution.py:511
  207.1 6.3 %all-to-all-start.5 = ((f32[16,32,4,128]{3,2,1,0:T(4,128)}), f32[16,32,4,128]{3,2,1,0:T(4,128)S(1)}, u32[]{:S(2)}, u32[]{:S(2)}) async-start(f32[16,32,4,128]{3,2,1,0:T(4,128)} %broadcast_in_dim.4), calls=%async_computation.5 | async-start | bytes 2097152 | tf_op jit(solution)/shard_map/all_to_all | solution.py:507
  213.4 14.1 %all-to-all-done.5 = f32[16,32,4,128]{3,2,1,0:T(4,128)S(1)} async-done(((f32[16,32,4,128]{3,2,1,0:T(4,128)}), f32[16,32,4,128]{3,2,1,0:T(4,128)S(1)}, u32[]{:S(2)}, u32[]{:S(2)}) %all-to-all-start.5) | async-done | bytes 1048608 | tf_op jit(solution)/shard_map/all_to_all | solution.py:507
  228.8 2.2 collective-permute-start.14
  231.0 7.6 %collective-permute-start.15 = (f32[64,128]{1,0:T(8,128)S(1)}, f32[64,128]{1,0:T(8,128)S(1)}, u32[]{:S(2)}, u32[]{:S(2)}) collective-permute-start(f32[64,128]{1,0:T(8,128)S(1)} %fine_up.1.refs_1_), channel_id=1, source_target_pairs={{1,0},{2,1},{3,2},{4,3},{5,4},{6,5},{7,6},{8,7},{9,8},{10,9},{11,1... | collective-permute-start | bytes 98312 | tf_op jit(solution)/shard_map/ppermute | solution.py:516
  242.0 1.9 collective-permute-start.16
  243.9 7.9 %collective-permute-start.17 = (f32[64,128]{1,0:T(8,128)S(1)}, f32[64,128]{1,0:T(8,128)S(1)}, u32[]{:S(2)}, u32[]{:S(2)}) collective-permute-start(f32[64,128]{1,0:T(8,128)S(1)} %get-tuple-element.27.refs_2_), channel_id=1, source_target_pairs={{1,0},{2,1},{3,2},{4,3},{5,4},{6,5},{7,6},{8,7},{9,8},{10,9},{11,1... | collective-permute-start | bytes 98312 | tf_op jit(solution)/shard_map/ppermute | solution.py:516
  253.4 2.6 %fine_end.1 = (f32[4,1024]{1,0:T(4,128)}, f32[4,1024]{1,0:T(4,128)}) custom-call(s32[1,1]{1,0:T(1,128)} %bitcast.refs_0_, f32[64,64]{1,0:T(8,128)S(1)} %get-tuple-element.26.refs_1_, f32[64,128]{1,0:T(8,128)S(1)} %get-tuple-element.27.refs_2_, f32[64,128]{1,0:T(8,128)S(1)} %collective-permute-done.16.refs_3_, f32[64,128]{1,0:T(8,128)S(1)} %collective-permute-done.17.refs_4_, ...), custom_call_target="tpu_custom_call" | custom-call | tf_op jit(solution)/shard_map/fine_end/pallas_call | solution.py:50
  (107 shorter events, 26.3 us)
Async XLA Ops:
  2.5 27.9 %collective-permute-start = (f32[16,1024]{1,0:T(8,128)S(1)}, f32[16,1024]{1,0:T(8,128)S(1)}, u32[]{:S(2)}, u32[]{:S(2)}) collective-permute-start(f32[16,1024]{1,0:T(8,128)S(1)} %select_maximum_fusion.refs_1_), channel_id=1, source_target_pairs={{0,1},{1,2},{2,3},{3,4},{4,5},{5,6},{6,7},{7,8},{8,9},{9,10},{10,1... | collective-permute-start | bytes 196616 | tf_op jit(solution)/shard_map/ppermute | solution.py:516
  5.9 24.5 %collective-permute-start.1 = (f32[16,1024]{1,0:T(8,128)S(1)}, f32[16,1024]{1,0:T(8,128)S(1)}, u32[]{:S(2)}, u32[]{:S(2)}) collective-permute-start(f32[16,1024]{1,0:T(8,128)S(1)} %select_maximum_fusion.refs_1_), channel_id=1, source_target_pairs={{1,0},{2,1},{3,2},{4,3},{5,4},{6,5},{7,6},{8,7},{9,8},{10,9},{11,1... | collective-permute-start | bytes 196616 | tf_op jit(solution)/shard_map/ppermute | solution.py:516
  17.4 17.1 %copy-start = (f32[16,3,4096]{2,0,1:T(8,128)S(1)}, f32[16,3,4096]{2,0,1:T(8,128)}, u32[]{:S(2)}) copy-start(f32[16,3,4096]{2,0,1:T(8,128)} %param.16) | copy-start | bytes 2359300
  18.6 9.8 %copy-start.18 = (s32[16,2]{0,1:T(2,128)S(1)}, s32[16,2]{0,1:T(2,128)}, u32[]{:S(2)}) copy-start(s32[16,2]{0,1:T(2,128)} %param.19) | copy-start | bytes 388
  18.6 13.3 %collective-permute-start.2 = (f32[3,8,4096]{2,1,0:T(8,128)S(1)}, f32[3,8,4096]{2,1,0:T(8,128)S(1)}, u32[]{:S(2)}, u32[]{:S(2)}) collective-permute-start(f32[3,8,4096]{2,1,0:T(8,128)S(1)} %get-tuple-element.29), channel_id=1, source_target_pairs={{0,1},{1,2},{2,3},{3,4},{4,5},{5,6},{6,7},{7,8},{8,9},{9,10},{10,1... | collective-permute-start | bytes 1179656 | tf_op jit(solution)/shard_map/ppermute | solution.py:516
  20.6 13.1 %collective-permute-start.3 = (f32[3,8,4096]{2,1,0:T(8,128)S(1)}, f32[3,8,4096]{2,1,0:T(8,128)S(1)}, u32[]{:S(2)}, u32[]{:S(2)}) collective-permute-start(f32[3,8,4096]{2,1,0:T(8,128)S(1)} %get-tuple-element.28), channel_id=1, source_target_pairs={{1,0},{2,1},{3,2},{4,3},{5,4},{6,5},{7,6},{8,7},{9,8},{10,9},{11,1... | collective-permute-start | bytes 1179656 | tf_op jit(solution)/shard_map/ppermute | solution.py:516
  35.5 13.5 %copy-start.17 = (s32[8,3]{0,1:T(4,128)S(1)}, s32[8,3]{0,1:T(4,128)}, u32[]{:S(2)}) copy-start(s32[8,3]{0,1:T(4,128)} %param.21) | copy-start | bytes 292
  35.5 14.4 %copy-start.6 = (f32[16,2,4096]{2,1,0:T(2,128)S(1)}, f32[16,2,4096]{2,1,0:T(2,128)}, u32[]{:S(2)}) copy-start(f32[16,2,4096]{2,1,0:T(2,128)} %refs_0_.1) | copy-start | bytes 1572868
  39.1 11.4 %collective-permute-start.4 = (f32[64,128]{1,0:T(8,128)}, f32[64,128]{1,0:T(8,128)S(1)}, u32[]{:S(2)}, u32[]{:S(2)}) collective-permute-start(f32[64,128]{1,0:T(8,128)} %get-tuple-element.16.refs_2_), channel_id=1, source_target_pairs={{0,1},{1,2},{2,3},{3,4},{4,5},{5,6},{6,7},{7,8},{8,9},{9,10},{10,1... | collective-permute-start | bytes 98312 | tf_op jit(solution)/shard_map/ppermute | solution.py:516
  41.0 9.9 %collective-permute-start.5 = (f32[64,128]{1,0:T(8,128)}, f32[64,128]{1,0:T(8,128)S(1)}, u32[]{:S(2)}, u32[]{:S(2)}) collective-permute-start(f32[64,128]{1,0:T(8,128)} %get-tuple-element.16.refs_2_), channel_id=1, source_target_pairs={{1,0},{2,1},{3,2},{4,3},{5,4},{6,5},{7,6},{8,7},{9,8},{10,9},{11,1... | collective-permute-start | bytes 98312 | tf_op jit(solution)/shard_map/ppermute | solution.py:516
  55.5 5.2 %copy-start.10 = (f32[8,4096]{1,0:T(8,128)S(1)}, f32[8,4096]{1,0:T(8,128)}, u32[]{:S(2)}) copy-start(f32[8,4096]{1,0:T(8,128)} %refs_1_.1) | copy-start | bytes 393220
  55.5 17.6 %all-to-all-start = ((f32[16,64,256]{2,1,0:T(8,128)}), f32[16,64,256]{2,1,0:T(8,128)S(1)}, u32[]{:S(2)}, u32[]{:S(2)}) async-start(f32[16,64,256]{2,1,0:T(8,128)} %copy-done.1), calls=%async_computation | async-start | bytes 2097152 | tf_op jit(solution)/shard_map/all_to_all | solution.py:507
  63.2 43.5 %collective-permute-start.6 = (f32[1352,128]{1,0:T(8,128)S(1)}, f32[1352,128]{1,0:T(8,128)}, u32[]{:S(2)}, u32[]{:S(2)}) collective-permute-start(f32[1352,128]{1,0:T(8,128)S(1)} %level_pack.1.refs_5_), channel_id=1, source_target_pairs={{0,12},{4,16},{8,20},{12,24},{16,28},{20,32},{24,36},{28,40},{32,4... | collective-permute-start | bytes 2076680 | tf_op jit(solution)/shard_map/ppermute | solution.py:516
  73.8 34.8 %all-to-all-start.1 = ((f32[32,2,256]{2,1,0:T(2,128)}), f32[32,2,256]{2,1,0:T(2,128)S(1)}, u32[]{:S(2)}, u32[]{:S(2)}) async-start(f32[32,2,256]{2,1,0:T(2,128)} %sum_rows.1), calls=%async_computation.1 | async-start | bytes 131072 | tf_op jit(solution)/shard_map/all_to_all | solution.py:511
  84.3 14.5 %collective-permute-start.12 = (f32[64,128]{1,0:T(8,128)S(1)}, f32[64,128]{1,0:T(8,128)S(1)}, u32[]{:S(2)}, u32[]{:S(2)}) collective-permute-start(f32[64,128]{1,0:T(8,128)S(1)} %slice.14), channel_id=1, source_target_pairs={{0,16},{4,20},{8,24},{12,28},{16,32},{20,36},{24,40},{28,44},{32,4... | collective-permute-start | bytes 98312 | tf_op jit(solution)/shard_map/ppermute | solution.py:516
  88.9 15.7 %collective-permute-start.13 = (f32[64,128]{1,0:T(8,128)S(1)}, f32[64,128]{1,0:T(8,128)S(1)}, u32[]{:S(2)}, u32[]{:S(2)}) collective-permute-start(f32[64,128]{1,0:T(8,128)S(1)} %slice.14), channel_id=1, source_target_pairs={{16,0},{20,4},{24,8},{28,12},{32,16},{36,20},{40,24},{44,28},{48,3... | collective-permute-start | bytes 98312 | tf_op jit(solution)/shard_map/ppermute | solution.py:516
  93.1 70.5 %collective-permute-start.7 = (f32[1352,128]{1,0:T(8,128)S(1)}, f32[1352,128]{1,0:T(8,128)S(1)}, u32[]{:S(2)}, u32[]{:S(2)}) collective-permute-start(f32[1352,128]{1,0:T(8,128)S(1)} %level_pack.1.refs_5_), channel_id=1, source_target_pairs={{0,8},{4,12},{8,16},{12,20},{16,24},{20,28},{24,32},{28,36},{32,40... | collective-permute-start | bytes 2076680 | tf_op jit(solution)/shard_map/ppermute | solution.py:516
  96.8 66.8 %collective-permute-start.8 = (f32[1352,128]{1,0:T(8,128)S(1)}, f32[1352,128]{1,0:T(8,128)}, u32[]{:S(2)}, u32[]{:S(2)}) collective-permute-start(f32[1352,128]{1,0:T(8,128)S(1)} %level_pack.1.refs_5_), channel_id=1, source_target_pairs={{0,4},{4,8},{8,12},{12,16},{16,20},{20,24},{24,28},{28,32},{32,36}... | collective-permute-start | bytes 2076680 | tf_op jit(solution)/shard_map/ppermute | solution.py:516
  98.8 64.8 %collective-permute-start.9 = (f32[1352,128]{1,0:T(8,128)S(1)}, f32[1352,128]{1,0:T(8,128)}, u32[]{:S(2)}, u32[]{:S(2)}) collective-permute-start(f32[1352,128]{1,0:T(8,128)S(1)} %level_pack.1.refs_5_), channel_id=1, source_target_pairs={{4,0},{8,4},{12,8},{16,12},{20,16},{24,20},{28,24},{32,28},{36,32}... | collective-permute-start | bytes 2076680 | tf_op jit(solution)/shard_map/ppermute | solution.py:516
  104.5 59.1 %collective-permute-start.10 = (f32[1352,128]{1,0:T(8,128)S(1)}, f32[1352,128]{1,0:T(8,128)}, u32[]{:S(2)}, u32[]{:S(2)}) collective-permute-start(f32[1352,128]{1,0:T(8,128)S(1)} %level_pack.1.refs_5_), channel_id=1, source_target_pairs={{8,0},{12,4},{16,8},{20,12},{24,16},{28,20},{32,24},{36,28},{40,32... | collective-permute-start | bytes 2076680 | tf_op jit(solution)/shard_map/ppermute | solution.py:516
  106.7 56.9 %collective-permute-start.11 = (f32[1352,128]{1,0:T(8,128)S(1)}, f32[1352,128]{1,0:T(8,128)}, u32[]{:S(2)}, u32[]{:S(2)}) collective-permute-start(f32[1352,128]{1,0:T(8,128)S(1)} %level_pack.1.refs_5_), channel_id=1, source_target_pairs={{12,0},{16,4},{20,8},{24,12},{28,16},{32,20},{36,24},{40,28},{44,3... | collective-permute-start | bytes 2076680 | tf_op jit(solution)/shard_map/ppermute | solution.py:516
  109.3 47.0 %all-to-all-start.2 = ((f32[32,2,256]{2,1,0:T(2,128)}), f32[32,2,256]{2,1,0:T(2,128)S(1)}, u32[]{:S(2)}, u32[]{:S(2)}) async-start(f32[32,2,256]{2,1,0:T(2,128)} %sum_all.1), calls=%async_computation.2 | async-start | bytes 131072 | tf_op jit(solution)/shard_map/all_to_all | solution.py:511
  157.5 12.7 %all-to-all-start.3 = ((f32[16,32,128]{2,1,0:T(8,128)}), f32[16,32,128]{2,1,0:T(8,128)S(1)}, u32[]{:S(2)}, u32[]{:S(2)}) async-start(f32[16,32,128]{2,1,0:T(8,128)} %windows.1), calls=%async_computation.3 | async-start | bytes 524288 | tf_op jit(solution)/shard_map/all_to_all | solution.py:507
  163.5 6.7 %copy-start.14 = (s32[1,384]{1,0:T(1,128)S(1)}, s32[1,384]{1,0:T(1,128)}, u32[]{:S(2)}) copy-start(s32[1,384]{1,0:T(1,128)} %constant.226.clone.refs_11_) | copy-start | bytes 4612
  207.1 20.5 %copy-start.3 = (bf16[2,512,128]{2,1,0:T(8,128)(2,1)S(1)}, bf16[2,512,128]{2,1,0:T(8,128)(2,1)}, u32[]{:S(2)}) copy-start(bf16[2,512,128]{2,1,0:T(8,128)(2,1)} %copy-done.2) | copy-start | bytes 786436
  207.1 20.5 %copy-start.5 = (bf16[2,512,128]{2,1,0:T(8,128)(2,1)S(1)}, bf16[2,512,128]{2,1,0:T(8,128)(2,1)}, u32[]{:S(2)}) copy-start(bf16[2,512,128]{2,1,0:T(8,128)(2,1)} %copy-done.4) | copy-start | bytes 786436
  207.1 20.5 %all-to-all-start.5 = ((f32[16,32,4,128]{3,2,1,0:T(4,128)}), f32[16,32,4,128]{3,2,1,0:T(4,128)S(1)}, u32[]{:S(2)}, u32[]{:S(2)}) async-start(f32[16,32,4,128]{3,2,1,0:T(4,128)} %broadcast_in_dim.4), calls=%async_computation.5 | async-start | bytes 2097152 | tf_op jit(solution)/shard_map/all_to_all | solution.py:507
  227.5 12.6 %copy-start.13 = (f32[64,128]{1,0:T(8,128)S(1)}, f32[64,128]{1,0:T(8,128)}, u32[]{:S(2)}) copy-start(f32[64,128]{1,0:T(8,128)} %copy-done.12) | copy-start | bytes 98308
  228.8 9.8 %collective-permute-start.14 = (f32[64,128]{1,0:T(8,128)S(1)}, f32[64,128]{1,0:T(8,128)S(1)}, u32[]{:S(2)}, u32[]{:S(2)}) collective-permute-start(f32[64,128]{1,0:T(8,128)S(1)} %fine_up.1.refs_1_), channel_id=1, source_target_pairs={{0,1},{1,2},{2,3},{3,4},{4,5},{5,6},{6,7},{7,8},{8,9},{9,10},{10,1... | collective-permute-start | bytes 98312 | tf_op jit(solution)/shard_map/ppermute | solution.py:516
  231.0 9.2 %collective-permute-start.15 = (f32[64,128]{1,0:T(8,128)S(1)}, f32[64,128]{1,0:T(8,128)S(1)}, u32[]{:S(2)}, u32[]{:S(2)}) collective-permute-start(f32[64,128]{1,0:T(8,128)S(1)} %fine_up.1.refs_1_), channel_id=1, source_target_pairs={{1,0},{2,1},{3,2},{4,3},{5,4},{6,5},{7,6},{8,7},{9,8},{10,9},{11,1... | collective-permute-start | bytes 98312 | tf_op jit(solution)/shard_map/ppermute | solution.py:516
  242.0 9.8 %collective-permute-start.16 = (f32[64,128]{1,0:T(8,128)S(1)}, f32[64,128]{1,0:T(8,128)S(1)}, u32[]{:S(2)}, u32[]{:S(2)}) collective-permute-start(f32[64,128]{1,0:T(8,128)S(1)} %get-tuple-element.27.refs_2_), channel_id=1, source_target_pairs={{0,1},{1,2},{2,3},{3,4},{4,5},{5,6},{6,7},{7,8},{8,9},{9,10},{10,1... | collective-permute-start | bytes 98312 | tf_op jit(solution)/shard_map/ppermute | solution.py:516
  243.9 9.5 %collective-permute-start.17 = (f32[64,128]{1,0:T(8,128)S(1)}, f32[64,128]{1,0:T(8,128)S(1)}, u32[]{:S(2)}, u32[]{:S(2)}) collective-permute-start(f32[64,128]{1,0:T(8,128)S(1)} %get-tuple-element.27.refs_2_), channel_id=1, source_target_pairs={{1,0},{2,1},{3,2},{4,3},{5,4},{6,5},{7,6},{8,7},{9,8},{10,9},{11,1... | collective-permute-start | bytes 98312 | tf_op jit(solution)/shard_map/ppermute | solution.py:516
  (11 other events, 16.2 us)

commit v2 on v1

--- a/solution.py
+++ b/solution.py
@@ -213,22 +213,23 @@
 
 
 def indices(payload):
-    return payload[8:11, :128].astype(I32)
-
-
-def fine_start(device, own, left, right, own_blocks, left_blocks, right_blocks):
+    return payload[:3, 1024:1152].astype(I32)
+
+
+def fine_start(device, own, left_all, right_all, own_blocks):
     parts = []
     for k in range(3):
         parts.append(tiles(own_blocks[k]))
     for k in range(3):
-        parts.append(jnp.concatenate([tiles(left_blocks[k]), tiles(right_blocks[k])], axis=0))
+        parts.append(jnp.concatenate([tiles(left_all[k]), tiles(right_all[k])], axis=0))
+    left, right = left_all[3], right_all[3]
     entries = jnp.concatenate([diagonal(parts[0], FINE_ORDER), diagonal(parts[3], RIM_ORDER)], axis=1)
     inverse = jnp.where(entries == 0.0, 0.0, 1.0 / entries)
     pairs = [split(p) for p in parts]
     hi = jnp.stack([p[0] for p in pairs]).reshape(2, 3, 512, 128)
     lo = jnp.stack([p[1] for p in pairs]).reshape(2, 3, 512, 128)
-    x = [columns_of(p[:4]) for p in (left, own, right)]
-    b = [columns_of(p[4:8]) for p in (left, own, right)]
+    x = [columns_of(p[:4, :1024]) for p in (left, own, right)]
+    b = [columns_of(p[4:, :1024]) for p in (left, own, right)]
     rhs = jnp.concatenate([b[1], rim(b[0], b[2])], axis=1)
     idx = [indices(p) for p in (own, left, right)]
     x1, send = first_passes(device[0, 0], x[1], (x[0], x[2]), rhs, hi, lo, inverse, idx)
@@ -335,19 +336,13 @@
     return diagonal(m, PLAIN_ORDER)
 
 
-def middle(place, parts, m3, m2, m1, p0, p1, p2, p3, far_low, far_high, unpack):
+STARTS = [0, 0, 0, 128]
+
+
+def middle_prep(place, m3, m2, m1, p0, p1, p2, p3, far_low, far_high):
     slab = place[0, 0]
-    sub = place[0, 1]
     packs = [m3, m2, m1, p0, p1, p2, p3]
     lane128 = iota((1, 128), 1)
-    pieces = []
-    for x in range(XN):
-        w = parts[x]
-        for y in range(1, YN):
-            w = w + parts[y * XN + x]
-        pieces.append(jnp.concatenate([w[:, :64], w[:, 64:]], axis=0))
-    g = mm(stacked(jnp.concatenate(pieces, axis=1)), one_hot(256, unpack), NN)
-    rhs = g[:64] + g[64:]
     quarter = iota((64, 128), 1) >> 5
     tiled = [far_low] + [p[D1_AT : D1_AT + 64] for p in packs] + [far_high]
     d1 = []
@@ -363,10 +358,48 @@
     for m in range(7):
         d2 = jnp.where(eighth == m + 1, packs[m][D2_AT : D2_AT + 64], d2)
     d2 = d2[:, :64]
-    halves = [split(p[: D1_AT]) for p in packs]
-
+    ix = [p[IX_AT : IX_AT + 8].astype(I32) for p in packs]
+    base = (slab - 4) * R1 * NRHS
+    tables = []
+    for c in range(4):
+        for k in range(3):
+            even = ix[2 * c - 1][k : k + 1] - base if c > 0 else jnp.full((1, 128), -1, I32)
+            odd = ix[2 * c][k : k + 1] - base
+            at = jnp.where(((lane128 >> 5) & 1) == 0, even, odd)
+            tables.append(one_hot(256, at - STARTS[c]))
+    c_tables = []
+    c_base = (slab - 4) * R2 * NRHS
+    group = (lane128 >> 3) & 7
+    for k in range(3):
+        at = jnp.full((1, 128), -1, I32)
+        for m in range(7):
+            at = jnp.where(group == m + 1, ix[m][3 + k : 4 + k] - c_base, at)
+        c_tables.append(one_hot(64, at))
+    halves = [split(p[:D1_AT]) for p in packs]
+    return (
+        jnp.stack([h[0] for h in halves]),
+        jnp.stack([h[1] for h in halves]),
+        d1,
+        d2,
+        jnp.stack(tables),
+        jnp.stack(c_tables),
+    )
+
+
+def middle(place, parts, b_hi, b_lo, d1, d2, tables, c_tables, unpack):
+    sub = place[0, 1]
+    blocks = (b_hi, b_lo)
+    lane128 = iota((1, 128), 1)
+    pieces = []
+    for x in range(XN):
+        w = parts[x]
+        for y in range(1, YN):
+            w = w + parts[y * XN + x]
+        pieces.append(jnp.concatenate([w[:, :64], w[:, 64:]], axis=0))
+    g = mm(stacked(jnp.concatenate(pieces, axis=1)), one_hot(256, unpack), NN)
+    rhs = g[:64] + g[64:]
     def rows(part, m, start, count):
-        return halves[max(m, 0)][part][start : start + count]
+        return blocks[part][max(m, 0), start : start + count]
 
     def pair(part, c, start, count):
         return jnp.concatenate(
@@ -375,24 +408,12 @@
 
     a_hi = [[pair(0, c, k * 256, 256) for k in range(3)] for c in range(4)]
     a_lo = [[pair(1, c, k * 256, 256) for k in range(3)] for c in range(4)]
-    ix = [p[IX_AT : IX_AT + 8].astype(I32) for p in packs]
-    base = (slab - 4) * R1 * NRHS
-    starts = [0, 0, 0, 128]
-    tables = []
-    for c in range(4):
-        line = []
-        for k in range(3):
-            even = ix[2 * c - 1][k : k + 1] - base if c > 0 else jnp.full((1, 128), -1, I32)
-            odd = ix[2 * c][k : k + 1] - base
-            at = jnp.where(((lane128 >> 5) & 1) == 0, even, odd)
-            line.append(one_hot(256, at - starts[c]))
-        tables.append(line)
 
     def apply1(v, chunks):
         x = stacked(v)
         return [
             forward(
-                a_hi[c], a_lo[c], [gathered(x[:, starts[c] : starts[c] + 256], t) for t in tables[c]], PLAIN_ORDER
+                a_hi[c], a_lo[c], [gathered(x[:, STARTS[c] : STARTS[c] + 256], tables[3 * c + k]) for k in range(3)], PLAIN_ORDER
             )
             for c in chunks
         ]
@@ -424,17 +445,11 @@
         p_hi, p_lo = rows(0, m, A1_ROWS, P1_ROWS), rows(1, m, A1_ROWS, P1_ROWS)
         u = u + mm(p_hi, b_hi, TN) + mm(p_hi, b_lo, TN) + mm(p_lo, b_hi, TN)
     r = u[:64, :64] + u[64:, 64:]
-    c_hi, c_lo, c_tables = [], [], []
-    c_base = (slab - 4) * R2 * NRHS
-    group = (lane128 >> 3) & 7
+    c_hi, c_lo = [], []
     for k in range(3):
         start = A1_ROWS + P1_ROWS + k * 64
         c_hi.append(jnp.concatenate([rows(0, m - 1, start, 64) for m in range(8)], axis=0))
         c_lo.append(jnp.concatenate([rows(1, m - 1, start, 64) for m in range(8)], axis=0))
-        at = jnp.full((1, 128), -1, I32)
-        for m in range(7):
-            at = jnp.where(group == m + 1, ix[m][3 + k : 4 + k] - c_base, at)
-        c_tables.append(one_hot(64, at))
     d = d2 * r / CENTER
     z = d
     for t in range(3):
@@ -468,13 +483,14 @@
     pick_rows = (iota((8, 64), 1) == iota((8, 64), 0) + sub * 8).astype(F32).astype(BF16)
     hi, lo = split(own)
     o = mm(pick_rows, hi, NT) + mm(pick_rows, lo, NT)
-    o = jnp.concatenate([o[:4], o[4:]], axis=1)
-    return (jnp.broadcast_to(o[None], (TN_, 4, 128)),)
+    o = jnp.concatenate([jnp.concatenate([o[:2], o[4:6]], axis=1), jnp.concatenate([o[2:4], o[6:]], axis=1)], axis=1)
+    return (jnp.broadcast_to(o[None], (TN_, 2, 256)),)
 
 
 def fine_up(rows_ref, odd_ref, all_ref, x_ref, hi_ref, lo_ref, out_ref, line):
     for p in range(32):
         v = all_ref[rows_ref[p]]
+        v = jnp.concatenate([v[:, :128], v[:, 128:]], axis=0)
         line[p * 4 : p * 4 + 4, :] = jnp.where(odd_ref[p] == 1, pltpu.roll(v, 64, 1), v)
     w = line[:, :64].T
     hi, lo = split(w)
@@ -564,13 +580,16 @@
     g = (g // 16) * 64 + ((g % 2) * 8 + (g % 16) // 2) * 4
     g = (g[:, :, None] + rhs4).reshape(3, 64)
     g = jnp.concatenate([g, g], axis=1).astype(F32)
-    own = jnp.concatenate([warm_start, right_side, jnp.pad(g, ((0, 5), (0, 896)))], axis=0)
-    left, right = shifted(own, both, 1), shifted(own, both, -1)
+    own = jnp.concatenate([warm_start, right_side], axis=0)
+    own = jnp.concatenate([own, jnp.pad(g, ((0, 5), (0, 2944)))], axis=1)
     blocks = fine_blocks.transpose(1, 0, 2)
-    left_blocks = shifted(blocks[:, 8:], both, 1)
-    right_blocks = shifted(blocks[:, :8], both, -1)
+    low, high = (
+        jnp.concatenate([part, own[None]], axis=0) for part in (blocks[:, :8], blocks[:, 8:])
+    )
 
     ix = jnp.concatenate([lane_index(middle_columns, 4), lane_index(coarse_columns, 16)], axis=0)
+    ix, low, high = lax.optimization_barrier((ix, low, high))
+    left, right = shifted(high, both, 1), shifted(low, both, -1)
     (pack,) = kern(
         level_pack,
         [((PACK_ROWS, 128), F32)],
@@ -585,7 +604,15 @@
     hi, lo, inverse, rhs, x1, send, idx = kern(
         fine_start,
         [((2, 3, 512, 128), BF16)] * 2 + [sends, sends, ((64, 64), F32), sends, ((3, 3, 128), I32)],
-        [device, own, left, right, blocks, left_blocks, right_blocks],
+        [device, own, left, right, blocks],
+        smem=(0,),
+    )
+    idx, near[0], near[6], near[2] = lax.optimization_barrier((idx, near[0], near[6], near[2]))
+    prepared = kern(
+        middle_prep,
+        [((7, D1_AT, 128), BF16)] * 2
+        + [((64, 384), F32), ((64, 64), F32), ((12, 256, 128), BF16), ((3, 64, 128), BF16)],
+        [place] + near + far,
         smem=(0,),
     )
     o = places(owner_rows)
@@ -599,6 +626,7 @@
     )
 
     (part,) = kern(sum_rows, [((TN_, 2, 256), F32)], [across(dense)])
+    part, *prepared = lax.optimization_barrier((part, *prepared))
     (part,) = kern(sum_all, [((TN_, 2, 256), F32)], [along(part)])
     q = jnp.arange(XN * YN * 64, dtype=I32)
     rel = (q % 64) // 8 - 4 + (sub == 0).astype(I32)
@@ -610,15 +638,15 @@
 
     (share,) = kern(
         middle,
-        [((TN_, 4, 128), F32)],
-        [place, part] + near + far + [jnp.asarray(unpack_table())],
+        [((TN_, 2, 256), F32)],
+        [place, part] + prepared + [jnp.asarray(unpack_table())],
         smem=(0,),
     )
     line = along(share)
-    every = across(jnp.broadcast_to(line[None], (XN * YN, TN_, 4, 128)))
+    every = across(jnp.broadcast_to(line[None], (XN * YN, TN_, 2, 256)))
     at = ((o // 256) * XN + (o % 8) // 2) * TN_ + (o // 8) % TN_
     x = fine_up_call(
-        at.reshape(32), (o % 2).reshape(32), every.reshape(XN * YN * TN_, 4, 128), x3, p_hi, p_lo
+        at.reshape(32), (o % 2).reshape(32), every.reshape(XN * YN * TN_, 2, 256), x3, p_hi, p_lo
     )
 
     x1, send = kern(

time: 257 us -> 249 us (0.969)
  starting transfers between devices: 119 us -> 88.4 us
  blocking collectives: 21.1 us -> 51.5 us
  waiting for transfers between devices: 71.8 us -> 51.2 us
  local copies, waits for them, and re-layouts: 11.9 us -> 21.7 us
  other arithmetic: 1.1 us -> 3.69 us
    all_to_all x2 -> x1, waiting for transfers between devices: 36.3 us -> 14.2 us  [along(): return lax.all_to_all(value, 'slab', 0, 0, tiled=True, axis_index_groups=ZC)]
    all_to_all x1 -> x2, blocking collectives: 21.1 us -> 38.3 us  [along(): return lax.all_to_all(value, 'slab', 0, 0, tiled=True, axis_index_groups=ZC)]
    all_to_all x2 -> x1, starting transfers between devices: 21.1 us -> 3.86 us  [along(): return lax.all_to_all(value, 'slab', 0, 0, tiled=True, axis_index_groups=ZC)]
    ppermute x18 -> x16, waiting for transfers between devices: 6.86 us -> 22.9 us  [shifted(): lax.ppermute(value, axis, [(i, i + by) for i in range(n) if 0 <= i + by <...]
    all_to_all x3 -> x2, waiting for transfers between devices: 28.6 us -> 14 us  [across(): lax.all_to_all(value, ('slab', 'sub'), 0, 0, tiled=True, axis_index_group...]
    all_to_all x0 -> x1, blocking collectives: none -> 13.1 us  [across(): lax.all_to_all(value, ('slab', 'sub'), 0, 0, tiled=True, axis_index_group...]
    unnamed x40 -> x64, local copies, waits for them, and re-layouts: 6.47 us -> 16.7 us
    ppermute x18 -> x16, starting transfers between devices: 80.3 us -> 73.4 us  [shifted(): lax.ppermute(value, axis, [(i, i + by) for i in range(n) if 0 <= i + by <...]
  transfers between devices with their start and end apart: 23 -> 19, of which waited for: 9 -> 8; matrix products, arithmetic and copies ran while one was open for 2% -> 0% of each run, Pallas kernels for 1% -> 3%
where the time goes in v2:
time: 249 us; the launch traced here: 248 us
  starting transfers between devices  88.4 us (36%)
  blocking collectives  51.5 us (21%)
  waiting for transfers between devices  51.2 us (21%)
  Pallas kernels  30.2 us (12%)
  local copies, waits for them, and re-layouts  21.7 us (9%)
  other arithmetic  3.69 us (1%)
    ppermute x16, starting transfers between devices, shifted(): lax.ppermute(value, axis, [(i, i + by) for i in range(n) if 0 <= i + by <...  73.4 us
    all_to_all x2, blocking collectives, along(): return lax.all_to_all(value, 'slab', 0, 0, tiled=True, axis_index_groups=ZC)  38.3 us
    pallas_call x11, Pallas kernels, kern(): pl.pallas_call(kernel, in_specs=specs, out_specs=[pl.BlockSpec(memory_spa...  29 us
    ppermute x16, waiting for transfers between devices, shifted(): lax.ppermute(value, axis, [(i, i + by) for i in range(n) if 0 <= i + by <...  22.9 us
    unnamed x64, local copies, waits for them, and re-layouts  16.7 us
    all_to_all x1, waiting for transfers between devices, along(): return lax.all_to_all(value, 'slab', 0, 0, tiled=True, axis_index_groups=ZC)  14.2 us
    all_to_all x2, waiting for transfers between devices, across(): lax.all_to_all(value, ('slab', 'sub'), 0, 0, tiled=True, axis_index_group...  14 us
    all_to_all x1, blocking collectives, across(): lax.all_to_all(value, ('slab', 'sub'), 0, 0, tiled=True, axis_index_group...  13.1 us
  transfers between devices with their start and end apart: 19, of which 8 were waited for; matrix products, arithmetic and copies ran while one was open for 0% of the time, Pallas kernels for 3%

profile of v2, /device:TPU:16, one launch (start us, length us, event | category | flops | bytes accessed | tf_op | source)
XLA Modules:
  0.0 247.7 jit_solution(5098363383769761192)
XLA Ops:
  7.3 3.4 %collective-permute-start = (f32[4,8,4096]{2,1,0:T(8,128)}, f32[4,8,4096]{2,1,0:T(8,128)S(1)}, u32[]{:S(2)}, u32[]{:S(2)}) collective-permute-start(f32[4,8,4096]{2,1,0:T(8,128)} %get-tuple-element.35), channel_id=1, source_target_pairs={{0,1},{1,2},{2,3},{3,4},{4,5},{5,6},{6,7},{7,8},{8,9},{9,10},{10,1... | collective-permute-start | bytes 1572872 | tf_op jit(solution)/shard_map/ppermute | solution.py:532
  10.7 11.4 %collective-permute-start.1 = (f32[4,8,4096]{2,1,0:T(8,128)}, f32[4,8,4096]{2,1,0:T(8,128)S(1)}, u32[]{:S(2)}, u32[]{:S(2)}) collective-permute-start(f32[4,8,4096]{2,1,0:T(8,128)} %get-tuple-element.36), channel_id=1, source_target_pairs={{1,0},{2,1},{3,2},{4,3},{5,4},{6,5},{7,6},{8,7},{9,8},{10,9},{11,1... | collective-permute-start | bytes 1572872 | tf_op jit(solution)/shard_map/ppermute | solution.py:532
  22.9 1.9 collective-permute-start.4
  24.8 6.7 %collective-permute-start.5 = (f32[1352,128]{1,0:T(8,128)S(1)}, f32[1352,128]{1,0:T(8,128)}, u32[]{:S(2)}, u32[]{:S(2)}) collective-permute-start(f32[1352,128]{1,0:T(8,128)S(1)} %level_pack.1.refs_4_), channel_id=1, source_target_pairs={{12,0},{16,4},{20,8},{24,12},{28,16},{32,20},{36,24},{40,28},{44,3... | collective-permute-start | bytes 2076680 | tf_op jit(solution)/shard_map/ppermute | solution.py:532
  31.5 1.9 collective-permute-start.6
  37.4 2.3 fine_start.1
  40.4 1.9 collective-permute-start.2
  42.3 7.9 %collective-permute-start.3 = (f32[64,128]{1,0:T(8,128)S(1)}, f32[64,128]{1,0:T(8,128)S(1)}, u32[]{:S(2)}, u32[]{:S(2)}) collective-permute-start(f32[64,128]{1,0:T(8,128)S(1)} %get-tuple-element.38.refs_2_), channel_id=1, source_target_pairs={{1,0},{2,1},{3,2},{4,3},{5,4},{6,5},{7,6},{8,7},{9,8},{10,9},{11,1... | collective-permute-start | bytes 98312 | tf_op jit(solution)/shard_map/ppermute | solution.py:532
  53.1 3.6 %collective-permute-done.6.refs_3_ = f32[1352,128]{1,0:T(8,128)} collective-permute-done((f32[1352,128]{1,0:T(8,128)S(1)}, f32[1352,128]{1,0:T(8,128)}, u32[]{:S(2)}, u32[]{:S(2)}) %collective-permute-start.6) | collective-permute-done | bytes 692256 | tf_op jit(solution)/shard_map/ppermute | solution.py:532
  59.4 2.8 %fine_down.1 = (f32[64,64]{1,0:T(8,128)S(1)}, f32[16,64,256]{2,1,0:T(8,128)S(1)}) custom-call(s32[1,1]{1,0:T(1,128)} %bitcast.refs_0_, f32[64,64]{1,0:T(8,128)S(1)} %get-tuple-element.37.refs_1_, f32[64,128]{1,0:T(8,128)S(1)} %get-tuple-element.38.refs_2_, f32[64,128]{1,0:T(8,128)S(1)} %collective-permute-done.2.refs_3_, ...), custom_call_target="tpu_custom_call" | custom-call | tf_op jit(solution)/shard_map/fine_down/pallas_call | solution.py:50
  63.2 5.0 %all-to-all-start = ((f32[16,64,256]{2,1,0:T(8,128)}), f32[16,64,256]{2,1,0:T(8,128)S(1)}, u32[]{:S(2)}, u32[]{:S(2)}) async-start(f32[16,64,256]{2,1,0:T(8,128)} %copy-done.3), calls=%async_computation | async-start | bytes 2097152 | tf_op jit(solution)/shard_map/all_to_all | solution.py:523
  68.2 1.9 collective-permute-start.7
  70.1 2.0 collective-permute-start.8
  72.1 6.0 %collective-permute-start.9 = (f32[1352,128]{1,0:T(8,128)S(1)}, f32[1352,128]{1,0:T(8,128)S(1)}, u32[]{:S(2)}, u32[]{:S(2)}) collective-permute-start(f32[1352,128]{1,0:T(8,128)S(1)} %level_pack.1.refs_4_), channel_id=1, source_target_pairs={{8,0},{12,4},{16,8},{20,12},{24,16},{28,20},{32,24},{36,28},{40,32... | collective-permute-start | bytes 2076680 | tf_op jit(solution)/shard_map/ppermute | solution.py:532
  78.1 1.9 collective-permute-start.10
  80.0 6.9 %collective-permute-start.11 = (f32[64,128]{1,0:T(8,128)S(1)}, f32[64,128]{1,0:T(8,128)S(1)}, u32[]{:S(2)}, u32[]{:S(2)}) collective-permute-start(f32[64,128]{1,0:T(8,128)S(1)} %slice.14), channel_id=1, source_target_pairs={{16,0},{20,4},{24,8},{28,12},{32,16},{36,20},{40,24},{44,28},{48,3... | collective-permute-start | bytes 98312 | tf_op jit(solution)/shard_map/ppermute | solution.py:532
  88.8 13.5 %collective-permute-done.11.refs_9_ = f32[64,128]{1,0:T(8,128)S(1)} collective-permute-done((f32[64,128]{1,0:T(8,128)S(1)}, f32[64,128]{1,0:T(8,128)S(1)}, u32[]{:S(2)}, u32[]{:S(2)}) %collective-permute-start.11) | collective-permute-done | bytes 32800 | tf_op jit(solution)/shard_map/ppermute | solution.py:532
  102.4 4.2 %middle_prep.1 = (bf16[7,1216,128]{2,1,0:T(8,128)(2,1)}, bf16[7,1216,128]{2,1,0:T(8,128)(2,1)}, f32[64,384]{1,0:T(8,128)S(1)}, f32[64,64]{1,0:T(8,128)S(1)}, bf1...) custom-call(s32[1,2]{1,0:T(1,128)S(1)} %add_bitcast_fusion.refs_0_, ...), custom_call_target="tpu_custom_call" | custom-call | tf_op jit(solution)/shard_map/middle_prep/pallas_call | solution.py:50
  108.8 20.9 %all_to_all.30.refs_0_ = f32[32,2,256]{2,1,0:T(2,128)S(1)} all-to-all(f32[32,2,256]{2,1,0:T(2,128)S(1)} %sum_rows.1), channel_id=1, replica_groups={{0,4,8,12,16,20,24,28,32,36,40,44,48,52,56,60,64,68,72,76,80,84,88,92,9..., dimensions={0} | all-to-all | bytes 131072 | tf_op jit(solution)/shard_map/all_to_all | solution.py:527
  130.3 3.9 %all-to-all-start.2 = ((f32[32,2,256]{2,1,0:T(2,128)}), f32[32,2,256]{2,1,0:T(2,128)S(1)}, u32[]{:S(2)}, u32[]{:S(2)}) async-start(f32[32,2,256]{2,1,0:T(2,128)} %sum_all.1), calls=%async_computation.2 | async-start | bytes 131072 | tf_op jit(solution)/shard_map/all_to_all | solution.py:527
  134.3 14.2 %all-to-all-done.2.refs_0_ = f32[32,2,256]{2,1,0:T(2,128)S(1)} async-done(((f32[32,2,256]{2,1,0:T(2,128)}), f32[32,2,256]{2,1,0:T(2,128)S(1)}, u32[]{:S(2)}, u32[]{:S(2)}) %all-to-all-start.2) | async-done | bytes 65568 | tf_op jit(solution)/shard_map/all_to_all | solution.py:527
  148.9 13.1 %all_to_all.31.refs_1_ = f32[16,32,128]{2,1,0:T(8,128)S(1)} all-to-all(f32[16,32,128]{2,1,0:T(8,128)S(1)} %windows.1), channel_id=1, replica_groups={{0,1,2,3,128,129,130,131,256,257,258,259,384,385,386,387},{4,5,6,7,132,..., dimensions={0} | all-to-all | bytes 524288 | tf_op jit(solution)/shard_map/all_to_all | solution.py:523
  166.8 13.2 %middle.1 = f32[32,2,256]{2,1,0:T(2,128)S(1)} custom-call(s32[1,2]{1,0:T(1,128)S(1)} %add_bitcast_fusion.refs_0_, f32[16,32,128]{2,1,0:T(8,128)S(1)} %all_to_all.31.refs_1_, bf16[7,1216,128]{2,1,0:T(8,128)(2,1)S(1)} %copy-done.1, bf16[7,1216,128]{2,1,0:T(8,128)(2,1)S(1)} %copy-done.2, f32[64,384]{1,0:T(8,128)S(1)} %get-tuple-element.60.refs_4_, ...), custom_call_target="tpu_custom_call" | custom-call | tf_op jit(solution)/shard_map/middle/pallas_call | solution.py:50
  180.1 17.4 %all_to_all.32 = f32[32,2,256]{2,1,0:T(2,128)S(1)} all-to-all(f32[32,2,256]{2,1,0:T(2,128)S(1)} %middle.1), channel_id=1, replica_groups={{0,4,8,12,16,20,24,28,32,36,40,44,48,52,56,60,64,68,72,76,80,84,88,92,9..., dimensions={0} | all-to-all | bytes 131072 | tf_op jit(solution)/shard_map/all_to_all | solution.py:527
  199.0 6.2 %all-to-all-start.5 = ((f32[16,32,2,256]{3,2,1,0:T(2,128)}), f32[16,32,2,256]{3,2,1,0:T(2,128)S(1)}, u32[]{:S(2)}, u32[]{:S(2)}) async-start(f32[16,32,2,256]{3,2,1,0:T(2,128)} %broadcast_in_dim.7), calls=%async_computation.5 | async-start | bytes 2097152 | tf_op jit(solution)/shard_map/all_to_all | solution.py:523
  205.2 14.0 %all-to-all-done.5 = f32[16,32,2,256]{3,2,1,0:T(2,128)S(1)} async-done(((f32[16,32,2,256]{3,2,1,0:T(2,128)}), f32[16,32,2,256]{3,2,1,0:T(2,128)S(1)}, u32[]{:S(2)}, u32[]{:S(2)}) %all-to-all-start.5) | async-done | bytes 1048608 | tf_op jit(solution)/shard_map/all_to_all | solution.py:523
  220.5 2.2 collective-permute-start.12
  222.7 7.6 %collective-permute-start.13 = (f32[64,128]{1,0:T(8,128)S(1)}, f32[64,128]{1,0:T(8,128)S(1)}, u32[]{:S(2)}, u32[]{:S(2)}) collective-permute-start(f32[64,128]{1,0:T(8,128)S(1)} %fine_up.1.refs_1_), channel_id=1, source_target_pairs={{1,0},{2,1},{3,2},{4,3},{5,4},{6,5},{7,6},{8,7},{9,8},{10,9},{11,1... | collective-permute-start | bytes 98312 | tf_op jit(solution)/shard_map/ppermute | solution.py:532
  231.9 1.9 fine_middle.1
  233.8 1.9 collective-permute-start.14
  235.7 7.9 %collective-permute-start.15 = (f32[64,128]{1,0:T(8,128)S(1)}, f32[64,128]{1,0:T(8,128)S(1)}, u32[]{:S(2)}, u32[]{:S(2)}) collective-permute-start(f32[64,128]{1,0:T(8,128)S(1)} %get-tuple-element.67.refs_2_), channel_id=1, source_target_pairs={{1,0},{2,1},{3,2},{4,3},{5,4},{6,5},{7,6},{8,7},{9,8},{10,9},{11,1... | collective-permute-start | bytes 98312 | tf_op jit(solution)/shard_map/ppermute | solution.py:532
  245.1 2.6 %fine_end.1 = (f32[4,1024]{1,0:T(4,128)}, f32[4,1024]{1,0:T(4,128)}) custom-call(s32[1,1]{1,0:T(1,128)} %bitcast.refs_0_, f32[64,64]{1,0:T(8,128)S(1)} %get-tuple-element.66.refs_1_, f32[64,128]{1,0:T(8,128)S(1)} %get-tuple-element.67.refs_2_, f32[64,128]{1,0:T(8,128)S(1)} %collective-permute-done.14.refs_3_, f32[64,128]{1,0:T(8,128)S(1)} %collective-permute-done.15.refs_4_, ...), custom_call_target="tpu_custom_call" | custom-call | tf_op jit(solution)/shard_map/fine_end/pallas_call | solution.py:50
  (128 shorter events, 34.4 us)
Async XLA Ops:
  0.6 21.6 %copy-start.17 = (f32[8,3,4096]{2,0,1:T(8,128)S(1)}, f32[8,3,4096]{2,0,1:T(8,128)}, u32[]{:S(2)}) copy-start(f32[8,3,4096]{2,0,1:T(8,128)} %param.20) | copy-start | bytes 1179652
  0.6 21.6 %copy-start.19 = (f32[2,3,4096]{2,0,1:T(2,128)S(1)}, f32[2,3,4096]{2,0,1:T(2,128)}, u32[]{:S(2)}) copy-start(f32[2,3,4096]{2,0,1:T(2,128)} %param.23) | copy-start | bytes 294916
  1.9 31.5 %copy-start.31 = (s32[16,2]{0,1:T(2,128)S(1)}, s32[16,2]{0,1:T(2,128)}, u32[]{:S(2)}) copy-start(s32[16,2]{0,1:T(2,128)} %param.19) | copy-start | bytes 388
  1.9 33.4 %copy-start = (f32[16,3,4096]{2,0,1:T(8,128)S(1)}, f32[16,3,4096]{2,0,1:T(8,128)}, u32[]{:S(2)}) copy-start(f32[16,3,4096]{2,0,1:T(8,128)} %param.16) | copy-start | bytes 2359300
  7.3 26.3 %collective-permute-start = (f32[4,8,4096]{2,1,0:T(8,128)}, f32[4,8,4096]{2,1,0:T(8,128)S(1)}, u32[]{:S(2)}, u32[]{:S(2)}) collective-permute-start(f32[4,8,4096]{2,1,0:T(8,128)} %get-tuple-element.35), channel_id=1, source_target_pairs={{0,1},{1,2},{2,3},{3,4},{4,5},{5,6},{6,7},{7,8},{8,9},{9,10},{10,1... | collective-permute-start | bytes 1572872 | tf_op jit(solution)/shard_map/ppermute | solution.py:532
  10.7 23.8 %collective-permute-start.1 = (f32[4,8,4096]{2,1,0:T(8,128)}, f32[4,8,4096]{2,1,0:T(8,128)S(1)}, u32[]{:S(2)}, u32[]{:S(2)}) collective-permute-start(f32[4,8,4096]{2,1,0:T(8,128)} %get-tuple-element.36), channel_id=1, source_target_pairs={{1,0},{2,1},{3,2},{4,3},{5,4},{6,5},{7,6},{8,7},{9,8},{10,9},{11,1... | collective-permute-start | bytes 1572872 | tf_op jit(solution)/shard_map/ppermute | solution.py:532
  22.9 30.2 %collective-permute-start.4 = (f32[1352,128]{1,0:T(8,128)S(1)}, f32[1352,128]{1,0:T(8,128)}, u32[]{:S(2)}, u32[]{:S(2)}) collective-permute-start(f32[1352,128]{1,0:T(8,128)S(1)} %level_pack.1.refs_4_), channel_id=1, source_target_pairs={{0,12},{4,16},{8,20},{12,24},{16,28},{20,32},{24,36},{28,40},{32,4... | collective-permute-start | bytes 2076680 | tf_op jit(solution)/shard_map/ppermute | solution.py:532
  24.8 28.3 %collective-permute-start.5 = (f32[1352,128]{1,0:T(8,128)S(1)}, f32[1352,128]{1,0:T(8,128)}, u32[]{:S(2)}, u32[]{:S(2)}) collective-permute-start(f32[1352,128]{1,0:T(8,128)S(1)} %level_pack.1.refs_4_), channel_id=1, source_target_pairs={{12,0},{16,4},{20,8},{24,12},{28,16},{32,20},{36,24},{40,28},{44,3... | collective-permute-start | bytes 2076680 | tf_op jit(solution)/shard_map/ppermute | solution.py:532
  31.5 25.2 %collective-permute-start.6 = (f32[1352,128]{1,0:T(8,128)S(1)}, f32[1352,128]{1,0:T(8,128)}, u32[]{:S(2)}, u32[]{:S(2)}) collective-permute-start(f32[1352,128]{1,0:T(8,128)S(1)} %level_pack.1.refs_4_), channel_id=1, source_target_pairs={{0,4},{4,8},{8,12},{12,16},{16,20},{20,24},{24,28},{28,32},{32,36}... | collective-permute-start | bytes 2076680 | tf_op jit(solution)/shard_map/ppermute | solution.py:532
  33.6 23.9 %copy-start.29 = (s32[2,2,8]{2,1,0:T(2,128)}, s32[2,2,8]{2,1,0:T(2,128)S(1)}, u32[]{:S(2)}) copy-start(s32[2,2,8]{2,1,0:T(2,128)S(1)} %copy.18) | copy-start | bytes 388
  40.4 17.1 %collective-permute-start.2 = (f32[64,128]{1,0:T(8,128)S(1)}, f32[64,128]{1,0:T(8,128)S(1)}, u32[]{:S(2)}, u32[]{:S(2)}) collective-permute-start(f32[64,128]{1,0:T(8,128)S(1)} %get-tuple-element.38.refs_2_), channel_id=1, source_target_pairs={{0,1},{1,2},{2,3},{3,4},{4,5},{5,6},{6,7},{7,8},{8,9},{9,10},{10,1... | collective-permute-start | bytes 98312 | tf_op jit(solution)/shard_map/ppermute | solution.py:532
  42.3 15.2 %collective-permute-start.3 = (f32[64,128]{1,0:T(8,128)S(1)}, f32[64,128]{1,0:T(8,128)S(1)}, u32[]{:S(2)}, u32[]{:S(2)}) collective-permute-start(f32[64,128]{1,0:T(8,128)S(1)} %get-tuple-element.38.refs_2_), channel_id=1, source_target_pairs={{1,0},{2,1},{3,2},{4,3},{5,4},{6,5},{7,6},{8,7},{9,8},{10,9},{11,1... | collective-permute-start | bytes 98312 | tf_op jit(solution)/shard_map/ppermute | solution.py:532
  63.2 39.1 %copy-start.26 = (f32[64,64]{1,0:T(8,128)}, f32[64,64]{1,0:T(8,128)S(1)}, u32[]{:S(2)}) copy-start(f32[64,64]{1,0:T(8,128)S(1)} %get-tuple-element.64.x_ref) | copy-start | bytes 49156
  63.2 45.5 %all-to-all-start = ((f32[16,64,256]{2,1,0:T(8,128)}), f32[16,64,256]{2,1,0:T(8,128)S(1)}, u32[]{:S(2)}, u32[]{:S(2)}) async-start(f32[16,64,256]{2,1,0:T(8,128)} %copy-done.3), calls=%async_computation | async-start | bytes 2097152 | tf_op jit(solution)/shard_map/all_to_all | solution.py:523
  68.2 34.1 %collective-permute-start.7 = (f32[1352,128]{1,0:T(8,128)S(1)}, f32[1352,128]{1,0:T(8,128)S(1)}, u32[]{:S(2)}, u32[]{:S(2)}) collective-permute-start(f32[1352,128]{1,0:T(8,128)S(1)} %level_pack.1.refs_4_), channel_id=1, source_target_pairs={{0,8},{4,12},{8,16},{12,20},{16,24},{20,28},{24,32},{28,36},{32,40... | collective-permute-start | bytes 2076680 | tf_op jit(solution)/shard_map/ppermute | solution.py:532
  70.1 32.2 %collective-permute-start.8 = (f32[1352,128]{1,0:T(8,128)S(1)}, f32[1352,128]{1,0:T(8,128)S(1)}, u32[]{:S(2)}, u32[]{:S(2)}) collective-permute-start(f32[1352,128]{1,0:T(8,128)S(1)} %level_pack.1.refs_4_), channel_id=1, source_target_pairs={{4,0},{8,4},{12,8},{16,12},{20,16},{24,20},{28,24},{32,28},{36,32}... | collective-permute-start | bytes 2076680 | tf_op jit(solution)/shard_map/ppermute | solution.py:532
  72.1 30.3 %collective-permute-start.9 = (f32[1352,128]{1,0:T(8,128)S(1)}, f32[1352,128]{1,0:T(8,128)S(1)}, u32[]{:S(2)}, u32[]{:S(2)}) collective-permute-start(f32[1352,128]{1,0:T(8,128)S(1)} %level_pack.1.refs_4_), channel_id=1, source_target_pairs={{8,0},{12,4},{16,8},{20,12},{24,16},{28,20},{32,24},{36,28},{40,32... | collective-permute-start | bytes 2076680 | tf_op jit(solution)/shard_map/ppermute | solution.py:532
  78.1 10.7 %collective-permute-start.10 = (f32[64,128]{1,0:T(8,128)S(1)}, f32[64,128]{1,0:T(8,128)S(1)}, u32[]{:S(2)}, u32[]{:S(2)}) collective-permute-start(f32[64,128]{1,0:T(8,128)S(1)} %slice.14), channel_id=1, source_target_pairs={{0,16},{4,20},{8,24},{12,28},{16,32},{20,36},{24,40},{28,44},{32,4... | collective-permute-start | bytes 98312 | tf_op jit(solution)/shard_map/ppermute | solution.py:532
  80.0 22.3 %collective-permute-start.11 = (f32[64,128]{1,0:T(8,128)S(1)}, f32[64,128]{1,0:T(8,128)S(1)}, u32[]{:S(2)}, u32[]{:S(2)}) collective-permute-start(f32[64,128]{1,0:T(8,128)S(1)} %slice.14), channel_id=1, source_target_pairs={{16,0},{20,4},{24,8},{28,12},{32,16},{36,20},{40,24},{44,28},{48,3... | collective-permute-start | bytes 98312 | tf_op jit(solution)/shard_map/ppermute | solution.py:532
  108.7 53.4 %copy-start.28 = (s32[1,384]{1,0:T(1,128)S(1)}, s32[1,384]{1,0:T(1,128)}, u32[]{:S(2)}) copy-start(s32[1,384]{1,0:T(1,128)} %constant.226.clone.refs_8_) | copy-start | bytes 4612
  108.7 53.4 %copy-start.11 = (bf16[12,256,128]{2,1,0:T(8,128)(2,1)S(1)}, bf16[12,256,128]{2,1,0:T(8,128)(2,1)}, u32[]{:S(2)}) copy-start(bf16[12,256,128]{2,1,0:T(8,128)(2,1)} %copy-done.10) | copy-start | bytes 2359300
  130.3 18.2 %all-to-all-start.2 = ((f32[32,2,256]{2,1,0:T(2,128)}), f32[32,2,256]{2,1,0:T(2,128)S(1)}, u32[]{:S(2)}, u32[]{:S(2)}) async-start(f32[32,2,256]{2,1,0:T(2,128)} %sum_all.1), calls=%async_computation.2 | async-start | bytes 131072 | tf_op jit(solution)/shard_map/all_to_all | solution.py:527
  180.0 25.1 %copy-start.30 = (s32[2,2,8]{2,1,0:T(2,128)S(1)}, s32[2,2,8]{2,1,0:T(2,128)}, u32[]{:S(2)}) copy-start(s32[2,2,8]{2,1,0:T(2,128)} %copy-done.29) | copy-start | bytes 388
  180.0 39.2 %copy-start.6 = (bf16[2,512,128]{2,1,0:T(8,128)(2,1)S(1)}, bf16[2,512,128]{2,1,0:T(8,128)(2,1)}, u32[]{:S(2)}) copy-start(bf16[2,512,128]{2,1,0:T(8,128)(2,1)} %copy-done.4) | copy-start | bytes 786436
  180.0 39.2 %copy-start.9 = (bf16[2,512,128]{2,1,0:T(8,128)(2,1)S(1)}, bf16[2,512,128]{2,1,0:T(8,128)(2,1)}, u32[]{:S(2)}) copy-start(bf16[2,512,128]{2,1,0:T(8,128)(2,1)} %copy-done.7) | copy-start | bytes 786436
  180.1 39.2 %copy-start.27 = (f32[64,64]{1,0:T(8,128)S(1)}, f32[64,64]{1,0:T(8,128)}, u32[]{:S(2)}) copy-start(f32[64,64]{1,0:T(8,128)} %copy-done.26) | copy-start | bytes 49156
  197.5 34.4 %copy-start.25 = (f32[64,128]{1,0:T(8,128)S(1)}, f32[64,128]{1,0:T(8,128)}, u32[]{:S(2)}) copy-start(f32[64,128]{1,0:T(8,128)} %copy-done.24) | copy-start | bytes 98308
  199.0 20.3 %all-to-all-start.5 = ((f32[16,32,2,256]{3,2,1,0:T(2,128)}), f32[16,32,2,256]{3,2,1,0:T(2,128)S(1)}, u32[]{:S(2)}, u32[]{:S(2)}) async-start(f32[16,32,2,256]{3,2,1,0:T(2,128)} %broadcast_in_dim.7), calls=%async_computation.5 | async-start | bytes 2097152 | tf_op jit(solution)/shard_map/all_to_all | solution.py:523
  220.5 9.8 %collective-permute-start.12 = (f32[64,128]{1,0:T(8,128)S(1)}, f32[64,128]{1,0:T(8,128)S(1)}, u32[]{:S(2)}, u32[]{:S(2)}) collective-permute-start(f32[64,128]{1,0:T(8,128)S(1)} %fine_up.1.refs_1_), channel_id=1, source_target_pairs={{0,1},{1,2},{2,3},{3,4},{4,5},{5,6},{6,7},{7,8},{8,9},{9,10},{10,1... | collective-permute-start | bytes 98312 | tf_op jit(solution)/shard_map/ppermute | solution.py:532
  222.7 9.1 %collective-permute-start.13 = (f32[64,128]{1,0:T(8,128)S(1)}, f32[64,128]{1,0:T(8,128)S(1)}, u32[]{:S(2)}, u32[]{:S(2)}) collective-permute-start(f32[64,128]{1,0:T(8,128)S(1)} %fine_up.1.refs_1_), channel_id=1, source_target_pairs={{1,0},{2,1},{3,2},{4,3},{5,4},{6,5},{7,6},{8,7},{9,8},{10,9},{11,1... | collective-permute-start | bytes 98312 | tf_op jit(solution)/shard_map/ppermute | solution.py:532
  233.8 9.8 %collective-permute-start.14 = (f32[64,128]{1,0:T(8,128)S(1)}, f32[64,128]{1,0:T(8,128)S(1)}, u32[]{:S(2)}, u32[]{:S(2)}) collective-permute-start(f32[64,128]{1,0:T(8,128)S(1)} %get-tuple-element.67.refs_2_), channel_id=1, source_target_pairs={{0,1},{1,2},{2,3},{3,4},{4,5},{5,6},{6,7},{7,8},{8,9},{9,10},{10,1... | collective-permute-start | bytes 98312 | tf_op jit(solution)/shard_map/ppermute | solution.py:532
  235.7 9.5 %collective-permute-start.15 = (f32[64,128]{1,0:T(8,128)S(1)}, f32[64,128]{1,0:T(8,128)S(1)}, u32[]{:S(2)}, u32[]{:S(2)}) collective-permute-start(f32[64,128]{1,0:T(8,128)S(1)} %get-tuple-element.67.refs_2_), channel_id=1, source_target_pairs={{1,0},{2,1},{3,2},{4,3},{5,4},{6,5},{7,6},{8,7},{9,8},{10,9},{11,1... | collective-permute-start | bytes 98312 | tf_op jit(solution)/shard_map/ppermute | solution.py:532
  (19 other events, 38.2 us)

commit v3 on v2

--- a/solution.py
+++ b/solution.py
@@ -213,23 +213,22 @@
 
 
 def indices(payload):
-    return payload[:3, 1024:1152].astype(I32)
-
-
-def fine_start(device, own, left_all, right_all, own_blocks):
+    return payload[8:11, :128].astype(I32)
+
+
+def fine_start(device, own, left, right, own_blocks, left_blocks, right_blocks):
     parts = []
     for k in range(3):
         parts.append(tiles(own_blocks[k]))
     for k in range(3):
-        parts.append(jnp.concatenate([tiles(left_all[k]), tiles(right_all[k])], axis=0))
-    left, right = left_all[3], right_all[3]
+        parts.append(jnp.concatenate([tiles(left_blocks[k]), tiles(right_blocks[k])], axis=0))
     entries = jnp.concatenate([diagonal(parts[0], FINE_ORDER), diagonal(parts[3], RIM_ORDER)], axis=1)
     inverse = jnp.where(entries == 0.0, 0.0, 1.0 / entries)
     pairs = [split(p) for p in parts]
     hi = jnp.stack([p[0] for p in pairs]).reshape(2, 3, 512, 128)
     lo = jnp.stack([p[1] for p in pairs]).reshape(2, 3, 512, 128)
-    x = [columns_of(p[:4, :1024]) for p in (left, own, right)]
-    b = [columns_of(p[4:, :1024]) for p in (left, own, right)]
+    x = [columns_of(p[:4]) for p in (left, own, right)]
+    b = [columns_of(p[4:8]) for p in (left, own, right)]
     rhs = jnp.concatenate([b[1], rim(b[0], b[2])], axis=1)
     idx = [indices(p) for p in (own, left, right)]
     x1, send = first_passes(device[0, 0], x[1], (x[0], x[2]), rhs, hi, lo, inverse, idx)
@@ -247,12 +246,17 @@
     for e in range(2):
         u = mm(p_hi[e], r_hi, TN) + mm(p_hi[e], r_lo, TN) + mm(p_lo[e], r_hi, TN)
         pieces.append(u[:64, :64] + u[64:, 64:])
-    x = stacked(jnp.concatenate(pieces, axis=1))
+    hi, lo = split(jnp.concatenate(pieces, axis=1))
+    rows = jnp.broadcast_to(dest[1:2].astype(F32), (16, 128)).astype(BF16)
+    x = jnp.concatenate([hi, lo, rows], axis=0)
     out = []
-    for q in range(XN * YN):
-        table = (iota((256, 128), 0) + q * 256 == dest).astype(F32).astype(BF16)
+    for q in range(0, XN * YN, 2):
+        table = (iota((128, 128), 0) + q * 64 == dest[:1]).astype(F32).astype(BF16)
         g = mm(x, table, NT)
-        out.append(g[:64] + g[64:])
+        v, at = g[:64] + g[64:128], g[128:136]
+        out.append(jnp.concatenate([jnp.concatenate([v[:32, :64], v[32:, :64]], axis=1), at], axis=0))
+        at = jnp.concatenate([at[:, 64:], at[:, :64]], axis=1)
+        out.append(jnp.concatenate([jnp.concatenate([v[:32, 64:], v[32:, 64:]], axis=1), at], axis=0))
     return jnp.stack(out)
 
 
@@ -284,7 +288,15 @@
 
 
 def sum_rows(parts):
-    total = jnp.sum(parts, axis=0)
+    total = jnp.zeros((128, 256), F32)
+    for q in range(0, XN * YN, 2):
+        v = jnp.concatenate(
+            [jnp.concatenate([parts[q + i, :32, :64], parts[q + i, :32, 64:]], axis=0) for i in range(2)], axis=1
+        )
+        at = jnp.concatenate([parts[q + i, 32:33, :64] for i in range(2)], axis=1).astype(I32)
+        table = (iota((256, 128), 0) + 1 == at).astype(F32).astype(BF16)
+        total = total + mm(stacked(v), table, NT)
+    total = total[:64] + total[64:]
     return (jnp.stack([total[2 * t : 2 * t + 2] for t in range(TN_)]),)
 
 
@@ -308,10 +320,11 @@
 A1_ROWS = 3 * R1 * 32
 P1_ROWS = R1 * 32
 A2_ROWS = 3 * R2 * 32
-D1_AT = A1_ROWS + P1_ROWS + A2_ROWS
+D1_AT = A1_ROWS + P1_ROWS
 D2_AT = D1_AT + 64
 IX_AT = D2_AT + 64
-PACK_ROWS = IX_AT + 8
+A2_AT = IX_AT + 8
+PACK_ROWS = A2_AT + A2_ROWS
 
 
 def level_pack(blocks, prolong, coarse, idx):
@@ -325,8 +338,8 @@
         jnp.concatenate(
             a1
             + [tiles(prolong)]
-            + a2
-            + [jnp.concatenate([d1] * 4, axis=1), jnp.concatenate([d2] * 16, axis=1), idx],
+            + [jnp.concatenate([d1] * 4, axis=1), jnp.concatenate([d2] * 16, axis=1), idx]
+            + a2,
             axis=0,
         ),
     )
@@ -339,8 +352,14 @@
 STARTS = [0, 0, 0, 128]
 
 
-def middle_prep(place, m3, m2, m1, p0, p1, p2, p3, far_low, far_high):
+def middle_prep(place, p0, m2, p2, crossed, twin, twin_m2, twin_p2, far_low, far_high):
     slab = place[0, 0]
+    even = (slab & 1) == 0
+    top = A2_AT
+    m3 = jnp.where(even, crossed, twin_m2[:top])
+    p3 = jnp.where(even, twin_p2[:top], crossed)
+    m1 = jnp.where(even, twin_m2, twin)
+    p1 = jnp.where(even, twin, twin_p2)
     packs = [m3, m2, m1, p0, p1, p2, p3]
     lane128 = iota((1, 128), 1)
     quarter = iota((64, 128), 1) >> 5
@@ -363,22 +382,25 @@
     tables = []
     for c in range(4):
         for k in range(3):
-            even = ix[2 * c - 1][k : k + 1] - base if c > 0 else jnp.full((1, 128), -1, I32)
-            odd = ix[2 * c][k : k + 1] - base
-            at = jnp.where(((lane128 >> 5) & 1) == 0, even, odd)
+            one = ix[2 * c - 1][k : k + 1] - base if c > 0 else jnp.full((1, 128), -1, I32)
+            two = ix[2 * c][k : k + 1] - base
+            at = jnp.where(((lane128 >> 5) & 1) == 0, one, two)
             tables.append(one_hot(256, at - STARTS[c]))
     c_tables = []
     c_base = (slab - 4) * R2 * NRHS
     group = (lane128 >> 3) & 7
     for k in range(3):
         at = jnp.full((1, 128), -1, I32)
-        for m in range(7):
+        for m in range(1, 6):
             at = jnp.where(group == m + 1, ix[m][3 + k : 4 + k] - c_base, at)
         c_tables.append(one_hot(64, at))
     halves = [split(p[:D1_AT]) for p in packs]
+    coarse = [split(p[A2_AT:]) for p in packs[1:6]]
     return (
         jnp.stack([h[0] for h in halves]),
         jnp.stack([h[1] for h in halves]),
+        jnp.stack([h[0] for h in coarse]),
+        jnp.stack([h[1] for h in coarse]),
         d1,
         d2,
         jnp.stack(tables),
@@ -386,7 +408,7 @@
     )
 
 
-def middle(place, parts, b_hi, b_lo, d1, d2, tables, c_tables, unpack):
+def middle(place, parts, b_hi, b_lo, q_hi, q_lo, d1, d2, tables, c_tables, unpack):
     sub = place[0, 1]
     blocks = (b_hi, b_lo)
     lane128 = iota((1, 128), 1)
@@ -447,9 +469,9 @@
     r = u[:64, :64] + u[64:, 64:]
     c_hi, c_lo = [], []
     for k in range(3):
-        start = A1_ROWS + P1_ROWS + k * 64
-        c_hi.append(jnp.concatenate([rows(0, m - 1, start, 64) for m in range(8)], axis=0))
-        c_lo.append(jnp.concatenate([rows(1, m - 1, start, 64) for m in range(8)], axis=0))
+        near = [min(max(m - 2, 0), 4) for m in range(8)]
+        c_hi.append(jnp.concatenate([q_hi[n, k * 64 : k * 64 + 64] for n in near], axis=0))
+        c_lo.append(jnp.concatenate([q_lo[n, k * 64 : k * 64 + 64] for n in near], axis=0))
     d = d2 * r / CENTER
     z = d
     for t in range(3):
@@ -532,16 +554,14 @@
     return lax.ppermute(value, axis, [(i, i + by) for i in range(n) if 0 <= i + by < n])
 
 
-def unpack_table():
-    idx = np.full((1, 384), -1, np.int32)
-    for rel in range(-4, 5):
-        for row in range(R1):
-            x, pair_row = row // 2, row % 2
-            m = rel + 4 - (1 if x == 0 else 0)
-            if 0 <= m < 8:
-                for r in range(NRHS):
-                    idx[0, (rel + 4) * 32 + row * 4 + r] = x * 64 + m * 8 + pair_row * 4 + r
-    return idx
+def unpack_table(spot):
+    lane = jnp.arange(384, dtype=I32)
+    rel, row = lane // 32 - 4, (lane % 32) // 4
+    x = (spot + rel) % XN
+    part = ((rel >= 0) & (rel < 4)).astype(I32)
+    idx = x * 64 + part * 32 + lane % 32
+    keep = (rel <= 4) & ((rel < 4) | (row < 4)) & ((rel > -4) | (row >= 4))
+    return jnp.where(keep, idx, -1).reshape(1, 384)
 
 
 def lane_index(columns, times):
@@ -580,22 +600,22 @@
     g = (g // 16) * 64 + ((g % 2) * 8 + (g % 16) // 2) * 4
     g = (g[:, :, None] + rhs4).reshape(3, 64)
     g = jnp.concatenate([g, g], axis=1).astype(F32)
-    own = jnp.concatenate([warm_start, right_side], axis=0)
-    own = jnp.concatenate([own, jnp.pad(g, ((0, 5), (0, 2944)))], axis=1)
+    own = jnp.concatenate([warm_start, right_side, jnp.pad(g, ((0, 5), (0, 896)))], axis=0)
     blocks = fine_blocks.transpose(1, 0, 2)
-    low, high = (
-        jnp.concatenate([part, own[None]], axis=0) for part in (blocks[:, :8], blocks[:, 8:])
-    )
+    left_blocks, right_blocks = shifted(blocks[:, 8:], both, 1), shifted(blocks[:, :8], both, -1)
+    left, right = shifted(own, both, 1), shifted(own, both, -1)
 
     ix = jnp.concatenate([lane_index(middle_columns, 4), lane_index(coarse_columns, 16)], axis=0)
-    ix, low, high = lax.optimization_barrier((ix, low, high))
-    left, right = shifted(high, both, 1), shifted(low, both, -1)
     (pack,) = kern(
         level_pack,
         [((PACK_ROWS, 128), F32)],
         [middle_blocks.transpose(1, 0, 2), middle_prolong, coarse_blocks.transpose(1, 0, 2), jnp.pad(ix, ((0, 2), (0, 0)))],
     )
-    near = [shifted(pack, "slab", by) for by in (3, 2, 1)] + [pack] + [shifted(pack, "slab", -by) for by in (1, 2, 3)]
+    left, right, pack = lax.optimization_barrier((left, right, pack))
+    m2, p2 = shifted(pack, "slab", 2), shifted(pack, "slab", -2)
+    count = lax.axis_size("slab")
+    pairs = [(i, i + 3 if i % 2 else i - 3) for i in range(count)]
+    crossed = lax.ppermute(pack[:A2_AT], "slab", [p for p in pairs if 0 <= p[1] < count])
     inverse1 = pack[D1_AT : D1_AT + 64]
     far = [shifted(inverse1, "slab", 4), shifted(inverse1, "slab", -4)]
     p_hi, p_lo = kern(prolong_parts, [((2, 512, 128), BF16)] * 2, [fine_prolong])
@@ -604,24 +624,30 @@
     hi, lo, inverse, rhs, x1, send, idx = kern(
         fine_start,
         [((2, 3, 512, 128), BF16)] * 2 + [sends, sends, ((64, 64), F32), sends, ((3, 3, 128), I32)],
-        [device, own, left, right, blocks],
+        [device, own, left, right, blocks, left_blocks, right_blocks],
         smem=(0,),
     )
-    idx, near[0], near[6], near[2] = lax.optimization_barrier((idx, near[0], near[6], near[2]))
+    o = places(owner_rows)
+    t = (o // 8) % TN_
+    dest = ((o // 256) * XN + t % XN) * 64 + (t // XN) * 8 + places(send_slots) * 4
+    dest_row = (t // XN) * 32 + (o % 8) * 4 + 1
+    dest = jnp.concatenate([(v[:, :, None] + rhs4).reshape(1, 128) for v in (dest, dest_row)], axis=0)
+    x3, dense = kern(
+        fine_down,
+        [((64, 64), F32), ((16, 40, 128), F32)],
+        [device, x1, send, shifted(send, both, 1), shifted(send, both, -1), hi, lo, inverse, idx, dest, p_hi, p_lo],
+        smem=(0,),
+    )
+
+    dense, m2, p2, crossed = lax.optimization_barrier((dense, m2, p2, crossed))
+    swap = [(i, i ^ 1) for i in range(count)]
+    twins = [lax.ppermute(v, "slab", swap) for v in (pack, m2, p2)]
     prepared = kern(
         middle_prep,
         [((7, D1_AT, 128), BF16)] * 2
+        + [((5, A2_ROWS, 128), BF16)] * 2
         + [((64, 384), F32), ((64, 64), F32), ((12, 256, 128), BF16), ((3, 64, 128), BF16)],
-        [place] + near + far,
-        smem=(0,),
-    )
-    o = places(owner_rows)
-    dest = ((o // 256) * XN + (o % 8) // 2) * 256 + ((o // 8) % TN_) * 8 + (o % 2) * 4
-    dest = (dest[:, :, None] + rhs4).reshape(1, 128)
-    x3, dense = kern(
-        fine_down,
-        [((64, 64), F32), ((16, 64, 256), F32)],
-        [device, x1, send, shifted(send, both, 1), shifted(send, both, -1), hi, lo, inverse, idx, dest, p_hi, p_lo],
+        [place, pack, m2, p2, crossed, *twins, *far],
         smem=(0,),
     )
 
@@ -629,17 +655,21 @@
     part, *prepared = lax.optimization_barrier((part, *prepared))
     (part,) = kern(sum_all, [((TN_, 2, 256), F32)], [along(part)])
     q = jnp.arange(XN * YN * 64, dtype=I32)
-    rel = (q % 64) // 8 - 4 + (sub == 0).astype(I32)
-    wanted = (q // 256) * TN_ + slab % TN_ + rel
-    wanted = jnp.where(wanted // TN_ == slab // TN_, (wanted % TN_) * 8 + q % 8, -1)
-    wanted = jnp.where((rel >= -4) & (wanted >= 0), wanted, -1)
+    spot = slab % TN_
+    near_by = (sub - spot) % XN
+    row = (q % 32) // 4
+    rel = jnp.where((q % 64) // 32 == 1, near_by, near_by - 4)
+    rel = jnp.where(((q % 64) // 32 == 0) & (near_by == 0) & (row < 4), 4, rel)
+    wanted = (q // 256) * TN_ + spot + rel
+    wanted = jnp.where(wanted // TN_ == slab // TN_, (wanted % TN_) // XN * 32 + q % 32, -1)
+    wanted = jnp.where(wanted >= 0, wanted, -1)
     (part,) = kern(windows, [((16, 32, 128), F32)], [along(part), wanted.reshape(1, 1024)])
     part = across(part)
 
     (share,) = kern(
         middle,
         [((TN_, 2, 256), F32)],
-        [place, part] + prepared + [jnp.asarray(unpack_table())],
+        [place, part] + prepared + [unpack_table(slab % TN_)],
         smem=(0,),
     )
     line = along(share)

time: 249 us -> 238 us (0.956)
  waiting for transfers between devices: 51.2 us -> 38.6 us
  starting transfers between devices: 88.4 us -> 101 us
  blocking collectives: 51.5 us -> 40.9 us
    ppermute x16 -> x14, waiting for transfers between devices: 22.9 us -> 4.25 us  [shifted(): lax.ppermute(value, axis, [(i, i + by) for i in range(n) if 0 <= i + by <...]
    all_to_all x1 -> x0, blocking collectives: 13.1 us -> none  [across(): lax.all_to_all(value, ('slab', 'sub'), 0, 0, tiled=True, axis_index_group...]
    ppermute x0 -> x4, starting transfers between devices: none -> 8.16 us  [the longest x3 6.25 us: body(): twins = [lax.ppermute(v, 'slab', swap) for v in (pack, m2, p2)]]
    all_to_all x2 -> x3, starting transfers between devices: 11.1 us -> 18.5 us  [across(): lax.all_to_all(value, ('slab', 'sub'), 0, 0, tiled=True, axis_index_group...]
    all_to_all x2 -> x3, waiting for transfers between devices: 14 us -> 20.1 us  [across(): lax.all_to_all(value, ('slab', 'sub'), 0, 0, tiled=True, axis_index_group...]
    unnamed x64 -> x44, local copies, waits for them, and re-layouts: 16.7 us -> 11.4 us
    ppermute x16 -> x14, starting transfers between devices: 73.4 us -> 70.7 us  [shifted(): lax.ppermute(value, axis, [(i, i + by) for i in range(n) if 0 <= i + by <...]
    all_to_all x2, blocking collectives: 38.3 us -> 40.9 us  [along(): return lax.all_to_all(value, 'slab', 0, 0, tiled=True, axis_index_groups=ZC)]
  transfers between devices with their start and end apart: 19 -> 22, of which waited for: 8 -> 6; matrix products, arithmetic and copies ran while one was open for 0% -> 3% of each run, Pallas kernels for 3% -> 3%
where the time goes in v3:
time: 238 us; the launch traced here: 237 us
  starting transfers between devices  101 us (42%)
  blocking collectives  40.9 us (17%)
  waiting for transfers between devices  38.6 us (16%)
  Pallas kernels  32.4 us (14%)
  local copies, waits for them, and re-layouts  20 us (8%)
  other arithmetic  2.7 us (1%)
    ppermute x14, starting transfers between devices, shifted(): lax.ppermute(value, axis, [(i, i + by) for i in range(n) if 0 <= i + by <...  70.7 us
    all_to_all x2, blocking collectives, along(): return lax.all_to_all(value, 'slab', 0, 0, tiled=True, axis_index_groups=ZC)  40.9 us
    pallas_call x11, Pallas kernels, kern(): pl.pallas_call(kernel, in_specs=specs, out_specs=[pl.BlockSpec(memory_spa...  31.2 us
    all_to_all x3, waiting for transfers between devices, across(): lax.all_to_all(value, ('slab', 'sub'), 0, 0, tiled=True, axis_index_group...  20.1 us
    all_to_all x3, starting transfers between devices, across(): lax.all_to_all(value, ('slab', 'sub'), 0, 0, tiled=True, axis_index_group...  18.5 us
    all_to_all x1, waiting for transfers between devices, along(): return lax.all_to_all(value, 'slab', 0, 0, tiled=True, axis_index_groups=ZC)  14.2 us
    unnamed x44, local copies, waits for them, and re-layouts  11.4 us
    ppermute x3, starting transfers between devices, body(): twins = [lax.ppermute(v, 'slab', swap) for v in (pack, m2, p2)]  6.25 us
  transfers between devices with their start and end apart: 22, of which 6 were waited for; matrix products, arithmetic and copies ran while one was open for 3% of the time, Pallas kernels for 3%

profile of v3, /device:TPU:16, one launch (start us, length us, event | category | flops | bytes accessed | tf_op | source)
XLA Modules:
  0.0 237.0 jit_solution(4741431425035934896)
XLA Ops:
  2.8 3.4 %collective-permute-start = (f32[16,1024]{1,0:T(8,128)S(1)}, f32[16,1024]{1,0:T(8,128)S(1)}, u32[]{:S(2)}, u32[]{:S(2)}) collective-permute-start(f32[16,1024]{1,0:T(8,128)S(1)} %select_maximum_fusion.refs_1_), channel_id=1, source_target_pairs={{0,1},{1,2},{2,3},{3,4},{4,5},{5,6},{6,7},{7,8},{8,9},{9,10},{10,1... | collective-permute-start | bytes 196616 | tf_op jit(solution)/shard_map/ppermute | solution.py:554
  6.2 11.4 %collective-permute-start.1 = (f32[16,1024]{1,0:T(8,128)S(1)}, f32[16,1024]{1,0:T(8,128)S(1)}, u32[]{:S(2)}, u32[]{:S(2)}) collective-permute-start(f32[16,1024]{1,0:T(8,128)S(1)} %select_maximum_fusion.refs_1_), channel_id=1, source_target_pairs={{1,0},{2,1},{3,2},{4,3},{5,4},{6,5},{7,6},{8,7},{9,8},{10,9},{11,1... | collective-permute-start | bytes 196616 | tf_op jit(solution)/shard_map/ppermute | solution.py:554
  17.7 2.0 fusion.24
  21.6 7.9 %collective-permute-start.3 = (f32[3,8,4096]{2,1,0:T(8,128)S(1)}, f32[3,8,4096]{2,1,0:T(8,128)S(1)}, u32[]{:S(2)}, u32[]{:S(2)}) collective-permute-start(f32[3,8,4096]{2,1,0:T(8,128)S(1)} %get-tuple-element.78), channel_id=1, source_target_pairs={{1,0},{2,1},{3,2},{4,3},{5,4},{6,5},{7,6},{8,7},{9,8},{10,9},{11,1... | collective-permute-start | bytes 1179656 | tf_op jit(solution)/shard_map/ppermute | solution.py:554
  32.9 1.9 collective-permute-start.6
  34.9 6.0 %collective-permute-start.7 = (f32[1352,128]{1,0:T(8,128)S(1)}, f32[1352,128]{1,0:T(8,128)}, u32[]{:S(2)}, u32[]{:S(2)}) collective-permute-start(f32[1352,128]{1,0:T(8,128)S(1)} %level_pack.1.refs_1_), channel_id=1, source_target_pairs={{8,0},{12,4},{16,8},{20,12},{24,16},{28,20},{32,24},{36,28},{40,32... | collective-permute-start | bytes 2076680 | tf_op jit(solution)/shard_map/ppermute | solution.py:554
  41.8 1.9 collective-permute-start.8
  48.5 2.3 fine_start.1
  51.4 1.9 collective-permute-start.4
  53.4 7.9 %collective-permute-start.5 = (f32[64,128]{1,0:T(8,128)S(1)}, f32[64,128]{1,0:T(8,128)S(1)}, u32[]{:S(2)}, u32[]{:S(2)}) collective-permute-start(f32[64,128]{1,0:T(8,128)S(1)} %get-tuple-element.42.refs_2_), channel_id=1, source_target_pairs={{1,0},{2,1},{3,2},{4,3},{5,4},{6,5},{7,6},{8,7},{9,8},{10,9},{11,1... | collective-permute-start | bytes 98312 | tf_op jit(solution)/shard_map/ppermute | solution.py:554
  63.1 1.9 collective-permute-start.9
  65.1 3.5 %fine_down.1 = (f32[64,64]{1,0:T(8,128)S(1)}, f32[16,40,128]{2,1,0:T(8,128)}) custom-call(s32[1,1]{1,0:T(1,128)} %bitcast.refs_0_, f32[64,64]{1,0:T(8,128)S(1)} %get-tuple-element.41.refs_1_, f32[64,128]{1,0:T(8,128)S(1)} %get-tuple-element.42.refs_2_, f32[64,128]{1,0:T(8,128)S(1)} %collective-permute-done.4.refs_3_, ...), custom_call_target="tpu_custom_call" | custom-call | tf_op jit(solution)/shard_map/fine_down/pallas_call | solution.py:50
  68.6 2.4 %collective-permute-start.10 = (f32[1352,128]{1,0:T(8,128)}, f32[1352,128]{1,0:T(8,128)}, u32[]{:S(2)}, u32[]{:S(2)}) collective-permute-start(f32[1352,128]{1,0:T(8,128)} %collective-permute-done.6.refs_2_), channel_id=1, source_target_pairs={{0,4},{4,0},{8,12},{12,8},{16,20},{20,16},{24,28},{28,24},{32,36},... | collective-permute-start | bytes 2076680 | tf_op jit(solution)/shard_map/ppermute | solution.py:644
  71.0 1.9 collective-permute-start.11
  72.9 4.9 %all-to-all-start = ((f32[16,40,128]{2,1,0:T(8,128)}), f32[16,40,128]{2,1,0:T(8,128)S(1)}, u32[]{:S(2)}, u32[]{:S(2)}) async-start(f32[16,40,128]{2,1,0:T(8,128)} %get-tuple-element.51), calls=%async_computation | async-start | bytes 655360 | tf_op jit(solution)/shard_map/all_to_all | solution.py:545
  77.9 1.9 collective-permute-start.12
  79.8 6.9 %collective-permute-start.13 = (f32[64,128]{1,0:T(8,128)S(1)}, f32[64,128]{1,0:T(8,128)S(1)}, u32[]{:S(2)}, u32[]{:S(2)}) collective-permute-start(f32[64,128]{1,0:T(8,128)S(1)} %slice.15), channel_id=1, source_target_pairs={{16,0},{20,4},{24,8},{28,12},{32,16},{36,20},{40,24},{44,28},{48,3... | collective-permute-start | bytes 98312 | tf_op jit(solution)/shard_map/ppermute | solution.py:554
  88.4 4.6 %middle_prep.1 = (bf16[7,1024,128]{2,1,0:T(8,128)(2,1)}, bf16[7,1024,128]{2,1,0:T(8,128)(2,1)}, bf16[5,192,128]{2,1,0:T(8,128)(2,1)S(1)}, bf16[5,192,128]{2,1,0:...) custom-call(s32[1,2]{1,0:T(1,128)S(1)} %add_bitcast_fusion.refs_0_, ...), custom_call_target="tpu_custom_call" | custom-call | tf_op jit(solution)/shard_map/middle_prep/pallas_call | solution.py:50
  94.4 23.6 %all_to_all.30.refs_0_ = f32[32,2,256]{2,1,0:T(2,128)S(1)} all-to-all(f32[32,2,256]{2,1,0:T(2,128)S(1)} %sum_rows.1), channel_id=1, replica_groups={{0,4,8,12,16,20,24,28,32,36,40,44,48,52,56,60,64,68,72,76,80,84,88,92,9..., dimensions={0} | all-to-all | bytes 131072 | tf_op jit(solution)/shard_map/all_to_all | solution.py:549
  118.7 3.8 %all-to-all-start.2 = ((f32[32,2,256]{2,1,0:T(2,128)}), f32[32,2,256]{2,1,0:T(2,128)S(1)}, u32[]{:S(2)}, u32[]{:S(2)}) async-start(f32[32,2,256]{2,1,0:T(2,128)} %sum_all.1), calls=%async_computation.2 | async-start | bytes 131072 | tf_op jit(solution)/shard_map/all_to_all | solution.py:549
  122.7 14.2 %all-to-all-done.2.refs_0_ = f32[32,2,256]{2,1,0:T(2,128)S(1)} async-done(((f32[32,2,256]{2,1,0:T(2,128)}), f32[32,2,256]{2,1,0:T(2,128)S(1)}, u32[]{:S(2)}, u32[]{:S(2)}) %all-to-all-start.2) | async-done | bytes 65568 | tf_op jit(solution)/shard_map/all_to_all | solution.py:549
  138.0 7.2 %all-to-all-start.3 = ((f32[16,32,128]{2,1,0:T(8,128)}), f32[16,32,128]{2,1,0:T(8,128)S(1)}, u32[]{:S(2)}, u32[]{:S(2)}) async-start(f32[16,32,128]{2,1,0:T(8,128)} %windows.1), calls=%async_computation.3 | async-start | bytes 524288 | tf_op jit(solution)/shard_map/all_to_all | solution.py:545
  145.2 6.1 %all-to-all-done.3.refs_1_ = f32[16,32,128]{2,1,0:T(8,128)S(1)} async-done(((f32[16,32,128]{2,1,0:T(8,128)}), f32[16,32,128]{2,1,0:T(8,128)S(1)}, u32[]{:S(2)}, u32[]{:S(2)}) %all-to-all-start.3) | async-done | bytes 262176 | tf_op jit(solution)/shard_map/all_to_all | solution.py:545
  156.2 13.2 %middle.1 = f32[32,2,256]{2,1,0:T(2,128)S(1)} custom-call(s32[1,2]{1,0:T(1,128)S(1)} %add_bitcast_fusion.refs_0_, f32[16,32,128]{2,1,0:T(8,128)S(1)} %all-to-all-done.3.refs_1_, bf16[7,1024,128]{2,1,0:T(8,128)(2,1)S(1)} %copy-done.1, bf16[7,1024,128]{2,1,0:T(8,128)(2,1)S(1)} %copy-done.2, bf16[5,192,128]{2,1,0:T(8,128)(2,1)S(1)} %copy-done.9, ...), custom_call_target="tpu_custom_call" | custom-call | tf_op jit(solution)/shard_map/middle/pallas_call | solution.py:50
  169.4 17.3 %all_to_all.31 = f32[32,2,256]{2,1,0:T(2,128)S(1)} all-to-all(f32[32,2,256]{2,1,0:T(2,128)S(1)} %middle.1), channel_id=1, replica_groups={{0,4,8,12,16,20,24,28,32,36,40,44,48,52,56,60,64,68,72,76,80,84,88,92,9..., dimensions={0} | all-to-all | bytes 131072 | tf_op jit(solution)/shard_map/all_to_all | solution.py:549
  188.1 6.3 %all-to-all-start.5 = ((f32[16,32,2,256]{3,2,1,0:T(2,128)}), f32[16,32,2,256]{3,2,1,0:T(2,128)S(1)}, u32[]{:S(2)}, u32[]{:S(2)}) async-start(f32[16,32,2,256]{3,2,1,0:T(2,128)} %broadcast_in_dim.18), calls=%async_computation.5 | async-start | bytes 2097152 | tf_op jit(solution)/shard_map/all_to_all | solution.py:545
  194.5 14.0 %all-to-all-done.5 = f32[16,32,2,256]{3,2,1,0:T(2,128)S(1)} async-done(((f32[16,32,2,256]{3,2,1,0:T(2,128)}), f32[16,32,2,256]{3,2,1,0:T(2,128)S(1)}, u32[]{:S(2)}, u32[]{:S(2)}) %all-to-all-start.5) | async-done | bytes 1048608 | tf_op jit(solution)/shard_map/all_to_all | solution.py:545
  209.8 2.2 collective-permute-start.14
  212.0 7.6 %collective-permute-start.15 = (f32[64,128]{1,0:T(8,128)S(1)}, f32[64,128]{1,0:T(8,128)S(1)}, u32[]{:S(2)}, u32[]{:S(2)}) collective-permute-start(f32[64,128]{1,0:T(8,128)S(1)} %fine_up.1.refs_1_), channel_id=1, source_target_pairs={{1,0},{2,1},{3,2},{4,3},{5,4},{6,5},{7,6},{8,7},{9,8},{10,9},{11,1... | collective-permute-start | bytes 98312 | tf_op jit(solution)/shard_map/ppermute | solution.py:554
  223.0 1.9 collective-permute-start.16
  224.9 7.9 %collective-permute-start.17 = (f32[64,128]{1,0:T(8,128)S(1)}, f32[64,128]{1,0:T(8,128)S(1)}, u32[]{:S(2)}, u32[]{:S(2)}) collective-permute-start(f32[64,128]{1,0:T(8,128)S(1)} %get-tuple-element.75.refs_2_), channel_id=1, source_target_pairs={{1,0},{2,1},{3,2},{4,3},{5,4},{6,5},{7,6},{8,7},{9,8},{10,9},{11,1... | collective-permute-start | bytes 98312 | tf_op jit(solution)/shard_map/ppermute | solution.py:554
  234.4 2.6 %fine_end.1 = (f32[4,1024]{1,0:T(4,128)}, f32[4,1024]{1,0:T(4,128)}) custom-call(s32[1,1]{1,0:T(1,128)} %bitcast.refs_0_, f32[64,64]{1,0:T(8,128)S(1)} %get-tuple-element.74.refs_1_, f32[64,128]{1,0:T(8,128)S(1)} %get-tuple-element.75.refs_2_, f32[64,128]{1,0:T(8,128)S(1)} %collective-permute-done.16.refs_3_, f32[64,128]{1,0:T(8,128)S(1)} %collective-permute-done.17.refs_4_, ...), custom_call_target="tpu_custom_call" | custom-call | tf_op jit(solution)/shard_map/fine_end/pallas_call | solution.py:50
  (121 shorter events, 33.1 us)
Async XLA Ops:
  0.6 30.8 %copy-start.20 = (s32[8,3]{0,1:T(4,128)S(1)}, s32[8,3]{0,1:T(4,128)}, u32[]{:S(2)}) copy-start(s32[8,3]{0,1:T(4,128)} %param.21) | copy-start | bytes 292
  0.6 31.3 %copy-start.21 = (s32[16,2]{0,1:T(2,128)S(1)}, s32[16,2]{0,1:T(2,128)}, u32[]{:S(2)}) copy-start(s32[16,2]{0,1:T(2,128)} %param.19) | copy-start | bytes 388
  0.7 31.6 %copy-start.5 = (f32[8,3,4096]{2,0,1:T(8,128)S(1)}, f32[8,3,4096]{2,0,1:T(8,128)}, u32[]{:S(2)}) copy-start(f32[8,3,4096]{2,0,1:T(8,128)} %param.20) | copy-start | bytes 1179652
  0.7 31.6 %copy-start.12 = (f32[8,4096]{1,0:T(8,128)S(1)}, f32[8,4096]{1,0:T(8,128)}, u32[]{:S(2)}) copy-start(f32[8,4096]{1,0:T(8,128)} %refs_1_.1) | copy-start | bytes 393220
  0.7 31.6 %copy-start.13 = (f32[2,3,4096]{2,0,1:T(2,128)S(1)}, f32[2,3,4096]{2,0,1:T(2,128)}, u32[]{:S(2)}) copy-start(f32[2,3,4096]{2,0,1:T(2,128)} %param.23) | copy-start | bytes 294916
  2.8 30.1 %collective-permute-start = (f32[16,1024]{1,0:T(8,128)S(1)}, f32[16,1024]{1,0:T(8,128)S(1)}, u32[]{:S(2)}, u32[]{:S(2)}) collective-permute-start(f32[16,1024]{1,0:T(8,128)S(1)} %select_maximum_fusion.refs_1_), channel_id=1, source_target_pairs={{0,1},{1,2},{2,3},{3,4},{4,5},{5,6},{6,7},{7,8},{8,9},{9,10},{10,1... | collective-permute-start | bytes 196616 | tf_op jit(solution)/shard_map/ppermute | solution.py:554
  6.2 26.7 %collective-permute-start.1 = (f32[16,1024]{1,0:T(8,128)S(1)}, f32[16,1024]{1,0:T(8,128)S(1)}, u32[]{:S(2)}, u32[]{:S(2)}) collective-permute-start(f32[16,1024]{1,0:T(8,128)S(1)} %select_maximum_fusion.refs_1_), channel_id=1, source_target_pairs={{1,0},{2,1},{3,2},{4,3},{5,4},{6,5},{7,6},{8,7},{9,8},{10,9},{11,1... | collective-permute-start | bytes 196616 | tf_op jit(solution)/shard_map/ppermute | solution.py:554
  17.7 28.1 %copy-start = (f32[16,3,4096]{2,0,1:T(8,128)S(1)}, f32[16,3,4096]{2,0,1:T(8,128)}, u32[]{:S(2)}) copy-start(f32[16,3,4096]{2,0,1:T(8,128)} %param.15) | copy-start | bytes 2359300
  19.7 25.4 %collective-permute-start.2 = (f32[3,8,4096]{2,1,0:T(8,128)}, f32[3,8,4096]{2,1,0:T(8,128)S(1)}, u32[]{:S(2)}, u32[]{:S(2)}) collective-permute-start(f32[3,8,4096]{2,1,0:T(8,128)} %get-tuple-element.79), channel_id=1, source_target_pairs={{0,1},{1,2},{2,3},{3,4},{4,5},{5,6},{6,7},{7,8},{8,9},{9,10},{10,1... | collective-permute-start | bytes 1179656 | tf_op jit(solution)/shard_map/ppermute | solution.py:554
  21.6 23.5 %collective-permute-start.3 = (f32[3,8,4096]{2,1,0:T(8,128)S(1)}, f32[3,8,4096]{2,1,0:T(8,128)S(1)}, u32[]{:S(2)}, u32[]{:S(2)}) collective-permute-start(f32[3,8,4096]{2,1,0:T(8,128)S(1)} %get-tuple-element.78), channel_id=1, source_target_pairs={{1,0},{2,1},{3,2},{4,3},{5,4},{6,5},{7,6},{8,7},{9,8},{10,9},{11,1... | collective-permute-start | bytes 1179656 | tf_op jit(solution)/shard_map/ppermute | solution.py:554
  32.9 12.2 %copy-start.14 = (f32[16,1024]{1,0:T(8,128)}, f32[16,1024]{1,0:T(8,128)S(1)}, u32[]{:S(2)}) copy-start(f32[16,1024]{1,0:T(8,128)S(1)} %collective-permute-done.refs_2_) | copy-start | bytes 196612
  32.9 12.2 %copy-start.16 = (f32[16,1024]{1,0:T(8,128)}, f32[16,1024]{1,0:T(8,128)S(1)}, u32[]{:S(2)}) copy-start(f32[16,1024]{1,0:T(8,128)S(1)} %collective-permute-done.1.refs_3_) | copy-start | bytes 196612
  32.9 35.6 %collective-permute-start.6 = (f32[1352,128]{1,0:T(8,128)S(1)}, f32[1352,128]{1,0:T(8,128)}, u32[]{:S(2)}, u32[]{:S(2)}) collective-permute-start(f32[1352,128]{1,0:T(8,128)S(1)} %level_pack.1.refs_1_), channel_id=1, source_target_pairs={{0,8},{4,12},{8,16},{12,20},{16,24},{20,28},{24,32},{28,36},{32,40... | collective-permute-start | bytes 2076680 | tf_op jit(solution)/shard_map/ppermute | solution.py:554
  34.9 33.7 %collective-permute-start.7 = (f32[1352,128]{1,0:T(8,128)S(1)}, f32[1352,128]{1,0:T(8,128)}, u32[]{:S(2)}, u32[]{:S(2)}) collective-permute-start(f32[1352,128]{1,0:T(8,128)S(1)} %level_pack.1.refs_1_), channel_id=1, source_target_pairs={{8,0},{12,4},{16,8},{20,12},{24,16},{28,20},{32,24},{36,28},{40,32... | collective-permute-start | bytes 2076680 | tf_op jit(solution)/shard_map/ppermute | solution.py:554
  41.8 26.8 %collective-permute-start.8 = (f32[1160,128]{1,0:T(8,128)}, f32[1160,128]{1,0:T(8,128)}, u32[]{:S(2)}, u32[]{:S(2)}) collective-permute-start(f32[1160,128]{1,0:T(8,128)} %slice.14), channel_id=1, source_target_pairs={{4,16},{12,24},{16,4},{20,32},{24,12},{28,40},{32,20},{36,48},{40,... | collective-permute-start | bytes 1781768 | tf_op jit(solution)/shard_map/ppermute | solution.py:618
  51.4 11.7 %collective-permute-start.4 = (f32[64,128]{1,0:T(8,128)S(1)}, f32[64,128]{1,0:T(8,128)S(1)}, u32[]{:S(2)}, u32[]{:S(2)}) collective-permute-start(f32[64,128]{1,0:T(8,128)S(1)} %get-tuple-element.42.refs_2_), channel_id=1, source_target_pairs={{0,1},{1,2},{2,3},{3,4},{4,5},{5,6},{6,7},{7,8},{8,9},{9,10},{10,1... | collective-permute-start | bytes 98312 | tf_op jit(solution)/shard_map/ppermute | solution.py:554
  53.4 11.7 %collective-permute-start.5 = (f32[64,128]{1,0:T(8,128)S(1)}, f32[64,128]{1,0:T(8,128)S(1)}, u32[]{:S(2)}, u32[]{:S(2)}) collective-permute-start(f32[64,128]{1,0:T(8,128)S(1)} %get-tuple-element.42.refs_2_), channel_id=1, source_target_pairs={{1,0},{2,1},{3,2},{4,3},{5,4},{6,5},{7,6},{8,7},{9,8},{10,9},{11,1... | collective-permute-start | bytes 98312 | tf_op jit(solution)/shard_map/ppermute | solution.py:554
  63.1 25.3 %collective-permute-start.9 = (f32[1352,128]{1,0:T(8,128)S(1)}, f32[1352,128]{1,0:T(8,128)}, u32[]{:S(2)}, u32[]{:S(2)}) collective-permute-start(f32[1352,128]{1,0:T(8,128)S(1)} %level_pack.1.refs_1_), channel_id=1, source_target_pairs={{0,4},{4,0},{8,12},{12,8},{16,20},{20,16},{24,28},{28,24},{32,36},... | collective-permute-start | bytes 2076680 | tf_op jit(solution)/shard_map/ppermute | solution.py:644
  68.6 19.8 %collective-permute-start.10 = (f32[1352,128]{1,0:T(8,128)}, f32[1352,128]{1,0:T(8,128)}, u32[]{:S(2)}, u32[]{:S(2)}) collective-permute-start(f32[1352,128]{1,0:T(8,128)} %collective-permute-done.6.refs_2_), channel_id=1, source_target_pairs={{0,4},{4,0},{8,12},{12,8},{16,20},{20,16},{24,28},{28,24},{32,36},... | collective-permute-start | bytes 2076680 | tf_op jit(solution)/shard_map/ppermute | solution.py:644
  71.0 17.4 %collective-permute-start.11 = (f32[1352,128]{1,0:T(8,128)}, f32[1352,128]{1,0:T(8,128)}, u32[]{:S(2)}, u32[]{:S(2)}) collective-permute-start(f32[1352,128]{1,0:T(8,128)} %collective-permute-done.7.refs_3_), channel_id=1, source_target_pairs={{0,4},{4,0},{8,12},{12,8},{16,20},{20,16},{24,28},{28,24},{32,36},... | collective-permute-start | bytes 2076680 | tf_op jit(solution)/shard_map/ppermute | solution.py:644
  72.9 13.9 %all-to-all-start = ((f32[16,40,128]{2,1,0:T(8,128)}), f32[16,40,128]{2,1,0:T(8,128)S(1)}, u32[]{:S(2)}, u32[]{:S(2)}) async-start(f32[16,40,128]{2,1,0:T(8,128)} %get-tuple-element.51), calls=%async_computation | async-start | bytes 655360 | tf_op jit(solution)/shard_map/all_to_all | solution.py:545
  77.9 9.4 %collective-permute-start.12 = (f32[64,128]{1,0:T(8,128)S(1)}, f32[64,128]{1,0:T(8,128)S(1)}, u32[]{:S(2)}, u32[]{:S(2)}) collective-permute-start(f32[64,128]{1,0:T(8,128)S(1)} %slice.15), channel_id=1, source_target_pairs={{0,16},{4,20},{8,24},{12,28},{16,32},{20,36},{24,40},{28,44},{32,4... | collective-permute-start | bytes 98312 | tf_op jit(solution)/shard_map/ppermute | solution.py:554
  79.8 8.6 %collective-permute-start.13 = (f32[64,128]{1,0:T(8,128)S(1)}, f32[64,128]{1,0:T(8,128)S(1)}, u32[]{:S(2)}, u32[]{:S(2)}) collective-permute-start(f32[64,128]{1,0:T(8,128)S(1)} %slice.15), channel_id=1, source_target_pairs={{16,0},{20,4},{24,8},{28,12},{32,16},{36,20},{40,24},{44,28},{48,3... | collective-permute-start | bytes 98312 | tf_op jit(solution)/shard_map/ppermute | solution.py:554
  94.4 56.9 %copy-start.3 = (bf16[12,256,128]{2,1,0:T(8,128)(2,1)S(1)}, bf16[12,256,128]{2,1,0:T(8,128)(2,1)}, u32[]{:S(2)}) copy-start(bf16[12,256,128]{2,1,0:T(8,128)(2,1)} %get-tuple-element.70.refs_8_) | copy-start | bytes 2359300
  118.7 18.2 %all-to-all-start.2 = ((f32[32,2,256]{2,1,0:T(2,128)}), f32[32,2,256]{2,1,0:T(2,128)S(1)}, u32[]{:S(2)}, u32[]{:S(2)}) async-start(f32[32,2,256]{2,1,0:T(2,128)} %sum_all.1), calls=%async_computation.2 | async-start | bytes 131072 | tf_op jit(solution)/shard_map/all_to_all | solution.py:549
  138.0 13.3 %all-to-all-start.3 = ((f32[16,32,128]{2,1,0:T(8,128)}), f32[16,32,128]{2,1,0:T(8,128)S(1)}, u32[]{:S(2)}, u32[]{:S(2)}) async-start(f32[16,32,128]{2,1,0:T(8,128)} %windows.1), calls=%async_computation.3 | async-start | bytes 524288 | tf_op jit(solution)/shard_map/all_to_all | solution.py:545
  188.1 33.0 %copy-start.19 = (f32[64,128]{1,0:T(8,128)S(1)}, f32[64,128]{1,0:T(8,128)}, u32[]{:S(2)}) copy-start(f32[64,128]{1,0:T(8,128)} %copy-done.18) | copy-start | bytes 98308
  188.1 20.4 %all-to-all-start.5 = ((f32[16,32,2,256]{3,2,1,0:T(2,128)}), f32[16,32,2,256]{3,2,1,0:T(2,128)S(1)}, u32[]{:S(2)}, u32[]{:S(2)}) async-start(f32[16,32,2,256]{3,2,1,0:T(2,128)} %broadcast_in_dim.18), calls=%async_computation.5 | async-start | bytes 2097152 | tf_op jit(solution)/shard_map/all_to_all | solution.py:545
  209.8 9.8 %collective-permute-start.14 = (f32[64,128]{1,0:T(8,128)S(1)}, f32[64,128]{1,0:T(8,128)S(1)}, u32[]{:S(2)}, u32[]{:S(2)}) collective-permute-start(f32[64,128]{1,0:T(8,128)S(1)} %fine_up.1.refs_1_), channel_id=1, source_target_pairs={{0,1},{1,2},{2,3},{3,4},{4,5},{5,6},{6,7},{7,8},{8,9},{9,10},{10,1... | collective-permute-start | bytes 98312 | tf_op jit(solution)/shard_map/ppermute | solution.py:554
  212.0 9.1 %collective-permute-start.15 = (f32[64,128]{1,0:T(8,128)S(1)}, f32[64,128]{1,0:T(8,128)S(1)}, u32[]{:S(2)}, u32[]{:S(2)}) collective-permute-start(f32[64,128]{1,0:T(8,128)S(1)} %fine_up.1.refs_1_), channel_id=1, source_target_pairs={{1,0},{2,1},{3,2},{4,3},{5,4},{6,5},{7,6},{8,7},{9,8},{10,9},{11,1... | collective-permute-start | bytes 98312 | tf_op jit(solution)/shard_map/ppermute | solution.py:554
  223.0 9.8 %collective-permute-start.16 = (f32[64,128]{1,0:T(8,128)S(1)}, f32[64,128]{1,0:T(8,128)S(1)}, u32[]{:S(2)}, u32[]{:S(2)}) collective-permute-start(f32[64,128]{1,0:T(8,128)S(1)} %get-tuple-element.75.refs_2_), channel_id=1, source_target_pairs={{0,1},{1,2},{2,3},{3,4},{4,5},{5,6},{6,7},{7,8},{8,9},{9,10},{10,1... | collective-permute-start | bytes 98312 | tf_op jit(solution)/shard_map/ppermute | solution.py:554
  224.9 9.5 %collective-permute-start.17 = (f32[64,128]{1,0:T(8,128)S(1)}, f32[64,128]{1,0:T(8,128)S(1)}, u32[]{:S(2)}, u32[]{:S(2)}) collective-permute-start(f32[64,128]{1,0:T(8,128)S(1)} %get-tuple-element.75.refs_2_), channel_id=1, source_target_pairs={{1,0},{2,1},{3,2},{4,3},{5,4},{6,5},{7,6},{8,7},{9,8},{10,9},{11,1... | collective-permute-start | bytes 98312 | tf_op jit(solution)/shard_map/ppermute | solution.py:554
  (12 other events, 11.3 us)

commit v4 on v3

--- a/solution.py
+++ b/solution.py
@@ -52,7 +52,7 @@
         in_specs=specs,
         out_specs=[pl.BlockSpec(memory_space=pltpu.VMEM) for _ in outs],
         out_shape=[jax.ShapeDtypeStruct(s, d) for s, d in outs],
-        compiler_params=pltpu.CompilerParams(vmem_limit_bytes=48 << 20),
+        compiler_params=pltpu.CompilerParams(vmem_limit_bytes=12 << 20),
         name=body.__name__,
     )(*args)
 
@@ -213,22 +213,23 @@
 
 
 def indices(payload):
-    return payload[8:11, :128].astype(I32)
-
-
-def fine_start(device, own, left, right, own_blocks, left_blocks, right_blocks):
+    return payload[:3, 1024:1152].astype(I32)
+
+
+def fine_start(device, own, left_all, right_all, own_blocks):
     parts = []
     for k in range(3):
         parts.append(tiles(own_blocks[k]))
     for k in range(3):
-        parts.append(jnp.concatenate([tiles(left_blocks[k]), tiles(right_blocks[k])], axis=0))
+        parts.append(jnp.concatenate([tiles(left_all[k]), tiles(right_all[k])], axis=0))
+    left, right = left_all[3], right_all[3]
     entries = jnp.concatenate([diagonal(parts[0], FINE_ORDER), diagonal(parts[3], RIM_ORDER)], axis=1)
     inverse = jnp.where(entries == 0.0, 0.0, 1.0 / entries)
     pairs = [split(p) for p in parts]
     hi = jnp.stack([p[0] for p in pairs]).reshape(2, 3, 512, 128)
     lo = jnp.stack([p[1] for p in pairs]).reshape(2, 3, 512, 128)
-    x = [columns_of(p[:4]) for p in (left, own, right)]
-    b = [columns_of(p[4:8]) for p in (left, own, right)]
+    x = [columns_of(p[:4, :1024]) for p in (left, own, right)]
+    b = [columns_of(p[4:, :1024]) for p in (left, own, right)]
     rhs = jnp.concatenate([b[1], rim(b[0], b[2])], axis=1)
     idx = [indices(p) for p in (own, left, right)]
     x1, send = first_passes(device[0, 0], x[1], (x[0], x[2]), rhs, hi, lo, inverse, idx)
@@ -352,10 +353,14 @@
 STARTS = [0, 0, 0, 128]
 
 
-def middle_prep(place, p0, m2, p2, crossed, twin, twin_m2, twin_p2, far_low, far_high):
+def middle_prep(place, p0, m2, p2, crossed, swapped, far):
     slab = place[0, 0]
     even = (slab & 1) == 0
     top = A2_AT
+    twin, twin_m2, twin_p2 = (swapped[i * PACK_ROWS : (i + 1) * PACK_ROWS] for i in range(3))
+    far_twin = swapped[3 * PACK_ROWS :]
+    far_low = jnp.where(even, far, far_twin)
+    far_high = jnp.where(even, far_twin, far)
     m3 = jnp.where(even, crossed, twin_m2[:top])
     p3 = jnp.where(even, twin_p2[:top], crossed)
     m1 = jnp.where(even, twin_m2, twin)
@@ -532,7 +537,7 @@
         out_specs=vmem,
         out_shape=jax.ShapeDtypeStruct((64, 128), F32),
         scratch_shapes=[pltpu.VMEM((128, 128), F32)],
-        compiler_params=pltpu.CompilerParams(vmem_limit_bytes=48 << 20),
+        compiler_params=pltpu.CompilerParams(vmem_limit_bytes=12 << 20),
         name="fine_up",
     )(rows, odd, gathered_rows, x, hi, lo)
 
@@ -600,33 +605,40 @@
     g = (g // 16) * 64 + ((g % 2) * 8 + (g % 16) // 2) * 4
     g = (g[:, :, None] + rhs4).reshape(3, 64)
     g = jnp.concatenate([g, g], axis=1).astype(F32)
-    own = jnp.concatenate([warm_start, right_side, jnp.pad(g, ((0, 5), (0, 896)))], axis=0)
+    own = jnp.concatenate([warm_start, right_side], axis=0)
+    own = jnp.concatenate([own, jnp.pad(g, ((0, 5), (0, 2944)))], axis=1)
     blocks = fine_blocks.transpose(1, 0, 2)
-    left_blocks, right_blocks = shifted(blocks[:, 8:], both, 1), shifted(blocks[:, :8], both, -1)
-    left, right = shifted(own, both, 1), shifted(own, both, -1)
+    low, high = (
+        jnp.concatenate([part, own[None]], axis=0) for part in (blocks[:, :8], blocks[:, 8:])
+    )
 
     ix = jnp.concatenate([lane_index(middle_columns, 4), lane_index(coarse_columns, 16)], axis=0)
+    ix, low, high = lax.optimization_barrier((ix, low, high))
+    left, right = shifted(high, both, 1), shifted(low, both, -1)
     (pack,) = kern(
         level_pack,
         [((PACK_ROWS, 128), F32)],
         [middle_blocks.transpose(1, 0, 2), middle_prolong, coarse_blocks.transpose(1, 0, 2), jnp.pad(ix, ((0, 2), (0, 0)))],
     )
-    left, right, pack = lax.optimization_barrier((left, right, pack))
-    m2, p2 = shifted(pack, "slab", 2), shifted(pack, "slab", -2)
-    count = lax.axis_size("slab")
-    pairs = [(i, i + 3 if i % 2 else i - 3) for i in range(count)]
-    crossed = lax.ppermute(pack[:A2_AT], "slab", [p for p in pairs if 0 <= p[1] < count])
-    inverse1 = pack[D1_AT : D1_AT + 64]
-    far = [shifted(inverse1, "slab", 4), shifted(inverse1, "slab", -4)]
     p_hi, p_lo = kern(prolong_parts, [((2, 512, 128), BF16)] * 2, [fine_prolong])
 
     sends = ((64, 128), F32)
     hi, lo, inverse, rhs, x1, send, idx = kern(
         fine_start,
         [((2, 3, 512, 128), BF16)] * 2 + [sends, sends, ((64, 64), F32), sends, ((3, 3, 128), I32)],
-        [device, own, left, right, blocks, left_blocks, right_blocks],
+        [device, own, left, right, blocks],
         smem=(0,),
     )
+    send, pack = lax.optimization_barrier((send, pack))
+    count = lax.axis_size("slab")
+    m2, p2 = shifted(pack, "slab", 2), shifted(pack, "slab", -2)
+
+    def crossing(value, by):
+        pairs = [(i, i + by if i % 2 == by % 2 else i - by) for i in range(count)]
+        return lax.ppermute(value, "slab", [p for p in pairs if 0 <= p[1] < count])
+
+    crossed = crossing(pack[:A2_AT], 3)
+    far = crossing(pack[D1_AT : D1_AT + 64], 4)
     o = places(owner_rows)
     t = (o // 8) % TN_
     dest = ((o // 256) * XN + t % XN) * 64 + (t // XN) * 8 + places(send_slots) * 4
@@ -639,20 +651,18 @@
         smem=(0,),
     )
 
-    dense, m2, p2, crossed = lax.optimization_barrier((dense, m2, p2, crossed))
-    swap = [(i, i ^ 1) for i in range(count)]
-    twins = [lax.ppermute(v, "slab", swap) for v in (pack, m2, p2)]
+    (part,) = kern(sum_rows, [((TN_, 2, 256), F32)], [across(dense)])
+    part, m2, p2, crossed, far = lax.optimization_barrier((part, m2, p2, crossed, far))
+    twin = jnp.concatenate([pack, m2, p2, crossed[D1_AT : D1_AT + 64]], axis=0)
+    twin = lax.ppermute(twin, "slab", [(i, i ^ 1) for i in range(count)])
     prepared = kern(
         middle_prep,
         [((7, D1_AT, 128), BF16)] * 2
         + [((5, A2_ROWS, 128), BF16)] * 2
         + [((64, 384), F32), ((64, 64), F32), ((12, 256, 128), BF16), ((3, 64, 128), BF16)],
-        [place, pack, m2, p2, crossed, *twins, *far],
+        [place, pack, m2, p2, crossed, twin, far],
         smem=(0,),
     )
-
-    (part,) = kern(sum_rows, [((TN_, 2, 256), F32)], [across(dense)])
-    part, *prepared = lax.optimization_barrier((part, *prepared))
     (part,) = kern(sum_all, [((TN_, 2, 256), F32)], [along(part)])
     q = jnp.arange(XN * YN * 64, dtype=I32)
     spot = slab % TN_
@@ -669,7 +679,7 @@
     (share,) = kern(
         middle,
         [((TN_, 2, 256), F32)],
-        [place, part] + prepared + [unpack_table(slab % TN_)],
+        [place, part] + list(prepared) + [unpack_table(slab % TN_)],
         smem=(0,),
     )
     line = along(share)

time: 238 us -> 245 us (1.029)
  the two profiles are of different devices: /device:TPU:16 before, /device:TPU:8 now
where the time goes in v4:
time: 245 us; the launch traced here: 244 us
  starting transfers between devices  81.5 us (33%)
  waiting for transfers between devices  59.1 us (24%)
  blocking collectives  40.9 us (17%)
  Pallas kernels  30.1 us (12%)
  local copies, waits for them, and re-layouts  24.3 us (10%)
  other arithmetic  6.46 us (3%)
    ppermute x10, starting transfers between devices, shifted(): lax.ppermute(value, axis, [(i, i + by) for i in range(n) if 0 <= i + by <...  50.7 us
    all_to_all x2, blocking collectives, along(): return lax.all_to_all(value, 'slab', 0, 0, tiled=True, axis_index_groups=ZC)  40.9 us
    pallas_call x11, Pallas kernels, kern(): pl.pallas_call(kernel, in_specs=specs, out_specs=[pl.BlockSpec(memory_spa...  28.8 us
    ppermute x10, waiting for transfers between devices, shifted(): lax.ppermute(value, axis, [(i, i + by) for i in range(n) if 0 <= i + by <...  25 us
    all_to_all x3, starting transfers between devices, across(): lax.all_to_all(value, ('slab', 'sub'), 0, 0, tiled=True, axis_index_group...  20 us
    all_to_all x3, waiting for transfers between devices, across(): lax.all_to_all(value, ('slab', 'sub'), 0, 0, tiled=True, axis_index_group...  18.6 us
    unnamed x56, local copies, waits for them, and re-layouts  17.3 us
    all_to_all x1, waiting for transfers between devices, along(): return lax.all_to_all(value, 'slab', 0, 0, tiled=True, axis_index_groups=ZC)  14.2 us
  transfers between devices with their start and end apart: 17, of which 10 were waited for; matrix products, arithmetic and copies ran while one was open for 1% of the time, Pallas kernels for 4%

profile of v4, /device:TPU:8, one launch (start us, length us, event | category | flops | bytes accessed | tf_op | source)
XLA Modules:
  0.0 243.6 jit_solution(17940920620431714867)
XLA Ops:
  7.3 3.4 %collective-permute-start = (f32[4,8,4096]{2,1,0:T(8,128)}, f32[4,8,4096]{2,1,0:T(8,128)S(1)}, u32[]{:S(2)}, u32[]{:S(2)}) collective-permute-start(f32[4,8,4096]{2,1,0:T(8,128)} %get-tuple-element.33), channel_id=1, source_target_pairs={{0,1},{1,2},{2,3},{3,4},{4,5},{5,6},{6,7},{7,8},{8,9},{9,10},{10,1... | collective-permute-start | bytes 1572872 | tf_op jit(solution)/shard_map/ppermute | solution.py:559
  10.7 11.4 %collective-permute-start.1 = (f32[4,8,4096]{2,1,0:T(8,128)}, f32[4,8,4096]{2,1,0:T(8,128)S(1)}, u32[]{:S(2)}, u32[]{:S(2)}) collective-permute-start(f32[4,8,4096]{2,1,0:T(8,128)} %get-tuple-element.34), channel_id=1, source_target_pairs={{1,0},{2,1},{3,2},{4,3},{5,4},{6,5},{7,6},{8,7},{9,8},{10,9},{11,1... | collective-permute-start | bytes 1572872 | tf_op jit(solution)/shard_map/ppermute | solution.py:559
  23.7 3.6 %collective-permute-done.refs_2_ = f32[4,8,4096]{2,1,0:T(8,128)S(1)} collective-permute-done((f32[4,8,4096]{2,1,0:T(8,128)}, f32[4,8,4096]{2,1,0:T(8,128)S(1)}, u32[]{:S(2)}, u32[]{:S(2)}) %collective-permute-start) | collective-permute-done | bytes 524320 | tf_op jit(solution)/shard_map/ppermute | solution.py:559
  32.1 2.3 fine_start.1
  34.4 1.9 collective-permute-start.4
  36.4 8.3 %collective-permute-start.5 = (f32[1352,128]{1,0:T(8,128)S(1)}, f32[1352,128]{1,0:T(8,128)}, u32[]{:S(2)}, u32[]{:S(2)}) collective-permute-start(f32[1352,128]{1,0:T(8,128)S(1)} %level_pack.1.refs_1_), channel_id=1, source_target_pairs={{8,0},{12,4},{16,8},{20,12},{24,16},{28,20},{32,24},{36,28},{40,32... | collective-permute-start | bytes 2076680 | tf_op jit(solution)/shard_map/ppermute | solution.py:559
  45.7 3.3 %collective-permute-start.6 = (f32[1160,128]{1,0:T(8,128)}, f32[1160,128]{1,0:T(8,128)}, u32[]{:S(2)}, u32[]{:S(2)}) collective-permute-start(f32[1160,128]{1,0:T(8,128)} %slice.17), channel_id=1, source_target_pairs={{4,16},{12,24},{16,4},{20,32},{24,12},{28,40},{32,20},{36,48},{40,... | collective-permute-start | bytes 1781768 | tf_op jit(solution)/shard_map/ppermute | solution.py:638
  49.2 2.2 collective-permute-start.2
  51.4 7.6 %collective-permute-start.3 = (f32[64,128]{1,0:T(8,128)S(1)}, f32[64,128]{1,0:T(8,128)S(1)}, u32[]{:S(2)}, u32[]{:S(2)}) collective-permute-start(f32[64,128]{1,0:T(8,128)S(1)} %get-tuple-element.38.refs_2_), channel_id=1, source_target_pairs={{1,0},{2,1},{3,2},{4,3},{5,4},{6,5},{7,6},{8,7},{9,8},{10,9},{11,1... | collective-permute-start | bytes 98312 | tf_op jit(solution)/shard_map/ppermute | solution.py:559
  60.3 9.6 %collective-permute-done.2.refs_3_ = f32[64,128]{1,0:T(8,128)S(1)} collective-permute-done((f32[64,128]{1,0:T(8,128)S(1)}, f32[64,128]{1,0:T(8,128)S(1)}, u32[]{:S(2)}, u32[]{:S(2)}) %collective-permute-start.2) | collective-permute-done | bytes 32800 | tf_op jit(solution)/shard_map/ppermute | solution.py:559
  69.9 2.2 collective-permute-done.3.refs_4_
  72.1 2.8 %fine_down.1 = (f32[64,64]{1,0:T(8,128)S(1)}, f32[16,40,128]{2,1,0:T(8,128)S(1)}) custom-call(s32[1,1]{1,0:T(1,128)} %bitcast.refs_0_, f32[64,64]{1,0:T(8,128)S(1)} %get-tuple-element.35.refs_1_, f32[64,128]{1,0:T(8,128)S(1)} %get-tuple-element.38.refs_2_, f32[64,128]{1,0:T(8,128)S(1)} %collective-permute-done.2.refs_3_, ...), custom_call_target="tpu_custom_call" | custom-call | tf_op jit(solution)/shard_map/fine_down/pallas_call | solution.py:50
  76.3 5.5 %all-to-all-start = ((f32[16,40,128]{2,1,0:T(8,128)}), f32[16,40,128]{2,1,0:T(8,128)S(1)}, u32[]{:S(2)}, u32[]{:S(2)}) async-start(f32[16,40,128]{2,1,0:T(8,128)} %copy-done.17), calls=%async_computation | async-start | bytes 655360 | tf_op jit(solution)/shard_map/all_to_all | solution.py:550
  81.8 1.9 collective-permute-start.7
  83.7 5.1 %all-to-all-done.refs_0_ = f32[16,40,128]{2,1,0:T(8,128)S(1)} async-done(((f32[16,40,128]{2,1,0:T(8,128)}), f32[16,40,128]{2,1,0:T(8,128)S(1)}, u32[]{:S(2)}, u32[]{:S(2)}) %all-to-all-start) | async-done | bytes 327712 | tf_op jit(solution)/shard_map/all_to_all | solution.py:550
  91.4 2.6 %pad_maximum_fusion = f32[4120,128]{1,0:T(8,128)} fusion(f32[64,128]{1,0:T(8,128)S(1)} %slice.19, f32[1352,128]{1,0:T(8,128)} %collective-permute-done.5.refs_3_, f32[1352,128]{1,0:T(8,128)S(1)} %collective-permute-done.4.refs_2_, f32[1352,128]{1,0:T(8,128)S(1)} %level_pack.1.refs_1_), kind=kLoop, calls=%fused_computation | loop fusion | flops 1582080 | bytes 4218880 | tf_op jit(solution)/shard_map/concatenate | solution.py:656
  94.0 1.9 collective-permute-start.8
  95.9 23.5 %all_to_all.30.refs_0_ = f32[32,2,256]{2,1,0:T(2,128)S(1)} all-to-all(f32[32,2,256]{2,1,0:T(2,128)S(1)} %sum_rows.1), channel_id=1, replica_groups={{0,4,8,12,16,20,24,28,32,36,40,44,48,52,56,60,64,68,72,76,80,84,88,92,9..., dimensions={0} | all-to-all | bytes 131072 | tf_op jit(solution)/shard_map/all_to_all | solution.py:554
  120.0 3.8 %all-to-all-start.2 = ((f32[32,2,256]{2,1,0:T(2,128)}), f32[32,2,256]{2,1,0:T(2,128)S(1)}, u32[]{:S(2)}, u32[]{:S(2)}) async-start(f32[32,2,256]{2,1,0:T(2,128)} %sum_all.1), calls=%async_computation.2 | async-start | bytes 131072 | tf_op jit(solution)/shard_map/all_to_all | solution.py:554
  124.0 14.2 %all-to-all-done.2.refs_0_ = f32[32,2,256]{2,1,0:T(2,128)S(1)} async-done(((f32[32,2,256]{2,1,0:T(2,128)}), f32[32,2,256]{2,1,0:T(2,128)S(1)}, u32[]{:S(2)}, u32[]{:S(2)}) %all-to-all-start.2) | async-done | bytes 65568 | tf_op jit(solution)/shard_map/all_to_all | solution.py:554
  139.4 7.2 %all-to-all-start.3 = ((f32[16,32,128]{2,1,0:T(8,128)}), f32[16,32,128]{2,1,0:T(8,128)S(1)}, u32[]{:S(2)}, u32[]{:S(2)}) async-start(f32[16,32,128]{2,1,0:T(8,128)} %windows.1), calls=%async_computation.3 | async-start | bytes 524288 | tf_op jit(solution)/shard_map/all_to_all | solution.py:550
  146.7 3.0 %middle_prep.1 = (bf16[7,1024,128]{2,1,0:T(8,128)(2,1)S(1)}, bf16[7,1024,128]{2,1,0:T(8,128)(2,1)S(1)}, bf16[5,192,128]{2,1,0:T(8,128)(2,1)S(1)}, bf16[5,192,128...) custom-call(s32[1,2]{1,0:T(1,128)S(1)} %add_bitcast_fusion.refs_0_, ...), custom_call_target="tpu_custom_call" | custom-call | tf_op jit(solution)/shard_map/middle_prep/pallas_call | solution.py:50
  160.5 13.2 %middle.1 = f32[32,2,256]{2,1,0:T(2,128)S(1)} custom-call(s32[1,2]{1,0:T(1,128)S(1)} %add_bitcast_fusion.refs_0_, f32[16,32,128]{2,1,0:T(8,128)S(1)} %all-to-all-done.3.refs_1_, bf16[7,1024,128]{2,1,0:T(8,128)(2,1)S(1)} %copy-done.2, bf16[7,1024,128]{2,1,0:T(8,128)(2,1)S(1)} %copy-done.4, bf16[5,192,128]{2,1,0:T(8,128)(2,1)S(1)} %copy-done.19, ...), custom_call_target="tpu_custom_call" | custom-call | tf_op jit(solution)/shard_map/middle/pallas_call | solution.py:50
  173.7 17.4 %all_to_all.31 = f32[32,2,256]{2,1,0:T(2,128)S(1)} all-to-all(f32[32,2,256]{2,1,0:T(2,128)S(1)} %middle.1), channel_id=1, replica_groups={{0,4,8,12,16,20,24,28,32,36,40,44,48,52,56,60,64,68,72,76,80,84,88,92,9..., dimensions={0} | all-to-all | bytes 131072 | tf_op jit(solution)/shard_map/all_to_all | solution.py:554
  192.6 7.2 %all-to-all-start.5 = ((f32[16,32,2,256]{3,2,1,0:T(2,128)}), f32[16,32,2,256]{3,2,1,0:T(2,128)S(1)}, u32[]{:S(2)}, u32[]{:S(2)}) async-start(f32[16,32,2,256]{3,2,1,0:T(2,128)} %broadcast_in_dim.22), calls=%async_computation.5 | async-start | bytes 2097152 | tf_op jit(solution)/shard_map/all_to_all | solution.py:550
  200.0 13.5 %all-to-all-done.5 = f32[16,32,2,256]{3,2,1,0:T(2,128)S(1)} async-done(((f32[16,32,2,256]{3,2,1,0:T(2,128)}), f32[16,32,2,256]{3,2,1,0:T(2,128)S(1)}, u32[]{:S(2)}, u32[]{:S(2)}) %all-to-all-start.5) | async-done | bytes 1048608 | tf_op jit(solution)/shard_map/all_to_all | solution.py:550
  214.7 3.5 %collective-permute-start.10 = (f32[64,128]{1,0:T(8,128)S(1)}, f32[64,128]{1,0:T(8,128)S(1)}, u32[]{:S(2)}, u32[]{:S(2)}) collective-permute-start(f32[64,128]{1,0:T(8,128)S(1)} %fine_up.1.refs_1_), channel_id=1, source_target_pairs={{1,0},{2,1},{3,2},{4,3},{5,4},{6,5},{7,6},{8,7},{9,8},{10,9},{11,1... | collective-permute-start | bytes 98312 | tf_op jit(solution)/shard_map/ppermute | solution.py:559
  218.3 2.5 %collective-permute-start.9 = (f32[64,128]{1,0:T(8,128)S(1)}, f32[64,128]{1,0:T(8,128)S(1)}, u32[]{:S(2)}, u32[]{:S(2)}) collective-permute-start(f32[64,128]{1,0:T(8,128)S(1)} %fine_up.1.refs_1_), channel_id=1, source_target_pairs={{0,1},{1,2},{2,3},{3,4},{4,5},{5,6},{6,7},{7,8},{8,9},{9,10},{10,1... | collective-permute-start | bytes 98312 | tf_op jit(solution)/shard_map/ppermute | solution.py:559
  220.8 6.9 %collective-permute-done.9.refs_2_ = f32[64,128]{1,0:T(8,128)S(1)} collective-permute-done((f32[64,128]{1,0:T(8,128)S(1)}, f32[64,128]{1,0:T(8,128)S(1)}, u32[]{:S(2)}, u32[]{:S(2)}) %collective-permute-start.9) | collective-permute-done | bytes 32800 | tf_op jit(solution)/shard_map/ppermute | solution.py:559
  229.6 1.9 collective-permute-start.11
  231.5 7.9 %collective-permute-start.12 = (f32[64,128]{1,0:T(8,128)S(1)}, f32[64,128]{1,0:T(8,128)S(1)}, u32[]{:S(2)}, u32[]{:S(2)}) collective-permute-start(f32[64,128]{1,0:T(8,128)S(1)} %get-tuple-element.63.refs_2_), channel_id=1, source_target_pairs={{1,0},{2,1},{3,2},{4,3},{5,4},{6,5},{7,6},{8,7},{9,8},{10,9},{11,1... | collective-permute-start | bytes 98312 | tf_op jit(solution)/shard_map/ppermute | solution.py:559
  241.0 2.6 %fine_end.1 = (f32[4,1024]{1,0:T(4,128)}, f32[4,1024]{1,0:T(4,128)}) custom-call(s32[1,1]{1,0:T(1,128)} %bitcast.refs_0_, f32[64,64]{1,0:T(8,128)S(1)} %get-tuple-element.62.refs_1_, f32[64,128]{1,0:T(8,128)S(1)} %get-tuple-element.63.refs_2_, f32[64,128]{1,0:T(8,128)S(1)} %collective-permute-done.11.refs_3_, f32[64,128]{1,0:T(8,128)S(1)} %collective-permute-done.12.refs_4_, ...), custom_call_target="tpu_custom_call" | custom-call | tf_op jit(solution)/shard_map/fine_end/pallas_call | solution.py:50
  (127 shorter events, 38.4 us)
Async XLA Ops:
  0.6 21.6 %copy-start.27 = (s32[16,2]{0,1:T(2,128)S(1)}, s32[16,2]{0,1:T(2,128)}, u32[]{:S(2)}) copy-start(s32[16,2]{0,1:T(2,128)} %param.19) | copy-start | bytes 388
  0.6 21.6 %copy-start.26 = (s32[16,2]{0,1:T(2,128)S(1)}, s32[16,2]{0,1:T(2,128)}, u32[]{:S(2)}) copy-start(s32[16,2]{0,1:T(2,128)} %param.18) | copy-start | bytes 388
  0.7 22.3 %copy-start.16 = (f32[8,3,4096]{2,0,1:T(8,128)S(1)}, f32[8,3,4096]{2,0,1:T(8,128)}, u32[]{:S(2)}) copy-start(f32[8,3,4096]{2,0,1:T(8,128)} %param.20) | copy-start | bytes 1179652
  0.7 22.3 %copy-start.23 = (f32[2,3,4096]{2,0,1:T(2,128)S(1)}, f32[2,3,4096]{2,0,1:T(2,128)}, u32[]{:S(2)}) copy-start(f32[2,3,4096]{2,0,1:T(2,128)} %param.23) | copy-start | bytes 294916
  0.7 22.3 %copy-start.22 = (f32[8,4096]{1,0:T(8,128)S(1)}, f32[8,4096]{1,0:T(8,128)}, u32[]{:S(2)}) copy-start(f32[8,4096]{1,0:T(8,128)} %refs_1_.1) | copy-start | bytes 393220
  1.9 28.1 %copy-start = (f32[16,3,4096]{2,0,1:T(8,128)S(1)}, f32[16,3,4096]{2,0,1:T(8,128)}, u32[]{:S(2)}) copy-start(f32[16,3,4096]{2,0,1:T(8,128)} %param.15) | copy-start | bytes 2359300
  7.3 20.0 %collective-permute-start = (f32[4,8,4096]{2,1,0:T(8,128)}, f32[4,8,4096]{2,1,0:T(8,128)S(1)}, u32[]{:S(2)}, u32[]{:S(2)}) collective-permute-start(f32[4,8,4096]{2,1,0:T(8,128)} %get-tuple-element.33), channel_id=1, source_target_pairs={{0,1},{1,2},{2,3},{3,4},{4,5},{5,6},{6,7},{7,8},{8,9},{9,10},{10,1... | collective-permute-start | bytes 1572872 | tf_op jit(solution)/shard_map/ppermute | solution.py:559
  10.7 18.5 %collective-permute-start.1 = (f32[4,8,4096]{2,1,0:T(8,128)}, f32[4,8,4096]{2,1,0:T(8,128)S(1)}, u32[]{:S(2)}, u32[]{:S(2)}) collective-permute-start(f32[4,8,4096]{2,1,0:T(8,128)} %get-tuple-element.34), channel_id=1, source_target_pairs={{1,0},{2,1},{3,2},{4,3},{5,4},{6,5},{7,6},{8,7},{9,8},{10,9},{11,1... | collective-permute-start | bytes 1572872 | tf_op jit(solution)/shard_map/ppermute | solution.py:559
  34.4 56.2 %collective-permute-start.4 = (f32[1352,128]{1,0:T(8,128)S(1)}, f32[1352,128]{1,0:T(8,128)S(1)}, u32[]{:S(2)}, u32[]{:S(2)}) collective-permute-start(f32[1352,128]{1,0:T(8,128)S(1)} %level_pack.1.refs_1_), channel_id=1, source_target_pairs={{0,8},{4,12},{8,16},{12,20},{16,24},{20,28},{24,32},{28,36},{32,40... | collective-permute-start | bytes 2076680 | tf_op jit(solution)/shard_map/ppermute | solution.py:559
  36.4 54.2 %collective-permute-start.5 = (f32[1352,128]{1,0:T(8,128)S(1)}, f32[1352,128]{1,0:T(8,128)}, u32[]{:S(2)}, u32[]{:S(2)}) collective-permute-start(f32[1352,128]{1,0:T(8,128)S(1)} %level_pack.1.refs_1_), channel_id=1, source_target_pairs={{8,0},{12,4},{16,8},{20,12},{24,16},{28,20},{32,24},{36,28},{40,32... | collective-permute-start | bytes 2076680 | tf_op jit(solution)/shard_map/ppermute | solution.py:559
  45.7 44.9 %collective-permute-start.6 = (f32[1160,128]{1,0:T(8,128)}, f32[1160,128]{1,0:T(8,128)}, u32[]{:S(2)}, u32[]{:S(2)}) collective-permute-start(f32[1160,128]{1,0:T(8,128)} %slice.17), channel_id=1, source_target_pairs={{4,16},{12,24},{16,4},{20,32},{24,12},{28,40},{32,20},{36,48},{40,... | collective-permute-start | bytes 1781768 | tf_op jit(solution)/shard_map/ppermute | solution.py:638
  49.2 20.7 %collective-permute-start.2 = (f32[64,128]{1,0:T(8,128)S(1)}, f32[64,128]{1,0:T(8,128)S(1)}, u32[]{:S(2)}, u32[]{:S(2)}) collective-permute-start(f32[64,128]{1,0:T(8,128)S(1)} %get-tuple-element.38.refs_2_), channel_id=1, source_target_pairs={{0,1},{1,2},{2,3},{3,4},{4,5},{5,6},{6,7},{7,8},{8,9},{9,10},{10,1... | collective-permute-start | bytes 98312 | tf_op jit(solution)/shard_map/ppermute | solution.py:559
  51.4 20.7 %collective-permute-start.3 = (f32[64,128]{1,0:T(8,128)S(1)}, f32[64,128]{1,0:T(8,128)S(1)}, u32[]{:S(2)}, u32[]{:S(2)}) collective-permute-start(f32[64,128]{1,0:T(8,128)S(1)} %get-tuple-element.38.refs_2_), channel_id=1, source_target_pairs={{1,0},{2,1},{3,2},{4,3},{5,4},{6,5},{7,6},{8,7},{9,8},{10,9},{11,1... | collective-permute-start | bytes 98312 | tf_op jit(solution)/shard_map/ppermute | solution.py:559
  60.3 14.6 %copy-start.7 = (bf16[2,512,128]{2,1,0:T(8,128)(2,1)}, bf16[2,512,128]{2,1,0:T(8,128)(2,1)S(1)}, u32[]{:S(2)}) copy-start(bf16[2,512,128]{2,1,0:T(8,128)(2,1)S(1)} %get-tuple-element.44.refs_11_.lo_ref) | copy-start | bytes 786436
  76.3 12.5 %all-to-all-start = ((f32[16,40,128]{2,1,0:T(8,128)}), f32[16,40,128]{2,1,0:T(8,128)S(1)}, u32[]{:S(2)}, u32[]{:S(2)}) async-start(f32[16,40,128]{2,1,0:T(8,128)} %copy-done.17), calls=%async_computation | async-start | bytes 655360 | tf_op jit(solution)/shard_map/all_to_all | solution.py:550
  81.8 8.8 %collective-permute-start.7 = (f32[64,128]{1,0:T(8,128)S(1)}, f32[64,128]{1,0:T(8,128)S(1)}, u32[]{:S(2)}, u32[]{:S(2)}) collective-permute-start(f32[64,128]{1,0:T(8,128)S(1)} %slice.18), channel_id=1, source_target_pairs={{0,16},{8,24},{16,32},{20,4},{24,40},{28,12},{32,48},{36,20},{40,5... | collective-permute-start | bytes 98312 | tf_op jit(solution)/shard_map/ppermute | solution.py:638
  94.0 52.7 %collective-permute-start.8 = (f32[4120,128]{1,0:T(8,128)}, f32[4120,128]{1,0:T(8,128)}, u32[]{:S(2)}, u32[]{:S(2)}) collective-permute-start(f32[4120,128]{1,0:T(8,128)} %pad_maximum_fusion), channel_id=1, source_target_pairs={{0,4},{4,0},{8,12},{12,8},{16,20},{20,16},{24,28},{28,24},{32,36},... | collective-permute-start | bytes 6328328 | tf_op jit(solution)/shard_map/ppermute | solution.py:657
  120.0 18.2 %all-to-all-start.2 = ((f32[32,2,256]{2,1,0:T(2,128)}), f32[32,2,256]{2,1,0:T(2,128)S(1)}, u32[]{:S(2)}, u32[]{:S(2)}) async-start(f32[32,2,256]{2,1,0:T(2,128)} %sum_all.1), calls=%async_computation.2 | async-start | bytes 131072 | tf_op jit(solution)/shard_map/all_to_all | solution.py:554
  139.4 15.2 %all-to-all-start.3 = ((f32[16,32,128]{2,1,0:T(8,128)}), f32[16,32,128]{2,1,0:T(8,128)S(1)}, u32[]{:S(2)}, u32[]{:S(2)}) async-start(f32[16,32,128]{2,1,0:T(8,128)} %windows.1), calls=%async_computation.3 | async-start | bytes 524288 | tf_op jit(solution)/shard_map/all_to_all | solution.py:550
  149.7 1.3 copy-start.1
  151.0 1.2 copy-start.3
  154.5 1.5 copy-start.2
  156.0 1.5 copy-start.4
  157.5 1.1 copy-start.10
  173.7 26.2 %copy-start.25 = (s32[2,2,8]{2,1,0:T(2,128)S(1)}, s32[2,2,8]{2,1,0:T(2,128)}, u32[]{:S(2)}) copy-start(s32[2,2,8]{2,1,0:T(2,128)} %copy-done.24) | copy-start | bytes 388
  173.7 39.8 %copy-start.6 = (bf16[2,512,128]{2,1,0:T(8,128)(2,1)S(1)}, bf16[2,512,128]{2,1,0:T(8,128)(2,1)}, u32[]{:S(2)}) copy-start(bf16[2,512,128]{2,1,0:T(8,128)(2,1)} %copy-done.5) | copy-start | bytes 786436
  173.7 39.8 %copy-start.8 = (bf16[2,512,128]{2,1,0:T(8,128)(2,1)S(1)}, bf16[2,512,128]{2,1,0:T(8,128)(2,1)}, u32[]{:S(2)}) copy-start(bf16[2,512,128]{2,1,0:T(8,128)(2,1)} %copy-done.7) | copy-start | bytes 786436
  192.6 20.9 %all-to-all-start.5 = ((f32[16,32,2,256]{3,2,1,0:T(2,128)}), f32[16,32,2,256]{3,2,1,0:T(2,128)S(1)}, u32[]{:S(2)}, u32[]{:S(2)}) async-start(f32[16,32,2,256]{3,2,1,0:T(2,128)} %broadcast_in_dim.22), calls=%async_computation.5 | async-start | bytes 2097152 | tf_op jit(solution)/shard_map/all_to_all | solution.py:550
  214.7 6.1 %collective-permute-start.10 = (f32[64,128]{1,0:T(8,128)S(1)}, f32[64,128]{1,0:T(8,128)S(1)}, u32[]{:S(2)}, u32[]{:S(2)}) collective-permute-start(f32[64,128]{1,0:T(8,128)S(1)} %fine_up.1.refs_1_), channel_id=1, source_target_pairs={{1,0},{2,1},{3,2},{4,3},{5,4},{6,5},{7,6},{8,7},{9,8},{10,9},{11,1... | collective-permute-start | bytes 98312 | tf_op jit(solution)/shard_map/ppermute | solution.py:559
  218.3 9.5 %collective-permute-start.9 = (f32[64,128]{1,0:T(8,128)S(1)}, f32[64,128]{1,0:T(8,128)S(1)}, u32[]{:S(2)}, u32[]{:S(2)}) collective-permute-start(f32[64,128]{1,0:T(8,128)S(1)} %fine_up.1.refs_1_), channel_id=1, source_target_pairs={{0,1},{1,2},{2,3},{3,4},{4,5},{5,6},{6,7},{7,8},{8,9},{9,10},{10,1... | collective-permute-start | bytes 98312 | tf_op jit(solution)/shard_map/ppermute | solution.py:559
  229.6 9.8 %collective-permute-start.11 = (f32[64,128]{1,0:T(8,128)S(1)}, f32[64,128]{1,0:T(8,128)S(1)}, u32[]{:S(2)}, u32[]{:S(2)}) collective-permute-start(f32[64,128]{1,0:T(8,128)S(1)} %get-tuple-element.63.refs_2_), channel_id=1, source_target_pairs={{0,1},{1,2},{2,3},{3,4},{4,5},{5,6},{6,7},{7,8},{8,9},{9,10},{10,1... | collective-permute-start | bytes 98312 | tf_op jit(solution)/shard_map/ppermute | solution.py:559
  231.5 9.4 %collective-permute-start.12 = (f32[64,128]{1,0:T(8,128)S(1)}, f32[64,128]{1,0:T(8,128)S(1)}, u32[]{:S(2)}, u32[]{:S(2)}) collective-permute-start(f32[64,128]{1,0:T(8,128)S(1)} %get-tuple-element.63.refs_2_), channel_id=1, source_target_pairs={{1,0},{2,1},{3,2},{4,3},{5,4},{6,5},{7,6},{8,7},{9,8},{10,9},{11,1... | collective-permute-start | bytes 98312 | tf_op jit(solution)/shard_map/ppermute | solution.py:559
  (13 other events, 10.9 us)

commit v5 on v3

--- a/solution.py
+++ b/solution.py
@@ -36,7 +36,7 @@
 PLAIN_ORDER = list(range(16))
 
 
-def kern(body, outs, args, smem=()):
+def kern(body, outs, args, smem=(), own=(), own_outs=False):
     count = len(args)
 
     def kernel(*refs):
@@ -44,15 +44,17 @@
         for ref, value in zip(refs[count:], body(*ins)):
             ref[...] = value
 
+    vmem = pl.BlockSpec(memory_space=pltpu.VMEM)
     specs = [
-        pl.BlockSpec(memory_space=pltpu.SMEM if i in smem else pltpu.VMEM) for i in range(count)
+        pl.BlockSpec(memory_space=pltpu.SMEM) if i in smem else pl.BlockSpec() if i in own else vmem
+        for i in range(count)
     ]
     return pl.pallas_call(
         kernel,
         in_specs=specs,
-        out_specs=[pl.BlockSpec(memory_space=pltpu.VMEM) for _ in outs],
+        out_specs=[pl.BlockSpec() if own_outs else vmem for _ in outs],
         out_shape=[jax.ShapeDtypeStruct(s, d) for s, d in outs],
-        compiler_params=pltpu.CompilerParams(vmem_limit_bytes=48 << 20),
+        compiler_params=pltpu.CompilerParams(vmem_limit_bytes=32 << 20),
         name=body.__name__,
     )(*args)
 
@@ -352,10 +354,14 @@
 STARTS = [0, 0, 0, 128]
 
 
-def middle_prep(place, p0, m2, p2, crossed, twin, twin_m2, twin_p2, far_low, far_high):
+def middle_prep(place, p0, m2, p2, crossed, swapped, far):
     slab = place[0, 0]
     even = (slab & 1) == 0
     top = A2_AT
+    twin, twin_m2, twin_p2 = (swapped[i * PACK_ROWS : (i + 1) * PACK_ROWS] for i in range(3))
+    far_twin = swapped[3 * PACK_ROWS :]
+    far_low = jnp.where(even, far, far_twin)
+    far_high = jnp.where(even, far_twin, far)
     m3 = jnp.where(even, crossed, twin_m2[:top])
     p3 = jnp.where(even, twin_p2[:top], crossed)
     m1 = jnp.where(even, twin_m2, twin)
@@ -509,6 +515,10 @@
     return (jnp.broadcast_to(o[None], (TN_, 2, 256)),)
 
 
+def level_cycle(place, parts, p0, m2, p2, crossed, swapped, far, unpack):
+    return middle(place, parts, *middle_prep(place, p0, m2, p2, crossed, swapped, far), unpack)
+
+
 def fine_up(rows_ref, odd_ref, all_ref, x_ref, hi_ref, lo_ref, out_ref, line):
     for p in range(32):
         v = all_ref[rows_ref[p]]
@@ -532,7 +542,7 @@
         out_specs=vmem,
         out_shape=jax.ShapeDtypeStruct((64, 128), F32),
         scratch_shapes=[pltpu.VMEM((128, 128), F32)],
-        compiler_params=pltpu.CompilerParams(vmem_limit_bytes=48 << 20),
+        compiler_params=pltpu.CompilerParams(vmem_limit_bytes=32 << 20),
         name="fine_up",
     )(rows, odd, gathered_rows, x, hi, lo)
 
@@ -614,10 +624,13 @@
     left, right, pack = lax.optimization_barrier((left, right, pack))
     m2, p2 = shifted(pack, "slab", 2), shifted(pack, "slab", -2)
     count = lax.axis_size("slab")
-    pairs = [(i, i + 3 if i % 2 else i - 3) for i in range(count)]
-    crossed = lax.ppermute(pack[:A2_AT], "slab", [p for p in pairs if 0 <= p[1] < count])
-    inverse1 = pack[D1_AT : D1_AT + 64]
-    far = [shifted(inverse1, "slab", 4), shifted(inverse1, "slab", -4)]
+
+    def crossing(value, by):
+        pairs = [(i, i + by if i % 2 == by % 2 else i - by) for i in range(count)]
+        return lax.ppermute(value, "slab", [p for p in pairs if 0 <= p[1] < count])
+
+    crossed = crossing(pack[:A2_AT], 3)
+    far = crossing(pack[D1_AT : D1_AT + 64], 4)
     p_hi, p_lo = kern(prolong_parts, [((2, 512, 128), BF16)] * 2, [fine_prolong])
 
     sends = ((64, 128), F32)
@@ -626,6 +639,7 @@
         [((2, 3, 512, 128), BF16)] * 2 + [sends, sends, ((64, 64), F32), sends, ((3, 3, 128), I32)],
         [device, own, left, right, blocks, left_blocks, right_blocks],
         smem=(0,),
+        own=range(1, 7),
     )
     o = places(owner_rows)
     t = (o // 8) % TN_
@@ -640,19 +654,10 @@
     )
 
     dense, m2, p2, crossed = lax.optimization_barrier((dense, m2, p2, crossed))
-    swap = [(i, i ^ 1) for i in range(count)]
-    twins = [lax.ppermute(v, "slab", swap) for v in (pack, m2, p2)]
-    prepared = kern(
-        middle_prep,
-        [((7, D1_AT, 128), BF16)] * 2
-        + [((5, A2_ROWS, 128), BF16)] * 2
-        + [((64, 384), F32), ((64, 64), F32), ((12, 256, 128), BF16), ((3, 64, 128), BF16)],
-        [place, pack, m2, p2, crossed, *twins, *far],
-        smem=(0,),
-    )
+    twin = jnp.concatenate([pack, m2, p2, crossed[D1_AT : D1_AT + 64]], axis=0)
+    twin = lax.ppermute(twin, "slab", [(i, i ^ 1) for i in range(count)])
 
     (part,) = kern(sum_rows, [((TN_, 2, 256), F32)], [across(dense)])
-    part, *prepared = lax.optimization_barrier((part, *prepared))
     (part,) = kern(sum_all, [((TN_, 2, 256), F32)], [along(part)])
     q = jnp.arange(XN * YN * 64, dtype=I32)
     spot = slab % TN_
@@ -667,10 +672,11 @@
     part = across(part)
 
     (share,) = kern(
-        middle,
+        level_cycle,
         [((TN_, 2, 256), F32)],
-        [place, part] + prepared + [unpack_table(slab % TN_)],
+        [place, part, pack, m2, p2, crossed, twin, far, unpack_table(slab % TN_)],
         smem=(0,),
+        own=range(2, 8),
     )
     line = along(share)
     every = across(jnp.broadcast_to(line[None], (XN * YN, TN_, 2, 256)))

time: 238 us -> 232 us (0.975)
  starting transfers between devices: 101 us -> 85.4 us
  blocking collectives: 40.9 us -> 54.9 us
  other arithmetic: 2.7 us -> 6.9 us
  Pallas kernels: 32.4 us -> 28.8 us
  local copies, waits for them, and re-layouts: 20 us -> 16.5 us
    all_to_all x0 -> x1, blocking collectives: none -> 12.2 us  [across(): lax.all_to_all(value, ('slab', 'sub'), 0, 0, tiled=True, axis_index_group...]
    ppermute x14 -> x12, starting transfers between devices: 70.7 us -> 61.9 us  [shifted(): lax.ppermute(value, axis, [(i, i + by) for i in range(n) if 0 <= i + by <...]
    ppermute x4 -> x3, waiting for transfers between devices: 0.01 us -> 6.35 us  [the longest x2 6.35 us: crossing(): return lax.ppermute(value, 'slab', [p for p in pairs if 0 <= p[1] < count])]
    all_to_all x3 -> x2, waiting for transfers between devices: 20.1 us -> 13.8 us  [across(): lax.all_to_all(value, ('slab', 'sub'), 0, 0, tiled=True, axis_index_group...]
    all_to_all x3 -> x2, starting transfers between devices: 18.5 us -> 13.4 us  [across(): lax.all_to_all(value, ('slab', 'sub'), 0, 0, tiled=True, axis_index_group...]
    unnamed x44 -> x34, local copies, waits for them, and re-layouts: 11.4 us -> 6.91 us
    pallas_call x11 -> x10, Pallas kernels: 31.2 us -> 27.5 us  [kern(): pl.pallas_call(kernel, in_specs=specs, out_specs=[pl.BlockSpec() if own_o...]
    concatenate x0 -> x1, other arithmetic: none -> 2.78 us  [body(): twin = jnp.concatenate([pack, m2, p2, crossed[D1_AT:D1_AT + 64]], axis=0)]
  transfers between devices with their start and end apart: 22 -> 18, of which waited for: 6 -> 5; matrix products, arithmetic and copies ran while one was open for 3% -> 4% of each run, Pallas kernels for 3% -> 4%
where the time goes in v5:
time: 232 us; the launch traced here: 231 us
  starting transfers between devices  85.4 us (37%)
  blocking collectives  54.9 us (24%)
  waiting for transfers between devices  37.5 us (16%)
  Pallas kernels  28.8 us (12%)
  local copies, waits for them, and re-layouts  16.5 us (7%)
  other arithmetic  6.9 us (3%)
    ppermute x12, starting transfers between devices, shifted(): lax.ppermute(value, axis, [(i, i + by) for i in range(n) if 0 <= i + by <...  61.9 us
    all_to_all x2, blocking collectives, along(): return lax.all_to_all(value, 'slab', 0, 0, tiled=True, axis_index_groups=ZC)  42.7 us
    pallas_call x10, Pallas kernels, kern(): pl.pallas_call(kernel, in_specs=specs, out_specs=[pl.BlockSpec() if own_o...  27.5 us
    all_to_all x1, waiting for transfers between devices, along(): return lax.all_to_all(value, 'slab', 0, 0, tiled=True, axis_index_groups=ZC)  14.2 us
    all_to_all x2, waiting for transfers between devices, across(): lax.all_to_all(value, ('slab', 'sub'), 0, 0, tiled=True, axis_index_group...  13.8 us
    all_to_all x2, starting transfers between devices, across(): lax.all_to_all(value, ('slab', 'sub'), 0, 0, tiled=True, axis_index_group...  13.4 us
    all_to_all x1, blocking collectives, across(): lax.all_to_all(value, ('slab', 'sub'), 0, 0, tiled=True, axis_index_group...  12.2 us
    unnamed x34, local copies, waits for them, and re-layouts  6.91 us
  transfers between devices with their start and end apart: 18, of which 5 were waited for; matrix products, arithmetic and copies ran while one was open for 4% of the time, Pallas kernels for 4%

profile of v5, /device:TPU:16, one launch (start us, length us, event | category | flops | bytes accessed | tf_op | source)
XLA Modules:
  0.0 231.0 jit_solution(5470224512165211857)
XLA Ops:
  2.8 3.4 %collective-permute-start = (f32[16,1024]{1,0:T(8,128)S(1)}, f32[16,1024]{1,0:T(8,128)S(1)}, u32[]{:S(2)}, u32[]{:S(2)}) collective-permute-start(f32[16,1024]{1,0:T(8,128)S(1)} %select_maximum_fusion.refs_1_), channel_id=1, source_target_pairs={{0,1},{1,2},{2,3},{3,4},{4,5},{5,6},{6,7},{7,8},{8,9},{9,10},{10,1... | collective-permute-start | bytes 196616 | tf_op jit(solution)/shard_map/ppermute | solution.py:564
  6.2 11.4 %collective-permute-start.1 = (f32[16,1024]{1,0:T(8,128)S(1)}, f32[16,1024]{1,0:T(8,128)S(1)}, u32[]{:S(2)}, u32[]{:S(2)}) collective-permute-start(f32[16,1024]{1,0:T(8,128)S(1)} %select_maximum_fusion.refs_1_), channel_id=1, source_target_pairs={{1,0},{2,1},{3,2},{4,3},{5,4},{6,5},{7,6},{8,7},{9,8},{10,9},{11,1... | collective-permute-start | bytes 196616 | tf_op jit(solution)/shard_map/ppermute | solution.py:564
  17.6 2.0 fusion.24
  19.6 1.9 collective-permute-start.2
  21.6 7.9 %collective-permute-start.3 = (f32[3,8,4096]{2,1,0:T(8,128)S(1)}, f32[3,8,4096]{2,1,0:T(8,128)S(1)}, u32[]{:S(2)}, u32[]{:S(2)}) collective-permute-start(f32[3,8,4096]{2,1,0:T(8,128)S(1)} %get-tuple-element.44), channel_id=1, source_target_pairs={{1,0},{2,1},{3,2},{4,3},{5,4},{6,5},{7,6},{8,7},{9,8},{10,9},{11,1... | collective-permute-start | bytes 1179656 | tf_op jit(solution)/shard_map/ppermute | solution.py:564
  36.0 1.9 collective-permute-start.6
  37.9 6.0 %collective-permute-start.7 = (f32[1352,128]{1,0:T(8,128)S(1)}, f32[1352,128]{1,0:T(8,128)}, u32[]{:S(2)}, u32[]{:S(2)}) collective-permute-start(f32[1352,128]{1,0:T(8,128)S(1)} %level_pack.1.refs_2_), channel_id=1, source_target_pairs={{8,0},{12,4},{16,8},{20,12},{24,16},{28,20},{32,24},{36,28},{40,32... | collective-permute-start | bytes 2076680 | tf_op jit(solution)/shard_map/ppermute | solution.py:564
  44.8 1.9 collective-permute-start.8
  51.7 2.3 %fine_start.1 = (bf16[2,3,512,128]{3,2,1,0:T(8,128)(2,1)S(1)}, bf16[2,3,512,128]{3,2,1,0:T(8,128)(2,1)S(1)}, f32[64,128]{1,0:T(8,128)S(1)}, f32[64,128]{1,0:T(8,...) custom-call(s32[1,1]{1,0:T(1,128)} %bitcast.refs_0_, ...), custom_call_target="tpu_custom_call" | custom-call | tf_op jit(solution)/shard_map/fine_start/pallas_call | solution.py:52
  54.7 1.9 collective-permute-start.4
  56.6 7.9 %collective-permute-start.5 = (f32[64,128]{1,0:T(8,128)S(1)}, f32[64,128]{1,0:T(8,128)S(1)}, u32[]{:S(2)}, u32[]{:S(2)}) collective-permute-start(f32[64,128]{1,0:T(8,128)S(1)} %get-tuple-element.25.refs_2_), channel_id=1, source_target_pairs={{1,0},{2,1},{3,2},{4,3},{5,4},{6,5},{7,6},{8,7},{9,8},{10,9},{11,1... | collective-permute-start | bytes 98312 | tf_op jit(solution)/shard_map/ppermute | solution.py:564
  66.5 2.8 %fine_down.1 = (f32[64,64]{1,0:T(8,128)S(1)}, f32[16,40,128]{2,1,0:T(8,128)S(1)}) custom-call(s32[1,1]{1,0:T(1,128)} %bitcast.refs_0_, f32[64,64]{1,0:T(8,128)S(1)} %get-tuple-element.24.refs_1_, f32[64,128]{1,0:T(8,128)S(1)} %get-tuple-element.25.refs_2_, f32[64,128]{1,0:T(8,128)S(1)} %collective-permute-done.4.refs_3_, ...), custom_call_target="tpu_custom_call" | custom-call | tf_op jit(solution)/shard_map/fine_down/pallas_call | solution.py:52
  70.0 2.8 %pad_maximum_fusion = f32[4120,128]{1,0:T(8,128)} fusion(f32[64,128]{1,0:T(8,128)S(1)} %slice.18, f32[1352,128]{1,0:T(8,128)} %collective-permute-done.7.refs_4_, f32[1352,128]{1,0:T(8,128)} %collective-permute-done.6.refs_3_, f32[1352,128]{1,0:T(8,128)S(1)} %level_pack.1.refs_2_), kind=kLoop, calls=%fused_computation | loop fusion | flops 1582080 | bytes 4218880 | tf_op jit(solution)/shard_map/concatenate | solution.py:657
  72.8 1.9 collective-permute-start.9
  74.7 12.2 %all_to_all.30.refs_0_ = f32[16,40,128]{2,1,0:T(8,128)S(1)} all-to-all(f32[16,40,128]{2,1,0:T(8,128)S(1)} %get-tuple-element.34), channel_id=1, replica_groups={{0,1,2,3,128,129,130,131,256,257,258,259,384,385,386,387},{4,5,6,7,132,..., dimensions={0} | all-to-all | bytes 655360 | tf_op jit(solution)/shard_map/all_to_all | solution.py:555
  87.4 25.2 %all_to_all.31.refs_0_ = f32[32,2,256]{2,1,0:T(2,128)S(1)} all-to-all(f32[32,2,256]{2,1,0:T(2,128)S(1)} %sum_rows.1), channel_id=1, replica_groups={{0,4,8,12,16,20,24,28,32,36,40,44,48,52,56,60,64,68,72,76,80,84,88,92,9..., dimensions={0} | all-to-all | bytes 131072 | tf_op jit(solution)/shard_map/all_to_all | solution.py:559
  113.3 3.9 %all-to-all-start.2 = ((f32[32,2,256]{2,1,0:T(2,128)}), f32[32,2,256]{2,1,0:T(2,128)S(1)}, u32[]{:S(2)}, u32[]{:S(2)}) async-start(f32[32,2,256]{2,1,0:T(2,128)} %sum_all.1), calls=%async_computation.2 | async-start | bytes 131072 | tf_op jit(solution)/shard_map/all_to_all | solution.py:559
  117.3 14.2 %all-to-all-done.2.refs_0_ = f32[32,2,256]{2,1,0:T(2,128)S(1)} async-done(((f32[32,2,256]{2,1,0:T(2,128)}), f32[32,2,256]{2,1,0:T(2,128)S(1)}, u32[]{:S(2)}, u32[]{:S(2)}) %all-to-all-start.2) | async-done | bytes 65568 | tf_op jit(solution)/shard_map/all_to_all | solution.py:559
  132.6 6.0 %all-to-all-start.3 = ((f32[16,32,128]{2,1,0:T(8,128)}), f32[16,32,128]{2,1,0:T(8,128)S(1)}, u32[]{:S(2)}, u32[]{:S(2)}) async-start(f32[16,32,128]{2,1,0:T(8,128)} %windows.1), calls=%async_computation.3 | async-start | bytes 524288 | tf_op jit(solution)/shard_map/all_to_all | solution.py:555
  138.7 2.4 %collective-permute-start.10 = (f32[64,128]{1,0:T(8,128)S(1)}, f32[64,128]{1,0:T(8,128)S(1)}, u32[]{:S(2)}, u32[]{:S(2)}) collective-permute-start(f32[64,128]{1,0:T(8,128)S(1)} %slice.19), channel_id=1, source_target_pairs={{0,16},{8,24},{16,32},{20,4},{24,40},{28,12},{32,48},{36,20},{40,5... | collective-permute-start | bytes 98312 | tf_op jit(solution)/shard_map/ppermute | solution.py:630
  141.2 6.3 %collective-permute-done.10.refs_7_ = f32[64,128]{1,0:T(8,128)S(1)} collective-permute-done((f32[64,128]{1,0:T(8,128)S(1)}, f32[64,128]{1,0:T(8,128)S(1)}, u32[]{:S(2)}, u32[]{:S(2)}) %collective-permute-start.10) | collective-permute-done | bytes 32800 | tf_op jit(solution)/shard_map/ppermute | solution.py:630
  147.5 14.9 %level_cycle.1 = f32[32,2,256]{2,1,0:T(2,128)S(1)} custom-call(s32[1,2]{1,0:T(1,128)S(1)} %add_bitcast_fusion.refs_0_, f32[16,32,128]{2,1,0:T(8,128)S(1)} %all-to-all-done.3.refs_1_, f32[1352,128]{1,0:T(8,128)S(1)} %level_pack.1.refs_2_, f32[1352,128]{1,0:T(8,128)} %collective-permute-done.6.refs_3_, f32[1352,128]{1,0:T(8,128)} %collective-permute-done.7.refs_4_, ...), custom_call_target="tpu_custom_call" | custom-call | tf_op jit(solution)/shard_map/level_cycle/pallas_call | solution.py:52
  162.4 17.4 %all_to_all.32 = f32[32,2,256]{2,1,0:T(2,128)S(1)} all-to-all(f32[32,2,256]{2,1,0:T(2,128)S(1)} %level_cycle.1), channel_id=1, replica_groups={{0,4,8,12,16,20,24,28,32,36,40,44,48,52,56,60,64,68,72,76,80,84,88,92,9..., dimensions={0} | all-to-all | bytes 131072 | tf_op jit(solution)/shard_map/all_to_all | solution.py:559
  181.2 7.4 %all-to-all-start.5 = ((f32[16,32,2,256]{3,2,1,0:T(2,128)}), f32[16,32,2,256]{3,2,1,0:T(2,128)S(1)}, u32[]{:S(2)}, u32[]{:S(2)}) async-start(f32[16,32,2,256]{3,2,1,0:T(2,128)} %broadcast_in_dim.18), calls=%async_computation.5 | async-start | bytes 2097152 | tf_op jit(solution)/shard_map/all_to_all | solution.py:555
  188.7 13.8 %all-to-all-done.5 = f32[16,32,2,256]{3,2,1,0:T(2,128)S(1)} async-done(((f32[16,32,2,256]{3,2,1,0:T(2,128)}), f32[16,32,2,256]{3,2,1,0:T(2,128)S(1)}, u32[]{:S(2)}, u32[]{:S(2)}) %all-to-all-start.5) | async-done | bytes 1048608 | tf_op jit(solution)/shard_map/all_to_all | solution.py:555
  203.8 2.4 %collective-permute-start.11 = (f32[64,128]{1,0:T(8,128)S(1)}, f32[64,128]{1,0:T(8,128)S(1)}, u32[]{:S(2)}, u32[]{:S(2)}) collective-permute-start(f32[64,128]{1,0:T(8,128)S(1)} %fine_up.1.refs_1_), channel_id=1, source_target_pairs={{0,1},{1,2},{2,3},{3,4},{4,5},{5,6},{6,7},{7,8},{8,9},{9,10},{10,1... | collective-permute-start | bytes 98312 | tf_op jit(solution)/shard_map/ppermute | solution.py:564
  206.2 7.3 %collective-permute-start.12 = (f32[64,128]{1,0:T(8,128)S(1)}, f32[64,128]{1,0:T(8,128)S(1)}, u32[]{:S(2)}, u32[]{:S(2)}) collective-permute-start(f32[64,128]{1,0:T(8,128)S(1)} %fine_up.1.refs_1_), channel_id=1, source_target_pairs={{1,0},{2,1},{3,2},{4,3},{5,4},{6,5},{7,6},{8,7},{9,8},{10,9},{11,1... | collective-permute-start | bytes 98312 | tf_op jit(solution)/shard_map/ppermute | solution.py:564
  213.6 1.6 collective-permute-done.12.refs_3_
  215.1 1.9 fine_middle.1
  217.0 1.9 collective-permute-start.13
  218.9 7.9 %collective-permute-start.14 = (f32[64,128]{1,0:T(8,128)S(1)}, f32[64,128]{1,0:T(8,128)S(1)}, u32[]{:S(2)}, u32[]{:S(2)}) collective-permute-start(f32[64,128]{1,0:T(8,128)S(1)} %get-tuple-element.41.refs_2_), channel_id=1, source_target_pairs={{1,0},{2,1},{3,2},{4,3},{5,4},{6,5},{7,6},{8,7},{9,8},{10,9},{11,1... | collective-permute-start | bytes 98312 | tf_op jit(solution)/shard_map/ppermute | solution.py:564
  228.4 2.6 %fine_end.1 = (f32[4,1024]{1,0:T(4,128)}, f32[4,1024]{1,0:T(4,128)}) custom-call(s32[1,1]{1,0:T(1,128)} %bitcast.refs_0_, f32[64,64]{1,0:T(8,128)S(1)} %get-tuple-element.40.refs_1_, f32[64,128]{1,0:T(8,128)S(1)} %get-tuple-element.41.refs_2_, f32[64,128]{1,0:T(8,128)S(1)} %collective-permute-done.13.refs_3_, f32[64,128]{1,0:T(8,128)S(1)} %collective-permute-done.14.refs_4_, ...), custom_call_target="tpu_custom_call" | custom-call | tf_op jit(solution)/shard_map/fine_end/pallas_call | solution.py:52
  (105 shorter events, 24.5 us)
Async XLA Ops:
  0.6 32.9 %copy-start.6 = (f32[8,3,4096]{2,0,1:T(8,128)S(1)}, f32[8,3,4096]{2,0,1:T(8,128)}, u32[]{:S(2)}) copy-start(f32[8,3,4096]{2,0,1:T(8,128)} %param.20) | copy-start | bytes 1179652
  2.8 33.2 %collective-permute-start = (f32[16,1024]{1,0:T(8,128)S(1)}, f32[16,1024]{1,0:T(8,128)S(1)}, u32[]{:S(2)}, u32[]{:S(2)}) collective-permute-start(f32[16,1024]{1,0:T(8,128)S(1)} %select_maximum_fusion.refs_1_), channel_id=1, source_target_pairs={{0,1},{1,2},{2,3},{3,4},{4,5},{5,6},{6,7},{7,8},{8,9},{9,10},{10,1... | collective-permute-start | bytes 196616 | tf_op jit(solution)/shard_map/ppermute | solution.py:564
  6.2 29.8 %collective-permute-start.1 = (f32[16,1024]{1,0:T(8,128)S(1)}, f32[16,1024]{1,0:T(8,128)S(1)}, u32[]{:S(2)}, u32[]{:S(2)}) collective-permute-start(f32[16,1024]{1,0:T(8,128)S(1)} %select_maximum_fusion.refs_1_), channel_id=1, source_target_pairs={{1,0},{2,1},{3,2},{4,3},{5,4},{6,5},{7,6},{8,7},{9,8},{10,9},{11,1... | collective-permute-start | bytes 196616 | tf_op jit(solution)/shard_map/ppermute | solution.py:564
  17.6 31.4 %copy-start = (f32[16,3,4096]{2,0,1:T(8,128)S(1)}, f32[16,3,4096]{2,0,1:T(8,128)}, u32[]{:S(2)}) copy-start(f32[16,3,4096]{2,0,1:T(8,128)} %param.15) | copy-start | bytes 2359300
  19.6 28.6 %collective-permute-start.2 = (f32[3,8,4096]{2,1,0:T(8,128)}, f32[3,8,4096]{2,1,0:T(8,128)S(1)}, u32[]{:S(2)}, u32[]{:S(2)}) collective-permute-start(f32[3,8,4096]{2,1,0:T(8,128)} %get-tuple-element.45), channel_id=1, source_target_pairs={{0,1},{1,2},{2,3},{3,4},{4,5},{5,6},{6,7},{7,8},{8,9},{9,10},{10,1... | collective-permute-start | bytes 1179656 | tf_op jit(solution)/shard_map/ppermute | solution.py:564
  21.6 26.7 %collective-permute-start.3 = (f32[3,8,4096]{2,1,0:T(8,128)S(1)}, f32[3,8,4096]{2,1,0:T(8,128)S(1)}, u32[]{:S(2)}, u32[]{:S(2)}) collective-permute-start(f32[3,8,4096]{2,1,0:T(8,128)S(1)} %get-tuple-element.44), channel_id=1, source_target_pairs={{1,0},{2,1},{3,2},{4,3},{5,4},{6,5},{7,6},{8,7},{9,8},{10,9},{11,1... | collective-permute-start | bytes 1179656 | tf_op jit(solution)/shard_map/ppermute | solution.py:564
  33.5 0.9 copy-start.9
  34.4 0.9 copy-start.10
  36.0 12.3 %copy-start.11 = (f32[16,1024]{1,0:T(8,128)}, f32[16,1024]{1,0:T(8,128)S(1)}, u32[]{:S(2)}) copy-start(f32[16,1024]{1,0:T(8,128)S(1)} %collective-permute-done.refs_2_) | copy-start | bytes 196612
  36.0 12.3 %copy-start.13 = (f32[16,1024]{1,0:T(8,128)}, f32[16,1024]{1,0:T(8,128)S(1)}, u32[]{:S(2)}) copy-start(f32[16,1024]{1,0:T(8,128)S(1)} %collective-permute-done.1.refs_3_) | copy-start | bytes 196612
  36.0 33.2 %collective-permute-start.6 = (f32[1352,128]{1,0:T(8,128)S(1)}, f32[1352,128]{1,0:T(8,128)}, u32[]{:S(2)}, u32[]{:S(2)}) collective-permute-start(f32[1352,128]{1,0:T(8,128)S(1)} %level_pack.1.refs_2_), channel_id=1, source_target_pairs={{0,8},{4,12},{8,16},{12,20},{16,24},{20,28},{24,32},{28,36},{32,40... | collective-permute-start | bytes 2076680 | tf_op jit(solution)/shard_map/ppermute | solution.py:564
  37.9 31.3 %collective-permute-start.7 = (f32[1352,128]{1,0:T(8,128)S(1)}, f32[1352,128]{1,0:T(8,128)}, u32[]{:S(2)}, u32[]{:S(2)}) collective-permute-start(f32[1352,128]{1,0:T(8,128)S(1)} %level_pack.1.refs_2_), channel_id=1, source_target_pairs={{8,0},{12,4},{16,8},{20,12},{24,16},{28,20},{32,24},{36,28},{40,32... | collective-permute-start | bytes 2076680 | tf_op jit(solution)/shard_map/ppermute | solution.py:564
  44.8 24.4 %collective-permute-start.8 = (f32[1160,128]{1,0:T(8,128)}, f32[1160,128]{1,0:T(8,128)}, u32[]{:S(2)}, u32[]{:S(2)}) collective-permute-start(f32[1160,128]{1,0:T(8,128)} %slice.17), channel_id=1, source_target_pairs={{4,16},{12,24},{16,4},{20,32},{24,12},{28,40},{32,20},{36,48},{40,... | collective-permute-start | bytes 1781768 | tf_op jit(solution)/shard_map/ppermute | solution.py:630
  49.0 1.0 copy-start.8
  50.0 0.8 copy-start.12
  54.7 11.8 %collective-permute-start.4 = (f32[64,128]{1,0:T(8,128)S(1)}, f32[64,128]{1,0:T(8,128)S(1)}, u32[]{:S(2)}, u32[]{:S(2)}) collective-permute-start(f32[64,128]{1,0:T(8,128)S(1)} %get-tuple-element.25.refs_2_), channel_id=1, source_target_pairs={{0,1},{1,2},{2,3},{3,4},{4,5},{5,6},{6,7},{7,8},{8,9},{9,10},{10,1... | collective-permute-start | bytes 98312 | tf_op jit(solution)/shard_map/ppermute | solution.py:564
  56.6 9.9 %collective-permute-start.5 = (f32[64,128]{1,0:T(8,128)S(1)}, f32[64,128]{1,0:T(8,128)S(1)}, u32[]{:S(2)}, u32[]{:S(2)}) collective-permute-start(f32[64,128]{1,0:T(8,128)S(1)} %get-tuple-element.25.refs_2_), channel_id=1, source_target_pairs={{1,0},{2,1},{3,2},{4,3},{5,4},{6,5},{7,6},{8,7},{9,8},{10,9},{11,1... | collective-permute-start | bytes 98312 | tf_op jit(solution)/shard_map/ppermute | solution.py:564
  65.1 1.0 copy-start.5
  66.4 6.4 %copy-start.1 = (bf16[2,512,128]{2,1,0:T(8,128)(2,1)}, bf16[2,512,128]{2,1,0:T(8,128)(2,1)S(1)}, u32[]{:S(2)}) copy-start(bf16[2,512,128]{2,1,0:T(8,128)(2,1)S(1)} %get-tuple-element.30.refs_10_.hi_ref) | copy-start | bytes 786436
  66.4 6.4 %copy-start.3 = (bf16[2,512,128]{2,1,0:T(8,128)(2,1)}, bf16[2,512,128]{2,1,0:T(8,128)(2,1)S(1)}, u32[]{:S(2)}) copy-start(bf16[2,512,128]{2,1,0:T(8,128)(2,1)S(1)} %get-tuple-element.31.refs_11_.lo_ref) | copy-start | bytes 786436
  72.8 74.7 %collective-permute-start.9 = (f32[4120,128]{1,0:T(8,128)}, f32[4120,128]{1,0:T(8,128)}, u32[]{:S(2)}, u32[]{:S(2)}) collective-permute-start(f32[4120,128]{1,0:T(8,128)} %pad_maximum_fusion), channel_id=1, source_target_pairs={{0,4},{4,0},{8,12},{12,8},{16,20},{20,16},{24,28},{28,24},{32,36},... | collective-permute-start | bytes 6328328 | tf_op jit(solution)/shard_map/ppermute | solution.py:658
  113.3 18.2 %all-to-all-start.2 = ((f32[32,2,256]{2,1,0:T(2,128)}), f32[32,2,256]{2,1,0:T(2,128)S(1)}, u32[]{:S(2)}, u32[]{:S(2)}) async-start(f32[32,2,256]{2,1,0:T(2,128)} %sum_all.1), calls=%async_computation.2 | async-start | bytes 131072 | tf_op jit(solution)/shard_map/all_to_all | solution.py:559
  132.6 14.9 %all-to-all-start.3 = ((f32[16,32,128]{2,1,0:T(8,128)}), f32[16,32,128]{2,1,0:T(8,128)S(1)}, u32[]{:S(2)}, u32[]{:S(2)}) async-start(f32[16,32,128]{2,1,0:T(8,128)} %windows.1), calls=%async_computation.3 | async-start | bytes 524288 | tf_op jit(solution)/shard_map/all_to_all | solution.py:555
  138.7 8.8 %collective-permute-start.10 = (f32[64,128]{1,0:T(8,128)S(1)}, f32[64,128]{1,0:T(8,128)S(1)}, u32[]{:S(2)}, u32[]{:S(2)}) collective-permute-start(f32[64,128]{1,0:T(8,128)S(1)} %slice.19), channel_id=1, source_target_pairs={{0,16},{8,24},{16,32},{20,4},{24,40},{28,12},{32,48},{36,20},{40,5... | collective-permute-start | bytes 98312 | tf_op jit(solution)/shard_map/ppermute | solution.py:630
  162.4 40.2 %copy-start.2 = (bf16[2,512,128]{2,1,0:T(8,128)(2,1)S(1)}, bf16[2,512,128]{2,1,0:T(8,128)(2,1)}, u32[]{:S(2)}) copy-start(bf16[2,512,128]{2,1,0:T(8,128)(2,1)} %copy-done.1) | copy-start | bytes 786436
  162.4 40.2 %copy-start.4 = (bf16[2,512,128]{2,1,0:T(8,128)(2,1)S(1)}, bf16[2,512,128]{2,1,0:T(8,128)(2,1)}, u32[]{:S(2)}) copy-start(bf16[2,512,128]{2,1,0:T(8,128)(2,1)} %copy-done.3) | copy-start | bytes 786436
  181.2 33.9 %copy-start.16 = (f32[64,128]{1,0:T(8,128)S(1)}, f32[64,128]{1,0:T(8,128)}, u32[]{:S(2)}) copy-start(f32[64,128]{1,0:T(8,128)} %copy-done.15) | copy-start | bytes 98308
  181.2 21.3 %all-to-all-start.5 = ((f32[16,32,2,256]{3,2,1,0:T(2,128)}), f32[16,32,2,256]{3,2,1,0:T(2,128)S(1)}, u32[]{:S(2)}, u32[]{:S(2)}) async-start(f32[16,32,2,256]{3,2,1,0:T(2,128)} %broadcast_in_dim.18), calls=%async_computation.5 | async-start | bytes 2097152 | tf_op jit(solution)/shard_map/all_to_all | solution.py:555
  203.8 9.8 %collective-permute-start.11 = (f32[64,128]{1,0:T(8,128)S(1)}, f32[64,128]{1,0:T(8,128)S(1)}, u32[]{:S(2)}, u32[]{:S(2)}) collective-permute-start(f32[64,128]{1,0:T(8,128)S(1)} %fine_up.1.refs_1_), channel_id=1, source_target_pairs={{0,1},{1,2},{2,3},{3,4},{4,5},{5,6},{6,7},{7,8},{8,9},{9,10},{10,1... | collective-permute-start | bytes 98312 | tf_op jit(solution)/shard_map/ppermute | solution.py:564
  206.2 8.9 %collective-permute-start.12 = (f32[64,128]{1,0:T(8,128)S(1)}, f32[64,128]{1,0:T(8,128)S(1)}, u32[]{:S(2)}, u32[]{:S(2)}) collective-permute-start(f32[64,128]{1,0:T(8,128)S(1)} %fine_up.1.refs_1_), channel_id=1, source_target_pairs={{1,0},{2,1},{3,2},{4,3},{5,4},{6,5},{7,6},{8,7},{9,8},{10,9},{11,1... | collective-permute-start | bytes 98312 | tf_op jit(solution)/shard_map/ppermute | solution.py:564
  217.0 9.8 %collective-permute-start.13 = (f32[64,128]{1,0:T(8,128)S(1)}, f32[64,128]{1,0:T(8,128)S(1)}, u32[]{:S(2)}, u32[]{:S(2)}) collective-permute-start(f32[64,128]{1,0:T(8,128)S(1)} %get-tuple-element.41.refs_2_), channel_id=1, source_target_pairs={{0,1},{1,2},{2,3},{3,4},{4,5},{5,6},{6,7},{7,8},{8,9},{9,10},{10,1... | collective-permute-start | bytes 98312 | tf_op jit(solution)/shard_map/ppermute | solution.py:564
  218.9 9.5 %collective-permute-start.14 = (f32[64,128]{1,0:T(8,128)S(1)}, f32[64,128]{1,0:T(8,128)S(1)}, u32[]{:S(2)}, u32[]{:S(2)}) collective-permute-start(f32[64,128]{1,0:T(8,128)S(1)} %get-tuple-element.41.refs_2_), channel_id=1, source_target_pairs={{1,0},{2,1},{3,2},{4,3},{5,4},{6,5},{7,6},{8,7},{9,8},{10,9},{11,1... | collective-permute-start | bytes 98312 | tf_op jit(solution)/shard_map/ppermute | solution.py:564
  (3 other events, 2.2 us)

commit v6 on v5

--- a/solution.py
+++ b/solution.py
@@ -1,6 +1,5 @@
 import jax
 import jax.numpy as jnp
-import numpy as np
 from jax import lax
 from jax.experimental import pallas as pl
 from jax.experimental.pallas import tpu as pltpu
@@ -215,26 +214,55 @@
 
 
 def indices(payload):
-    return payload[8:11, :128].astype(I32)
-
-
-def fine_start(device, own, left, right, own_blocks, left_blocks, right_blocks):
+    return payload[:3, 1024:1152].astype(I32)
+
+
+def fine_start(device, own, left_all, right_all, own_blocks):
     parts = []
     for k in range(3):
         parts.append(tiles(own_blocks[k]))
     for k in range(3):
-        parts.append(jnp.concatenate([tiles(left_blocks[k]), tiles(right_blocks[k])], axis=0))
+        parts.append(jnp.concatenate([tiles(left_all[k]), tiles(right_all[k])], axis=0))
     entries = jnp.concatenate([diagonal(parts[0], FINE_ORDER), diagonal(parts[3], RIM_ORDER)], axis=1)
     inverse = jnp.where(entries == 0.0, 0.0, 1.0 / entries)
     pairs = [split(p) for p in parts]
     hi = jnp.stack([p[0] for p in pairs]).reshape(2, 3, 512, 128)
     lo = jnp.stack([p[1] for p in pairs]).reshape(2, 3, 512, 128)
-    x = [columns_of(p[:4]) for p in (left, own, right)]
-    b = [columns_of(p[4:8]) for p in (left, own, right)]
+    left, right = left_all[3], right_all[3]
+    x = [columns_of(p[:4, :1024]) for p in (left, own, right)]
+    b = [columns_of(p[4:, :1024]) for p in (left, own, right)]
     rhs = jnp.concatenate([b[1], rim(b[0], b[2])], axis=1)
     idx = [indices(p) for p in (own, left, right)]
     x1, send = first_passes(device[0, 0], x[1], (x[0], x[2]), rhs, hi, lo, inverse, idx)
     return hi, lo, inverse, rhs, x1, send, jnp.stack(idx)
+
+
+def lanes_of(values, first=0):
+    lane = iota((1, 128), 1)
+    v = jnp.zeros((1, 128), I32)
+    for n, value in enumerate(values):
+        v = jnp.where((lane >> 2) == first + n, value * NRHS + (lane & 3), v)
+    return v
+
+
+def repeated(v, width):
+    shift = width
+    while shift < 128:
+        v = v + pltpu.roll(v, shift, 1)
+        shift *= 2
+    return v
+
+
+def payload(x, b, columns):
+    lines = []
+    for k in range(3):
+        values = [None] * R0
+        for i in range(R0):
+            g = columns[i, k]
+            values[FINE_ORDER[i]] = (g >> 4) * 16 + (g & 1) * 8 + ((g & 15) >> 1)
+        lines.append(repeated(lanes_of(values), 64))
+    v = jnp.concatenate(lines + [jnp.zeros((5, 128), I32)], axis=0).astype(F32)
+    return (jnp.concatenate([jnp.concatenate([x, b], axis=0), v, jnp.zeros((8, 2944), F32)], axis=1),)
 
 
 def restrict(dest, residual, p_hi, p_lo):
@@ -262,7 +290,15 @@
     return jnp.stack(out)
 
 
-def fine_down(device, x, own, left, right, hi, lo, inverse, idx, dest, p_hi, p_lo):
+def fine_down(device, x, own, left, right, hi, lo, inverse, idx, owner, slot, p_hi, p_lo):
+    spots, lines = [None] * 32, [None] * 32
+    for e in range(2):
+        for i in range(R0):
+            j, at = owner[i, e], e * R0 + FINE_ORDER[i]
+            t = (j >> 3) & (TN_ - 1)
+            spots[at] = ((j >> 8) * XN + (t & (XN - 1))) * 16 + (t >> 2) * 2 + slot[i, e]
+            lines[at] = (t >> 2) * 8 + (j & 7)
+    dest = jnp.concatenate([lanes_of(spots), lanes_of(lines) + 1], axis=0)
     solution, residual = last_passes(
         device[0, 0], x, own, left, right, hi, lo, inverse, [idx[i] for i in range(3)]
     )
@@ -329,7 +365,10 @@
 PACK_ROWS = A2_AT + A2_ROWS
 
 
-def level_pack(blocks, prolong, coarse, idx):
+def level_pack(blocks, prolong, coarse, columns, coarse_columns):
+    lines = [repeated(lanes_of([columns[i, k] for i in range(R1)]), 32) for k in range(3)]
+    lines += [repeated(lanes_of([coarse_columns[i, k] for i in range(R2)]), 8) for k in range(3)]
+    idx = jnp.concatenate(lines + [jnp.zeros((2, 128), I32)], axis=0).astype(F32)
     a1 = [tiles(blocks[k]) for k in range(3)]
     a2 = [lanes_in(coarse[k].reshape(R2 * 32, 128)) for k in range(3)]
     pad = jnp.zeros((256, 128), F32)
@@ -519,11 +558,13 @@
     return middle(place, parts, *middle_prep(place, p0, m2, p2, crossed, swapped, far), unpack)
 
 
-def fine_up(rows_ref, odd_ref, all_ref, x_ref, hi_ref, lo_ref, out_ref, line):
-    for p in range(32):
-        v = all_ref[rows_ref[p]]
+def fine_up(owner_ref, all_ref, x_ref, hi_ref, lo_ref, out_ref, line):
+    for n in range(32):
+        e, i = n // R0, n % R0
+        p, j = e * R0 + FINE_ORDER[i], owner_ref[i, e]
+        v = all_ref[((j >> 8) * XN + ((j & 7) >> 1)) * TN_ + ((j >> 3) & (TN_ - 1))]
         v = jnp.concatenate([v[:, :128], v[:, 128:]], axis=0)
-        line[p * 4 : p * 4 + 4, :] = jnp.where(odd_ref[p] == 1, pltpu.roll(v, 64, 1), v)
+        line[p * 4 : p * 4 + 4, :] = jnp.where((j & 1) == 1, pltpu.roll(v, 64, 1), v)
     w = line[:, :64].T
     hi, lo = split(w)
     hi, lo = hi.astype(F32), lo.astype(F32)
@@ -534,17 +575,17 @@
     out_ref[...] = double(x)
 
 
-def fine_up_call(rows, odd, gathered_rows, x, hi, lo):
+def fine_up_call(owner, gathered_rows, x, hi, lo):
     smem, vmem = pl.BlockSpec(memory_space=pltpu.SMEM), pl.BlockSpec(memory_space=pltpu.VMEM)
     return pl.pallas_call(
         fine_up,
-        in_specs=[smem, smem, vmem, vmem, vmem, vmem],
+        in_specs=[smem, vmem, vmem, vmem, vmem],
         out_specs=vmem,
         out_shape=jax.ShapeDtypeStruct((64, 128), F32),
         scratch_shapes=[pltpu.VMEM((128, 128), F32)],
         compiler_params=pltpu.CompilerParams(vmem_limit_bytes=32 << 20),
         name="fine_up",
-    )(rows, odd, gathered_rows, x, hi, lo)
+    )(owner, gathered_rows, x, hi, lo)
 
 
 XY = [[(y * TN_ + t) * XN + x for y in range(YN) for x in range(XN)] for t in range(TN_)]
@@ -572,16 +613,6 @@
     idx = x * 64 + part * 32 + lane % 32
     keep = (rel <= 4) & ((rel < 4) | (row < 4)) & ((rel > -4) | (row >= 4))
     return jnp.where(keep, idx, -1).reshape(1, 384)
-
-
-def lane_index(columns, times):
-    t = columns.T
-    v = (t[:, :, None] * NRHS + jnp.arange(NRHS, dtype=I32)).reshape(3, -1)
-    return jnp.concatenate([v] * times, axis=1).astype(F32)
-
-
-def places(values):
-    return values.reshape(8, 2, -1).transpose(2, 1, 0).reshape(values.shape[1], 16)
 
 
 def body(
@@ -604,24 +635,19 @@
     sub = lax.axis_index("sub").astype(I32)
     device = (slab * XN + sub).reshape(1, 1)
     place = jnp.stack([slab, sub]).reshape(1, 2)
-    rhs4 = jnp.arange(NRHS, dtype=I32)
-
-    g = places(fine_columns)
-    g = (g // 16) * 64 + ((g % 2) * 8 + (g % 16) // 2) * 4
-    g = (g[:, :, None] + rhs4).reshape(3, 64)
-    g = jnp.concatenate([g, g], axis=1).astype(F32)
-    own = jnp.concatenate([warm_start, right_side, jnp.pad(g, ((0, 5), (0, 896)))], axis=0)
+
+    (own,) = kern(payload, [((8, 4096), F32)], [warm_start, right_side, fine_columns], smem=(2,))
     blocks = fine_blocks.transpose(1, 0, 2)
-    left_blocks, right_blocks = shifted(blocks[:, 8:], both, 1), shifted(blocks[:, :8], both, -1)
-    left, right = shifted(own, both, 1), shifted(own, both, -1)
-
-    ix = jnp.concatenate([lane_index(middle_columns, 4), lane_index(coarse_columns, 16)], axis=0)
+    low, high = (jnp.concatenate([part, own[None]], axis=0) for part in (blocks[:, :8], blocks[:, 8:]))
+    middle_columns, low, high = lax.optimization_barrier((middle_columns, low, high))
+    left, right = shifted(high, both, 1), shifted(low, both, -1)
+
     (pack,) = kern(
         level_pack,
         [((PACK_ROWS, 128), F32)],
-        [middle_blocks.transpose(1, 0, 2), middle_prolong, coarse_blocks.transpose(1, 0, 2), jnp.pad(ix, ((0, 2), (0, 0)))],
-    )
-    left, right, pack = lax.optimization_barrier((left, right, pack))
+        [middle_blocks.transpose(1, 0, 2), middle_prolong, coarse_blocks.transpose(1, 0, 2), middle_columns, coarse_columns],
+        smem=(3, 4),
+    )
     m2, p2 = shifted(pack, "slab", 2), shifted(pack, "slab", -2)
     count = lax.axis_size("slab")
 
@@ -629,36 +655,32 @@
         pairs = [(i, i + by if i % 2 == by % 2 else i - by) for i in range(count)]
         return lax.ppermute(value, "slab", [p for p in pairs if 0 <= p[1] < count])
 
-    crossed = crossing(pack[:A2_AT], 3)
-    far = crossing(pack[D1_AT : D1_AT + 64], 4)
     p_hi, p_lo = kern(prolong_parts, [((2, 512, 128), BF16)] * 2, [fine_prolong])
 
     sends = ((64, 128), F32)
     hi, lo, inverse, rhs, x1, send, idx = kern(
         fine_start,
         [((2, 3, 512, 128), BF16)] * 2 + [sends, sends, ((64, 64), F32), sends, ((3, 3, 128), I32)],
-        [device, own, left, right, blocks, left_blocks, right_blocks],
+        [device, own, left, right, blocks],
         smem=(0,),
-        own=range(1, 7),
-    )
-    o = places(owner_rows)
-    t = (o // 8) % TN_
-    dest = ((o // 256) * XN + t % XN) * 64 + (t // XN) * 8 + places(send_slots) * 4
-    dest_row = (t // XN) * 32 + (o % 8) * 4 + 1
-    dest = jnp.concatenate([(v[:, :, None] + rhs4).reshape(1, 128) for v in (dest, dest_row)], axis=0)
+        own=range(1, 5),
+    )
+    send, pack = lax.optimization_barrier((send, pack))
+    crossed = crossing(pack[:A2_AT], 3)
     x3, dense = kern(
         fine_down,
         [((64, 64), F32), ((16, 40, 128), F32)],
-        [device, x1, send, shifted(send, both, 1), shifted(send, both, -1), hi, lo, inverse, idx, dest, p_hi, p_lo],
-        smem=(0,),
+        [device, x1, send, shifted(send, both, 1), shifted(send, both, -1), hi, lo, inverse, idx, owner_rows, send_slots, p_hi, p_lo],
+        smem=(0, 9, 10),
     )
 
     dense, m2, p2, crossed = lax.optimization_barrier((dense, m2, p2, crossed))
+    (part,) = kern(sum_rows, [((TN_, 2, 256), F32)], [across(dense)])
+    (part,) = kern(sum_all, [((TN_, 2, 256), F32)], [along(part)])
+    part, m2, p2, crossed, pack = lax.optimization_barrier((part, m2, p2, crossed, pack))
     twin = jnp.concatenate([pack, m2, p2, crossed[D1_AT : D1_AT + 64]], axis=0)
     twin = lax.ppermute(twin, "slab", [(i, i ^ 1) for i in range(count)])
-
-    (part,) = kern(sum_rows, [((TN_, 2, 256), F32)], [across(dense)])
-    (part,) = kern(sum_all, [((TN_, 2, 256), F32)], [along(part)])
+    far = crossing(pack[D1_AT : D1_AT + 64], 4)
     q = jnp.arange(XN * YN * 64, dtype=I32)
     spot = slab % TN_
     near_by = (sub - spot) % XN
@@ -680,10 +702,7 @@
     )
     line = along(share)
     every = across(jnp.broadcast_to(line[None], (XN * YN, TN_, 2, 256)))
-    at = ((o // 256) * XN + (o % 8) // 2) * TN_ + (o // 8) % TN_
-    x = fine_up_call(
-        at.reshape(32), (o % 2).reshape(32), every.reshape(XN * YN * TN_, 2, 256), x3, p_hi, p_lo
-    )
+    x = fine_up_call(owner_rows, every.reshape(XN * YN * TN_, 2, 256), x3, p_hi, p_lo)
 
     x1, send = kern(
         fine_middle,

time: 232 us -> 225 us (0.970)
  the two profiles are of different devices: /device:TPU:16 before, /device:TPU:8 now
where the time goes in v6:
time: 225 us; the launch traced here: 223 us
  blocking collectives  76.7 us (34%)
  starting transfers between devices  66.8 us (30%)
  waiting for transfers between devices  32.6 us (14%)
  Pallas kernels  31.2 us (14%)
  local copies, waits for them, and re-layouts  10.8 us (5%)
  other arithmetic  4.04 us (2%)
    ppermute x10, starting transfers between devices, shifted(): lax.ppermute(value, axis, [(i, i + by) for i in range(n) if 0 <= i + by <...  48.2 us
    all_to_all x2, blocking collectives, along(): return lax.all_to_all(value, 'slab', 0, 0, tiled=True, axis_index_groups=ZC)  43.5 us
    all_to_all x2, blocking collectives, across(): lax.all_to_all(value, ('slab', 'sub'), 0, 0, tiled=True, axis_index_group...  33.2 us
    pallas_call x11, Pallas kernels, kern(): pl.pallas_call(kernel, in_specs=specs, out_specs=[pl.BlockSpec() if own_o...  29.8 us
    all_to_all x1, waiting for transfers between devices, along(): return lax.all_to_all(value, 'slab', 0, 0, tiled=True, axis_index_groups=ZC)  14.2 us
    ppermute x10, waiting for transfers between devices, shifted(): lax.ppermute(value, axis, [(i, i + by) for i in range(n) if 0 <= i + by <...  12 us
    unnamed x45, local copies, waits for them, and re-layouts  8.27 us
    ppermute x2, starting transfers between devices, crossing(): return lax.ppermute(value, 'slab', [p for p in pairs if 0 <= p[1] < count])  7.4 us
  transfers between devices with their start and end apart: 15, of which 5 were waited for; matrix products, arithmetic and copies ran while one was open for 1% of the time, Pallas kernels for 4%

profile of v6, /device:TPU:8, one launch (start us, length us, event | category | flops | bytes accessed | tf_op | source)
XLA Modules:
  0.0 223.3 jit_solution(11971682652166414178)
XLA Ops:
  6.1 3.4 %collective-permute-start = (f32[4,8,4096]{2,1,0:T(8,128)}, f32[4,8,4096]{2,1,0:T(8,128)S(1)}, u32[]{:S(2)}, u32[]{:S(2)}) collective-permute-start(f32[4,8,4096]{2,1,0:T(8,128)} %get-tuple-element.29), channel_id=1, source_target_pairs={{0,1},{1,2},{2,3},{3,4},{4,5},{5,6},{6,7},{7,8},{8,9},{9,10},{10,1... | collective-permute-start | bytes 1572872 | tf_op jit(solution)/shard_map/ppermute | solution.py:605
  9.5 11.4 %collective-permute-start.1 = (f32[4,8,4096]{2,1,0:T(8,128)}, f32[4,8,4096]{2,1,0:T(8,128)S(1)}, u32[]{:S(2)}, u32[]{:S(2)}) collective-permute-start(f32[4,8,4096]{2,1,0:T(8,128)} %get-tuple-element.30), channel_id=1, source_target_pairs={{1,0},{2,1},{3,2},{4,3},{5,4},{6,5},{7,6},{8,7},{9,8},{10,9},{11,1... | collective-permute-start | bytes 1572872 | tf_op jit(solution)/shard_map/ppermute | solution.py:605
  21.1 1.3 level_pack.1.refs_2_
  22.4 1.9 collective-permute-start.4
  24.3 6.0 %collective-permute-start.5 = (f32[1352,128]{1,0:T(8,128)S(1)}, f32[1352,128]{1,0:T(8,128)}, u32[]{:S(2)}, u32[]{:S(2)}) collective-permute-start(f32[1352,128]{1,0:T(8,128)S(1)} %level_pack.1.refs_2_), channel_id=1, source_target_pairs={{8,0},{12,4},{16,8},{20,12},{24,16},{28,20},{32,24},{36,28},{40,32... | collective-permute-start | bytes 2076680 | tf_op jit(solution)/shard_map/ppermute | solution.py:605
  34.0 2.3 %fine_start.1 = (bf16[2,3,512,128]{3,2,1,0:T(8,128)(2,1)S(1)}, bf16[2,3,512,128]{3,2,1,0:T(8,128)(2,1)S(1)}, f32[64,128]{1,0:T(8,128)S(1)}, f32[64,128]{1,0:T(8,...) custom-call(s32[1,1]{1,0:T(1,128)} %bitcast.refs_0_, ...), custom_call_target="tpu_custom_call" | custom-call | tf_op jit(solution)/shard_map/fine_start/pallas_call | solution.py:51
  37.3 5.0 %collective-permute-start.6 = (f32[1160,128]{1,0:T(8,128)}, f32[1160,128]{1,0:T(8,128)S(1)}, u32[]{:S(2)}, u32[]{:S(2)}) collective-permute-start(f32[1160,128]{1,0:T(8,128)} %slice.17), channel_id=1, source_target_pairs={{4,16},{12,24},{16,4},{20,32},{24,12},{28,40},{32,20},{36,48},{40,... | collective-permute-start | bytes 1781768 | tf_op jit(solution)/shard_map/ppermute | solution.py:656
  42.3 2.3 %collective-permute-start.2 = (f32[64,128]{1,0:T(8,128)S(1)}, f32[64,128]{1,0:T(8,128)S(1)}, u32[]{:S(2)}, u32[]{:S(2)}) collective-permute-start(f32[64,128]{1,0:T(8,128)S(1)} %get-tuple-element.34.refs_2_), channel_id=1, source_target_pairs={{0,1},{1,2},{2,3},{3,4},{4,5},{5,6},{6,7},{7,8},{8,9},{9,10},{10,1... | collective-permute-start | bytes 98312 | tf_op jit(solution)/shard_map/ppermute | solution.py:605
  44.6 7.5 %collective-permute-start.3 = (f32[64,128]{1,0:T(8,128)S(1)}, f32[64,128]{1,0:T(8,128)}, u32[]{:S(2)}, u32[]{:S(2)}) collective-permute-start(f32[64,128]{1,0:T(8,128)S(1)} %get-tuple-element.34.refs_2_), channel_id=1, source_target_pairs={{1,0},{2,1},{3,2},{4,3},{5,4},{6,5},{7,6},{8,7},{9,8},{10,9},{11,1... | collective-permute-start | bytes 98312 | tf_op jit(solution)/shard_map/ppermute | solution.py:605
  53.5 3.4 %collective-permute-done.2.refs_3_ = f32[64,128]{1,0:T(8,128)S(1)} collective-permute-done((f32[64,128]{1,0:T(8,128)S(1)}, f32[64,128]{1,0:T(8,128)S(1)}, u32[]{:S(2)}, u32[]{:S(2)}) %collective-permute-start.2) | collective-permute-done | bytes 32800 | tf_op jit(solution)/shard_map/ppermute | solution.py:605
  56.9 3.6 %fine_down.1 = (f32[64,64]{1,0:T(8,128)S(1)}, f32[16,40,128]{2,1,0:T(8,128)S(1)}) custom-call(s32[1,1]{1,0:T(1,128)} %bitcast.refs_0_, f32[64,64]{1,0:T(8,128)S(1)} %get-tuple-element.31.refs_1_, f32[64,128]{1,0:T(8,128)S(1)} %get-tuple-element.34.refs_2_, f32[64,128]{1,0:T(8,128)S(1)} %collective-permute-done.2.refs_3_, ...), custom_call_target="tpu_custom_call" | custom-call | tf_op jit(solution)/shard_map/fine_down/pallas_call | solution.py:51
  60.6 12.0 %all_to_all.30.refs_0_ = f32[16,40,128]{2,1,0:T(8,128)S(1)} all-to-all(f32[16,40,128]{2,1,0:T(8,128)S(1)} %get-tuple-element.43), channel_id=1, replica_groups={{0,1,2,3,128,129,130,131,256,257,258,259,384,385,386,387},{4,5,6,7,132,..., dimensions={0} | all-to-all | bytes 655360 | tf_op jit(solution)/shard_map/all_to_all | solution.py:596
  73.1 26.2 %all_to_all.31.refs_0_ = f32[32,2,256]{2,1,0:T(2,128)S(1)} all-to-all(f32[32,2,256]{2,1,0:T(2,128)S(1)} %sum_rows.1), channel_id=1, replica_groups={{0,4,8,12,16,20,24,28,32,36,40,44,48,52,56,60,64,68,72,76,80,84,88,92,9..., dimensions={0} | all-to-all | bytes 131072 | tf_op jit(solution)/shard_map/all_to_all | solution.py:600
  100.0 2.8 %pad_maximum_fusion = f32[4120,128]{1,0:T(8,128)} fusion(f32[64,128]{1,0:T(8,128)S(1)} %slice.18, f32[1352,128]{1,0:T(8,128)} %collective-permute-done.5.refs_4_, f32[1352,128]{1,0:T(8,128)} %collective-permute-done.4.refs_3_, f32[1352,128]{1,0:T(8,128)S(1)} %level_pack.1.refs_2_), kind=kLoop, calls=%fused_computation | loop fusion | flops 1582080 | bytes 4218880 | tf_op jit(solution)/shard_map/concatenate | solution.py:681
  102.8 1.9 collective-permute-start.7
  104.7 3.9 %all-to-all-start.2 = ((f32[32,2,256]{2,1,0:T(2,128)}), f32[32,2,256]{2,1,0:T(2,128)S(1)}, u32[]{:S(2)}, u32[]{:S(2)}) async-start(f32[32,2,256]{2,1,0:T(2,128)} %sum_all.1), calls=%async_computation.2 | async-start | bytes 131072 | tf_op jit(solution)/shard_map/all_to_all | solution.py:600
  108.7 14.2 %all-to-all-done.2.refs_0_ = f32[32,2,256]{2,1,0:T(2,128)S(1)} async-done(((f32[32,2,256]{2,1,0:T(2,128)}), f32[32,2,256]{2,1,0:T(2,128)S(1)}, u32[]{:S(2)}, u32[]{:S(2)}) %all-to-all-start.2) | async-done | bytes 65568 | tf_op jit(solution)/shard_map/all_to_all | solution.py:600
  124.0 5.5 %all-to-all-start.3 = ((f32[16,32,128]{2,1,0:T(8,128)}), f32[16,32,128]{2,1,0:T(8,128)S(1)}, u32[]{:S(2)}, u32[]{:S(2)}) async-start(f32[16,32,128]{2,1,0:T(8,128)} %windows.1), calls=%async_computation.3 | async-start | bytes 524288 | tf_op jit(solution)/shard_map/all_to_all | solution.py:596
  129.5 2.4 %collective-permute-start.8 = (f32[64,128]{1,0:T(8,128)S(1)}, f32[64,128]{1,0:T(8,128)S(1)}, u32[]{:S(2)}, u32[]{:S(2)}) collective-permute-start(f32[64,128]{1,0:T(8,128)S(1)} %slice.19), channel_id=1, source_target_pairs={{0,16},{8,24},{16,32},{20,4},{24,40},{28,12},{32,48},{36,20},{40,5... | collective-permute-start | bytes 98312 | tf_op jit(solution)/shard_map/ppermute | solution.py:656
  132.0 6.3 %collective-permute-done.8.refs_7_ = f32[64,128]{1,0:T(8,128)S(1)} collective-permute-done((f32[64,128]{1,0:T(8,128)S(1)}, f32[64,128]{1,0:T(8,128)S(1)}, u32[]{:S(2)}, u32[]{:S(2)}) %collective-permute-start.8) | collective-permute-done | bytes 32800 | tf_op jit(solution)/shard_map/ppermute | solution.py:656
  139.4 14.7 %level_cycle.1 = f32[32,2,256]{2,1,0:T(2,128)S(1)} custom-call(s32[1,2]{1,0:T(1,128)S(1)} %add_bitcast_fusion.refs_0_, f32[16,32,128]{2,1,0:T(8,128)S(1)} %all-to-all-done.3.refs_1_, f32[1352,128]{1,0:T(8,128)S(1)} %level_pack.1.refs_2_, f32[1352,128]{1,0:T(8,128)} %collective-permute-done.4.refs_3_, f32[1352,128]{1,0:T(8,128)} %collective-permute-done.5.refs_4_, ...), custom_call_target="tpu_custom_call" | custom-call | tf_op jit(solution)/shard_map/level_cycle/pallas_call | solution.py:51
  154.2 17.3 %all_to_all.32 = f32[32,2,256]{2,1,0:T(2,128)S(1)} all-to-all(f32[32,2,256]{2,1,0:T(2,128)S(1)} %level_cycle.1), channel_id=1, replica_groups={{0,4,8,12,16,20,24,28,32,36,40,44,48,52,56,60,64,68,72,76,80,84,88,92,9..., dimensions={0} | all-to-all | bytes 131072 | tf_op jit(solution)/shard_map/all_to_all | solution.py:600
  171.9 21.2 %all_to_all.33 = f32[16,32,2,256]{3,2,1,0:T(2,128)S(1)} all-to-all(f32[16,32,2,256]{3,2,1,0:T(2,128)S(1)} %broadcast_in_dim.28), channel_id=1, replica_groups={{0,1,2,3,128,129,130,131,256,257,258,259,384,385,386,387},{4,5,6,7,132,..., dimensions={0} | all-to-all | bytes 2097152 | tf_op jit(solution)/shard_map/all_to_all | solution.py:596
  193.1 1.4 fine_up.1.refs_1_
  194.5 3.5 %collective-permute-start.10 = (f32[64,128]{1,0:T(8,128)S(1)}, f32[64,128]{1,0:T(8,128)S(1)}, u32[]{:S(2)}, u32[]{:S(2)}) collective-permute-start(f32[64,128]{1,0:T(8,128)S(1)} %fine_up.1.refs_1_), channel_id=1, source_target_pairs={{1,0},{2,1},{3,2},{4,3},{5,4},{6,5},{7,6},{8,7},{9,8},{10,9},{11,1... | collective-permute-start | bytes 98312 | tf_op jit(solution)/shard_map/ppermute | solution.py:605
  198.0 2.3 %collective-permute-start.9 = (f32[64,128]{1,0:T(8,128)S(1)}, f32[64,128]{1,0:T(8,128)S(1)}, u32[]{:S(2)}, u32[]{:S(2)}) collective-permute-start(f32[64,128]{1,0:T(8,128)S(1)} %fine_up.1.refs_1_), channel_id=1, source_target_pairs={{0,1},{1,2},{2,3},{3,4},{4,5},{5,6},{6,7},{7,8},{8,9},{9,10},{10,1... | collective-permute-start | bytes 98312 | tf_op jit(solution)/shard_map/ppermute | solution.py:605
  200.3 7.1 %collective-permute-done.9.refs_2_ = f32[64,128]{1,0:T(8,128)S(1)} collective-permute-done((f32[64,128]{1,0:T(8,128)S(1)}, f32[64,128]{1,0:T(8,128)S(1)}, u32[]{:S(2)}, u32[]{:S(2)}) %collective-permute-start.9) | collective-permute-done | bytes 32800 | tf_op jit(solution)/shard_map/ppermute | solution.py:605
  207.4 1.9 fine_middle.1
  209.3 1.9 collective-permute-start.11
  211.2 7.9 %collective-permute-start.12 = (f32[64,128]{1,0:T(8,128)S(1)}, f32[64,128]{1,0:T(8,128)S(1)}, u32[]{:S(2)}, u32[]{:S(2)}) collective-permute-start(f32[64,128]{1,0:T(8,128)S(1)} %get-tuple-element.55.refs_2_), channel_id=1, source_target_pairs={{1,0},{2,1},{3,2},{4,3},{5,4},{6,5},{7,6},{8,7},{9,8},{10,9},{11,1... | collective-permute-start | bytes 98312 | tf_op jit(solution)/shard_map/ppermute | solution.py:605
  219.1 1.6 collective-permute-done.12.refs_4_
  220.7 2.6 %fine_end.1 = (f32[4,1024]{1,0:T(4,128)}, f32[4,1024]{1,0:T(4,128)}) custom-call(s32[1,1]{1,0:T(1,128)} %bitcast.refs_0_, f32[64,64]{1,0:T(8,128)S(1)} %get-tuple-element.54.refs_1_, f32[64,128]{1,0:T(8,128)S(1)} %get-tuple-element.55.refs_2_, f32[64,128]{1,0:T(8,128)S(1)} %collective-permute-done.11.refs_3_, f32[64,128]{1,0:T(8,128)S(1)} %collective-permute-done.12.refs_4_, ...), custom_call_target="tpu_custom_call" | custom-call | tf_op jit(solution)/shard_map/fine_end/pallas_call | solution.py:51
  (70 shorter events, 15.5 us)
Async XLA Ops:
  0.6 20.3 %copy-start.18 = (s32[8,3]{0,1:T(4,128)S(1)}, s32[8,3]{0,1:T(4,128)}, u32[]{:S(2)}) copy-start(s32[8,3]{0,1:T(4,128)} %param.21) | copy-start | bytes 292
  0.6 20.4 %copy-start.8 = (f32[8,3,4096]{2,0,1:T(8,128)S(1)}, f32[8,3,4096]{2,0,1:T(8,128)}, u32[]{:S(2)}) copy-start(f32[8,3,4096]{2,0,1:T(8,128)} %param.20) | copy-start | bytes 1179652
  0.7 20.4 %copy-start.10 = (f32[2,3,4096]{2,0,1:T(2,128)S(1)}, f32[2,3,4096]{2,0,1:T(2,128)}, u32[]{:S(2)}) copy-start(f32[2,3,4096]{2,0,1:T(2,128)} %param.23) | copy-start | bytes 294916
  0.7 20.4 %copy-start.9 = (f32[8,4096]{1,0:T(8,128)S(1)}, f32[8,4096]{1,0:T(8,128)}, u32[]{:S(2)}) copy-start(f32[8,4096]{1,0:T(8,128)} %refs_1_.3) | copy-start | bytes 393220
  0.7 20.4 %copy-start.17 = (s32[2,3]{1,0:T(2,128)S(1)}, s32[2,3]{1,0:T(2,128)}, u32[]{:S(2)}) copy-start(s32[2,3]{1,0:T(2,128)} %refs_4_.1) | copy-start | bytes 76
  1.9 30.0 %copy-start = (f32[16,3,4096]{2,0,1:T(8,128)S(1)}, f32[16,3,4096]{2,0,1:T(8,128)}, u32[]{:S(2)}) copy-start(f32[16,3,4096]{2,0,1:T(8,128)} %param.15) | copy-start | bytes 2359300
  6.1 24.2 %collective-permute-start = (f32[4,8,4096]{2,1,0:T(8,128)}, f32[4,8,4096]{2,1,0:T(8,128)S(1)}, u32[]{:S(2)}, u32[]{:S(2)}) collective-permute-start(f32[4,8,4096]{2,1,0:T(8,128)} %get-tuple-element.29), channel_id=1, source_target_pairs={{0,1},{1,2},{2,3},{3,4},{4,5},{5,6},{6,7},{7,8},{8,9},{9,10},{10,1... | collective-permute-start | bytes 1572872 | tf_op jit(solution)/shard_map/ppermute | solution.py:605
  9.5 21.7 %collective-permute-start.1 = (f32[4,8,4096]{2,1,0:T(8,128)}, f32[4,8,4096]{2,1,0:T(8,128)S(1)}, u32[]{:S(2)}, u32[]{:S(2)}) collective-permute-start(f32[4,8,4096]{2,1,0:T(8,128)} %get-tuple-element.30), channel_id=1, source_target_pairs={{1,0},{2,1},{3,2},{4,3},{5,4},{6,5},{7,6},{8,7},{9,8},{10,9},{11,1... | collective-permute-start | bytes 1572872 | tf_op jit(solution)/shard_map/ppermute | solution.py:605
  22.3 31.0 %copy-start.19 = (s32[16,2]{0,1:T(2,128)S(1)}, s32[16,2]{0,1:T(2,128)}, u32[]{:S(2)}) copy-start(s32[16,2]{0,1:T(2,128)} %param.18) | copy-start | bytes 388
  22.4 31.1 %copy-start.20 = (s32[16,2]{0,1:T(2,128)S(1)}, s32[16,2]{0,1:T(2,128)}, u32[]{:S(2)}) copy-start(s32[16,2]{0,1:T(2,128)} %param.19) | copy-start | bytes 388
  22.4 38.2 %collective-permute-start.4 = (f32[1352,128]{1,0:T(8,128)S(1)}, f32[1352,128]{1,0:T(8,128)}, u32[]{:S(2)}, u32[]{:S(2)}) collective-permute-start(f32[1352,128]{1,0:T(8,128)S(1)} %level_pack.1.refs_2_), channel_id=1, source_target_pairs={{0,8},{4,12},{8,16},{12,20},{16,24},{20,28},{24,32},{28,36},{32,40... | collective-permute-start | bytes 2076680 | tf_op jit(solution)/shard_map/ppermute | solution.py:605
  24.3 36.3 %collective-permute-start.5 = (f32[1352,128]{1,0:T(8,128)S(1)}, f32[1352,128]{1,0:T(8,128)}, u32[]{:S(2)}, u32[]{:S(2)}) collective-permute-start(f32[1352,128]{1,0:T(8,128)S(1)} %level_pack.1.refs_2_), channel_id=1, source_target_pairs={{8,0},{12,4},{16,8},{20,12},{24,16},{28,20},{32,24},{36,28},{40,32... | collective-permute-start | bytes 2076680 | tf_op jit(solution)/shard_map/ppermute | solution.py:605
  32.0 1.0 copy-start.4
  33.0 1.0 copy-start.6
  36.4 8.2 %copy-start.11 = (f32[64,128]{1,0:T(8,128)}, f32[64,128]{1,0:T(8,128)S(1)}, u32[]{:S(2)}) copy-start(f32[64,128]{1,0:T(8,128)S(1)} %get-tuple-element.53.refs_4_) | copy-start | bytes 98308
  37.3 23.3 %collective-permute-start.6 = (f32[1160,128]{1,0:T(8,128)}, f32[1160,128]{1,0:T(8,128)S(1)}, u32[]{:S(2)}, u32[]{:S(2)}) collective-permute-start(f32[1160,128]{1,0:T(8,128)} %slice.17), channel_id=1, source_target_pairs={{4,16},{12,24},{16,4},{20,32},{24,12},{28,40},{32,20},{36,48},{40,... | collective-permute-start | bytes 1781768 | tf_op jit(solution)/shard_map/ppermute | solution.py:656
  42.3 14.6 %collective-permute-start.2 = (f32[64,128]{1,0:T(8,128)S(1)}, f32[64,128]{1,0:T(8,128)S(1)}, u32[]{:S(2)}, u32[]{:S(2)}) collective-permute-start(f32[64,128]{1,0:T(8,128)S(1)} %get-tuple-element.34.refs_2_), channel_id=1, source_target_pairs={{0,1},{1,2},{2,3},{3,4},{4,5},{5,6},{6,7},{7,8},{8,9},{9,10},{10,1... | collective-permute-start | bytes 98312 | tf_op jit(solution)/shard_map/ppermute | solution.py:605
  44.6 12.3 %collective-permute-start.3 = (f32[64,128]{1,0:T(8,128)S(1)}, f32[64,128]{1,0:T(8,128)}, u32[]{:S(2)}, u32[]{:S(2)}) collective-permute-start(f32[64,128]{1,0:T(8,128)S(1)} %get-tuple-element.34.refs_2_), channel_id=1, source_target_pairs={{1,0},{2,1},{3,2},{4,3},{5,4},{6,5},{7,6},{8,7},{9,8},{10,9},{11,1... | collective-permute-start | bytes 98312 | tf_op jit(solution)/shard_map/ppermute | solution.py:605
  52.1 1.0 copy-start.7
  60.6 42.3 %copy-start.13 = (f32[64,64]{1,0:T(8,128)}, f32[64,64]{1,0:T(8,128)S(1)}, u32[]{:S(2)}) copy-start(f32[64,64]{1,0:T(8,128)S(1)} %get-tuple-element.52.x_ref) | copy-start | bytes 49156
  60.6 42.2 %copy-start.1 = (f32[1160,128]{1,0:T(8,128)}, f32[1160,128]{1,0:T(8,128)S(1)}, u32[]{:S(2)}) copy-start(f32[1160,128]{1,0:T(8,128)S(1)} %collective-permute-done.6.refs_5_) | copy-start | bytes 1781764
  102.8 35.6 %collective-permute-start.7 = (f32[4120,128]{1,0:T(8,128)}, f32[4120,128]{1,0:T(8,128)}, u32[]{:S(2)}, u32[]{:S(2)}) collective-permute-start(f32[4120,128]{1,0:T(8,128)} %pad_maximum_fusion), channel_id=1, source_target_pairs={{0,4},{4,0},{8,12},{12,8},{16,20},{20,16},{24,28},{28,24},{32,36},... | collective-permute-start | bytes 6328328 | tf_op jit(solution)/shard_map/ppermute | solution.py:682
  104.7 18.2 %all-to-all-start.2 = ((f32[32,2,256]{2,1,0:T(2,128)}), f32[32,2,256]{2,1,0:T(2,128)S(1)}, u32[]{:S(2)}, u32[]{:S(2)}) async-start(f32[32,2,256]{2,1,0:T(2,128)} %sum_all.1), calls=%async_computation.2 | async-start | bytes 131072 | tf_op jit(solution)/shard_map/all_to_all | solution.py:600
  124.0 14.3 %all-to-all-start.3 = ((f32[16,32,128]{2,1,0:T(8,128)}), f32[16,32,128]{2,1,0:T(8,128)S(1)}, u32[]{:S(2)}, u32[]{:S(2)}) async-start(f32[16,32,128]{2,1,0:T(8,128)} %windows.1), calls=%async_computation.3 | async-start | bytes 524288 | tf_op jit(solution)/shard_map/all_to_all | solution.py:596
  129.5 8.8 %collective-permute-start.8 = (f32[64,128]{1,0:T(8,128)S(1)}, f32[64,128]{1,0:T(8,128)S(1)}, u32[]{:S(2)}, u32[]{:S(2)}) collective-permute-start(f32[64,128]{1,0:T(8,128)S(1)} %slice.19), channel_id=1, source_target_pairs={{0,16},{8,24},{16,32},{20,4},{24,40},{28,12},{32,48},{36,20},{40,5... | collective-permute-start | bytes 98312 | tf_op jit(solution)/shard_map/ppermute | solution.py:656
  138.4 1.1 copy-start.2
  154.2 38.9 %copy-start.14 = (f32[64,64]{1,0:T(8,128)S(1)}, f32[64,64]{1,0:T(8,128)}, u32[]{:S(2)}) copy-start(f32[64,64]{1,0:T(8,128)} %copy-done.13) | copy-start | bytes 49156
  171.9 35.5 %copy-start.12 = (f32[64,128]{1,0:T(8,128)S(1)}, f32[64,128]{1,0:T(8,128)}, u32[]{:S(2)}) copy-start(f32[64,128]{1,0:T(8,128)} %copy-done.11) | copy-start | bytes 98308
  194.5 5.9 %collective-permute-start.10 = (f32[64,128]{1,0:T(8,128)S(1)}, f32[64,128]{1,0:T(8,128)S(1)}, u32[]{:S(2)}, u32[]{:S(2)}) collective-permute-start(f32[64,128]{1,0:T(8,128)S(1)} %fine_up.1.refs_1_), channel_id=1, source_target_pairs={{1,0},{2,1},{3,2},{4,3},{5,4},{6,5},{7,6},{8,7},{9,8},{10,9},{11,1... | collective-permute-start | bytes 98312 | tf_op jit(solution)/shard_map/ppermute | solution.py:605
  198.0 9.5 %collective-permute-start.9 = (f32[64,128]{1,0:T(8,128)S(1)}, f32[64,128]{1,0:T(8,128)S(1)}, u32[]{:S(2)}, u32[]{:S(2)}) collective-permute-start(f32[64,128]{1,0:T(8,128)S(1)} %fine_up.1.refs_1_), channel_id=1, source_target_pairs={{0,1},{1,2},{2,3},{3,4},{4,5},{5,6},{6,7},{7,8},{8,9},{9,10},{10,1... | collective-permute-start | bytes 98312 | tf_op jit(solution)/shard_map/ppermute | solution.py:605
  209.3 9.8 %collective-permute-start.11 = (f32[64,128]{1,0:T(8,128)S(1)}, f32[64,128]{1,0:T(8,128)S(1)}, u32[]{:S(2)}, u32[]{:S(2)}) collective-permute-start(f32[64,128]{1,0:T(8,128)S(1)} %get-tuple-element.55.refs_2_), channel_id=1, source_target_pairs={{0,1},{1,2},{2,3},{3,4},{4,5},{5,6},{6,7},{7,8},{8,9},{9,10},{10,1... | collective-permute-start | bytes 98312 | tf_op jit(solution)/shard_map/ppermute | solution.py:605
  211.2 9.4 %collective-permute-start.12 = (f32[64,128]{1,0:T(8,128)S(1)}, f32[64,128]{1,0:T(8,128)S(1)}, u32[]{:S(2)}, u32[]{:S(2)}) collective-permute-start(f32[64,128]{1,0:T(8,128)S(1)} %get-tuple-element.55.refs_2_), channel_id=1, source_target_pairs={{1,0},{2,1},{3,2},{4,3},{5,4},{6,5},{7,6},{8,7},{9,8},{10,9},{11,1... | collective-permute-start | bytes 98312 | tf_op jit(solution)/shard_map/ppermute | solution.py:605
  (4 other events, 3.0 us)

commit v7 on v6

--- a/solution.py
+++ b/solution.py
@@ -325,7 +325,8 @@
     return jnp.stack([p[0] for p in parts]), jnp.stack([p[1] for p in parts])
 
 
-def sum_rows(parts):
+def line_windows(place, parts):
+    sub = place[0, 1]
     total = jnp.zeros((128, 256), F32)
     for q in range(0, XN * YN, 2):
         v = jnp.concatenate(
@@ -334,25 +335,25 @@
         at = jnp.concatenate([parts[q + i, 32:33, :64] for i in range(2)], axis=1).astype(I32)
         table = (iota((256, 128), 0) + 1 == at).astype(F32).astype(BF16)
         total = total + mm(stacked(v), table, NT)
-    total = total[:64] + total[64:]
-    return (jnp.stack([total[2 * t : 2 * t + 2] for t in range(TN_)]),)
+    x = stacked(total[:64] + total[64:])
+    lane = iota((1, 128), 1)
+    out = []
+    for t in range(0, TN_, 2):
+        spot = t + (lane >> 6)
+        source = (spot + offset(lane, (sub - spot) & 3)) & (TN_ - 1)
+        g = mm(x, one_hot(256, (source >> 2) * 32 + (lane & 31)), NN)
+        g = g[:64] + g[64:]
+        out += [jnp.concatenate([v[:32], v[32:]], axis=1) for v in (g[:, :64], g[:, 64:])]
+    return (jnp.stack(out),)
+
+
+def offset(lane, ahead):
+    rel = jnp.where((lane & 32) == 0, ahead - 4, ahead)
+    return jnp.where(((lane & 32) == 0) & (ahead == 0) & ((lane & 31) < 16), 4, rel)
 
 
 def sum_all(parts):
-    return (jnp.broadcast_to(jnp.sum(parts, axis=0)[None], parts.shape),)
-
-
-def windows(parts, idx):
-    x = stacked(jnp.concatenate([parts[t] for t in range(TN_)], axis=0))
-    out = []
-    for q in range(XN * YN):
-        half = idx[:, (q // 2) * 128 : (q // 2) * 128 + 128]
-        if q % 2 == 0:
-            g = mm(x, one_hot(256, half), NN)
-            g = g[:64] + g[64:]
-        v = g[:, (q % 2) * 64 : (q % 2) * 64 + 64]
-        out.append(jnp.concatenate([v[:32], v[32:]], axis=1))
-    return (jnp.stack(out),)
+    return (jnp.broadcast_to(jnp.sum(parts, axis=0)[None], (XN * YN, 32, 128)),)
 
 
 A1_ROWS = 3 * R1 * 32
@@ -454,14 +455,18 @@
 
 
 def middle(place, parts, b_hi, b_lo, q_hi, q_lo, d1, d2, tables, c_tables, unpack):
-    sub = place[0, 1]
+    slab, sub = place[0, 0], place[0, 1]
     blocks = (b_hi, b_lo)
     lane128 = iota((1, 128), 1)
     pieces = []
     for x in range(XN):
-        w = parts[x]
-        for y in range(1, YN):
-            w = w + parts[y * XN + x]
+        spot = slab & (TN_ - 1)
+        at = spot + offset(lane128, (x - spot) & 3)
+        row = (slab >> 5) + jnp.where(at < 0, -1, jnp.where(at >= TN_, 1, 0))
+        row = jnp.broadcast_to(row, (32, 128))
+        w = jnp.zeros((32, 128), F32)
+        for y in range(YN):
+            w = jnp.where(row == y, parts[y * XN + x], w)
         pieces.append(jnp.concatenate([w[:, :64], w[:, 64:]], axis=0))
     g = mm(stacked(jnp.concatenate(pieces, axis=1)), one_hot(256, unpack), NN)
     rhs = g[:64] + g[64:]
@@ -665,32 +670,23 @@
         smem=(0,),
         own=range(1, 5),
     )
-    send, pack = lax.optimization_barrier((send, pack))
+    left, right = shifted(send, both, 1), shifted(send, both, -1)
+    left, right, pack = lax.optimization_barrier((left, right, pack))
     crossed = crossing(pack[:A2_AT], 3)
     x3, dense = kern(
         fine_down,
         [((64, 64), F32), ((16, 40, 128), F32)],
-        [device, x1, send, shifted(send, both, 1), shifted(send, both, -1), hi, lo, inverse, idx, owner_rows, send_slots, p_hi, p_lo],
+        [device, x1, send, left, right, hi, lo, inverse, idx, owner_rows, send_slots, p_hi, p_lo],
         smem=(0, 9, 10),
     )
 
-    dense, m2, p2, crossed = lax.optimization_barrier((dense, m2, p2, crossed))
-    (part,) = kern(sum_rows, [((TN_, 2, 256), F32)], [across(dense)])
-    (part,) = kern(sum_all, [((TN_, 2, 256), F32)], [along(part)])
+    dense, m2, p2 = lax.optimization_barrier((dense, m2, p2))
+    (part,) = kern(line_windows, [((TN_, 32, 128), F32)], [place, across(dense)], smem=(0,))
     part, m2, p2, crossed, pack = lax.optimization_barrier((part, m2, p2, crossed, pack))
     twin = jnp.concatenate([pack, m2, p2, crossed[D1_AT : D1_AT + 64]], axis=0)
     twin = lax.ppermute(twin, "slab", [(i, i ^ 1) for i in range(count)])
     far = crossing(pack[D1_AT : D1_AT + 64], 4)
-    q = jnp.arange(XN * YN * 64, dtype=I32)
-    spot = slab % TN_
-    near_by = (sub - spot) % XN
-    row = (q % 32) // 4
-    rel = jnp.where((q % 64) // 32 == 1, near_by, near_by - 4)
-    rel = jnp.where(((q % 64) // 32 == 0) & (near_by == 0) & (row < 4), 4, rel)
-    wanted = (q // 256) * TN_ + spot + rel
-    wanted = jnp.where(wanted // TN_ == slab // TN_, (wanted % TN_) // XN * 32 + q % 32, -1)
-    wanted = jnp.where(wanted >= 0, wanted, -1)
-    (part,) = kern(windows, [((16, 32, 128), F32)], [along(part), wanted.reshape(1, 1024)])
+    (part,) = kern(sum_all, [((XN * YN, 32, 128), F32)], [along(part)])
     part = across(part)
 
     (share,) = kern(

time: 225 us -> 217 us (0.964)
  blocking collectives: 76.7 us -> 38.5 us
  starting transfers between devices: 66.8 us -> 82.2 us
  waiting for transfers between devices: 32.6 us -> 46.4 us
    all_to_all x2 -> x1, blocking collectives: 43.5 us -> 17.3 us  [along(): return lax.all_to_all(value, 'slab', 0, 0, tiled=True, axis_index_groups=ZC)]
    all_to_all x1, waiting for transfers between devices: 14.2 us -> 28 us  [along(): return lax.all_to_all(value, 'slab', 0, 0, tiled=True, axis_index_groups=ZC)]
    all_to_all x2 -> x1, blocking collectives: 33.2 us -> 21.2 us  [across(): lax.all_to_all(value, ('slab', 'sub'), 0, 0, tiled=True, axis_index_group...]
    all_to_all x1 -> x2, starting transfers between devices: 5.45 us -> 14.7 us  [across(): lax.all_to_all(value, ('slab', 'sub'), 0, 0, tiled=True, axis_index_group...]
    ppermute x10, waiting for transfers between devices: 12 us -> 4.71 us  [shifted(): lax.ppermute(value, axis, [(i, i + by) for i in range(n) if 0 <= i + by <...]
    all_to_all x1 -> x2, waiting for transfers between devices: 0.01 us -> 6.95 us  [across(): lax.all_to_all(value, ('slab', 'sub'), 0, 0, tiled=True, axis_index_group...]
    all_to_all x1, starting transfers between devices: 3.86 us -> 8.98 us  [along(): return lax.all_to_all(value, 'slab', 0, 0, tiled=True, axis_index_groups=ZC)]
    ppermute x10, starting transfers between devices: 48.2 us -> 52.1 us  [shifted(): lax.ppermute(value, axis, [(i, i + by) for i in range(n) if 0 <= i + by <...]
  transfers between devices with their start and end apart: 15 -> 16, of which waited for: 5 -> 6; matrix products, arithmetic and copies ran while one was open for 1% -> 2% of each run, Pallas kernels for 4% -> 5%
where the time goes in v7:
time: 217 us; the launch traced here: 216 us
  starting transfers between devices  82.2 us (38%)
  waiting for transfers between devices  46.4 us (21%)
  blocking collectives  38.5 us (18%)
  Pallas kernels  32.5 us (15%)
  local copies, waits for them, and re-layouts  11.2 us (5%)
  other arithmetic  3.92 us (2%)
    ppermute x10, starting transfers between devices, shifted(): lax.ppermute(value, axis, [(i, i + by) for i in range(n) if 0 <= i + by <...  52.1 us
    pallas_call x10, Pallas kernels, kern(): pl.pallas_call(kernel, in_specs=specs, out_specs=[pl.BlockSpec() if own_o...  31 us
    all_to_all x1, waiting for transfers between devices, along(): return lax.all_to_all(value, 'slab', 0, 0, tiled=True, axis_index_groups=ZC)  28 us
    all_to_all x1, blocking collectives, across(): lax.all_to_all(value, ('slab', 'sub'), 0, 0, tiled=True, axis_index_group...  21.2 us
    all_to_all x1, blocking collectives, along(): return lax.all_to_all(value, 'slab', 0, 0, tiled=True, axis_index_groups=ZC)  17.3 us
    all_to_all x2, starting transfers between devices, across(): lax.all_to_all(value, ('slab', 'sub'), 0, 0, tiled=True, axis_index_group...  14.7 us
    all_to_all x1, starting transfers between devices, along(): return lax.all_to_all(value, 'slab', 0, 0, tiled=True, axis_index_groups=ZC)  8.98 us
    unnamed x35, local copies, waits for them, and re-layouts  7.87 us
  transfers between devices with their start and end apart: 16, of which 6 were waited for; matrix products, arithmetic and copies ran while one was open for 2% of the time, Pallas kernels for 5%

profile of v7, /device:TPU:8, one launch (start us, length us, event | category | flops | bytes accessed | tf_op | source)
XLA Modules:
  0.0 215.5 jit_solution(2555587863342871882)
XLA Ops:
  6.0 3.4 %collective-permute-start = (f32[4,8,4096]{2,1,0:T(8,128)}, f32[4,8,4096]{2,1,0:T(8,128)S(1)}, u32[]{:S(2)}, u32[]{:S(2)}) collective-permute-start(f32[4,8,4096]{2,1,0:T(8,128)} %get-tuple-element.29), channel_id=1, source_target_pairs={{0,1},{1,2},{2,3},{3,4},{4,5},{5,6},{6,7},{7,8},{8,9},{9,10},{10,1... | collective-permute-start | bytes 1572872 | tf_op jit(solution)/shard_map/ppermute | solution.py:610
  9.4 11.4 %collective-permute-start.1 = (f32[4,8,4096]{2,1,0:T(8,128)}, f32[4,8,4096]{2,1,0:T(8,128)S(1)}, u32[]{:S(2)}, u32[]{:S(2)}) collective-permute-start(f32[4,8,4096]{2,1,0:T(8,128)} %get-tuple-element.30), channel_id=1, source_target_pairs={{1,0},{2,1},{3,2},{4,3},{5,4},{6,5},{7,6},{8,7},{9,8},{10,9},{11,1... | collective-permute-start | bytes 1572872 | tf_op jit(solution)/shard_map/ppermute | solution.py:610
  22.3 1.9 collective-permute-start.4
  24.2 6.0 %collective-permute-start.5 = (f32[1352,128]{1,0:T(8,128)S(1)}, f32[1352,128]{1,0:T(8,128)}, u32[]{:S(2)}, u32[]{:S(2)}) collective-permute-start(f32[1352,128]{1,0:T(8,128)S(1)} %level_pack.1.refs_2_), channel_id=1, source_target_pairs={{8,0},{12,4},{16,8},{20,12},{24,16},{28,20},{32,24},{36,28},{40,32... | collective-permute-start | bytes 2076680 | tf_op jit(solution)/shard_map/ppermute | solution.py:610
  34.0 2.3 %fine_start.1 = (bf16[2,3,512,128]{3,2,1,0:T(8,128)(2,1)S(1)}, bf16[2,3,512,128]{3,2,1,0:T(8,128)(2,1)S(1)}, f32[64,128]{1,0:T(8,128)S(1)}, f32[64,128]{1,0:T(8,...) custom-call(s32[1,1]{1,0:T(1,128)} %bitcast.refs_0_, ...), custom_call_target="tpu_custom_call" | custom-call | tf_op jit(solution)/shard_map/fine_start/pallas_call | solution.py:51
  36.3 1.9 collective-permute-start.2
  38.2 7.9 %collective-permute-start.3 = (f32[64,128]{1,0:T(8,128)S(1)}, f32[64,128]{1,0:T(8,128)S(1)}, u32[]{:S(2)}, u32[]{:S(2)}) collective-permute-start(f32[64,128]{1,0:T(8,128)S(1)} %get-tuple-element.32.refs_2_), channel_id=1, source_target_pairs={{1,0},{2,1},{3,2},{4,3},{5,4},{6,5},{7,6},{8,7},{9,8},{10,9},{11,1... | collective-permute-start | bytes 98312 | tf_op jit(solution)/shard_map/ppermute | solution.py:610
  46.1 1.6 collective-permute-done.3.refs_4_
  48.5 2.1 collective-permute-start.6
  52.1 4.4 %fine_down.1 = (f32[64,64]{1,0:T(8,128)S(1)}, f32[16,40,128]{2,1,0:T(8,128)}) custom-call(s32[1,1]{1,0:T(1,128)} %bitcast.refs_0_, f32[64,64]{1,0:T(8,128)S(1)} %get-tuple-element.31.refs_1_, f32[64,128]{1,0:T(8,128)S(1)} %get-tuple-element.32.refs_2_, f32[64,128]{1,0:T(8,128)S(1)} %collective-permute-done.2.refs_3_, ...), custom_call_target="tpu_custom_call" | custom-call | tf_op jit(solution)/shard_map/fine_down/pallas_call | solution.py:51
  56.5 9.3 %all-to-all-start = ((f32[16,40,128]{2,1,0:T(8,128)}), f32[16,40,128]{2,1,0:T(8,128)S(1)}, u32[]{:S(2)}, u32[]{:S(2)}) async-start(f32[16,40,128]{2,1,0:T(8,128)} %get-tuple-element.43), calls=%async_computation | async-start | bytes 655360 | tf_op jit(solution)/shard_map/all_to_all | solution.py:601
  65.8 6.9 %all-to-all-done.refs_1_ = f32[16,40,128]{2,1,0:T(8,128)S(1)} async-done(((f32[16,40,128]{2,1,0:T(8,128)}), f32[16,40,128]{2,1,0:T(8,128)S(1)}, u32[]{:S(2)}, u32[]{:S(2)}) %all-to-all-start) | async-done | bytes 327712 | tf_op jit(solution)/shard_map/all_to_all | solution.py:601
  72.7 2.6 %line_windows.1 = f32[32,32,128]{2,1,0:T(8,128)} custom-call(s32[1,2]{1,0:T(1,128)S(1)} %add_bitcast_fusion.refs_0_, f32[16,40,128]{2,1,0:T(8,128)S(1)} %all-to-all-done.refs_1_), custom_call_target="tpu_custom_call" | custom-call | tf_op jit(solution)/shard_map/line_windows/pallas_call | solution.py:51
  75.3 9.0 %all-to-all-start.1 = ((f32[32,32,128]{2,1,0:T(8,128)}), f32[32,32,128]{2,1,0:T(8,128)S(1)}, u32[]{:S(2)}, u32[]{:S(2)}) async-start(f32[32,32,128]{2,1,0:T(8,128)} %line_windows.1), calls=%async_computation.1 | async-start | bytes 1048576 | tf_op jit(solution)/shard_map/all_to_all | solution.py:605
  85.0 2.8 %pad_maximum_fusion = f32[4120,128]{1,0:T(8,128)} fusion(f32[64,128]{1,0:T(8,128)S(1)} %slice.18, f32[1352,128]{1,0:T(8,128)} %collective-permute-done.5.refs_4_, f32[1352,128]{1,0:T(8,128)} %collective-permute-done.4.refs_3_, f32[1352,128]{1,0:T(8,128)S(1)} %level_pack.1.refs_2_), kind=kLoop, calls=%fused_computation | loop fusion | flops 1582080 | bytes 4218880 | tf_op jit(solution)/shard_map/concatenate | solution.py:686
  87.8 2.2 %collective-permute-start.7 = (f32[4120,128]{1,0:T(8,128)}, f32[4120,128]{1,0:T(8,128)}, u32[]{:S(2)}, u32[]{:S(2)}) collective-permute-start(f32[4120,128]{1,0:T(8,128)} %pad_maximum_fusion), channel_id=1, source_target_pairs={{0,4},{4,0},{8,12},{12,8},{16,20},{20,16},{24,28},{28,24},{32,36},... | collective-permute-start | bytes 6328328 | tf_op jit(solution)/shard_map/ppermute | solution.py:687
  90.0 28.0 %all-to-all-done.1.refs_0_ = f32[32,32,128]{2,1,0:T(8,128)S(1)} async-done(((f32[32,32,128]{2,1,0:T(8,128)}), f32[32,32,128]{2,1,0:T(8,128)S(1)}, u32[]{:S(2)}, u32[]{:S(2)}) %all-to-all-start.1) | async-done | bytes 524320 | tf_op jit(solution)/shard_map/all_to_all | solution.py:605
  118.8 5.5 %all-to-all-start.2 = ((f32[16,32,128]{2,1,0:T(8,128)}), f32[16,32,128]{2,1,0:T(8,128)S(1)}, u32[]{:S(2)}, u32[]{:S(2)}) async-start(f32[16,32,128]{2,1,0:T(8,128)} %copy-done.1), calls=%async_computation.2 | async-start | bytes 524288 | tf_op jit(solution)/shard_map/all_to_all | solution.py:601
  124.3 2.1 collective-permute-start.8
  126.4 6.7 %collective-permute-done.8.refs_7_ = f32[64,128]{1,0:T(8,128)S(1)} collective-permute-done((f32[64,128]{1,0:T(8,128)S(1)}, f32[64,128]{1,0:T(8,128)S(1)}, u32[]{:S(2)}, u32[]{:S(2)}) %collective-permute-start.8) | collective-permute-done | bytes 32800 | tf_op jit(solution)/shard_map/ppermute | solution.py:661
  133.1 14.9 %level_cycle.1 = f32[32,2,256]{2,1,0:T(2,128)S(1)} custom-call(s32[1,2]{1,0:T(1,128)S(1)} %add_bitcast_fusion.refs_0_, f32[16,32,128]{2,1,0:T(8,128)S(1)} %all-to-all-done.2.refs_1_, f32[1352,128]{1,0:T(8,128)S(1)} %level_pack.1.refs_2_, f32[1352,128]{1,0:T(8,128)} %collective-permute-done.4.refs_3_, f32[1352,128]{1,0:T(8,128)} %collective-permute-done.5.refs_4_, ...), custom_call_target="tpu_custom_call" | custom-call | tf_op jit(solution)/shard_map/level_cycle/pallas_call | solution.py:51
  148.0 17.3 %all_to_all.25 = f32[32,2,256]{2,1,0:T(2,128)S(1)} all-to-all(f32[32,2,256]{2,1,0:T(2,128)S(1)} %level_cycle.1), channel_id=1, replica_groups={{0,4,8,12,16,20,24,28,32,36,40,44,48,52,56,60,64,68,72,76,80,84,88,92,9..., dimensions={0} | all-to-all | bytes 131072 | tf_op jit(solution)/shard_map/all_to_all | solution.py:605
  165.7 21.2 %all_to_all.26 = f32[16,32,2,256]{3,2,1,0:T(2,128)S(1)} all-to-all(f32[16,32,2,256]{3,2,1,0:T(2,128)S(1)} %broadcast_in_dim.7), channel_id=1, replica_groups={{0,1,2,3,128,129,130,131,256,257,258,259,384,385,386,387},{4,5,6,7,132,..., dimensions={0} | all-to-all | bytes 2097152 | tf_op jit(solution)/shard_map/all_to_all | solution.py:601
  186.9 1.4 fine_up.1.refs_1_
  188.3 2.2 %collective-permute-start.9 = (f32[64,128]{1,0:T(8,128)S(1)}, f32[64,128]{1,0:T(8,128)S(1)}, u32[]{:S(2)}, u32[]{:S(2)}) collective-permute-start(f32[64,128]{1,0:T(8,128)S(1)} %fine_up.1.refs_1_), channel_id=1, source_target_pairs={{0,1},{1,2},{2,3},{3,4},{4,5},{5,6},{6,7},{7,8},{8,9},{9,10},{10,1... | collective-permute-start | bytes 98312 | tf_op jit(solution)/shard_map/ppermute | solution.py:610
  190.5 7.6 %collective-permute-start.10 = (f32[64,128]{1,0:T(8,128)S(1)}, f32[64,128]{1,0:T(8,128)S(1)}, u32[]{:S(2)}, u32[]{:S(2)}) collective-permute-start(f32[64,128]{1,0:T(8,128)S(1)} %fine_up.1.refs_1_), channel_id=1, source_target_pairs={{1,0},{2,1},{3,2},{4,3},{5,4},{6,5},{7,6},{8,7},{9,8},{10,9},{11,1... | collective-permute-start | bytes 98312 | tf_op jit(solution)/shard_map/ppermute | solution.py:610
  198.1 1.6 collective-permute-done.10.refs_3_
  199.7 1.9 fine_middle.1
  201.5 1.9 collective-permute-start.11
  203.5 7.9 %collective-permute-start.12 = (f32[64,128]{1,0:T(8,128)S(1)}, f32[64,128]{1,0:T(8,128)S(1)}, u32[]{:S(2)}, u32[]{:S(2)}) collective-permute-start(f32[64,128]{1,0:T(8,128)S(1)} %get-tuple-element.55.refs_2_), channel_id=1, source_target_pairs={{1,0},{2,1},{3,2},{4,3},{5,4},{6,5},{7,6},{8,7},{9,8},{10,9},{11,1... | collective-permute-start | bytes 98312 | tf_op jit(solution)/shard_map/ppermute | solution.py:610
  211.3 1.6 collective-permute-done.12.refs_4_
  212.9 2.6 %fine_end.1 = (f32[4,1024]{1,0:T(4,128)}, f32[4,1024]{1,0:T(4,128)}) custom-call(s32[1,1]{1,0:T(1,128)} %bitcast.refs_0_, f32[64,64]{1,0:T(8,128)S(1)} %get-tuple-element.54.refs_1_, f32[64,128]{1,0:T(8,128)S(1)} %get-tuple-element.55.refs_2_, f32[64,128]{1,0:T(8,128)S(1)} %collective-permute-done.11.refs_3_, f32[64,128]{1,0:T(8,128)S(1)} %collective-permute-done.12.refs_4_, ...), custom_call_target="tpu_custom_call" | custom-call | tf_op jit(solution)/shard_map/fine_end/pallas_call | solution.py:51
  (58 shorter events, 14.7 us)
Async XLA Ops:
  0.6 20.2 %copy-start.13 = (s32[8,3]{0,1:T(4,128)S(1)}, s32[8,3]{0,1:T(4,128)}, u32[]{:S(2)}) copy-start(s32[8,3]{0,1:T(4,128)} %param.21) | copy-start | bytes 292
  0.6 20.3 %copy-start.7 = (f32[8,3,4096]{2,0,1:T(8,128)S(1)}, f32[8,3,4096]{2,0,1:T(8,128)}, u32[]{:S(2)}) copy-start(f32[8,3,4096]{2,0,1:T(8,128)} %param.20) | copy-start | bytes 1179652
  0.7 20.3 %copy-start.8 = (f32[8,4096]{1,0:T(8,128)S(1)}, f32[8,4096]{1,0:T(8,128)}, u32[]{:S(2)}) copy-start(f32[8,4096]{1,0:T(8,128)} %refs_1_.3) | copy-start | bytes 393220
  0.7 20.3 %copy-start.9 = (f32[2,3,4096]{2,0,1:T(2,128)S(1)}, f32[2,3,4096]{2,0,1:T(2,128)}, u32[]{:S(2)}) copy-start(f32[2,3,4096]{2,0,1:T(2,128)} %param.23) | copy-start | bytes 294916
  0.7 20.3 %copy-start.12 = (s32[2,3]{1,0:T(2,128)S(1)}, s32[2,3]{1,0:T(2,128)}, u32[]{:S(2)}) copy-start(s32[2,3]{1,0:T(2,128)} %refs_4_.1) | copy-start | bytes 76
  2.7 0.7 copy-start.10
  3.4 0.7 copy-start.11
  4.1 27.8 %copy-start = (f32[16,3,4096]{2,0,1:T(8,128)S(1)}, f32[16,3,4096]{2,0,1:T(8,128)}, u32[]{:S(2)}) copy-start(f32[16,3,4096]{2,0,1:T(8,128)} %param.15) | copy-start | bytes 2359300
  6.0 24.2 %collective-permute-start = (f32[4,8,4096]{2,1,0:T(8,128)}, f32[4,8,4096]{2,1,0:T(8,128)S(1)}, u32[]{:S(2)}, u32[]{:S(2)}) collective-permute-start(f32[4,8,4096]{2,1,0:T(8,128)} %get-tuple-element.29), channel_id=1, source_target_pairs={{0,1},{1,2},{2,3},{3,4},{4,5},{5,6},{6,7},{7,8},{8,9},{9,10},{10,1... | collective-permute-start | bytes 1572872 | tf_op jit(solution)/shard_map/ppermute | solution.py:610
  9.4 21.6 %collective-permute-start.1 = (f32[4,8,4096]{2,1,0:T(8,128)}, f32[4,8,4096]{2,1,0:T(8,128)S(1)}, u32[]{:S(2)}, u32[]{:S(2)}) collective-permute-start(f32[4,8,4096]{2,1,0:T(8,128)} %get-tuple-element.30), channel_id=1, source_target_pairs={{1,0},{2,1},{3,2},{4,3},{5,4},{6,5},{7,6},{8,7},{9,8},{10,9},{11,1... | collective-permute-start | bytes 1572872 | tf_op jit(solution)/shard_map/ppermute | solution.py:610
  21.0 29.6 %copy-start.14 = (s32[16,2]{0,1:T(2,128)S(1)}, s32[16,2]{0,1:T(2,128)}, u32[]{:S(2)}) copy-start(s32[16,2]{0,1:T(2,128)} %param.18) | copy-start | bytes 388
  21.0 29.7 %copy-start.15 = (s32[16,2]{0,1:T(2,128)S(1)}, s32[16,2]{0,1:T(2,128)}, u32[]{:S(2)}) copy-start(s32[16,2]{0,1:T(2,128)} %param.19) | copy-start | bytes 388
  22.3 34.2 %collective-permute-start.4 = (f32[1352,128]{1,0:T(8,128)S(1)}, f32[1352,128]{1,0:T(8,128)}, u32[]{:S(2)}, u32[]{:S(2)}) collective-permute-start(f32[1352,128]{1,0:T(8,128)S(1)} %level_pack.1.refs_2_), channel_id=1, source_target_pairs={{0,8},{4,12},{8,16},{12,20},{16,24},{20,28},{24,32},{28,36},{32,40... | collective-permute-start | bytes 2076680 | tf_op jit(solution)/shard_map/ppermute | solution.py:610
  24.2 32.3 %collective-permute-start.5 = (f32[1352,128]{1,0:T(8,128)S(1)}, f32[1352,128]{1,0:T(8,128)}, u32[]{:S(2)}, u32[]{:S(2)}) collective-permute-start(f32[1352,128]{1,0:T(8,128)S(1)} %level_pack.1.refs_2_), channel_id=1, source_target_pairs={{8,0},{12,4},{16,8},{20,12},{24,16},{28,20},{32,24},{36,28},{40,32... | collective-permute-start | bytes 2076680 | tf_op jit(solution)/shard_map/ppermute | solution.py:610
  30.3 0.8 copy-start.2
  31.1 0.8 copy-start.4
  31.9 1.0 copy-start.3
  32.9 1.0 copy-start.5
  36.3 9.8 %collective-permute-start.2 = (f32[64,128]{1,0:T(8,128)S(1)}, f32[64,128]{1,0:T(8,128)S(1)}, u32[]{:S(2)}, u32[]{:S(2)}) collective-permute-start(f32[64,128]{1,0:T(8,128)S(1)} %get-tuple-element.32.refs_2_), channel_id=1, source_target_pairs={{0,1},{1,2},{2,3},{3,4},{4,5},{5,6},{6,7},{7,8},{8,9},{9,10},{10,1... | collective-permute-start | bytes 98312 | tf_op jit(solution)/shard_map/ppermute | solution.py:610
  38.2 9.4 %collective-permute-start.3 = (f32[64,128]{1,0:T(8,128)S(1)}, f32[64,128]{1,0:T(8,128)S(1)}, u32[]{:S(2)}, u32[]{:S(2)}) collective-permute-start(f32[64,128]{1,0:T(8,128)S(1)} %get-tuple-element.32.refs_2_), channel_id=1, source_target_pairs={{1,0},{2,1},{3,2},{4,3},{5,4},{6,5},{7,6},{8,7},{9,8},{10,9},{11,1... | collective-permute-start | bytes 98312 | tf_op jit(solution)/shard_map/ppermute | solution.py:610
  48.5 26.8 %collective-permute-start.6 = (f32[1160,128]{1,0:T(8,128)}, f32[1160,128]{1,0:T(8,128)}, u32[]{:S(2)}, u32[]{:S(2)}) collective-permute-start(f32[1160,128]{1,0:T(8,128)} %slice.17), channel_id=1, source_target_pairs={{4,16},{12,24},{16,4},{20,32},{24,12},{28,40},{32,20},{36,48},{40,... | collective-permute-start | bytes 1781768 | tf_op jit(solution)/shard_map/ppermute | solution.py:661
  50.8 1.0 copy-start.6
  56.5 16.3 %all-to-all-start = ((f32[16,40,128]{2,1,0:T(8,128)}), f32[16,40,128]{2,1,0:T(8,128)S(1)}, u32[]{:S(2)}, u32[]{:S(2)}) async-start(f32[16,40,128]{2,1,0:T(8,128)} %get-tuple-element.43), calls=%async_computation | async-start | bytes 655360 | tf_op jit(solution)/shard_map/all_to_all | solution.py:601
  75.3 42.7 %all-to-all-start.1 = ((f32[32,32,128]{2,1,0:T(8,128)}), f32[32,32,128]{2,1,0:T(8,128)S(1)}, u32[]{:S(2)}, u32[]{:S(2)}) async-start(f32[32,32,128]{2,1,0:T(8,128)} %line_windows.1), calls=%async_computation.1 | async-start | bytes 1048576 | tf_op jit(solution)/shard_map/all_to_all | solution.py:605
  87.8 45.3 %collective-permute-start.7 = (f32[4120,128]{1,0:T(8,128)}, f32[4120,128]{1,0:T(8,128)}, u32[]{:S(2)}, u32[]{:S(2)}) collective-permute-start(f32[4120,128]{1,0:T(8,128)} %pad_maximum_fusion), channel_id=1, source_target_pairs={{0,4},{4,0},{8,12},{12,8},{16,20},{20,16},{24,28},{28,24},{32,36},... | collective-permute-start | bytes 6328328 | tf_op jit(solution)/shard_map/ppermute | solution.py:687
  118.1 0.7 copy-start.1
  118.8 14.3 %all-to-all-start.2 = ((f32[16,32,128]{2,1,0:T(8,128)}), f32[16,32,128]{2,1,0:T(8,128)S(1)}, u32[]{:S(2)}, u32[]{:S(2)}) async-start(f32[16,32,128]{2,1,0:T(8,128)} %copy-done.1), calls=%async_computation.2 | async-start | bytes 524288 | tf_op jit(solution)/shard_map/all_to_all | solution.py:601
  124.3 8.8 %collective-permute-start.8 = (f32[64,128]{1,0:T(8,128)S(1)}, f32[64,128]{1,0:T(8,128)S(1)}, u32[]{:S(2)}, u32[]{:S(2)}) collective-permute-start(f32[64,128]{1,0:T(8,128)S(1)} %slice.19), channel_id=1, source_target_pairs={{0,16},{8,24},{16,32},{20,4},{24,40},{28,12},{32,48},{36,20},{40,5... | collective-permute-start | bytes 98312 | tf_op jit(solution)/shard_map/ppermute | solution.py:661
  188.3 9.8 %collective-permute-start.9 = (f32[64,128]{1,0:T(8,128)S(1)}, f32[64,128]{1,0:T(8,128)S(1)}, u32[]{:S(2)}, u32[]{:S(2)}) collective-permute-start(f32[64,128]{1,0:T(8,128)S(1)} %fine_up.1.refs_1_), channel_id=1, source_target_pairs={{0,1},{1,2},{2,3},{3,4},{4,5},{5,6},{6,7},{7,8},{8,9},{9,10},{10,1... | collective-permute-start | bytes 98312 | tf_op jit(solution)/shard_map/ppermute | solution.py:610
  190.5 9.2 %collective-permute-start.10 = (f32[64,128]{1,0:T(8,128)S(1)}, f32[64,128]{1,0:T(8,128)S(1)}, u32[]{:S(2)}, u32[]{:S(2)}) collective-permute-start(f32[64,128]{1,0:T(8,128)S(1)} %fine_up.1.refs_1_), channel_id=1, source_target_pairs={{1,0},{2,1},{3,2},{4,3},{5,4},{6,5},{7,6},{8,7},{9,8},{10,9},{11,1... | collective-permute-start | bytes 98312 | tf_op jit(solution)/shard_map/ppermute | solution.py:610
  201.5 9.8 %collective-permute-start.11 = (f32[64,128]{1,0:T(8,128)S(1)}, f32[64,128]{1,0:T(8,128)S(1)}, u32[]{:S(2)}, u32[]{:S(2)}) collective-permute-start(f32[64,128]{1,0:T(8,128)S(1)} %get-tuple-element.55.refs_2_), channel_id=1, source_target_pairs={{0,1},{1,2},{2,3},{3,4},{4,5},{5,6},{6,7},{7,8},{8,9},{9,10},{10,1... | collective-permute-start | bytes 98312 | tf_op jit(solution)/shard_map/ppermute | solution.py:610
  203.5 9.5 %collective-permute-start.12 = (f32[64,128]{1,0:T(8,128)S(1)}, f32[64,128]{1,0:T(8,128)S(1)}, u32[]{:S(2)}, u32[]{:S(2)}) collective-permute-start(f32[64,128]{1,0:T(8,128)S(1)} %get-tuple-element.55.refs_2_), channel_id=1, source_target_pairs={{1,0},{2,1},{3,2},{4,3},{5,4},{6,5},{7,6},{8,7},{9,8},{10,9},{11,1... | collective-permute-start | bytes 98312 | tf_op jit(solution)/shard_map/ppermute | solution.py:610

commit v8 on v7

--- a/solution.py
+++ b/solution.py
@@ -253,7 +253,7 @@
     return v
 
 
-def payload(x, b, columns):
+def payload(x, b, columns, blocks):
     lines = []
     for k in range(3):
         values = [None] * R0
@@ -262,7 +262,8 @@
             values[FINE_ORDER[i]] = (g >> 4) * 16 + (g & 1) * 8 + ((g & 15) >> 1)
         lines.append(repeated(lanes_of(values), 64))
     v = jnp.concatenate(lines + [jnp.zeros((5, 128), I32)], axis=0).astype(F32)
-    return (jnp.concatenate([jnp.concatenate([x, b], axis=0), v, jnp.zeros((8, 2944), F32)], axis=1),)
+    v = jnp.concatenate([jnp.concatenate([x, b], axis=0), v, jnp.zeros((8, 2944), F32)], axis=1)[None]
+    return [v[0]] + [jnp.concatenate([part, v], axis=0) for part in (blocks[:, :8], blocks[:, 8:])]
 
 
 def restrict(dest, residual, p_hi, p_lo):
@@ -641,9 +642,10 @@
     device = (slab * XN + sub).reshape(1, 1)
     place = jnp.stack([slab, sub]).reshape(1, 2)
 
-    (own,) = kern(payload, [((8, 4096), F32)], [warm_start, right_side, fine_columns], smem=(2,))
     blocks = fine_blocks.transpose(1, 0, 2)
-    low, high = (jnp.concatenate([part, own[None]], axis=0) for part in (blocks[:, :8], blocks[:, 8:]))
+    own, low, high = kern(
+        payload, [((8, 4096), F32)] + [((4, 8, 4096), F32)] * 2, [warm_start, right_side, fine_columns, blocks], smem=(2,)
+    )
     middle_columns, low, high = lax.optimization_barrier((middle_columns, low, high))
     left, right = shifted(high, both, 1), shifted(low, both, -1)
 
@@ -673,6 +675,7 @@
     left, right = shifted(send, both, 1), shifted(send, both, -1)
     left, right, pack = lax.optimization_barrier((left, right, pack))
     crossed = crossing(pack[:A2_AT], 3)
+    far = crossing(pack[D1_AT : D1_AT + 64], 4)
     x3, dense = kern(
         fine_down,
         [((64, 64), F32), ((16, 40, 128), F32)],
@@ -682,10 +685,9 @@
 
     dense, m2, p2 = lax.optimization_barrier((dense, m2, p2))
     (part,) = kern(line_windows, [((TN_, 32, 128), F32)], [place, across(dense)], smem=(0,))
-    part, m2, p2, crossed, pack = lax.optimization_barrier((part, m2, p2, crossed, pack))
+    part, m2, p2, crossed, far, pack = lax.optimization_barrier((part, m2, p2, crossed, far, pack))
     twin = jnp.concatenate([pack, m2, p2, crossed[D1_AT : D1_AT + 64]], axis=0)
     twin = lax.ppermute(twin, "slab", [(i, i ^ 1) for i in range(count)])
-    far = crossing(pack[D1_AT : D1_AT + 64], 4)
     (part,) = kern(sum_all, [((XN * YN, 32, 128), F32)], [along(part)])
     part = across(part)
 

time: 217 us -> 216 us (level)
  starting transfers between devices: 82.2 us -> 78.1 us
  local copies, waits for them, and re-layouts: 11.2 us -> 15.2 us
  blocking collectives: 38.5 us -> 36.2 us
    ppermute x2, waiting for transfers between devices: 6.68 us -> 0.01 us  [crossing(): return lax.ppermute(value, 'slab', [p for p in pairs if 0 <= p[1] < count])]
    all_to_all x2, starting transfers between devices: 14.7 us -> 9 us  [across(): lax.all_to_all(value, ('slab', 'sub'), 0, 0, tiled=True, axis_index_group...]
    all_to_all x2, waiting for transfers between devices: 6.95 us -> 12.1 us  [across(): lax.all_to_all(value, ('slab', 'sub'), 0, 0, tiled=True, axis_index_group...]
    unnamed x35, local copies, waits for them, and re-layouts: 7.87 us -> 12.4 us
    ppermute x10, waiting for transfers between devices: 4.71 us -> 8.14 us  [shifted(): lax.ppermute(value, axis, [(i, i + by) for i in range(n) if 0 <= i + by <...]
    all_to_all x1, blocking collectives: 21.2 us -> 18.9 us  [across(): lax.all_to_all(value, ('slab', 'sub'), 0, 0, tiled=True, axis_index_group...]
  transfers between devices with their start and end apart: 16 -> 16, of which waited for: 6 -> 6; matrix products, arithmetic and copies ran while one was open for 2% -> 3% of each run, Pallas kernels for 5% -> 5%
where the time goes in v8:
time: 216 us; the launch traced here: 215 us
  starting transfers between devices  78.1 us (36%)
  waiting for transfers between devices  48.3 us (22%)
  blocking collectives  36.2 us (17%)
  Pallas kernels  33.5 us (16%)
  local copies, waits for them, and re-layouts  15.2 us (7%)
  other arithmetic  2.89 us (1%)
    ppermute x10, starting transfers between devices, shifted(): lax.ppermute(value, axis, [(i, i + by) for i in range(n) if 0 <= i + by <...  52.1 us
    pallas_call x10, Pallas kernels, kern(): pl.pallas_call(kernel, in_specs=specs, out_specs=[pl.BlockSpec() if own_o...  32 us
    all_to_all x1, waiting for transfers between devices, along(): return lax.all_to_all(value, 'slab', 0, 0, tiled=True, axis_index_groups=ZC)  28 us
    all_to_all x1, blocking collectives, across(): lax.all_to_all(value, ('slab', 'sub'), 0, 0, tiled=True, axis_index_group...  18.9 us
    all_to_all x1, blocking collectives, along(): return lax.all_to_all(value, 'slab', 0, 0, tiled=True, axis_index_groups=ZC)  17.3 us
    unnamed x35, local copies, waits for them, and re-layouts  12.4 us
    all_to_all x2, waiting for transfers between devices, across(): lax.all_to_all(value, ('slab', 'sub'), 0, 0, tiled=True, axis_index_group...  12.1 us
    all_to_all x1, starting transfers between devices, along(): return lax.all_to_all(value, 'slab', 0, 0, tiled=True, axis_index_groups=ZC)  11 us
  transfers between devices with their start and end apart: 16, of which 6 were waited for; matrix products, arithmetic and copies ran while one was open for 3% of the time, Pallas kernels for 5%

profile of v8, /device:TPU:8, one launch (start us, length us, event | category | flops | bytes accessed | tf_op | source)
XLA Modules:
  0.0 215.0 jit_solution(13982382941915020636)
XLA Ops:
  4.0 1.9 payload.1
  5.8 3.4 %collective-permute-start = (f32[4,8,4096]{2,1,0:T(8,128)}, f32[4,8,4096]{2,1,0:T(8,128)S(1)}, u32[]{:S(2)}, u32[]{:S(2)}) collective-permute-start(f32[4,8,4096]{2,1,0:T(8,128)} %get-tuple-element.36), channel_id=1, source_target_pairs={{0,1},{1,2},{2,3},{3,4},{4,5},{5,6},{6,7},{7,8},{8,9},{9,10},{10,1... | collective-permute-start | bytes 1572872 | tf_op jit(solution)/shard_map/ppermute | solution.py:611
  9.2 11.4 %collective-permute-start.1 = (f32[4,8,4096]{2,1,0:T(8,128)}, f32[4,8,4096]{2,1,0:T(8,128)S(1)}, u32[]{:S(2)}, u32[]{:S(2)}) collective-permute-start(f32[4,8,4096]{2,1,0:T(8,128)} %get-tuple-element.37), channel_id=1, source_target_pairs={{1,0},{2,1},{3,2},{4,3},{5,4},{6,5},{7,6},{8,7},{9,8},{10,9},{11,1... | collective-permute-start | bytes 1572872 | tf_op jit(solution)/shard_map/ppermute | solution.py:611
  26.2 1.9 collective-permute-start.4
  28.1 6.0 %collective-permute-start.5 = (f32[1352,128]{1,0:T(8,128)S(1)}, f32[1352,128]{1,0:T(8,128)}, u32[]{:S(2)}, u32[]{:S(2)}) collective-permute-start(f32[1352,128]{1,0:T(8,128)S(1)} %level_pack.1.refs_2_), channel_id=1, source_target_pairs={{8,0},{12,4},{16,8},{20,12},{24,16},{28,20},{32,24},{36,28},{40,32... | collective-permute-start | bytes 2076680 | tf_op jit(solution)/shard_map/ppermute | solution.py:611
  37.9 2.3 %fine_start.1 = (bf16[2,3,512,128]{3,2,1,0:T(8,128)(2,1)S(1)}, bf16[2,3,512,128]{3,2,1,0:T(8,128)(2,1)S(1)}, f32[64,128]{1,0:T(8,128)S(1)}, f32[64,128]{1,0:T(8,...) custom-call(s32[1,1]{1,0:T(1,128)} %bitcast.refs_0_, ...), custom_call_target="tpu_custom_call" | custom-call | tf_op jit(solution)/shard_map/fine_start/pallas_call | solution.py:51
  40.2 1.9 collective-permute-start.2
  42.1 7.9 %collective-permute-start.3 = (f32[64,128]{1,0:T(8,128)S(1)}, f32[64,128]{1,0:T(8,128)S(1)}, u32[]{:S(2)}, u32[]{:S(2)}) collective-permute-start(f32[64,128]{1,0:T(8,128)S(1)} %get-tuple-element.39.refs_2_), channel_id=1, source_target_pairs={{1,0},{2,1},{3,2},{4,3},{5,4},{6,5},{7,6},{8,7},{9,8},{10,9},{11,1... | collective-permute-start | bytes 98312 | tf_op jit(solution)/shard_map/ppermute | solution.py:611
  50.0 5.0 %collective-permute-done.3.refs_4_ = f32[64,128]{1,0:T(8,128)S(1)} collective-permute-done((f32[64,128]{1,0:T(8,128)S(1)}, f32[64,128]{1,0:T(8,128)S(1)}, u32[]{:S(2)}, u32[]{:S(2)}) %collective-permute-start.3) | collective-permute-done | bytes 32800 | tf_op jit(solution)/shard_map/ppermute | solution.py:611
  55.8 1.9 collective-permute-start.6
  59.2 4.4 %fine_down.1 = (f32[64,64]{1,0:T(8,128)S(1)}, f32[16,40,128]{2,1,0:T(8,128)}) custom-call(s32[1,1]{1,0:T(1,128)} %bitcast.refs_0_, f32[64,64]{1,0:T(8,128)S(1)} %get-tuple-element.38.refs_1_, f32[64,128]{1,0:T(8,128)S(1)} %get-tuple-element.39.refs_2_, f32[64,128]{1,0:T(8,128)S(1)} %collective-permute-done.2.refs_3_, ...), custom_call_target="tpu_custom_call" | custom-call | tf_op jit(solution)/shard_map/fine_down/pallas_call | solution.py:51
  63.6 3.4 %all-to-all-start = ((f32[16,40,128]{2,1,0:T(8,128)}), f32[16,40,128]{2,1,0:T(8,128)S(1)}, u32[]{:S(2)}, u32[]{:S(2)}) async-start(f32[16,40,128]{2,1,0:T(8,128)} %get-tuple-element.50), calls=%async_computation | async-start | bytes 655360 | tf_op jit(solution)/shard_map/all_to_all | solution.py:602
  67.0 1.9 collective-permute-start.7
  69.1 4.9 %all-to-all-done.refs_1_ = f32[16,40,128]{2,1,0:T(8,128)S(1)} async-done(((f32[16,40,128]{2,1,0:T(8,128)}), f32[16,40,128]{2,1,0:T(8,128)S(1)}, u32[]{:S(2)}, u32[]{:S(2)}) %all-to-all-start) | async-done | bytes 327712 | tf_op jit(solution)/shard_map/all_to_all | solution.py:602
  73.9 2.6 %line_windows.1 = f32[32,32,128]{2,1,0:T(8,128)} custom-call(s32[1,2]{1,0:T(1,128)S(1)} %add_bitcast_fusion.refs_0_, f32[16,40,128]{2,1,0:T(8,128)S(1)} %all-to-all-done.refs_1_), custom_call_target="tpu_custom_call" | custom-call | tf_op jit(solution)/shard_map/line_windows/pallas_call | solution.py:51
  76.5 11.0 %all-to-all-start.1 = ((f32[32,32,128]{2,1,0:T(8,128)}), f32[32,32,128]{2,1,0:T(8,128)S(1)}, u32[]{:S(2)}, u32[]{:S(2)}) async-start(f32[32,32,128]{2,1,0:T(8,128)} %line_windows.1), calls=%async_computation.1 | async-start | bytes 1048576 | tf_op jit(solution)/shard_map/all_to_all | solution.py:606
  88.2 2.8 %pad_maximum_fusion = f32[4120,128]{1,0:T(8,128)} fusion(f32[64,128]{1,0:T(8,128)S(1)} %slice.11, f32[1352,128]{1,0:T(8,128)} %collective-permute-done.5.refs_4_, f32[1352,128]{1,0:T(8,128)} %collective-permute-done.4.refs_3_, f32[1352,128]{1,0:T(8,128)S(1)} %level_pack.1.refs_2_), kind=kLoop, calls=%fused_computation | loop fusion | flops 1582080 | bytes 4218880 | tf_op jit(solution)/shard_map/concatenate | solution.py:689
  91.0 2.2 %collective-permute-start.8 = (f32[4120,128]{1,0:T(8,128)}, f32[4120,128]{1,0:T(8,128)}, u32[]{:S(2)}, u32[]{:S(2)}) collective-permute-start(f32[4120,128]{1,0:T(8,128)} %pad_maximum_fusion), channel_id=1, source_target_pairs={{0,4},{4,0},{8,12},{12,8},{16,20},{20,16},{24,28},{28,24},{32,36},... | collective-permute-start | bytes 6328328 | tf_op jit(solution)/shard_map/ppermute | solution.py:690
  93.2 28.0 %all-to-all-done.1.refs_0_ = f32[32,32,128]{2,1,0:T(8,128)S(1)} async-done(((f32[32,32,128]{2,1,0:T(8,128)}), f32[32,32,128]{2,1,0:T(8,128)S(1)}, u32[]{:S(2)}, u32[]{:S(2)}) %all-to-all-start.1) | async-done | bytes 524320 | tf_op jit(solution)/shard_map/all_to_all | solution.py:606
  122.0 5.6 %all-to-all-start.2 = ((f32[16,32,128]{2,1,0:T(8,128)}), f32[16,32,128]{2,1,0:T(8,128)S(1)}, u32[]{:S(2)}, u32[]{:S(2)}) async-start(f32[16,32,128]{2,1,0:T(8,128)} %copy-done.2), calls=%async_computation.2 | async-start | bytes 524288 | tf_op jit(solution)/shard_map/all_to_all | solution.py:602
  127.6 7.2 %all-to-all-done.2.refs_1_ = f32[16,32,128]{2,1,0:T(8,128)S(1)} async-done(((f32[16,32,128]{2,1,0:T(8,128)}), f32[16,32,128]{2,1,0:T(8,128)S(1)}, u32[]{:S(2)}, u32[]{:S(2)}) %all-to-all-start.2) | async-done | bytes 262176 | tf_op jit(solution)/shard_map/all_to_all | solution.py:602
  134.8 14.9 %level_cycle.1 = f32[32,2,256]{2,1,0:T(2,128)S(1)} custom-call(s32[1,2]{1,0:T(1,128)S(1)} %add_bitcast_fusion.refs_0_, f32[16,32,128]{2,1,0:T(8,128)S(1)} %all-to-all-done.2.refs_1_, f32[1352,128]{1,0:T(8,128)S(1)} %level_pack.1.refs_2_, f32[1352,128]{1,0:T(8,128)} %collective-permute-done.4.refs_3_, f32[1352,128]{1,0:T(8,128)} %collective-permute-done.5.refs_4_, ...), custom_call_target="tpu_custom_call" | custom-call | tf_op jit(solution)/shard_map/level_cycle/pallas_call | solution.py:51
  149.7 17.3 %all_to_all.25 = f32[32,2,256]{2,1,0:T(2,128)S(1)} all-to-all(f32[32,2,256]{2,1,0:T(2,128)S(1)} %level_cycle.1), channel_id=1, replica_groups={{0,4,8,12,16,20,24,28,32,36,40,44,48,52,56,60,64,68,72,76,80,84,88,92,9..., dimensions={0} | all-to-all | bytes 131072 | tf_op jit(solution)/shard_map/all_to_all | solution.py:606
  167.4 18.9 %all_to_all.26 = f32[16,32,2,256]{3,2,1,0:T(2,128)S(1)} all-to-all(f32[16,32,2,256]{3,2,1,0:T(2,128)S(1)} %broadcast_in_dim.4), channel_id=1, replica_groups={{0,1,2,3,128,129,130,131,256,257,258,259,384,385,386,387},{4,5,6,7,132,..., dimensions={0} | all-to-all | bytes 2097152 | tf_op jit(solution)/shard_map/all_to_all | solution.py:602
  187.8 2.2 %collective-permute-start.9 = (f32[64,128]{1,0:T(8,128)S(1)}, f32[64,128]{1,0:T(8,128)S(1)}, u32[]{:S(2)}, u32[]{:S(2)}) collective-permute-start(f32[64,128]{1,0:T(8,128)S(1)} %fine_up.1.refs_1_), channel_id=1, source_target_pairs={{0,1},{1,2},{2,3},{3,4},{4,5},{5,6},{6,7},{7,8},{8,9},{9,10},{10,1... | collective-permute-start | bytes 98312 | tf_op jit(solution)/shard_map/ppermute | solution.py:611
  189.9 7.6 %collective-permute-start.10 = (f32[64,128]{1,0:T(8,128)S(1)}, f32[64,128]{1,0:T(8,128)S(1)}, u32[]{:S(2)}, u32[]{:S(2)}) collective-permute-start(f32[64,128]{1,0:T(8,128)S(1)} %fine_up.1.refs_1_), channel_id=1, source_target_pairs={{1,0},{2,1},{3,2},{4,3},{5,4},{6,5},{7,6},{8,7},{9,8},{10,9},{11,1... | collective-permute-start | bytes 98312 | tf_op jit(solution)/shard_map/ppermute | solution.py:611
  197.6 1.6 collective-permute-done.10.refs_3_
  199.1 1.9 fine_middle.1
  201.0 1.9 collective-permute-start.11
  202.9 7.9 %collective-permute-start.12 = (f32[64,128]{1,0:T(8,128)S(1)}, f32[64,128]{1,0:T(8,128)S(1)}, u32[]{:S(2)}, u32[]{:S(2)}) collective-permute-start(f32[64,128]{1,0:T(8,128)S(1)} %get-tuple-element.63.refs_2_), channel_id=1, source_target_pairs={{1,0},{2,1},{3,2},{4,3},{5,4},{6,5},{7,6},{8,7},{9,8},{10,9},{11,1... | collective-permute-start | bytes 98312 | tf_op jit(solution)/shard_map/ppermute | solution.py:611
  210.8 1.6 collective-permute-done.12.refs_4_
  212.4 2.6 %fine_end.1 = (f32[4,1024]{1,0:T(4,128)}, f32[4,1024]{1,0:T(4,128)}) custom-call(s32[1,1]{1,0:T(1,128)} %bitcast.refs_0_, f32[64,64]{1,0:T(8,128)S(1)} %get-tuple-element.62.refs_1_, f32[64,128]{1,0:T(8,128)S(1)} %get-tuple-element.63.refs_2_, f32[64,128]{1,0:T(8,128)S(1)} %collective-permute-done.11.refs_3_, f32[64,128]{1,0:T(8,128)S(1)} %collective-permute-done.12.refs_4_, ...), custom_call_target="tpu_custom_call" | custom-call | tf_op jit(solution)/shard_map/fine_end/pallas_call | solution.py:51
  (56 shorter events, 18.3 us)
Async XLA Ops:
  1.4 1.1 copy-start
  2.5 0.7 copy-start.11
  3.2 0.7 copy-start.12
  4.0 31.8 %copy-start.1 = (f32[16,3,4096]{2,0,1:T(8,128)S(1)}, f32[16,3,4096]{2,0,1:T(8,128)}, u32[]{:S(2)}) copy-start(f32[16,3,4096]{2,0,1:T(8,128)} %param.15) | copy-start | bytes 2359300
  5.8 28.3 %collective-permute-start = (f32[4,8,4096]{2,1,0:T(8,128)}, f32[4,8,4096]{2,1,0:T(8,128)S(1)}, u32[]{:S(2)}, u32[]{:S(2)}) collective-permute-start(f32[4,8,4096]{2,1,0:T(8,128)} %get-tuple-element.36), channel_id=1, source_target_pairs={{0,1},{1,2},{2,3},{3,4},{4,5},{5,6},{6,7},{7,8},{8,9},{9,10},{10,1... | collective-permute-start | bytes 1572872 | tf_op jit(solution)/shard_map/ppermute | solution.py:611
  9.2 25.8 %collective-permute-start.1 = (f32[4,8,4096]{2,1,0:T(8,128)}, f32[4,8,4096]{2,1,0:T(8,128)S(1)}, u32[]{:S(2)}, u32[]{:S(2)}) collective-permute-start(f32[4,8,4096]{2,1,0:T(8,128)} %get-tuple-element.37), channel_id=1, source_target_pairs={{1,0},{2,1},{3,2},{4,3},{5,4},{6,5},{7,6},{8,7},{9,8},{10,9},{11,1... | collective-permute-start | bytes 1572872 | tf_op jit(solution)/shard_map/ppermute | solution.py:611
  21.4 1.0 copy-start.8
  22.4 0.9 copy-start.9
  23.3 0.9 copy-start.10
  24.2 0.7 copy-start.13
  24.9 32.8 %copy-start.14 = (s32[16,2]{0,1:T(2,128)S(1)}, s32[16,2]{0,1:T(2,128)}, u32[]{:S(2)}) copy-start(s32[16,2]{0,1:T(2,128)} %param.18) | copy-start | bytes 388
  24.9 32.9 %copy-start.15 = (s32[16,2]{0,1:T(2,128)S(1)}, s32[16,2]{0,1:T(2,128)}, u32[]{:S(2)}) copy-start(s32[16,2]{0,1:T(2,128)} %param.19) | copy-start | bytes 388
  26.2 37.4 %collective-permute-start.4 = (f32[1352,128]{1,0:T(8,128)S(1)}, f32[1352,128]{1,0:T(8,128)}, u32[]{:S(2)}, u32[]{:S(2)}) collective-permute-start(f32[1352,128]{1,0:T(8,128)S(1)} %level_pack.1.refs_2_), channel_id=1, source_target_pairs={{0,8},{4,12},{8,16},{12,20},{16,24},{20,28},{24,32},{28,36},{32,40... | collective-permute-start | bytes 2076680 | tf_op jit(solution)/shard_map/ppermute | solution.py:611
  28.1 35.5 %collective-permute-start.5 = (f32[1352,128]{1,0:T(8,128)S(1)}, f32[1352,128]{1,0:T(8,128)}, u32[]{:S(2)}, u32[]{:S(2)}) collective-permute-start(f32[1352,128]{1,0:T(8,128)S(1)} %level_pack.1.refs_2_), channel_id=1, source_target_pairs={{8,0},{12,4},{16,8},{20,12},{24,16},{28,20},{32,24},{36,28},{40,32... | collective-permute-start | bytes 2076680 | tf_op jit(solution)/shard_map/ppermute | solution.py:611
  34.2 0.8 copy-start.3
  35.0 0.8 copy-start.5
  35.8 1.0 copy-start.4
  36.8 1.0 copy-start.6
  40.2 9.8 %collective-permute-start.2 = (f32[64,128]{1,0:T(8,128)S(1)}, f32[64,128]{1,0:T(8,128)S(1)}, u32[]{:S(2)}, u32[]{:S(2)}) collective-permute-start(f32[64,128]{1,0:T(8,128)S(1)} %get-tuple-element.39.refs_2_), channel_id=1, source_target_pairs={{0,1},{1,2},{2,3},{3,4},{4,5},{5,6},{6,7},{7,8},{8,9},{9,10},{10,1... | collective-permute-start | bytes 98312 | tf_op jit(solution)/shard_map/ppermute | solution.py:611
  42.1 12.9 %collective-permute-start.3 = (f32[64,128]{1,0:T(8,128)S(1)}, f32[64,128]{1,0:T(8,128)S(1)}, u32[]{:S(2)}, u32[]{:S(2)}) collective-permute-start(f32[64,128]{1,0:T(8,128)S(1)} %get-tuple-element.39.refs_2_), channel_id=1, source_target_pairs={{1,0},{2,1},{3,2},{4,3},{5,4},{6,5},{7,6},{8,7},{9,8},{10,9},{11,1... | collective-permute-start | bytes 98312 | tf_op jit(solution)/shard_map/ppermute | solution.py:611
  55.8 20.7 %collective-permute-start.6 = (f32[1160,128]{1,0:T(8,128)}, f32[1160,128]{1,0:T(8,128)}, u32[]{:S(2)}, u32[]{:S(2)}) collective-permute-start(f32[1160,128]{1,0:T(8,128)} %slice.9), channel_id=1, source_target_pairs={{4,16},{12,24},{16,4},{20,32},{24,12},{28,40},{32,20},{36,48},{40,... | collective-permute-start | bytes 1781768 | tf_op jit(solution)/shard_map/ppermute | solution.py:663
  57.9 1.0 copy-start.7
  63.6 10.3 %all-to-all-start = ((f32[16,40,128]{2,1,0:T(8,128)}), f32[16,40,128]{2,1,0:T(8,128)S(1)}, u32[]{:S(2)}, u32[]{:S(2)}) async-start(f32[16,40,128]{2,1,0:T(8,128)} %get-tuple-element.50), calls=%async_computation | async-start | bytes 655360 | tf_op jit(solution)/shard_map/all_to_all | solution.py:602
  67.0 9.4 %collective-permute-start.7 = (f32[64,128]{1,0:T(8,128)S(1)}, f32[64,128]{1,0:T(8,128)S(1)}, u32[]{:S(2)}, u32[]{:S(2)}) collective-permute-start(f32[64,128]{1,0:T(8,128)S(1)} %slice.10), channel_id=1, source_target_pairs={{0,16},{8,24},{16,32},{20,4},{24,40},{28,12},{32,48},{36,20},{40,5... | collective-permute-start | bytes 98312 | tf_op jit(solution)/shard_map/ppermute | solution.py:663
  76.5 44.7 %all-to-all-start.1 = ((f32[32,32,128]{2,1,0:T(8,128)}), f32[32,32,128]{2,1,0:T(8,128)S(1)}, u32[]{:S(2)}, u32[]{:S(2)}) async-start(f32[32,32,128]{2,1,0:T(8,128)} %line_windows.1), calls=%async_computation.1 | async-start | bytes 1048576 | tf_op jit(solution)/shard_map/all_to_all | solution.py:606
  91.0 36.6 %collective-permute-start.8 = (f32[4120,128]{1,0:T(8,128)}, f32[4120,128]{1,0:T(8,128)}, u32[]{:S(2)}, u32[]{:S(2)}) collective-permute-start(f32[4120,128]{1,0:T(8,128)} %pad_maximum_fusion), channel_id=1, source_target_pairs={{0,4},{4,0},{8,12},{12,8},{16,20},{20,16},{24,28},{28,24},{32,36},... | collective-permute-start | bytes 6328328 | tf_op jit(solution)/shard_map/ppermute | solution.py:690
  121.3 0.7 copy-start.2
  122.0 12.8 %all-to-all-start.2 = ((f32[16,32,128]{2,1,0:T(8,128)}), f32[16,32,128]{2,1,0:T(8,128)S(1)}, u32[]{:S(2)}, u32[]{:S(2)}) async-start(f32[16,32,128]{2,1,0:T(8,128)} %copy-done.2), calls=%async_computation.2 | async-start | bytes 524288 | tf_op jit(solution)/shard_map/all_to_all | solution.py:602
  187.8 9.8 %collective-permute-start.9 = (f32[64,128]{1,0:T(8,128)S(1)}, f32[64,128]{1,0:T(8,128)S(1)}, u32[]{:S(2)}, u32[]{:S(2)}) collective-permute-start(f32[64,128]{1,0:T(8,128)S(1)} %fine_up.1.refs_1_), channel_id=1, source_target_pairs={{0,1},{1,2},{2,3},{3,4},{4,5},{5,6},{6,7},{7,8},{8,9},{9,10},{10,1... | collective-permute-start | bytes 98312 | tf_op jit(solution)/shard_map/ppermute | solution.py:611
  189.9 9.2 %collective-permute-start.10 = (f32[64,128]{1,0:T(8,128)S(1)}, f32[64,128]{1,0:T(8,128)S(1)}, u32[]{:S(2)}, u32[]{:S(2)}) collective-permute-start(f32[64,128]{1,0:T(8,128)S(1)} %fine_up.1.refs_1_), channel_id=1, source_target_pairs={{1,0},{2,1},{3,2},{4,3},{5,4},{6,5},{7,6},{8,7},{9,8},{10,9},{11,1... | collective-permute-start | bytes 98312 | tf_op jit(solution)/shard_map/ppermute | solution.py:611
  201.0 9.8 %collective-permute-start.11 = (f32[64,128]{1,0:T(8,128)S(1)}, f32[64,128]{1,0:T(8,128)S(1)}, u32[]{:S(2)}, u32[]{:S(2)}) collective-permute-start(f32[64,128]{1,0:T(8,128)S(1)} %get-tuple-element.63.refs_2_), channel_id=1, source_target_pairs={{0,1},{1,2},{2,3},{3,4},{4,5},{5,6},{6,7},{7,8},{8,9},{9,10},{10,1... | collective-permute-start | bytes 98312 | tf_op jit(solution)/shard_map/ppermute | solution.py:611
  202.9 9.5 %collective-permute-start.12 = (f32[64,128]{1,0:T(8,128)S(1)}, f32[64,128]{1,0:T(8,128)S(1)}, u32[]{:S(2)}, u32[]{:S(2)}) collective-permute-start(f32[64,128]{1,0:T(8,128)S(1)} %get-tuple-element.63.refs_2_), channel_id=1, source_target_pairs={{1,0},{2,1},{3,2},{4,3},{5,4},{6,5},{7,6},{8,7},{9,8},{10,9},{11,1... | collective-permute-start | bytes 98312 | tf_op jit(solution)/shard_map/ppermute | solution.py:611

commit v9 on v8

--- a/solution.py
+++ b/solution.py
@@ -377,7 +377,7 @@
     d1 = 1.0 / diagonal_plain(jnp.concatenate([a1[0], pad], axis=0))[:, :32]
     pad = jnp.zeros((448, 128), F32)
     d2 = 1.0 / diagonal_plain(jnp.concatenate([a2[0], pad], axis=0))[:, :8]
-    return (
+    full = (
         jnp.concatenate(
             a1
             + [tiles(prolong)]
@@ -385,7 +385,8 @@
             + a2,
             axis=0,
         ),
-    )
+    )[0]
+    return full, full[:A2_AT]
 
 
 def diagonal_plain(m):
@@ -649,9 +650,9 @@
     middle_columns, low, high = lax.optimization_barrier((middle_columns, low, high))
     left, right = shifted(high, both, 1), shifted(low, both, -1)
 
-    (pack,) = kern(
+    pack, short = kern(
         level_pack,
-        [((PACK_ROWS, 128), F32)],
+        [((PACK_ROWS, 128), F32), ((A2_AT, 128), F32)],
         [middle_blocks.transpose(1, 0, 2), middle_prolong, coarse_blocks.transpose(1, 0, 2), middle_columns, coarse_columns],
         smem=(3, 4),
     )
@@ -673,8 +674,8 @@
         own=range(1, 5),
     )
     left, right = shifted(send, both, 1), shifted(send, both, -1)
-    left, right, pack = lax.optimization_barrier((left, right, pack))
-    crossed = crossing(pack[:A2_AT], 3)
+    left, right, pack, short = lax.optimization_barrier((left, right, pack, short))
+    crossed = crossing(short, 3)
     far = crossing(pack[D1_AT : D1_AT + 64], 4)
     x3, dense = kern(
         fine_down,

time: 216 us -> 222 us (1.028)
  local copies, waits for them, and re-layouts: 15.2 us -> 22.1 us
    unnamed x35 -> x67, local copies, waits for them, and re-layouts: 12.4 us -> 20.2 us
  transfers between devices with their start and end apart: 16 -> 16, of which waited for: 6 -> 6; matrix products, arithmetic and copies ran while one was open for 3% -> 2% of each run, Pallas kernels for 5% -> 5%
where the time goes in v9:
time: 222 us; the launch traced here: 221 us
  starting transfers between devices  78.7 us (35%)
  waiting for transfers between devices  47.2 us (21%)
  blocking collectives  36.3 us (16%)
  Pallas kernels  32.5 us (15%)
  local copies, waits for them, and re-layouts  22.1 us (10%)
  other arithmetic  2.7 us (1%)
    ppermute x10, starting transfers between devices, shifted(): lax.ppermute(value, axis, [(i, i + by) for i in range(n) if 0 <= i + by <...  52.1 us
    pallas_call x10, Pallas kernels, kern(): pl.pallas_call(kernel, in_specs=specs, out_specs=[pl.BlockSpec() if own_o...  31.1 us
    all_to_all x1, waiting for transfers between devices, along(): return lax.all_to_all(value, 'slab', 0, 0, tiled=True, axis_index_groups=ZC)  28.2 us
    unnamed x67, local copies, waits for them, and re-layouts  20.2 us
    all_to_all x1, blocking collectives, across(): lax.all_to_all(value, ('slab', 'sub'), 0, 0, tiled=True, axis_index_group...  18.9 us
    all_to_all x1, blocking collectives, along(): return lax.all_to_all(value, 'slab', 0, 0, tiled=True, axis_index_groups=ZC)  17.4 us
    all_to_all x2, waiting for transfers between devices, across(): lax.all_to_all(value, ('slab', 'sub'), 0, 0, tiled=True, axis_index_group...  12.2 us
    all_to_all x1, starting transfers between devices, along(): return lax.all_to_all(value, 'slab', 0, 0, tiled=True, axis_index_groups=ZC)  11.4 us
  transfers between devices with their start and end apart: 16, of which 6 were waited for; matrix products, arithmetic and copies ran while one was open for 2% of the time, Pallas kernels for 5%

profile of v9, /device:TPU:8, one launch (start us, length us, event | category | flops | bytes accessed | tf_op | source)
XLA Modules:
  0.0 220.6 jit_solution(2082911633002297836)
XLA Ops:
  4.0 1.8 payload.1
  6.5 3.4 %collective-permute-start = (f32[4,8,4096]{2,1,0:T(8,128)}, f32[4,8,4096]{2,1,0:T(8,128)S(1)}, u32[]{:S(2)}, u32[]{:S(2)}) collective-permute-start(f32[4,8,4096]{2,1,0:T(8,128)} %get-tuple-element.39), channel_id=1, source_target_pairs={{0,1},{1,2},{2,3},{3,4},{4,5},{5,6},{6,7},{7,8},{8,9},{9,10},{10,1... | collective-permute-start | bytes 1572872 | tf_op jit(solution)/shard_map/ppermute | solution.py:612
  9.9 11.4 %collective-permute-start.1 = (f32[4,8,4096]{2,1,0:T(8,128)}, f32[4,8,4096]{2,1,0:T(8,128)S(1)}, u32[]{:S(2)}, u32[]{:S(2)}) collective-permute-start(f32[4,8,4096]{2,1,0:T(8,128)} %get-tuple-element.40), channel_id=1, source_target_pairs={{1,0},{2,1},{3,2},{4,3},{5,4},{6,5},{7,6},{8,7},{9,8},{10,9},{11,1... | collective-permute-start | bytes 1572872 | tf_op jit(solution)/shard_map/ppermute | solution.py:612
  27.6 1.9 collective-permute-start.4
  29.6 6.0 %collective-permute-start.5 = (f32[1352,128]{1,0:T(8,128)S(1)}, f32[1352,128]{1,0:T(8,128)}, u32[]{:S(2)}, u32[]{:S(2)}) collective-permute-start(f32[1352,128]{1,0:T(8,128)S(1)} %get-tuple-element.61.refs_2_), channel_id=1, source_target_pairs={{8,0},{12,4},{16,8},{20,12},{24,16},{28,20},{32,24},{36,28},{40,32... | collective-permute-start | bytes 2076680 | tf_op jit(solution)/shard_map/ppermute | solution.py:612
  39.5 2.3 %fine_start.1 = (bf16[2,3,512,128]{3,2,1,0:T(8,128)(2,1)S(1)}, bf16[2,3,512,128]{3,2,1,0:T(8,128)(2,1)S(1)}, f32[64,128]{1,0:T(8,128)S(1)}, f32[64,128]{1,0:T(8,...) custom-call(s32[1,1]{1,0:T(1,128)} %bitcast.refs_0_, f32[8,4096]{1,0:T(8,128)S(1)} %copy-done.14, ...), custom_call_target="tpu_custom_call" | custom-call | tf_op jit(solution)/shard_map/fine_start/pallas_call | solution.py:51
  43.1 1.9 collective-permute-start.2
  45.0 7.9 %collective-permute-start.3 = (f32[64,128]{1,0:T(8,128)S(1)}, f32[64,128]{1,0:T(8,128)S(1)}, u32[]{:S(2)}, u32[]{:S(2)}) collective-permute-start(f32[64,128]{1,0:T(8,128)S(1)} %get-tuple-element.42.refs_2_), channel_id=1, source_target_pairs={{1,0},{2,1},{3,2},{4,3},{5,4},{6,5},{7,6},{8,7},{9,8},{10,9},{11,1... | collective-permute-start | bytes 98312 | tf_op jit(solution)/shard_map/ppermute | solution.py:612
  53.5 3.6 %collective-permute-done.3.refs_4_ = f32[64,128]{1,0:T(8,128)S(1)} collective-permute-done((f32[64,128]{1,0:T(8,128)S(1)}, f32[64,128]{1,0:T(8,128)S(1)}, u32[]{:S(2)}, u32[]{:S(2)}) %collective-permute-start.3) | collective-permute-done | bytes 32800 | tf_op jit(solution)/shard_map/ppermute | solution.py:612
  57.1 1.9 collective-permute-start.6
  62.1 3.6 %fine_down.1 = (f32[64,64]{1,0:T(8,128)S(1)}, f32[16,40,128]{2,1,0:T(8,128)S(1)}) custom-call(s32[1,1]{1,0:T(1,128)} %bitcast.refs_0_, f32[64,64]{1,0:T(8,128)S(1)} %copy-done.19, f32[64,128]{1,0:T(8,128)S(1)} %copy-done.21, f32[64,128]{1,0:T(8,128)S(1)} %collective-permute-done.2.refs_3_, f32[64,128]{1,0:T(8,128)S(1)} %collective-permute-done.3.refs_4_, ...), custom_call_target="tpu_custom_call" | custom-call | tf_op jit(solution)/shard_map/fine_down/pallas_call | solution.py:51
  67.0 3.7 %all-to-all-start = ((f32[16,40,128]{2,1,0:T(8,128)}), f32[16,40,128]{2,1,0:T(8,128)S(1)}, u32[]{:S(2)}, u32[]{:S(2)}) async-start(f32[16,40,128]{2,1,0:T(8,128)} %copy-done.11), calls=%async_computation | async-start | bytes 655360 | tf_op jit(solution)/shard_map/all_to_all | solution.py:603
  70.7 1.9 collective-permute-start.7
  72.7 5.0 %all-to-all-done.refs_1_ = f32[16,40,128]{2,1,0:T(8,128)S(1)} async-done(((f32[16,40,128]{2,1,0:T(8,128)}), f32[16,40,128]{2,1,0:T(8,128)S(1)}, u32[]{:S(2)}, u32[]{:S(2)}) %all-to-all-start) | async-done | bytes 327712 | tf_op jit(solution)/shard_map/all_to_all | solution.py:603
  77.7 2.6 %line_windows.1 = f32[32,32,128]{2,1,0:T(8,128)} custom-call(s32[1,2]{1,0:T(1,128)S(1)} %add_bitcast_fusion.refs_0_, f32[16,40,128]{2,1,0:T(8,128)S(1)} %all-to-all-done.refs_1_), custom_call_target="tpu_custom_call" | custom-call | tf_op jit(solution)/shard_map/line_windows/pallas_call | solution.py:51
  80.9 11.4 %all-to-all-start.1 = ((f32[32,32,128]{2,1,0:T(8,128)}), f32[32,32,128]{2,1,0:T(8,128)S(1)}, u32[]{:S(2)}, u32[]{:S(2)}) async-start(f32[32,32,128]{2,1,0:T(8,128)} %line_windows.1), calls=%async_computation.1 | async-start | bytes 1048576 | tf_op jit(solution)/shard_map/all_to_all | solution.py:607
  93.1 2.6 %pad_maximum_fusion = f32[4120,128]{1,0:T(8,128)} fusion(f32[64,128]{1,0:T(8,128)S(1)} %slice.7, f32[1352,128]{1,0:T(8,128)} %collective-permute-done.5.refs_4_, f32[1352,128]{1,0:T(8,128)S(1)} %collective-permute-done.4.refs_3_, f32[1352,128]{1,0:T(8,128)S(1)} %get-tuple-element.61.refs_2_), kind=kLoop, calls=%fused_computation | loop fusion | flops 1582080 | bytes 4218880 | tf_op jit(solution)/shard_map/concatenate | solution.py:690
  95.7 2.2 collective-permute-start.8
  97.9 28.2 %all-to-all-done.1.refs_0_ = f32[32,32,128]{2,1,0:T(8,128)S(1)} async-done(((f32[32,32,128]{2,1,0:T(8,128)}), f32[32,32,128]{2,1,0:T(8,128)S(1)}, u32[]{:S(2)}, u32[]{:S(2)}) %all-to-all-start.1) | async-done | bytes 524320 | tf_op jit(solution)/shard_map/all_to_all | solution.py:607
  126.9 5.6 %all-to-all-start.2 = ((f32[16,32,128]{2,1,0:T(8,128)}), f32[16,32,128]{2,1,0:T(8,128)S(1)}, u32[]{:S(2)}, u32[]{:S(2)}) async-start(f32[16,32,128]{2,1,0:T(8,128)} %copy-done.6), calls=%async_computation.2 | async-start | bytes 524288 | tf_op jit(solution)/shard_map/all_to_all | solution.py:603
  132.5 7.2 %all-to-all-done.2.refs_1_ = f32[16,32,128]{2,1,0:T(8,128)S(1)} async-done(((f32[16,32,128]{2,1,0:T(8,128)}), f32[16,32,128]{2,1,0:T(8,128)S(1)}, u32[]{:S(2)}, u32[]{:S(2)}) %all-to-all-start.2) | async-done | bytes 262176 | tf_op jit(solution)/shard_map/all_to_all | solution.py:603
  140.4 14.7 %level_cycle.1 = f32[32,2,256]{2,1,0:T(2,128)S(1)} custom-call(s32[1,2]{1,0:T(1,128)S(1)} %add_bitcast_fusion.refs_0_, f32[16,32,128]{2,1,0:T(8,128)S(1)} %all-to-all-done.2.refs_1_, f32[1352,128]{1,0:T(8,128)S(1)} %get-tuple-element.61.refs_2_, f32[1352,128]{1,0:T(8,128)S(1)} %collective-permute-done.4.refs_3_, f32[1352,128]{1,0:T(8,128)} %collective-permute-done.5.refs_4_, ...), custom_call_target="tpu_custom_call" | custom-call | tf_op jit(solution)/shard_map/level_cycle/pallas_call | solution.py:51
  155.2 17.4 %all_to_all.25 = f32[32,2,256]{2,1,0:T(2,128)S(1)} all-to-all(f32[32,2,256]{2,1,0:T(2,128)S(1)} %level_cycle.1), channel_id=1, replica_groups={{0,4,8,12,16,20,24,28,32,36,40,44,48,52,56,60,64,68,72,76,80,84,88,92,9..., dimensions={0} | all-to-all | bytes 131072 | tf_op jit(solution)/shard_map/all_to_all | solution.py:607
  173.0 18.9 %all_to_all.26 = f32[16,32,2,256]{3,2,1,0:T(2,128)S(1)} all-to-all(f32[16,32,2,256]{3,2,1,0:T(2,128)S(1)} %broadcast_in_dim.4), channel_id=1, replica_groups={{0,1,2,3,128,129,130,131,256,257,258,259,384,385,386,387},{4,5,6,7,132,..., dimensions={0} | all-to-all | bytes 2097152 | tf_op jit(solution)/shard_map/all_to_all | solution.py:603
  193.3 2.2 collective-permute-start.9
  195.5 7.6 %collective-permute-start.10 = (f32[64,128]{1,0:T(8,128)S(1)}, f32[64,128]{1,0:T(8,128)S(1)}, u32[]{:S(2)}, u32[]{:S(2)}) collective-permute-start(f32[64,128]{1,0:T(8,128)S(1)} %fine_up.1.refs_1_), channel_id=1, source_target_pairs={{1,0},{2,1},{3,2},{4,3},{5,4},{6,5},{7,6},{8,7},{9,8},{10,9},{11,1... | collective-permute-start | bytes 98312 | tf_op jit(solution)/shard_map/ppermute | solution.py:612
  203.1 1.6 collective-permute-done.10.refs_3_
  204.7 1.9 fine_middle.1
  206.6 1.9 collective-permute-start.11
  208.5 7.9 %collective-permute-start.12 = (f32[64,128]{1,0:T(8,128)S(1)}, f32[64,128]{1,0:T(8,128)S(1)}, u32[]{:S(2)}, u32[]{:S(2)}) collective-permute-start(f32[64,128]{1,0:T(8,128)S(1)} %get-tuple-element.69.refs_2_), channel_id=1, source_target_pairs={{1,0},{2,1},{3,2},{4,3},{5,4},{6,5},{7,6},{8,7},{9,8},{10,9},{11,1... | collective-permute-start | bytes 98312 | tf_op jit(solution)/shard_map/ppermute | solution.py:612
  216.4 1.6 collective-permute-done.12.refs_4_
  218.0 2.6 %fine_end.1 = (f32[4,1024]{1,0:T(4,128)}, f32[4,1024]{1,0:T(4,128)}) custom-call(s32[1,1]{1,0:T(1,128)} %bitcast.refs_0_, f32[64,64]{1,0:T(8,128)S(1)} %get-tuple-element.68.refs_1_, f32[64,128]{1,0:T(8,128)S(1)} %get-tuple-element.69.refs_2_, f32[64,128]{1,0:T(8,128)S(1)} %collective-permute-done.11.refs_3_, f32[64,128]{1,0:T(8,128)S(1)} %collective-permute-done.12.refs_4_, ...), custom_call_target="tpu_custom_call" | custom-call | tf_op jit(solution)/shard_map/fine_end/pallas_call | solution.py:51
  (87 shorter events, 25.2 us)
Async XLA Ops:
  0.6 58.4 %copy-start.30 = (s32[16,2]{0,1:T(2,128)S(1)}, s32[16,2]{0,1:T(2,128)}, u32[]{:S(2)}) copy-start(s32[16,2]{0,1:T(2,128)} %param.18) | copy-start | bytes 388
  0.6 58.5 %copy-start.31 = (s32[16,2]{0,1:T(2,128)S(1)}, s32[16,2]{0,1:T(2,128)}, u32[]{:S(2)}) copy-start(s32[16,2]{0,1:T(2,128)} %param.19) | copy-start | bytes 388
  1.4 1.1 copy-start
  6.5 29.2 %collective-permute-start = (f32[4,8,4096]{2,1,0:T(8,128)}, f32[4,8,4096]{2,1,0:T(8,128)S(1)}, u32[]{:S(2)}, u32[]{:S(2)}) collective-permute-start(f32[4,8,4096]{2,1,0:T(8,128)} %get-tuple-element.39), channel_id=1, source_target_pairs={{0,1},{1,2},{2,3},{3,4},{4,5},{5,6},{6,7},{7,8},{8,9},{9,10},{10,1... | collective-permute-start | bytes 1572872 | tf_op jit(solution)/shard_map/ppermute | solution.py:612
  9.9 25.8 %collective-permute-start.1 = (f32[4,8,4096]{2,1,0:T(8,128)}, f32[4,8,4096]{2,1,0:T(8,128)S(1)}, u32[]{:S(2)}, u32[]{:S(2)}) collective-permute-start(f32[4,8,4096]{2,1,0:T(8,128)} %get-tuple-element.40), channel_id=1, source_target_pairs={{1,0},{2,1},{3,2},{4,3},{5,4},{6,5},{7,6},{8,7},{9,8},{10,9},{11,1... | collective-permute-start | bytes 1572872 | tf_op jit(solution)/shard_map/ppermute | solution.py:612
  22.1 1.0 copy-start.10
  23.1 0.9 copy-start.12
  24.0 0.9 copy-start.15
  27.6 39.4 %collective-permute-start.4 = (f32[1352,128]{1,0:T(8,128)S(1)}, f32[1352,128]{1,0:T(8,128)S(1)}, u32[]{:S(2)}, u32[]{:S(2)}) collective-permute-start(f32[1352,128]{1,0:T(8,128)S(1)} %get-tuple-element.61.refs_2_), channel_id=1, source_target_pairs={{0,8},{4,12},{8,16},{12,20},{16,24},{20,28},{24,32},{28,36},{32,40... | collective-permute-start | bytes 2076680 | tf_op jit(solution)/shard_map/ppermute | solution.py:612
  29.6 37.5 %collective-permute-start.5 = (f32[1352,128]{1,0:T(8,128)S(1)}, f32[1352,128]{1,0:T(8,128)}, u32[]{:S(2)}, u32[]{:S(2)}) collective-permute-start(f32[1352,128]{1,0:T(8,128)S(1)} %get-tuple-element.61.refs_2_), channel_id=1, source_target_pairs={{8,0},{12,4},{16,8},{20,12},{24,16},{28,20},{32,24},{36,28},{40,32... | collective-permute-start | bytes 2076680 | tf_op jit(solution)/shard_map/ppermute | solution.py:612
  36.4 1.1 copy-start.1
  37.6 1.0 copy-start.8
  38.6 0.9 copy-start.14
  43.1 10.4 %collective-permute-start.2 = (f32[64,128]{1,0:T(8,128)S(1)}, f32[64,128]{1,0:T(8,128)S(1)}, u32[]{:S(2)}, u32[]{:S(2)}) collective-permute-start(f32[64,128]{1,0:T(8,128)S(1)} %get-tuple-element.42.refs_2_), channel_id=1, source_target_pairs={{0,1},{1,2},{2,3},{3,4},{4,5},{5,6},{6,7},{7,8},{8,9},{9,10},{10,1... | collective-permute-start | bytes 98312 | tf_op jit(solution)/shard_map/ppermute | solution.py:612
  45.0 12.1 %collective-permute-start.3 = (f32[64,128]{1,0:T(8,128)S(1)}, f32[64,128]{1,0:T(8,128)S(1)}, u32[]{:S(2)}, u32[]{:S(2)}) collective-permute-start(f32[64,128]{1,0:T(8,128)S(1)} %get-tuple-element.42.refs_2_), channel_id=1, source_target_pairs={{1,0},{2,1},{3,2},{4,3},{5,4},{6,5},{7,6},{8,7},{9,8},{10,9},{11,1... | collective-permute-start | bytes 98312 | tf_op jit(solution)/shard_map/ppermute | solution.py:612
  57.1 23.8 %collective-permute-start.6 = (f32[1160,128]{1,0:T(8,128)}, f32[1160,128]{1,0:T(8,128)}, u32[]{:S(2)}, u32[]{:S(2)}) collective-permute-start(f32[1160,128]{1,0:T(8,128)} %copy-done.29), channel_id=1, source_target_pairs={{4,16},{12,24},{16,4},{20,32},{24,12},{28,40},{32,20},{36,48},{40,... | collective-permute-start | bytes 1781768 | tf_op jit(solution)/shard_map/ppermute | solution.py:664
  59.2 1.0 copy-start.9
  60.5 6.5 %copy-start.2 = (bf16[2,512,128]{2,1,0:T(8,128)(2,1)}, bf16[2,512,128]{2,1,0:T(8,128)(2,1)S(1)}, u32[]{:S(2)}) copy-start(bf16[2,512,128]{2,1,0:T(8,128)(2,1)S(1)} %get-tuple-element.52.refs_11_.hi_ref) | copy-start | bytes 786436
  60.5 6.5 %copy-start.4 = (bf16[2,512,128]{2,1,0:T(8,128)(2,1)}, bf16[2,512,128]{2,1,0:T(8,128)(2,1)S(1)}, u32[]{:S(2)}) copy-start(bf16[2,512,128]{2,1,0:T(8,128)(2,1)S(1)} %get-tuple-element.53.refs_12_.lo_ref) | copy-start | bytes 786436
  67.0 10.7 %all-to-all-start = ((f32[16,40,128]{2,1,0:T(8,128)}), f32[16,40,128]{2,1,0:T(8,128)S(1)}, u32[]{:S(2)}, u32[]{:S(2)}) async-start(f32[16,40,128]{2,1,0:T(8,128)} %copy-done.11), calls=%async_computation | async-start | bytes 655360 | tf_op jit(solution)/shard_map/all_to_all | solution.py:603
  70.7 9.6 %collective-permute-start.7 = (f32[64,128]{1,0:T(8,128)S(1)}, f32[64,128]{1,0:T(8,128)S(1)}, u32[]{:S(2)}, u32[]{:S(2)}) collective-permute-start(f32[64,128]{1,0:T(8,128)S(1)} %slice.6), channel_id=1, source_target_pairs={{0,16},{8,24},{16,32},{20,4},{24,40},{28,12},{32,48},{36,20},{40,5... | collective-permute-start | bytes 98312 | tf_op jit(solution)/shard_map/ppermute | solution.py:664
  80.9 45.2 %all-to-all-start.1 = ((f32[32,32,128]{2,1,0:T(8,128)}), f32[32,32,128]{2,1,0:T(8,128)S(1)}, u32[]{:S(2)}, u32[]{:S(2)}) async-start(f32[32,32,128]{2,1,0:T(8,128)} %line_windows.1), calls=%async_computation.1 | async-start | bytes 1048576 | tf_op jit(solution)/shard_map/all_to_all | solution.py:607
  95.7 36.7 %collective-permute-start.8 = (f32[4120,128]{1,0:T(8,128)}, f32[4120,128]{1,0:T(8,128)}, u32[]{:S(2)}, u32[]{:S(2)}) collective-permute-start(f32[4120,128]{1,0:T(8,128)} %pad_maximum_fusion), channel_id=1, source_target_pairs={{0,4},{4,0},{8,12},{12,8},{16,20},{20,16},{24,28},{28,24},{32,36},... | collective-permute-start | bytes 6328328 | tf_op jit(solution)/shard_map/ppermute | solution.py:691
  126.9 12.8 %all-to-all-start.2 = ((f32[16,32,128]{2,1,0:T(8,128)}), f32[16,32,128]{2,1,0:T(8,128)S(1)}, u32[]{:S(2)}, u32[]{:S(2)}) async-start(f32[16,32,128]{2,1,0:T(8,128)} %copy-done.6), calls=%async_computation.2 | async-start | bytes 524288 | tf_op jit(solution)/shard_map/all_to_all | solution.py:603
  155.1 36.8 %copy-start.3 = (bf16[2,512,128]{2,1,0:T(8,128)(2,1)S(1)}, bf16[2,512,128]{2,1,0:T(8,128)(2,1)}, u32[]{:S(2)}) copy-start(bf16[2,512,128]{2,1,0:T(8,128)(2,1)} %copy-done.2) | copy-start | bytes 786436
  155.1 36.8 %copy-start.5 = (bf16[2,512,128]{2,1,0:T(8,128)(2,1)S(1)}, bf16[2,512,128]{2,1,0:T(8,128)(2,1)}, u32[]{:S(2)}) copy-start(bf16[2,512,128]{2,1,0:T(8,128)(2,1)} %copy-done.4) | copy-start | bytes 786436
  155.2 36.8 %copy-start.25 = (f32[64,64]{1,0:T(8,128)S(1)}, f32[64,64]{1,0:T(8,128)}, u32[]{:S(2)}) copy-start(f32[64,64]{1,0:T(8,128)} %copy-done.24) | copy-start | bytes 49156
  173.0 31.7 %copy-start.23 = (f32[64,128]{1,0:T(8,128)S(1)}, f32[64,128]{1,0:T(8,128)}, u32[]{:S(2)}) copy-start(f32[64,128]{1,0:T(8,128)} %copy-done.22) | copy-start | bytes 98308
  193.3 9.8 %collective-permute-start.9 = (f32[64,128]{1,0:T(8,128)S(1)}, f32[64,128]{1,0:T(8,128)S(1)}, u32[]{:S(2)}, u32[]{:S(2)}) collective-permute-start(f32[64,128]{1,0:T(8,128)S(1)} %fine_up.1.refs_1_), channel_id=1, source_target_pairs={{0,1},{1,2},{2,3},{3,4},{4,5},{5,6},{6,7},{7,8},{8,9},{9,10},{10,1... | collective-permute-start | bytes 98312 | tf_op jit(solution)/shard_map/ppermute | solution.py:612
  195.5 9.2 %collective-permute-start.10 = (f32[64,128]{1,0:T(8,128)S(1)}, f32[64,128]{1,0:T(8,128)S(1)}, u32[]{:S(2)}, u32[]{:S(2)}) collective-permute-start(f32[64,128]{1,0:T(8,128)S(1)} %fine_up.1.refs_1_), channel_id=1, source_target_pairs={{1,0},{2,1},{3,2},{4,3},{5,4},{6,5},{7,6},{8,7},{9,8},{10,9},{11,1... | collective-permute-start | bytes 98312 | tf_op jit(solution)/shard_map/ppermute | solution.py:612
  206.6 9.8 %collective-permute-start.11 = (f32[64,128]{1,0:T(8,128)S(1)}, f32[64,128]{1,0:T(8,128)S(1)}, u32[]{:S(2)}, u32[]{:S(2)}) collective-permute-start(f32[64,128]{1,0:T(8,128)S(1)} %get-tuple-element.69.refs_2_), channel_id=1, source_target_pairs={{0,1},{1,2},{2,3},{3,4},{4,5},{5,6},{6,7},{7,8},{8,9},{9,10},{10,1... | collective-permute-start | bytes 98312 | tf_op jit(solution)/shard_map/ppermute | solution.py:612
  208.5 9.5 %collective-permute-start.12 = (f32[64,128]{1,0:T(8,128)S(1)}, f32[64,128]{1,0:T(8,128)S(1)}, u32[]{:S(2)}, u32[]{:S(2)}) collective-permute-start(f32[64,128]{1,0:T(8,128)S(1)} %get-tuple-element.69.refs_2_), channel_id=1, source_target_pairs={{1,0},{2,1},{3,2},{4,3},{5,4},{6,5},{7,6},{8,7},{9,8},{10,9},{11,1... | collective-permute-start | bytes 98312 | tf_op jit(solution)/shard_map/ppermute | solution.py:612
  (16 other events, 11.2 us)
